TPU v7x, 256 devices: a whole 4x4x8 slice. The times are simulated.
256 devices in a mesh: kmer: 16 (over y, z_hi), samp: 16 (over z_lo, x, core).
Axes of the slice: x: 4, y: 4, z: 8 (z_hi: 4, z_lo: 2; z = z_hi * 2 + z_lo), core: 2. Of those that a mesh axis runs over, the one named last changes fastest.
Arguments:
- tiles: bfloat16 [22528, 128, 128], P(('kmer', 'samp')), may hold values from 0 to 8
- omega: bfloat16 [16384, 128], P('samp'), may hold values from -0.5 to 0.5
- tile_rows: int32 [22528], P(('kmer', 'samp')), may hold values from 0 to 55, as said below
- tile_cols: int32 [22528], P(('kmer', 'samp')), may hold values from 0 to 7
- tile_count: int32 [256], P(('kmer', 'samp')), may hold values from 11 to 88, as said below
Outputs:
- sketch: bfloat16 [114688, 128], P(('kmer', 'samp'))
- co_sketch: float32 [16384, 128], P(('samp', 'kmer'))
Inputs may be any that keep to these rules, and one draw needn't show every extreme that they name: `tile_rows`: on each device the used slots name distinct pairs of k-mer block and sample block. `tile_count`: at least one device uses all 88 slots.
All inputs are finite; a program needn't handle non-finite values.
Results may differ from a plain program's by a relative error of at most 0.014.
Values may be sent and summed in bfloat16 or wider, within the bound.
No kernel may reach another device: no remote copies, remote signals or barrier semaphores. Data moves between devices by JAX's collectives and lax.ppermute only.
A program may use at most 64 MiB of HBM per device.

v0:
```python
import jax
import jax.numpy as jnp
from jax import lax
from jax.sharding import PartitionSpec as P

KB_DEV = 56


def forward_terms(tiles, table, tile_rows, tile_cols, count, out_blocks):
    slot_total = tiles.shape[0]
    live = lax.iota(jnp.int32, slot_total) < count
    chosen = table[tile_cols]
    prod = jnp.einsum("tkc,tcr->tkr", tiles, chosen, preferred_element_type=jnp.float32)
    prod = jnp.where(live[:, None, None], prod, jnp.float32(0.0))
    return jax.ops.segment_sum(prod, tile_rows, num_segments=out_blocks)


def backward_terms(tiles, table, tile_rows, tile_cols, count, out_blocks):
    slot_total = tiles.shape[0]
    live = lax.iota(jnp.int32, slot_total) < count
    picked = table[tile_rows]
    prod = jnp.einsum("tkc,tkr->tcr", tiles, picked, preferred_element_type=jnp.float32)
    prod = jnp.where(live[:, None, None], prod, jnp.float32(0.0))
    return jax.ops.segment_sum(prod, tile_cols, num_segments=out_blocks)


def shards(tiles, omega, tile_rows, tile_cols, tile_count):
    tile = tiles.shape[1]
    rank = omega.shape[1]
    sample_blocks = omega.shape[0] // tile
    count = tile_count[0]
    omega_blocks = omega.reshape(sample_blocks, tile, rank)
    partial_rows = forward_terms(tiles, omega_blocks, tile_rows, tile_cols, count, KB_DEV)
    partial_rows = partial_rows.reshape(KB_DEV * tile, rank)
    summed = lax.psum(partial_rows.astype(jnp.bfloat16), "samp")
    own_rows = summed.shape[0] // lax.axis_size("samp")
    sketch = lax.dynamic_slice_in_dim(summed, lax.axis_index("samp") * own_rows, own_rows, 0)
    sketch_blocks = summed.reshape(KB_DEV, tile, rank)
    co_partial = backward_terms(tiles, sketch_blocks, tile_rows, tile_cols, count, sample_blocks)
    co_partial = co_partial.reshape(sample_blocks * tile, rank)
    factor = 1.0 / (KB_DEV * tile * lax.axis_size("kmer")) ** 0.5
    co_total = lax.psum(co_partial.astype(jnp.bfloat16), "kmer").astype(jnp.float32)
    share_rows = co_total.shape[0] // lax.axis_size("kmer")
    co_sketch = lax.dynamic_slice_in_dim(
        co_total, lax.axis_index("kmer") * share_rows, share_rows, 0
    ) * jnp.float32(factor)
    return (sketch, co_sketch)


def solution(mesh):
    placed = (
        P(("kmer", "samp"), None, None),
        P("samp", None),
        P(("kmer", "samp")),
        P(("kmer", "samp")),
        P(("kmer", "samp")),
    )
    return jax.shard_map(
        shards,
        mesh=mesh,
        in_specs=placed,
        out_specs=(P(("kmer", "samp"), None), P(("samp", "kmer"), None)),
        check_vma=False,
    )
```

profile of v0, /device:TPU:24, one launch (start us, length us, event | category | flops | bytes accessed | tf_op | source)
XLA Modules:
  0.0 381.4 jit_solution(12764706739560385234)
XLA Ops:
  7.2 0.0 copy-start
  7.2 0.0 all-reduce.3.cloned.1.call-start
  8.0 0.7 compare_select_fusion.1
  8.7 3.6 gather_fusion
  12.3 0.0 copy-done
  12.3 6.6 %select_bitcast_fusion.1 = f32[88,128,128]{1,2,0:T(8,128)} fusion(pred[88]{0:T(512)(128)(4,1)S(1)} %iota_compare_fusion, bf16[88,128,128]{2,1,0:T(8,128)(2,1)} %gather_fusion, bf16[88,128,128]{2,1,0:T(8,128)(2,1)S(1)} %copy-done), kind=kOutput, calls=%fused_computation.5 | convolution fusion | flops 370540544 | bytes 11534424 | tf_op jit(solution)/shard_map/tkc,tcr->tkr/dot_general | solution.py:13
  18.9 6.3 %copy.10 = f32[88,128,128]{2,1,0:T(8,128)} copy(f32[88,128,128]{1,2,0:T(8,128)} %select_bitcast_fusion.1) | data formatting | bytes 11534336 | tf_op jit(solution)/shard_map/jit(_where)/select_n | solution.py:14
  25.1 0.0 copy-start.1
  25.1 2.3 broadcast_in_dim.36
  27.4 0.0 copy-done.1
  27.4 19.9 %scatter_fusion = f32[56,128,128]{2,1,0:T(8,128)} fusion(f32[56,128,128]{2,1,0:T(8,128)} %broadcast_in_dim.36, s32[88]{0:T(128)S(1)} %copy-done.1, f32[88,128,128]{2,1,0:T(8,128)} %copy.10), kind=kCustom, calls=%fused_computation.2 | custom fusion | flops 1441792 | bytes 17301856 | tf_op jit(solution)/shard_map/scatter-add | solution.py:15
  47.3 3.6 convert_element_type.15
  50.9 0.0 all-reduce.3.cloned.1.call-update
  50.9 0.0 all-reduce.5.cloned.1.call-start
  51.0 129.5 %all-reduce.3.cloned.1.call-done = bf16[7168,128]{1,0:T(8,128)(2,1)} async-done(((bf16[7168,128]{1,0:T(8,128)(2,1)}), bf16[7168,128]{1,0:T(8,128)(2,1)}) %all-reduce.3.cloned.1.call-update) | async-done | bytes 1835024 | tf_op jit(solution)/shard_map/psum | solution.py:35
  180.5 4.1 %gather_fusion.1 = bf16[88,128,128]{2,1,0:T(8,128)(2,1)} fusion(bf16[56,128,128]{2,1,0:T(8,128)(2,1)} %bitcast.16, s32[1024]{0:T(1024)S(1)} %pad_clamp_fusion), kind=kCustom, calls=%fused_computation.1 | custom fusion | bytes 5767520 | tf_op jit(solution)/shard_map/gather | solution.py:21
  184.6 5.7 %select_bitcast_fusion = f32[88,128,128]{1,2,0:T(8,128)} fusion(pred[88]{0:T(512)(128)(4,1)S(1)} %iota_compare_fusion, bf16[88,128,128]{2,1,0:T(8,128)(2,1)} %gather_fusion.1, bf16[88,128,128]{2,1,0:T(8,128)(2,1)S(1)} %copy-done), kind=kOutput, calls=%fused_computation.4 | convolution fusion | flops 370540544 | bytes 11534424 | tf_op jit(solution)/shard_map/tkc,tkr->tcr/dot_general | solution.py:22
  190.3 0.0 copy-start.2
  190.3 6.3 %copy.12 = f32[88,128,128]{2,1,0:T(8,128)} copy(f32[88,128,128]{1,2,0:T(8,128)} %select_bitcast_fusion) | data formatting | bytes 11534336 | tf_op jit(solution)/shard_map/jit(_where)/select_n | solution.py:23
  196.7 0.0 copy-done.2
  196.7 12.7 %scatter_fusion.1 = f32[8,128,128]{2,1,0:T(8,128)S(1)} fusion(f32[8,128,128]{2,1,0:T(8,128)S(1)} %broadcast_in_dim.41, s32[88]{0:T(128)S(1)} %copy-done.2, f32[88,128,128]{2,1,0:T(8,128)} %copy.12), kind=kCustom, calls=%fused_computation.3 | custom fusion | flops 1441792 | bytes 17301856 | tf_op jit(solution)/shard_map/scatter-add | solution.py:24
  209.4 0.7 convert_element_type.17
  210.1 0.0 all-reduce.5.cloned.1.call-update
  210.2 1.6 constant_dynamic-slice_fusion
  211.7 161.5 %all-reduce.5.cloned.1.call-done = bf16[1024,128]{1,0:T(8,128)(2,1)} async-done(((bf16[1024,128]{1,0:T(8,128)(2,1)}), bf16[1024,128]{1,0:T(8,128)(2,1)}) %all-reduce.5.cloned.1.call-update) | async-done | bytes 262160 | tf_op jit(solution)/shard_map/psum | solution.py:42
  373.2 1.3 convert_multiply_fusion
  (5 shorter events, 0.1 us)
Async XLA Ops:
  7.2 5.1 %copy-start = (bf16[88,128,128]{2,1,0:T(8,128)(2,1)S(1)}, bf16[88,128,128]{2,1,0:T(8,128)(2,1)}, u32[]{:S(2)}) copy-start(bf16[88,128,128]{2,1,0:T(8,128)(2,1)} %param.5) | copy-start | bytes 8650756
  7.2 173.3 %all-reduce.3.cloned.1.call-start = ((), (), s32[]{:S(2)}) async-start(), calls=%async_computation | async-start | bytes 3670016 | tf_op jit(solution)/shard_map/psum | solution.py:35
  25.1 2.3 copy-start.1
  50.9 322.2 %all-reduce.5.cloned.1.call-start = ((), (), s32[]{:S(2)}) async-start(), calls=%async_computation.1 | async-start | bytes 524288 | tf_op jit(solution)/shard_map/psum | solution.py:42
  190.3 6.4 %copy-start.2 = (s32[88]{0:T(128)S(1)}, s32[88]{0:T(128)}, u32[]{:S(2)}) copy-start(s32[88]{0:T(128)} %param.8) | copy-start | bytes 1060
Sparse Core Ops, SparseCore 0:
  51.1 129.3 all-reduce.2
  210.3 162.8 all-reduce.4
where the time goes:
time: 387 us; the launch traced here: 381 us
  waiting for transfers between devices  291 us (75%)
  other arithmetic  39 us (10%)
  local copies, waits for them, and re-layouts  24.2 us (6%)
  between operations  14.9 us (4%)
  matrix products  12.3 us (3%)
    psum x1, waiting for transfers between devices, shards(): lax.psum(co_partial.astype(jnp.bfloat16), 'kmer').astype(jnp.float32)  161 us
    psum x1, waiting for transfers between devices, shards(): summed = lax.psum(partial_rows.astype(jnp.bfloat16), 'samp')  129 us
    scatter-add x1, other arithmetic, forward_terms(): return jax.ops.segment_sum(prod, tile_rows, num_segments=out_blocks)  19.9 us
    scatter-add x1, other arithmetic, backward_terms(): return jax.ops.segment_sum(prod, tile_cols, num_segments=out_blocks)  12.7 us
  transfers between devices with their start and end apart: 2, of which 2 were waited for; matrix products, arithmetic and copies ran while one was open for 0% of the time, Pallas kernels for 0%

commit v1 on v0

v1 whole, which is shorter than its diff:
```python
import functools

import jax
import jax.numpy as jnp
from jax import lax
from jax.experimental import pallas as pl
from jax.experimental.pallas import tpu as pltpu
from jax.sharding import PartitionSpec as P

TILE = 128
KB_DEV = 56
SB_DEV = 8
HALF_BLOCKS = KB_DEV // 2
HALF = HALF_BLOCKS * TILE
CHUNK = HALF // 8
UNROLL = 4
VMEM_LIMIT = 48 * 1024 * 1024

ROUNDS = (
    ((2, 1), (2, 1)),
    ((1, 1), (3, 0)),
    ((3, 0), (1, 1)),
    ((1, 0), (3, 1)),
    ((3, 1), (1, 0)),
    ((2, 0), (0, 1)),
    ((0, 1), (2, 0)),
)


def vm():
    return pl.BlockSpec(memory_space=pltpu.VMEM)


def sm():
    return pl.BlockSpec(memory_space=pltpu.SMEM)


def params():
    return pltpu.CompilerParams(vmem_limit_bytes=VMEM_LIMIT)


def place():
    j = lax.axis_index("samp")
    return j // 8, (j // 2) % 4, j % 2


def pairs(r):
    out = []
    for s in range(16):
        z, x, c = s // 8, (s // 2) % 4, s % 2
        dx, dz = ROUNDS[r][c]
        out.append((s, (z ^ dz) * 8 + ((x + dx) % 4) * 2 + c))
    return out


def peer_chunk(r, sign):
    z, x, c = place()
    (dx0, dz0), (dx1, dz1) = ROUNDS[r]
    dx = jnp.where(c == 0, dx0, dx1) * sign
    dz = jnp.where(c == 0, dz0, dz1)
    zz = z + dz - 2 * z * dz
    return zz * 4 + (x + dx + 4) % 4


def select_slots(rows, cols, count, half, l_slot, l_row, l_col):
    def visit(s, n):
        row = rows[s] - half * HALF_BLOCKS
        l_slot[n] = s
        l_row[n] = row
        l_col[n] = cols[s]
        mine = jnp.logical_and(row >= 0, row < HALF_BLOCKS)
        return n + mine.astype(jnp.int32)

    n = lax.fori_loop(0, count[0], visit, jnp.int32(0))
    for u in range(UNROLL):
        l_slot[n + u] = 0
        l_row[n + u] = HALF_BLOCKS
        l_col[n + u] = SB_DEV
    return n


def block(i):
    return pl.ds(pl.multiple_of(i * TILE, TILE), TILE)


def forward_kernel(mine, rows, cols, count, tiles, omega, out, acc, l_slot, l_row, l_col):
    _, _, c = place()
    half = c if mine else 1 - c
    n = select_slots(rows, cols, count, half, l_slot, l_row, l_col)
    acc[...] = jnp.zeros_like(acc)

    def step(g, carry):
        prods = []
        for u in range(UNROLL):
            k = g * UNROLL + u
            col = jnp.minimum(l_col[k], SB_DEV - 1)
            prods.append(
                jnp.dot(tiles[l_slot[k]], omega[block(col), :], preferred_element_type=jnp.float32)
            )
        for u in range(UNROLL):
            where = block(l_row[g * UNROLL + u])
            acc[where, :] = acc[where, :] + prods[u]
        return carry

    lax.fori_loop(0, (n + UNROLL - 1) // UNROLL, step, 0)
    out[...] = acc[pl.ds(0, HALF), :].astype(jnp.bfloat16)


def forward(mine, rows, cols, count, tiles, omega):
    cap = tiles.shape[0]
    return pl.pallas_call(
        functools.partial(forward_kernel, mine),
        out_shape=jax.ShapeDtypeStruct((HALF, TILE), jnp.bfloat16),
        in_specs=[sm(), sm(), sm(), vm(), vm()],
        out_specs=vm(),
        scratch_shapes=[pltpu.VMEM((HALF + TILE, TILE), jnp.float32)]
        + [pltpu.SMEM((cap + UNROLL,), jnp.int32)] * 3,
        compiler_params=params(),
        name="forward_mine" if mine else "forward_other",
    )(rows, cols, count, tiles, omega)


def turn_kernel(tiles, out):
    def one(s, carry):
        out[s] = tiles[s].T
        return carry

    lax.fori_loop(0, tiles.shape[0], one, 0, unroll=4)


def turn(tiles):
    return pl.pallas_call(
        turn_kernel,
        out_shape=jax.ShapeDtypeStruct(tiles.shape, tiles.dtype),
        in_specs=[vm()],
        out_specs=vm(),
        compiler_params=params(),
        name="turn_tiles",
    )(tiles)


def chunk_at(i):
    return pl.ds(pl.multiple_of(i * CHUNK, CHUNK), CHUNK)


def pair_kernel(a, b, own, *sends):
    def total(i):
        at = chunk_at(i)
        return (a[at, :].astype(jnp.float32) + b[at, :].astype(jnp.float32)).astype(jnp.bfloat16)

    z, x, _ = place()
    for r, send in enumerate(sends):
        send[...] = total(peer_chunk(r, 1))
    own[...] = total(z * 4 + x)


def pair_sum(a, b):
    shape = jax.ShapeDtypeStruct((CHUNK, TILE), jnp.bfloat16)
    return pl.pallas_call(
        pair_kernel,
        out_shape=[shape] * 8,
        in_specs=[vm(), vm()],
        out_specs=[vm()] * 8,
        compiler_params=params(),
        name="pair_sum",
    )(a, b)


def chunk_kernel(*refs):
    out = refs[-1]
    total = refs[0][...].astype(jnp.float32)
    for ref in refs[1:-1]:
        total = total + ref[...].astype(jnp.float32)
    out[...] = total.astype(jnp.bfloat16)


def chunk_sum(parts):
    return pl.pallas_call(
        chunk_kernel,
        out_shape=jax.ShapeDtypeStruct((CHUNK, TILE), jnp.bfloat16),
        in_specs=[vm()] * len(parts),
        out_specs=vm(),
        compiler_params=params(),
        name="chunk_sum",
    )(*parts)


def gather_kernel(*refs):
    z, x, _ = place()
    out = refs[-1]
    out[chunk_at(z * 4 + x), :] = refs[0][...]
    for r, ref in enumerate(refs[1:-1]):
        out[chunk_at(peer_chunk(r, -1)), :] = ref[...]


def gather_half(own, got):
    return pl.pallas_call(
        gather_kernel,
        out_shape=jax.ShapeDtypeStruct((HALF, TILE), jnp.bfloat16),
        in_specs=[vm()] * 8,
        out_specs=vm(),
        compiler_params=params(),
        name="gather_half",
    )(own, *got)


def backward_slots(n, l_slot, l_row, l_col, turned, table, acc):
    def step(g, carry):
        prods = []
        for u in range(UNROLL):
            k = g * UNROLL + u
            row = jnp.minimum(l_row[k], HALF_BLOCKS - 1)
            prods.append(
                jnp.dot(turned[l_slot[k]], table[block(row), :], preferred_element_type=jnp.float32)
            )
        for u in range(UNROLL):
            where = block(l_col[g * UNROLL + u])
            acc[where, :] = acc[where, :] + prods[u]
        return carry

    lax.fori_loop(0, (n + UNROLL - 1) // UNROLL, step, 0)


def backward_mine_kernel(rows, cols, count, turned, table, out, l_slot, l_row, l_col):
    _, _, c = place()
    n = select_slots(rows, cols, count, c, l_slot, l_row, l_col)
    out[...] = jnp.zeros_like(out)
    backward_slots(n, l_slot, l_row, l_col, turned, table, out)


def backward_mine(rows, cols, count, turned, table):
    cap = turned.shape[0]
    return pl.pallas_call(
        backward_mine_kernel,
        out_shape=jax.ShapeDtypeStruct(((SB_DEV + 1) * TILE, TILE), jnp.float32),
        in_specs=[sm(), sm(), sm(), vm(), vm()],
        out_specs=vm(),
        scratch_shapes=[pltpu.SMEM((cap + UNROLL,), jnp.int32)] * 3,
        compiler_params=params(),
        name="backward_mine",
    )(rows, cols, count, turned, table)


def backward_other_kernel(
    rows, cols, count, turned, first, own, table, out, sketch, acc, l_slot, l_row, l_col
):
    z, x, c = place()
    n = select_slots(rows, cols, count, 1 - c, l_slot, l_row, l_col)
    acc[...] = first[...]
    backward_slots(n, l_slot, l_row, l_col, turned, table, acc)
    out[...] = acc[pl.ds(0, SB_DEV * TILE), :].astype(jnp.bfloat16)
    at = chunk_at(x * 2 + c)

    @pl.when(z == c)
    def _():
        sketch[...] = own[at, :]

    @pl.when(z != c)
    def _():
        sketch[...] = table[at, :]


def backward_other(rows, cols, count, turned, first, own, table):
    cap = turned.shape[0]
    return pl.pallas_call(
        backward_other_kernel,
        out_shape=[
            jax.ShapeDtypeStruct((SB_DEV * TILE, TILE), jnp.bfloat16),
            jax.ShapeDtypeStruct((CHUNK, TILE), jnp.bfloat16),
        ],
        in_specs=[sm(), sm(), sm(), vm(), vm(), vm(), vm()],
        out_specs=[vm(), vm()],
        scratch_shapes=[pltpu.VMEM(((SB_DEV + 1) * TILE, TILE), jnp.float32)]
        + [pltpu.SMEM((cap + UNROLL,), jnp.int32)] * 3,
        compiler_params=params(),
        name="backward_other",
    )(rows, cols, count, turned, first, own, table)


def last_kernel(factor, parts, out):
    total = parts[0].astype(jnp.float32)
    for i in range(1, parts.shape[0]):
        total = total + parts[i].astype(jnp.float32)
    out[...] = total * factor


def last_sum(factor, parts):
    return pl.pallas_call(
        functools.partial(last_kernel, factor),
        out_shape=jax.ShapeDtypeStruct(parts.shape[1:], jnp.float32),
        in_specs=[vm()],
        out_specs=vm(),
        compiler_params=params(),
        name="last_sum",
    )(parts)


def shards(tiles, omega, tile_rows, tile_cols, tile_count):
    swap = [(s, s ^ 1) for s in range(16)]
    kmers = lax.axis_size("kmer")
    other = forward(False, tile_rows, tile_cols, tile_count, tiles, omega)
    mine = forward(True, tile_rows, tile_cols, tile_count, tiles, omega)
    got = lax.ppermute(other, "samp", swap)
    own, *sends = pair_sum(mine, got)
    turned = turn(tiles)
    parts = [lax.ppermute(s, "samp", pairs(r)) for r, s in enumerate(sends)]
    chunk = chunk_sum([own, *parts])
    pieces = [lax.ppermute(chunk, "samp", pairs(r)) for r in range(7)]
    own_half = gather_half(chunk, pieces)
    other_half = lax.ppermute(own_half, "samp", swap)
    first = backward_mine(tile_rows, tile_cols, tile_count, turned, own_half)
    zpart, sketch = backward_other(
        tile_rows, tile_cols, tile_count, turned, first, own_half, other_half
    )
    shares = lax.all_to_all(zpart.reshape(kmers, -1, TILE), "kmer", 0, 0)
    factor = 1.0 / (KB_DEV * TILE * kmers) ** 0.5
    return sketch, last_sum(factor, shares)


def solution(mesh):
    placed = (
        P(("kmer", "samp"), None, None),
        P("samp", None),
        P(("kmer", "samp")),
        P(("kmer", "samp")),
        P(("kmer", "samp")),
    )
    return jax.shard_map(
        shards,
        mesh=mesh,
        in_specs=placed,
        out_specs=(P(("kmer", "samp"), None), P(("samp", "kmer"), None)),
        check_vma=False,
    )
```

time: 387 us -> 78.8 us (0.20)
  the two profiles are of different devices: /device:TPU:24 before, /device:TPU:4 now
where the time goes in v1:
time: 78.8 us; the launch traced here: 78.1 us
  blocking collectives  27 us (34%)
  starting transfers between devices  24.5 us (31%)
  waiting for transfers between devices  11.8 us (15%)
  Pallas kernels  9.34 us (12%)
  local copies, waits for them, and re-layouts  4.08 us (5%)
  between operations  1.41 us (2%)
    all_to_all x1, blocking collectives, shards(): shares = lax.all_to_all(zpart.reshape(kmers, -1, TILE), 'kmer', 0, 0)  27 us
    ppermute x7, starting transfers between devices, shards(): parts = [lax.ppermute(s, 'samp', pairs(r)) for r, s in enumerate(sends)]  14.4 us
    ppermute x7, starting transfers between devices, shards(): pieces = [lax.ppermute(chunk, 'samp', pairs(r)) for r in range(7)]  9.92 us
    ppermute x7, waiting for transfers between devices, shards(): parts = [lax.ppermute(s, 'samp', pairs(r)) for r, s in enumerate(sends)]  6.26 us
    ppermute x7, waiting for transfers between devices, shards(): pieces = [lax.ppermute(chunk, 'samp', pairs(r)) for r in range(7)]  4.57 us
    unnamed x10, local copies, waits for them, and re-layouts  4.08 us
    pallas_call x2, Pallas kernels, forward(): pl.pallas_call(functools.partial(forward_kernel, mine), out_shape=jax.Sha...  3 us
    pallas_call x1, Pallas kernels, backward_other(): pl.pallas_call(backward_other_kernel, out_shape=[jax.ShapeDtypeStruct((SB...  2.02 us
  transfers between devices with their start and end apart: 16, of which 10 were waited for; matrix products, arithmetic and copies ran while one was open for 0% of the time, Pallas kernels for 6%

profile of v1, /device:TPU:4, one launch (start us, length us, event | category | flops | bytes accessed | tf_op | source)
XLA Modules:
  0.0 78.1 jit_solution(503491912924961489)
XLA Ops:
  1.3 1.8 %copy-done = bf16[88,128,128]{2,1,0:T(8,128)(2,1)S(1)} copy-done((bf16[88,128,128]{2,1,0:T(8,128)(2,1)S(1)}, bf16[88,128,128]{2,1,0:T(8,128)(2,1)}, u32[]{:S(2)}) %copy-start) | copy-done | bytes 2883608
  3.1 0.9 %copy-done.2 = bf16[1024,128]{1,0:T(8,128)(2,1)S(1)} copy-done((bf16[1024,128]{1,0:T(8,128)(2,1)S(1)}, bf16[1024,128]{1,0:T(8,128)(2,1)}, u32[]{:S(2)}) %copy-start.2) | copy-done | bytes 262168
  4.0 0.7 copy-done.3
  4.7 0.7 copy-done.4
  5.4 1.5 %forward_other.1 = bf16[3584,128]{1,0:T(8,128)(2,1)S(1)} custom-call(s32[88]{0:T(128)S(1)} %copy-done.3, s32[88]{0:T(128)S(1)} %copy-done.4, s32[1]{0:T(128)S(6)} %copy.7.count, bf16[88,128,128]{2,1,0:T(8,128)(2,1)S(1)} %copy-done, bf16[1024,128]{1,0:T(8,128)(2,1)S(1)} %copy-done.2), custom_call_target="tpu_custom_call" | custom-call | tf_op jit(solution)/shard_map/forward_other/pallas_call | solution.py:111
  7.0 1.5 %forward_mine.1.a = bf16[3584,128]{1,0:T(8,128)(2,1)S(1)} custom-call(s32[88]{0:T(128)S(1)} %copy-done.3, s32[88]{0:T(128)S(1)} %copy-done.4, s32[1]{0:T(128)S(6)} %copy.7.count, bf16[88,128,128]{2,1,0:T(8,128)(2,1)S(1)} %copy-done, bf16[1024,128]{1,0:T(8,128)(2,1)S(1)} %copy-done.2), custom_call_target="tpu_custom_call" | custom-call | tf_op jit(solution)/shard_map/forward_mine/pallas_call | solution.py:111
  8.5 0.9 %collective-permute-done.b = bf16[3584,128]{1,0:T(8,128)(2,1)S(1)} collective-permute-done((bf16[3584,128]{1,0:T(8,128)(2,1)S(1)}, bf16[3584,128]{1,0:T(8,128)(2,1)S(1)}, u32[]{:S(2)}, u32[]{:S(2)}) %collective-permute-start) | collective-permute-done | bytes 917536 | tf_op jit(solution)/shard_map/ppermute | solution.py:303
  9.4 0.2 pair_sum.1
  9.6 1.9 %collective-permute-start.1 = (bf16[448,128]{1,0:T(8,128)(2,1)S(1)}, bf16[448,128]{1,0:T(8,128)(2,1)S(1)}, u32[]{:S(2)}, u32[]{:S(2)}) collective-permute-start(bf16[448,128]{1,0:T(8,128)(2,1)S(1)} %get-tuple-element.13), channel_id=1, source_target_pairs={{0,12},{1,13},{2,14},{3,15},{4,8},{5,9},{6,10},{7,11},{8,4},{9,5},... | collective-permute-start | bytes 344072 | tf_op jit(solution)/shard_map/ppermute | solution.py:306
  11.6 3.0 %collective-permute-start.2 = (bf16[448,128]{1,0:T(8,128)(2,1)S(1)}, bf16[448,128]{1,0:T(8,128)(2,1)S(1)}, u32[]{:S(2)}, u32[]{:S(2)}) collective-permute-start(bf16[448,128]{1,0:T(8,128)(2,1)S(1)} %get-tuple-element.14), channel_id=1, source_target_pairs={{0,10},{1,7},{2,12},{3,1},{4,14},{5,3},{6,8},{7,5},{8,2},{9,15},{1... | collective-permute-start | bytes 344072 | tf_op jit(solution)/shard_map/ppermute | solution.py:306
  14.6 2.1 %collective-permute-start.3 = (bf16[448,128]{1,0:T(8,128)(2,1)S(1)}, bf16[448,128]{1,0:T(8,128)(2,1)S(1)}, u32[]{:S(2)}, u32[]{:S(2)}) collective-permute-start(bf16[448,128]{1,0:T(8,128)(2,1)S(1)} %get-tuple-element.15), channel_id=1, source_target_pairs={{0,6},{1,11},{2,0},{3,13},{4,2},{5,15},{6,4},{7,9},{8,14},{9,3},{1... | collective-permute-start | bytes 344072 | tf_op jit(solution)/shard_map/ppermute | solution.py:306
  16.8 1.4 %collective-permute-done.1.refs_1_ = bf16[448,128]{1,0:T(8,128)(2,1)S(1)} collective-permute-done((bf16[448,128]{1,0:T(8,128)(2,1)S(1)}, bf16[448,128]{1,0:T(8,128)(2,1)S(1)}, u32[]{:S(2)}, u32[]{:S(2)}) %collective-permute-start.1) | collective-permute-done | bytes 114720 | tf_op jit(solution)/shard_map/ppermute | solution.py:306
  18.2 7.2 %collective-permute-start.6 = (bf16[448,128]{1,0:T(8,128)(2,1)S(1)}, bf16[448,128]{1,0:T(8,128)(2,1)S(1)}, u32[]{:S(2)}, u32[]{:S(2)}) collective-permute-start(bf16[448,128]{1,0:T(8,128)(2,1)S(1)} %get-tuple-element.18), channel_id=1, source_target_pairs={{0,4},{1,9},{2,6},{3,11},{4,0},{5,13},{6,2},{7,15},{8,12},{9,1},{1... | collective-permute-start | bytes 344072 | tf_op jit(solution)/shard_map/ppermute | solution.py:306
  25.4 0.7 collective-permute-done.5.refs_5_
  26.1 2.0 %collective-permute-done.6.refs_6_ = bf16[448,128]{1,0:T(8,128)(2,1)S(1)} collective-permute-done((bf16[448,128]{1,0:T(8,128)(2,1)S(1)}, bf16[448,128]{1,0:T(8,128)(2,1)S(1)}, u32[]{:S(2)}, u32[]{:S(2)}) %collective-permute-start.6) | collective-permute-done | bytes 114720 | tf_op jit(solution)/shard_map/ppermute | solution.py:306
  28.2 2.1 %collective-permute-done.7.refs_7_ = bf16[448,128]{1,0:T(8,128)(2,1)S(1)} collective-permute-done((bf16[448,128]{1,0:T(8,128)(2,1)S(1)}, bf16[448,128]{1,0:T(8,128)(2,1)S(1)}, u32[]{:S(2)}, u32[]{:S(2)}) %collective-permute-start.7) | collective-permute-done | bytes 114720 | tf_op jit(solution)/shard_map/ppermute | solution.py:306
  30.5 2.0 %collective-permute-start.13 = (bf16[448,128]{1,0:T(8,128)(2,1)S(1)}, bf16[448,128]{1,0:T(8,128)(2,1)S(1)}, u32[]{:S(2)}, u32[]{:S(2)}) collective-permute-start(bf16[448,128]{1,0:T(8,128)(2,1)S(1)} %chunk_sum.1.refs_0_), channel_id=1, source_target_pairs={{0,4},{1,9},{2,6},{3,11},{4,0},{5,13},{6,2},{7,15},{8,12},{9,1},{1... | collective-permute-start | bytes 344072 | tf_op jit(solution)/shard_map/ppermute | solution.py:308
  32.5 0.8 %collective-permute-start.12 = (bf16[448,128]{1,0:T(8,128)(2,1)S(1)}, bf16[448,128]{1,0:T(8,128)(2,1)S(1)}, u32[]{:S(2)}, u32[]{:S(2)}) collective-permute-start(bf16[448,128]{1,0:T(8,128)(2,1)S(1)} %chunk_sum.1.refs_0_), channel_id=1, source_target_pairs={{0,14},{1,3},{2,8},{3,5},{4,10},{5,7},{6,12},{7,1},{8,6},{9,11},{1... | collective-permute-start | bytes 344072 | tf_op jit(solution)/shard_map/ppermute | solution.py:308
  33.4 2.1 %collective-permute-start.11 = (bf16[448,128]{1,0:T(8,128)(2,1)S(1)}, bf16[448,128]{1,0:T(8,128)(2,1)S(1)}, u32[]{:S(2)}, u32[]{:S(2)}) collective-permute-start(bf16[448,128]{1,0:T(8,128)(2,1)S(1)} %chunk_sum.1.refs_0_), channel_id=1, source_target_pairs={{0,2},{1,15},{2,4},{3,9},{4,6},{5,11},{6,0},{7,13},{8,10},{9,7},{1... | collective-permute-start | bytes 344072 | tf_op jit(solution)/shard_map/ppermute | solution.py:308
  35.4 0.7 collective-permute-start.10
  36.1 0.4 collective-permute-done.14.refs_7_
  36.5 1.0 %collective-permute-start.9 = (bf16[448,128]{1,0:T(8,128)(2,1)S(1)}, bf16[448,128]{1,0:T(8,128)(2,1)S(1)}, u32[]{:S(2)}, u32[]{:S(2)}) collective-permute-start(bf16[448,128]{1,0:T(8,128)(2,1)S(1)} %chunk_sum.1.refs_0_), channel_id=1, source_target_pairs={{0,10},{1,7},{2,12},{3,1},{4,14},{5,3},{6,8},{7,5},{8,2},{9,15},{1... | collective-permute-start | bytes 344072 | tf_op jit(solution)/shard_map/ppermute | solution.py:308
  37.5 0.3 collective-permute-done.13.refs_6_
  37.8 3.3 %collective-permute-start.8 = (bf16[448,128]{1,0:T(8,128)(2,1)S(1)}, bf16[448,128]{1,0:T(8,128)(2,1)S(1)}, u32[]{:S(2)}, u32[]{:S(2)}) collective-permute-start(bf16[448,128]{1,0:T(8,128)(2,1)S(1)} %chunk_sum.1.refs_0_), channel_id=1, source_target_pairs={{0,12},{1,13},{2,14},{3,15},{4,8},{5,9},{6,10},{7,11},{8,4},{9,5},... | collective-permute-start | bytes 344072 | tf_op jit(solution)/shard_map/ppermute | solution.py:308
  41.0 0.5 collective-permute-done.10.refs_3_
  41.6 0.8 %collective-permute-done.9.refs_2_ = bf16[448,128]{1,0:T(8,128)(2,1)S(1)} collective-permute-done((bf16[448,128]{1,0:T(8,128)(2,1)S(1)}, bf16[448,128]{1,0:T(8,128)(2,1)S(1)}, u32[]{:S(2)}, u32[]{:S(2)}) %collective-permute-start.9) | collective-permute-done | bytes 114720 | tf_op jit(solution)/shard_map/ppermute | solution.py:308
  42.4 2.5 %collective-permute-done.8.refs_1_ = bf16[448,128]{1,0:T(8,128)(2,1)S(1)} collective-permute-done((bf16[448,128]{1,0:T(8,128)(2,1)S(1)}, bf16[448,128]{1,0:T(8,128)(2,1)S(1)}, u32[]{:S(2)}, u32[]{:S(2)}) %collective-permute-start.8) | collective-permute-done | bytes 114720 | tf_op jit(solution)/shard_map/ppermute | solution.py:308
  45.2 1.9 %turn_tiles.1.turned = bf16[88,128,128]{2,1,0:T(8,128)(2,1)S(1)} custom-call(bf16[88,128,128]{2,1,0:T(8,128)(2,1)S(1)} %copy-done.1), custom_call_target="tpu_custom_call" | custom-call | tf_op jit(solution)/shard_map/turn_tiles/pallas_call | solution.py:132
  47.1 1.3 %backward_mine.1.first = f32[1152,128]{1,0:T(8,128)S(1)} custom-call(s32[88]{0:T(128)S(1)} %copy-done.3, s32[88]{0:T(128)S(1)} %copy-done.4, s32[1]{0:T(128)S(6)} %copy.7.count, bf16[88,128,128]{2,1,0:T(8,128)(2,1)S(1)} %turn_tiles.1.turned, bf16[3584,128]{1,0:T(8,128)(2,1)S(1)} %gather_half.1.table.own), custom_call_target="tpu_custom_call" | custom-call | tf_op jit(solution)/shard_map/backward_mine/pallas_call | solution.py:233
  48.4 2.0 %backward_other.1 = (bf16[1024,128]{1,0:T(8,128)(2,1)S(1)}, bf16[448,128]{1,0:T(8,128)(2,1)}) custom-call(s32[88]{0:T(128)S(1)} %copy-done.3, s32[88]{0:T(128)S(1)} %copy-done.4, s32[1]{0:T(128)S(6)} %copy.7.count, bf16[88,128,128]{2,1,0:T(8,128)(2,1)S(1)} %turn_tiles.1.turned, f32[1152,128]{1,0:T(8,128)S(1)} %backward_mine.1.first, ...), custom_call_target="tpu_custom_call" | custom-call | tf_op jit(solution)/shard_map/backward_other/pallas_call | solution.py:265
  50.4 27.0 %all_to_all.5.parts = bf16[16,64,128]{2,1,0:T(8,128)(2,1)S(1)} all-to-all(bf16[16,64,128]{2,1,0:T(8,128)(2,1)S(1)} %bitcast.1), channel_id=1, replica_groups=mesh['kmer'=16,'samp'=16] {'kmer'}, dimensions={0} | all-to-all | bytes 524288 | tf_op jit(solution)/shard_map/all_to_all | solution.py:315
  77.5 0.7 last_sum.1
  (20 shorter events, 0.7 us)
Async XLA Ops:
  1.3 1.8 %copy-start = (bf16[88,128,128]{2,1,0:T(8,128)(2,1)S(1)}, bf16[88,128,128]{2,1,0:T(8,128)(2,1)}, u32[]{:S(2)}) copy-start(bf16[88,128,128]{2,1,0:T(8,128)(2,1)} %tiles.5) | copy-start | bytes 8650756
  3.1 0.9 %copy-start.2 = (bf16[1024,128]{1,0:T(8,128)(2,1)S(1)}, bf16[1024,128]{1,0:T(8,128)(2,1)}, u32[]{:S(2)}) copy-start(bf16[1024,128]{1,0:T(8,128)(2,1)} %omega.3) | copy-start | bytes 786436
  4.0 0.7 copy-start.3
  4.7 0.7 copy-start.4
  6.9 2.6 %collective-permute-start = (bf16[3584,128]{1,0:T(8,128)(2,1)S(1)}, bf16[3584,128]{1,0:T(8,128)(2,1)S(1)}, u32[]{:S(2)}, u32[]{:S(2)}) collective-permute-start(bf16[3584,128]{1,0:T(8,128)(2,1)S(1)} %forward_other.1), channel_id=1, source_target_pairs={{0,1},{1,0},{2,3},{3,2},{4,5},{5,4},{6,7},{7,6},{8,9},{9,8},{10,11... | collective-permute-start | bytes 2752520 | tf_op jit(solution)/shard_map/ppermute | solution.py:303
  8.5 36.7 %copy-start.1 = (bf16[88,128,128]{2,1,0:T(8,128)(2,1)S(1)}, bf16[88,128,128]{2,1,0:T(8,128)(2,1)}, u32[]{:S(2)}) copy-start(bf16[88,128,128]{2,1,0:T(8,128)(2,1)} %tiles.5) | copy-start | bytes 8650756
  9.6 8.5 %collective-permute-start.1 = (bf16[448,128]{1,0:T(8,128)(2,1)S(1)}, bf16[448,128]{1,0:T(8,128)(2,1)S(1)}, u32[]{:S(2)}, u32[]{:S(2)}) collective-permute-start(bf16[448,128]{1,0:T(8,128)(2,1)S(1)} %get-tuple-element.13), channel_id=1, source_target_pairs={{0,12},{1,13},{2,14},{3,15},{4,8},{5,9},{6,10},{7,11},{8,4},{9,5},... | collective-permute-start | bytes 344072 | tf_op jit(solution)/shard_map/ppermute | solution.py:306
  11.6 13.9 %collective-permute-start.2 = (bf16[448,128]{1,0:T(8,128)(2,1)S(1)}, bf16[448,128]{1,0:T(8,128)(2,1)S(1)}, u32[]{:S(2)}, u32[]{:S(2)}) collective-permute-start(bf16[448,128]{1,0:T(8,128)(2,1)S(1)} %get-tuple-element.14), channel_id=1, source_target_pairs={{0,10},{1,7},{2,12},{3,1},{4,14},{5,3},{6,8},{7,5},{8,2},{9,15},{1... | collective-permute-start | bytes 344072 | tf_op jit(solution)/shard_map/ppermute | solution.py:306
  14.6 10.9 %collective-permute-start.3 = (bf16[448,128]{1,0:T(8,128)(2,1)S(1)}, bf16[448,128]{1,0:T(8,128)(2,1)S(1)}, u32[]{:S(2)}, u32[]{:S(2)}) collective-permute-start(bf16[448,128]{1,0:T(8,128)(2,1)S(1)} %get-tuple-element.15), channel_id=1, source_target_pairs={{0,6},{1,11},{2,0},{3,13},{4,2},{5,15},{6,4},{7,9},{8,14},{9,3},{1... | collective-permute-start | bytes 344072 | tf_op jit(solution)/shard_map/ppermute | solution.py:306
  16.6 8.8 %collective-permute-start.4 = (bf16[448,128]{1,0:T(8,128)(2,1)S(1)}, bf16[448,128]{1,0:T(8,128)(2,1)S(1)}, u32[]{:S(2)}, u32[]{:S(2)}) collective-permute-start(bf16[448,128]{1,0:T(8,128)(2,1)S(1)} %get-tuple-element.16), channel_id=1, source_target_pairs={{0,2},{1,15},{2,4},{3,9},{4,6},{5,11},{6,0},{7,13},{8,10},{9,7},{1... | collective-permute-start | bytes 344072 | tf_op jit(solution)/shard_map/ppermute | solution.py:306
  16.6 9.5 %collective-permute-start.5 = (bf16[448,128]{1,0:T(8,128)(2,1)S(1)}, bf16[448,128]{1,0:T(8,128)(2,1)S(1)}, u32[]{:S(2)}, u32[]{:S(2)}) collective-permute-start(bf16[448,128]{1,0:T(8,128)(2,1)S(1)} %get-tuple-element.17), channel_id=1, source_target_pairs={{0,14},{1,3},{2,8},{3,5},{4,10},{5,7},{6,12},{7,1},{8,6},{9,11},{1... | collective-permute-start | bytes 344072 | tf_op jit(solution)/shard_map/ppermute | solution.py:306
  18.2 10.0 %collective-permute-start.6 = (bf16[448,128]{1,0:T(8,128)(2,1)S(1)}, bf16[448,128]{1,0:T(8,128)(2,1)S(1)}, u32[]{:S(2)}, u32[]{:S(2)}) collective-permute-start(bf16[448,128]{1,0:T(8,128)(2,1)S(1)} %get-tuple-element.18), channel_id=1, source_target_pairs={{0,4},{1,9},{2,6},{3,11},{4,0},{5,13},{6,2},{7,15},{8,12},{9,1},{1... | collective-permute-start | bytes 344072 | tf_op jit(solution)/shard_map/ppermute | solution.py:306
  25.4 4.9 %collective-permute-start.7 = (bf16[448,128]{1,0:T(8,128)(2,1)S(1)}, bf16[448,128]{1,0:T(8,128)(2,1)S(1)}, u32[]{:S(2)}, u32[]{:S(2)}) collective-permute-start(bf16[448,128]{1,0:T(8,128)(2,1)S(1)} %get-tuple-element.19), channel_id=1, source_target_pairs={{0,8},{1,5},{2,10},{3,7},{4,12},{5,1},{6,14},{7,3},{8,0},{9,13},{1... | collective-permute-start | bytes 344072 | tf_op jit(solution)/shard_map/ppermute | solution.py:306
  30.4 6.0 %collective-permute-start.14 = (bf16[448,128]{1,0:T(8,128)(2,1)S(1)}, bf16[448,128]{1,0:T(8,128)(2,1)S(1)}, u32[]{:S(2)}, u32[]{:S(2)}) collective-permute-start(bf16[448,128]{1,0:T(8,128)(2,1)S(1)} %chunk_sum.1.refs_0_), channel_id=1, source_target_pairs={{0,8},{1,5},{2,10},{3,7},{4,12},{5,1},{6,14},{7,3},{8,0},{9,13},{1... | collective-permute-start | bytes 344072 | tf_op jit(solution)/shard_map/ppermute | solution.py:308
  30.5 7.2 %collective-permute-start.13 = (bf16[448,128]{1,0:T(8,128)(2,1)S(1)}, bf16[448,128]{1,0:T(8,128)(2,1)S(1)}, u32[]{:S(2)}, u32[]{:S(2)}) collective-permute-start(bf16[448,128]{1,0:T(8,128)(2,1)S(1)} %chunk_sum.1.refs_0_), channel_id=1, source_target_pairs={{0,4},{1,9},{2,6},{3,11},{4,0},{5,13},{6,2},{7,15},{8,12},{9,1},{1... | collective-permute-start | bytes 344072 | tf_op jit(solution)/shard_map/ppermute | solution.py:308
  32.5 8.5 %collective-permute-start.12 = (bf16[448,128]{1,0:T(8,128)(2,1)S(1)}, bf16[448,128]{1,0:T(8,128)(2,1)S(1)}, u32[]{:S(2)}, u32[]{:S(2)}) collective-permute-start(bf16[448,128]{1,0:T(8,128)(2,1)S(1)} %chunk_sum.1.refs_0_), channel_id=1, source_target_pairs={{0,14},{1,3},{2,8},{3,5},{4,10},{5,7},{6,12},{7,1},{8,6},{9,11},{1... | collective-permute-start | bytes 344072 | tf_op jit(solution)/shard_map/ppermute | solution.py:308
  33.4 7.7 %collective-permute-start.11 = (bf16[448,128]{1,0:T(8,128)(2,1)S(1)}, bf16[448,128]{1,0:T(8,128)(2,1)S(1)}, u32[]{:S(2)}, u32[]{:S(2)}) collective-permute-start(bf16[448,128]{1,0:T(8,128)(2,1)S(1)} %chunk_sum.1.refs_0_), channel_id=1, source_target_pairs={{0,2},{1,15},{2,4},{3,9},{4,6},{5,11},{6,0},{7,13},{8,10},{9,7},{1... | collective-permute-start | bytes 344072 | tf_op jit(solution)/shard_map/ppermute | solution.py:308
  35.4 6.1 %collective-permute-start.10 = (bf16[448,128]{1,0:T(8,128)(2,1)S(1)}, bf16[448,128]{1,0:T(8,128)(2,1)S(1)}, u32[]{:S(2)}, u32[]{:S(2)}) collective-permute-start(bf16[448,128]{1,0:T(8,128)(2,1)S(1)} %chunk_sum.1.refs_0_), channel_id=1, source_target_pairs={{0,6},{1,11},{2,0},{3,13},{4,2},{5,15},{6,4},{7,9},{8,14},{9,3},{1... | collective-permute-start | bytes 344072 | tf_op jit(solution)/shard_map/ppermute | solution.py:308
  36.5 5.9 %collective-permute-start.9 = (bf16[448,128]{1,0:T(8,128)(2,1)S(1)}, bf16[448,128]{1,0:T(8,128)(2,1)S(1)}, u32[]{:S(2)}, u32[]{:S(2)}) collective-permute-start(bf16[448,128]{1,0:T(8,128)(2,1)S(1)} %chunk_sum.1.refs_0_), channel_id=1, source_target_pairs={{0,10},{1,7},{2,12},{3,1},{4,14},{5,3},{6,8},{7,5},{8,2},{9,15},{1... | collective-permute-start | bytes 344072 | tf_op jit(solution)/shard_map/ppermute | solution.py:308
  37.8 7.2 %collective-permute-start.8 = (bf16[448,128]{1,0:T(8,128)(2,1)S(1)}, bf16[448,128]{1,0:T(8,128)(2,1)S(1)}, u32[]{:S(2)}, u32[]{:S(2)}) collective-permute-start(bf16[448,128]{1,0:T(8,128)(2,1)S(1)} %chunk_sum.1.refs_0_), channel_id=1, source_target_pairs={{0,12},{1,13},{2,14},{3,15},{4,8},{5,9},{6,10},{7,11},{8,4},{9,5},... | collective-permute-start | bytes 344072 | tf_op jit(solution)/shard_map/ppermute | solution.py:308
  45.0 3.4 %collective-permute-start.15 = (bf16[3584,128]{1,0:T(8,128)(2,1)S(1)}, bf16[3584,128]{1,0:T(8,128)(2,1)S(1)}, u32[]{:S(2)}, u32[]{:S(2)}) collective-permute-start(bf16[3584,128]{1,0:T(8,128)(2,1)S(1)} %gather_half.1.table.own), channel_id=1, source_target_pairs={{0,1},{1,0},{2,3},{3,2},{4,5},{5,4},{6,7},{7,6},{8,9},{9,8},{10,11... | collective-permute-start | bytes 2752520 | tf_op jit(solution)/shard_map/ppermute | solution.py:310

commit v2 on v1

v2 whole, which is shorter than its diff:
```python
import functools

import jax
import jax.numpy as jnp
from jax import lax
from jax.experimental import pallas as pl
from jax.experimental.pallas import tpu as pltpu
from jax.sharding import PartitionSpec as P

TILE = 128
KB_DEV = 56
SB_DEV = 8
HALF_BLOCKS = KB_DEV // 2
HALF = HALF_BLOCKS * TILE
CHUNK = HALF // 8
UNROLL = 12
LIST = 128
VMEM_LIMIT = 48 * 1024 * 1024

ROUNDS = (
    ((2, 1), (2, 1)),
    ((1, 1), (3, 0)),
    ((3, 0), (1, 1)),
    ((1, 0), (3, 1)),
    ((3, 1), (1, 0)),
    ((2, 0), (0, 1)),
    ((0, 1), (2, 0)),
)

LINE = ((1, 3), (3, 1), (2, 2))


def vm():
    return pl.BlockSpec(memory_space=pltpu.VMEM)


def sm():
    return pl.BlockSpec(memory_space=pltpu.SMEM)


def params():
    return pltpu.CompilerParams(vmem_limit_bytes=VMEM_LIMIT)


def place():
    j = lax.axis_index("samp")
    return j // 8, (j // 2) % 4, j % 2


def pairs(r):
    out = []
    for s in range(16):
        z, x, c = s // 8, (s // 2) % 4, s % 2
        dx, dz = ROUNDS[r][c]
        out.append((s, (z ^ dz) * 8 + ((x + dx) % 4) * 2 + c))
    return out


def peer_chunk(r, sign):
    z, x, c = place()
    (dx0, dz0), (dx1, dz1) = ROUNDS[r]
    dx = jnp.where(c == 0, dx0, dx1) * sign
    dz = jnp.where(c == 0, dz0, dz1)
    zz = z + dz - 2 * z * dz
    return zz * 4 + (x + dx + 4) % 4


def block(i):
    return pl.ds(pl.multiple_of(i * TILE, TILE), TILE)


def unpack(word):
    return lax.rem(word, 128), lax.rem(lax.div(word, 128), 64), lax.div(word, 8192)


def list_slots(rows, cols, count, base, far, near):
    cap = rows.shape[0]

    def visit(s, carry):
        n_far, n_near = carry
        row = rows[s] - base
        inside = jnp.logical_and(row >= 0, row < HALF_BLOCKS)
        within = jnp.where(inside, row, rows[s] - (HALF_BLOCKS - base))
        word = s + within * 128 + cols[s] * 8192
        far[n_far] = word
        near[n_near] = word
        used = (s < count).astype(jnp.int32)
        here = inside.astype(jnp.int32)
        return n_far + used * (1 - here), n_near + used * here

    n_far, n_near = lax.fori_loop(0, cap, visit, (jnp.int32(0), jnp.int32(0)), unroll=8)
    pad = HALF_BLOCKS * 128 + SB_DEV * 8192
    pad_far, pad_near = pad + lax.rem(far[0], 128), pad + lax.rem(near[0], 128)
    for u in range(UNROLL):
        far[n_far + u] = pad_far
        near[n_near + u] = pad_near
    far[LIST - 1] = n_far
    near[LIST - 1] = n_near
    return n_far, n_near


def forward_slots(n, entries, tiles, omega, acc, out):
    acc[...] = jnp.zeros_like(acc)

    def step(g, carry):
        prods, where = [], []
        for u in range(UNROLL):
            slot, row, col = unpack(entries[g * UNROLL + u])
            col = jnp.minimum(col, SB_DEV - 1)
            where.append(block(row))
            prods.append(
                jnp.dot(tiles[slot], omega[block(col), :], preferred_element_type=jnp.float32)
            )
        for at, prod in zip(where, prods):
            acc[at, :] = acc[at, :] + prod
        return carry

    lax.fori_loop(0, (n + UNROLL - 1) // UNROLL, step, 0)
    out[...] = acc[pl.ds(0, HALF), :].astype(jnp.bfloat16)


def forward_far_kernel(
    rows, cols, count, tiles, omega, out, held, table, far, near, acc, s_rows, s_cols, sems
):
    small = [
        pltpu.make_async_copy(rows, s_rows, sems.at[0]),
        pltpu.make_async_copy(cols, s_cols, sems.at[1]),
    ]
    for copy in small:
        copy.start()
    fetch_omega = pltpu.make_async_copy(omega, table, sems.at[2])
    fetch_omega.start()
    for copy in small:
        copy.wait()
    _, _, c = place()
    n_far, n_near = list_slots(s_rows, s_cols, count[0], c * HALF_BLOCKS, far, near)

    def fetch(entries, sem, k):
        slot = lax.rem(entries[k], 128)
        return pltpu.make_async_copy(tiles.at[slot], held.at[slot], sem)

    def start(entries, sem, n):
        def one(k, carry):
            fetch(entries, sem, k).start()
            return carry

        lax.fori_loop(0, n, one, 0)

    def wait(entries, sem, n):
        def one(k, carry):
            fetch(entries, sem, k).wait()
            return carry

        lax.fori_loop(0, n, one, 0)

    start(far, sems.at[3], n_far)
    start(near, sems.at[4], n_near)
    fetch_omega.wait()
    wait(far, sems.at[3], n_far)
    forward_slots(n_far, far, held, table, acc, out)
    wait(near, sems.at[4], n_near)


def forward_far(rows, cols, count, tiles, omega):
    cap = tiles.shape[0]
    anywhere = pl.BlockSpec(memory_space=pltpu.HBM)
    entries = jax.ShapeDtypeStruct((LIST,), jnp.int32)
    return pl.pallas_call(
        forward_far_kernel,
        out_shape=[
            jax.ShapeDtypeStruct((HALF, TILE), jnp.bfloat16),
            jax.ShapeDtypeStruct(tiles.shape, tiles.dtype),
            jax.ShapeDtypeStruct(omega.shape, omega.dtype),
            entries,
            entries,
        ],
        in_specs=[anywhere, anywhere, sm(), anywhere, anywhere],
        out_specs=[vm(), vm(), vm(), sm(), sm()],
        scratch_shapes=[
            pltpu.VMEM((HALF + TILE, TILE), jnp.float32),
            pltpu.SMEM((cap,), jnp.int32),
            pltpu.SMEM((cap,), jnp.int32),
            pltpu.SemaphoreType.DMA((5,)),
        ],
        compiler_params=params(),
        name="forward_far",
    )(*(pltpu.with_memory_space_constraint(v, pltpu.HBM) for v in (rows, cols)), count,
      *(pltpu.with_memory_space_constraint(v, pltpu.HBM) for v in (tiles, omega)))


def forward_near_kernel(near, held, table, out, acc):
    forward_slots(near[LIST - 1], near, held, table, acc, out)


def forward_near(near, held, table):
    return pl.pallas_call(
        forward_near_kernel,
        out_shape=jax.ShapeDtypeStruct((HALF, TILE), jnp.bfloat16),
        in_specs=[sm(), vm(), vm()],
        out_specs=vm(),
        scratch_shapes=[pltpu.VMEM((HALF + TILE, TILE), jnp.float32)],
        compiler_params=params(),
        name="forward_near",
    )(near, held, table)


def turn_kernel(far, near, tiles, out):
    def one(g, carry):
        for u in range(4):
            out[g * 4 + u] = tiles[g * 4 + u].T
        return carry

    lax.fori_loop(0, (far[LIST - 1] + near[LIST - 1] + 3) // 4, one, 0)


def turn(far, near, tiles):
    return pl.pallas_call(
        turn_kernel,
        out_shape=jax.ShapeDtypeStruct(tiles.shape, tiles.dtype),
        in_specs=[sm(), sm(), vm()],
        out_specs=vm(),
        compiler_params=params(),
        name="turn_tiles",
    )(far, near, tiles)


def chunk_at(i):
    return pl.ds(pl.multiple_of(i * CHUNK, CHUNK), CHUNK)


def pair_kernel(a, b, own, *sends):
    def total(i):
        at = chunk_at(i)
        return (a[at, :].astype(jnp.float32) + b[at, :].astype(jnp.float32)).astype(jnp.bfloat16)

    z, x, _ = place()
    for r, send in enumerate(sends):
        send[...] = total(peer_chunk(r, 1))
    own[...] = total(z * 4 + x)


def pair_sum(a, b):
    shape = jax.ShapeDtypeStruct((CHUNK, TILE), jnp.bfloat16)
    return pl.pallas_call(
        pair_kernel,
        out_shape=[shape] * 8,
        in_specs=[vm(), vm()],
        out_specs=[vm()] * 8,
        compiler_params=params(),
        name="pair_sum",
    )(a, b)


def chunk_kernel(*refs):
    out = refs[-1]
    total = refs[0][...].astype(jnp.float32)
    for ref in refs[1:-1]:
        total = total + ref[...].astype(jnp.float32)
    out[...] = total.astype(jnp.bfloat16)


def chunk_sum(parts):
    return pl.pallas_call(
        chunk_kernel,
        out_shape=jax.ShapeDtypeStruct((CHUNK, TILE), jnp.bfloat16),
        in_specs=[vm()] * len(parts),
        out_specs=vm(),
        compiler_params=params(),
        name="chunk_sum",
    )(*parts)


def gather_kernel(*refs):
    z, x, _ = place()
    out = refs[-1]
    out[chunk_at(z * 4 + x), :] = refs[0][...]
    for r, ref in enumerate(refs[1:-1]):
        out[chunk_at(peer_chunk(r, -1)), :] = ref[...]


def gather_half(own, got):
    return pl.pallas_call(
        gather_kernel,
        out_shape=jax.ShapeDtypeStruct((HALF, TILE), jnp.bfloat16),
        in_specs=[vm()] * 8,
        out_specs=vm(),
        compiler_params=params(),
        name="gather_half",
    )(own, *got)


def backward_slots(n, entries, turned, table, acc):
    def step(g, carry):
        prods, where = [], []
        for u in range(UNROLL):
            slot, row, col = unpack(entries[g * UNROLL + u])
            row = jnp.minimum(row, HALF_BLOCKS - 1)
            where.append(block(col))
            prods.append(
                jnp.dot(turned[slot], table[block(row), :], preferred_element_type=jnp.float32)
            )
        for at, prod in zip(where, prods):
            acc[at, :] = acc[at, :] + prod
        return carry

    lax.fori_loop(0, (n + UNROLL - 1) // UNROLL, step, 0)


def backward_near_kernel(near, turned, table, out):
    out[...] = jnp.zeros_like(out)
    backward_slots(near[LIST - 1], near, turned, table, out)


def backward_near(near, turned, table):
    return pl.pallas_call(
        backward_near_kernel,
        out_shape=jax.ShapeDtypeStruct(((SB_DEV + 1) * TILE, TILE), jnp.float32),
        in_specs=[sm(), vm(), vm()],
        out_specs=vm(),
        compiler_params=params(),
        name="backward_near",
    )(near, turned, table)


def line_offset(r, sign):
    _, _, c = place()
    return jnp.where(c == 0, LINE[r][0], LINE[r][1]) * sign


def share_at(i, size):
    return pl.ds(pl.multiple_of(lax.rem(i + 4, 4) * size, size), size)


def kmer_place():
    i = lax.axis_index("kmer")
    return i // 4, i % 4


def backward_far_kernel(far, turned, first, own, table, keep, s0, s1, s2, sketch, acc):
    acc[...] = first[...]
    backward_slots(far[LIST - 1], far, turned, table, acc)
    y, _ = kmer_place()
    size = keep.shape[0]
    for r, send in enumerate((s0, s1, s2)):
        send[...] = acc[share_at(y + line_offset(r, 1), size), :].astype(jnp.bfloat16)
    keep[...] = acc[share_at(y, size), :]
    z, x, c = place()
    at = chunk_at(x * 2 + c)

    @pl.when(z == c)
    def _():
        sketch[...] = own[at, :]

    @pl.when(z != c)
    def _():
        sketch[...] = table[at, :]


def backward_far(far, turned, first, own, table):
    share = SB_DEV * TILE // 4
    send = jax.ShapeDtypeStruct((share, TILE), jnp.bfloat16)
    return pl.pallas_call(
        backward_far_kernel,
        out_shape=[
            jax.ShapeDtypeStruct((share, TILE), jnp.float32),
            send,
            send,
            send,
            jax.ShapeDtypeStruct((CHUNK, TILE), jnp.bfloat16),
        ],
        in_specs=[sm(), vm(), vm(), vm(), vm()],
        out_specs=[vm()] * 5,
        scratch_shapes=[pltpu.VMEM(((SB_DEV + 1) * TILE, TILE), jnp.float32)],
        compiler_params=params(),
        name="backward_far",
    )(far, turned, first, own, table)


def line_kernel(own, g0, g1, g2, keep, s0, s1, s2, acc):
    total = own[...]
    for got in (g0, g1, g2):
        total = total + got[...].astype(jnp.float32)
    acc[...] = total
    _, zh = kmer_place()
    size = keep.shape[0]
    for r, send in enumerate((s0, s1, s2)):
        send[...] = acc[share_at(zh + line_offset(r, 1), size), :].astype(jnp.bfloat16)
    keep[...] = acc[share_at(zh, size), :]


def line_sum(own, got):
    share = own.shape[0] // 4
    send = jax.ShapeDtypeStruct((share, TILE), jnp.bfloat16)
    return pl.pallas_call(
        line_kernel,
        out_shape=[jax.ShapeDtypeStruct((share, TILE), jnp.float32), send, send, send],
        in_specs=[vm()] * 4,
        out_specs=[vm()] * 4,
        scratch_shapes=[pltpu.VMEM(own.shape, jnp.float32)],
        compiler_params=params(),
        name="line_sum",
    )(own, *got)


def last_kernel(factor, own, g0, g1, g2, out):
    total = own[...]
    for got in (g0, g1, g2):
        total = total + got[...].astype(jnp.float32)
    out[...] = total * factor


def last_sum(factor, own, got):
    return pl.pallas_call(
        functools.partial(last_kernel, factor),
        out_shape=jax.ShapeDtypeStruct(own.shape, jnp.float32),
        in_specs=[vm()] * 4,
        out_specs=vm(),
        compiler_params=params(),
        name="last_sum",
    )(own, *got)


def line_permute(value, r, along_y):
    out = []
    for i in range(16):
        for j in range(16):
            y, zh = i // 4, i % 4
            off = LINE[r][j % 2]
            to = ((y + off) % 4) * 4 + zh if along_y else y * 4 + (zh + off) % 4
            out.append((i * 16 + j, to * 16 + j))
    return lax.ppermute(value, ("kmer", "samp"), out)


def shards(tiles, omega, tile_rows, tile_cols, tile_count):
    swap = [(s, s ^ 1) for s in range(16)]
    kmers = lax.axis_size("kmer")
    other, held, table, far, near = forward_far(tile_rows, tile_cols, tile_count, tiles, omega)
    got = lax.ppermute(other, "samp", swap)
    mine = forward_near(near, held, table)
    own, *sends = pair_sum(mine, got)
    held, _ = lax.optimization_barrier((held, own))
    turned = turn(far, near, held)
    parts = [lax.ppermute(s, "samp", pairs(r)) for r, s in enumerate(sends)]
    own, turned = lax.optimization_barrier((own, turned))
    chunk = chunk_sum([own, *parts])
    pieces = [lax.ppermute(chunk, "samp", pairs(r)) for r in range(7)]
    own_half = gather_half(chunk, pieces)
    other_half = lax.ppermute(own_half, "samp", swap)
    first = backward_near(near, turned, own_half)
    keep, *shares, sketch = backward_far(far, turned, first, own_half, other_half)
    got = [line_permute(s, r, True) for r, s in enumerate(shares)]
    keep, *shares = line_sum(keep, got)
    got = [line_permute(s, r, False) for r, s in enumerate(shares)]
    factor = 1.0 / (KB_DEV * TILE * kmers) ** 0.5
    return sketch, last_sum(factor, keep, got)


def solution(mesh):
    placed = (
        P(("kmer", "samp"), None, None),
        P("samp", None),
        P(("kmer", "samp")),
        P(("kmer", "samp")),
        P(("kmer", "samp")),
    )
    return jax.shard_map(
        shards,
        mesh=mesh,
        in_specs=placed,
        out_specs=(P(("kmer", "samp"), None), P(("samp", "kmer"), None)),
        check_vma=False,
    )
```

time: 78.8 us -> 71.5 us (0.907)
  the two profiles are of different devices: /device:TPU:4 before, /device:TPU:24 now
where the time goes in v2:
time: 71.5 us; the launch traced here: 70.1 us
  starting transfers between devices  39.7 us (56%)
  waiting for transfers between devices  19.8 us (28%)
  Pallas kernels  9.23 us (13%)
  between operations  1.38 us (2%)
    ppermute x6, starting transfers between devices, line_permute(): return lax.ppermute(value, ('kmer', 'samp'), out)  15 us
    ppermute x7, starting transfers between devices, shards(): parts = [lax.ppermute(s, 'samp', pairs(r)) for r, s in enumerate(sends)]  13.4 us
    ppermute x7, starting transfers between devices, shards(): pieces = [lax.ppermute(chunk, 'samp', pairs(r)) for r in range(7)]  10.9 us
    ppermute x6, waiting for transfers between devices, line_permute(): return lax.ppermute(value, ('kmer', 'samp'), out)  7.15 us
    ppermute x7, waiting for transfers between devices, shards(): pieces = [lax.ppermute(chunk, 'samp', pairs(r)) for r in range(7)]  6.01 us
    ppermute x7, waiting for transfers between devices, shards(): parts = [lax.ppermute(s, 'samp', pairs(r)) for r, s in enumerate(sends)]  3.61 us
    pallas_call x1, Pallas kernels, forward_far(): pl.pallas_call(forward_far_kernel, out_shape=[jax.ShapeDtypeStruct((HALF,...  3.56 us
    ppermute x1, waiting for transfers between devices, shards(): other_half = lax.ppermute(own_half, 'samp', swap)  1.59 us
  transfers between devices with their start and end apart: 22, of which 12 were waited for; matrix products, arithmetic and copies ran while one was open for 0% of the time, Pallas kernels for 4%

profile of v2, /device:TPU:24, one launch (start us, length us, event | category | flops | bytes accessed | tf_op | source)
XLA Modules:
  0.0 70.1 jit_solution(15824635471036651061)
XLA Ops:
  1.3 3.6 %forward_far.1 = (bf16[3584,128]{1,0:T(8,128)(2,1)S(1)}, bf16[88,128,128]{2,1,0:T(8,128)(2,1)S(1)}, bf16[1024,128]{1,0:T(8,128)(2,1)S(1)}, s32[128]{0:T(128)S(1)}, s32[128]{0:T(128)S(1)}) custom-call(s32[88]{0:T(128)} %rows.1, s32[88]{0:T(128)} %cols.1, s32[1]{0:T(128)S(6)} %copy.7.count, bf16[88,128,128]{2,1,0:T(8,128)(2,1)} %tiles.1, bf16[1024,128]{1,0:T(8,128)(2,1)} %omega.1), custom_call_target="tpu_custom_call" | custom-call | tf_op jit(solution)/shard_map/forward_far/pallas_call | solution.py:168
  4.9 1.0 %forward_near.1.a = bf16[3584,128]{1,0:T(8,128)(2,1)S(1)} custom-call(s32[128]{0:T(128)S(1)} %get-tuple-element.28.near, bf16[88,128,128]{2,1,0:T(8,128)(2,1)S(1)} %get-tuple-element.33.held.tiles, bf16[1024,128]{1,0:T(8,128)(2,1)S(1)} %get-tuple-element.30.table), custom_call_target="tpu_custom_call" | custom-call | tf_op jit(solution)/shard_map/forward_near/pallas_call | solution.py:196
  6.0 1.4 %collective-permute-done.b = bf16[3584,128]{1,0:T(8,128)(2,1)S(1)} collective-permute-done((bf16[3584,128]{1,0:T(8,128)(2,1)S(1)}, bf16[3584,128]{1,0:T(8,128)(2,1)S(1)}, u32[]{:S(2)}, u32[]{:S(2)}) %collective-permute-start) | collective-permute-done | bytes 917536 | tf_op jit(solution)/shard_map/ppermute | solution.py:438
  7.6 4.4 %collective-permute-start.1 = (bf16[448,128]{1,0:T(8,128)(2,1)S(1)}, bf16[448,128]{1,0:T(8,128)(2,1)S(1)}, u32[]{:S(2)}, u32[]{:S(2)}) collective-permute-start(bf16[448,128]{1,0:T(8,128)(2,1)S(1)} %get-tuple-element.36), channel_id=1, source_target_pairs={{0,12},{1,13},{2,14},{3,15},{4,8},{5,9},{6,10},{7,11},{8,4},{9,5},... | collective-permute-start | bytes 344072 | tf_op jit(solution)/shard_map/ppermute | solution.py:443
  12.1 1.5 %collective-permute-start.2 = (bf16[448,128]{1,0:T(8,128)(2,1)S(1)}, bf16[448,128]{1,0:T(8,128)(2,1)S(1)}, u32[]{:S(2)}, u32[]{:S(2)}) collective-permute-start(bf16[448,128]{1,0:T(8,128)(2,1)S(1)} %get-tuple-element.37), channel_id=1, source_target_pairs={{0,10},{1,7},{2,12},{3,1},{4,14},{5,3},{6,8},{7,5},{8,2},{9,15},{1... | collective-permute-start | bytes 344072 | tf_op jit(solution)/shard_map/ppermute | solution.py:443
  13.6 1.2 %collective-permute-start.3 = (bf16[448,128]{1,0:T(8,128)(2,1)S(1)}, bf16[448,128]{1,0:T(8,128)(2,1)S(1)}, u32[]{:S(2)}, u32[]{:S(2)}) collective-permute-start(bf16[448,128]{1,0:T(8,128)(2,1)S(1)} %get-tuple-element.38), channel_id=1, source_target_pairs={{0,6},{1,11},{2,0},{3,13},{4,2},{5,15},{6,4},{7,9},{8,14},{9,3},{1... | collective-permute-start | bytes 344072 | tf_op jit(solution)/shard_map/ppermute | solution.py:443
  14.8 0.8 %collective-permute-start.4 = (bf16[448,128]{1,0:T(8,128)(2,1)S(1)}, bf16[448,128]{1,0:T(8,128)(2,1)S(1)}, u32[]{:S(2)}, u32[]{:S(2)}) collective-permute-start(bf16[448,128]{1,0:T(8,128)(2,1)S(1)} %get-tuple-element.39), channel_id=1, source_target_pairs={{0,2},{1,15},{2,4},{3,9},{4,6},{5,11},{6,0},{7,13},{8,10},{9,7},{1... | collective-permute-start | bytes 344072 | tf_op jit(solution)/shard_map/ppermute | solution.py:443
  15.6 3.8 %collective-permute-start.5 = (bf16[448,128]{1,0:T(8,128)(2,1)S(1)}, bf16[448,128]{1,0:T(8,128)(2,1)S(1)}, u32[]{:S(2)}, u32[]{:S(2)}) collective-permute-start(bf16[448,128]{1,0:T(8,128)(2,1)S(1)} %get-tuple-element.40), channel_id=1, source_target_pairs={{0,14},{1,3},{2,8},{3,5},{4,10},{5,7},{6,12},{7,1},{8,6},{9,11},{1... | collective-permute-start | bytes 344072 | tf_op jit(solution)/shard_map/ppermute | solution.py:443
  19.4 0.7 %collective-permute-done.2.refs_2_ = bf16[448,128]{1,0:T(8,128)(2,1)S(1)} collective-permute-done((bf16[448,128]{1,0:T(8,128)(2,1)S(1)}, bf16[448,128]{1,0:T(8,128)(2,1)S(1)}, u32[]{:S(2)}, u32[]{:S(2)}) %collective-permute-start.2) | collective-permute-done | bytes 114720 | tf_op jit(solution)/shard_map/ppermute | solution.py:443
  20.2 1.6 %collective-permute-start.7 = (bf16[448,128]{1,0:T(8,128)(2,1)S(1)}, bf16[448,128]{1,0:T(8,128)(2,1)S(1)}, u32[]{:S(2)}, u32[]{:S(2)}) collective-permute-start(bf16[448,128]{1,0:T(8,128)(2,1)S(1)} %get-tuple-element.42), channel_id=1, source_target_pairs={{0,8},{1,5},{2,10},{3,7},{4,12},{5,1},{6,14},{7,3},{8,0},{9,13},{1... | collective-permute-start | bytes 344072 | tf_op jit(solution)/shard_map/ppermute | solution.py:443
  21.8 1.1 %turn_tiles.1.turned = bf16[88,128,128]{2,1,0:T(8,128)(2,1)S(1)} custom-call(s32[128]{0:T(128)S(1)} %get-tuple-element.27.far, s32[128]{0:T(128)S(1)} %get-tuple-element.28.near, bf16[88,128,128]{2,1,0:T(8,128)(2,1)S(1)} %get-tuple-element.33.held.tiles), custom_call_target="tpu_custom_call" | custom-call | tf_op jit(solution)/shard_map/turn_tiles/pallas_call | solution.py:217
  22.9 2.8 %collective-permute-done.6.refs_6_ = bf16[448,128]{1,0:T(8,128)(2,1)S(1)} collective-permute-done((bf16[448,128]{1,0:T(8,128)(2,1)S(1)}, bf16[448,128]{1,0:T(8,128)(2,1)S(1)}, u32[]{:S(2)}, u32[]{:S(2)}) %collective-permute-start.6) | collective-permute-done | bytes 114720 | tf_op jit(solution)/shard_map/ppermute | solution.py:443
  25.9 0.9 %collective-permute-start.14 = (bf16[448,128]{1,0:T(8,128)(2,1)S(1)}, bf16[448,128]{1,0:T(8,128)(2,1)S(1)}, u32[]{:S(2)}, u32[]{:S(2)}) collective-permute-start(bf16[448,128]{1,0:T(8,128)(2,1)S(1)} %chunk_sum.1.refs_0_), channel_id=1, source_target_pairs={{0,8},{1,5},{2,10},{3,7},{4,12},{5,1},{6,14},{7,3},{8,0},{9,13},{1... | collective-permute-start | bytes 344072 | tf_op jit(solution)/shard_map/ppermute | solution.py:446
  26.8 2.4 %collective-permute-start.13 = (bf16[448,128]{1,0:T(8,128)(2,1)S(1)}, bf16[448,128]{1,0:T(8,128)(2,1)S(1)}, u32[]{:S(2)}, u32[]{:S(2)}) collective-permute-start(bf16[448,128]{1,0:T(8,128)(2,1)S(1)} %chunk_sum.1.refs_0_), channel_id=1, source_target_pairs={{0,4},{1,9},{2,6},{3,11},{4,0},{5,13},{6,2},{7,15},{8,12},{9,1},{1... | collective-permute-start | bytes 344072 | tf_op jit(solution)/shard_map/ppermute | solution.py:446
  29.2 1.0 %collective-permute-start.12 = (bf16[448,128]{1,0:T(8,128)(2,1)S(1)}, bf16[448,128]{1,0:T(8,128)(2,1)S(1)}, u32[]{:S(2)}, u32[]{:S(2)}) collective-permute-start(bf16[448,128]{1,0:T(8,128)(2,1)S(1)} %chunk_sum.1.refs_0_), channel_id=1, source_target_pairs={{0,14},{1,3},{2,8},{3,5},{4,10},{5,7},{6,12},{7,1},{8,6},{9,11},{1... | collective-permute-start | bytes 344072 | tf_op jit(solution)/shard_map/ppermute | solution.py:446
  30.2 1.2 %collective-permute-start.11 = (bf16[448,128]{1,0:T(8,128)(2,1)S(1)}, bf16[448,128]{1,0:T(8,128)(2,1)S(1)}, u32[]{:S(2)}, u32[]{:S(2)}) collective-permute-start(bf16[448,128]{1,0:T(8,128)(2,1)S(1)} %chunk_sum.1.refs_0_), channel_id=1, source_target_pairs={{0,2},{1,15},{2,4},{3,9},{4,6},{5,11},{6,0},{7,13},{8,10},{9,7},{1... | collective-permute-start | bytes 344072 | tf_op jit(solution)/shard_map/ppermute | solution.py:446
  31.5 2.0 %collective-permute-start.10 = (bf16[448,128]{1,0:T(8,128)(2,1)S(1)}, bf16[448,128]{1,0:T(8,128)(2,1)S(1)}, u32[]{:S(2)}, u32[]{:S(2)}) collective-permute-start(bf16[448,128]{1,0:T(8,128)(2,1)S(1)} %chunk_sum.1.refs_0_), channel_id=1, source_target_pairs={{0,6},{1,11},{2,0},{3,13},{4,2},{5,15},{6,4},{7,9},{8,14},{9,3},{1... | collective-permute-start | bytes 344072 | tf_op jit(solution)/shard_map/ppermute | solution.py:446
  33.5 0.7 collective-permute-start.9
  34.1 2.7 %collective-permute-start.8 = (bf16[448,128]{1,0:T(8,128)(2,1)S(1)}, bf16[448,128]{1,0:T(8,128)(2,1)S(1)}, u32[]{:S(2)}, u32[]{:S(2)}) collective-permute-start(bf16[448,128]{1,0:T(8,128)(2,1)S(1)} %chunk_sum.1.refs_0_), channel_id=1, source_target_pairs={{0,12},{1,13},{2,14},{3,15},{4,8},{5,9},{6,10},{7,11},{8,4},{9,5},... | collective-permute-start | bytes 344072 | tf_op jit(solution)/shard_map/ppermute | solution.py:446
  37.6 3.2 %collective-permute-done.9.refs_2_ = bf16[448,128]{1,0:T(8,128)(2,1)S(1)} collective-permute-done((bf16[448,128]{1,0:T(8,128)(2,1)S(1)}, bf16[448,128]{1,0:T(8,128)(2,1)S(1)}, u32[]{:S(2)}, u32[]{:S(2)}) %collective-permute-start.9) | collective-permute-done | bytes 114720 | tf_op jit(solution)/shard_map/ppermute | solution.py:446
  40.7 2.1 %collective-permute-done.8.refs_1_ = bf16[448,128]{1,0:T(8,128)(2,1)S(1)} collective-permute-done((bf16[448,128]{1,0:T(8,128)(2,1)S(1)}, bf16[448,128]{1,0:T(8,128)(2,1)S(1)}, u32[]{:S(2)}, u32[]{:S(2)}) %collective-permute-start.8) | collective-permute-done | bytes 114720 | tf_op jit(solution)/shard_map/ppermute | solution.py:446
  43.2 0.9 %backward_near.1.first = f32[1152,128]{1,0:T(8,128)S(1)} custom-call(s32[128]{0:T(128)S(1)} %get-tuple-element.28.near, bf16[88,128,128]{2,1,0:T(8,128)(2,1)S(1)} %turn_tiles.1.turned, bf16[3584,128]{1,0:T(8,128)(2,1)S(1)} %gather_half.1.table.own), custom_call_target="tpu_custom_call" | custom-call | tf_op jit(solution)/shard_map/backward_near/pallas_call | solution.py:315
  44.1 1.6 %collective-permute-done.15.table = bf16[3584,128]{1,0:T(8,128)(2,1)S(1)} collective-permute-done((bf16[3584,128]{1,0:T(8,128)(2,1)S(1)}, bf16[3584,128]{1,0:T(8,128)(2,1)S(1)}, u32[]{:S(2)}, u32[]{:S(2)}) %collective-permute-start.15) | collective-permute-done | bytes 917536 | tf_op jit(solution)/shard_map/ppermute | solution.py:448
  45.7 1.6 %backward_far.1 = (f32[256,128]{1,0:T(8,128)S(1)}, bf16[256,128]{1,0:T(8,128)(2,1)S(1)}, bf16[256,128]{1,0:T(8,128)(2,1)S(1)}, bf16[256,128]{1,0:T(8,128)(2,1)S(1)}, bf16[448,128]{1,0:T(8,128)(2,1)}) custom-call(s32[128]{0:T(128)S(1)} %get-tuple-element.27.far, bf16[88,128,128]{2,1,0:T(8,128)(2,1)S(1)} %turn_tiles.1.turned, ...), custom_call_target="tpu_custom_call" | custom-call | tf_op jit(solution)/shard_map/backward_far/pallas_call | solution.py:362
  47.7 1.6 %collective-permute-start.17 = (bf16[256,128]{1,0:T(8,128)(2,1)S(1)}, bf16[256,128]{1,0:T(8,128)(2,1)S(1)}, u32[]{:S(2)}, u32[]{:S(2)}) collective-permute-start(bf16[256,128]{1,0:T(8,128)(2,1)S(1)} %get-tuple-element.46), channel_id=1, source_target_pairs={{0,192},{1,65},{2,194},{3,67},{4,196},{5,69},{6,198},{7,71},{8,200... | collective-permute-start | bytes 196616 | tf_op jit(solution)/shard_map/ppermute | solution.py:431
  49.3 2.0 %collective-permute-start.18 = (bf16[256,128]{1,0:T(8,128)(2,1)S(1)}, bf16[256,128]{1,0:T(8,128)(2,1)S(1)}, u32[]{:S(2)}, u32[]{:S(2)}) collective-permute-start(bf16[256,128]{1,0:T(8,128)(2,1)S(1)} %get-tuple-element.47), channel_id=1, source_target_pairs={{0,128},{1,129},{2,130},{3,131},{4,132},{5,133},{6,134},{7,135},{8... | collective-permute-start | bytes 196616 | tf_op jit(solution)/shard_map/ppermute | solution.py:431
  51.5 1.6 %collective-permute-done.17.g1 = bf16[256,128]{1,0:T(8,128)(2,1)S(1)} collective-permute-done((bf16[256,128]{1,0:T(8,128)(2,1)S(1)}, bf16[256,128]{1,0:T(8,128)(2,1)S(1)}, u32[]{:S(2)}, u32[]{:S(2)}) %collective-permute-start.17) | collective-permute-done | bytes 65568 | tf_op jit(solution)/shard_map/ppermute | solution.py:431
  53.1 2.4 %collective-permute-done.18.g2 = bf16[256,128]{1,0:T(8,128)(2,1)S(1)} collective-permute-done((bf16[256,128]{1,0:T(8,128)(2,1)S(1)}, bf16[256,128]{1,0:T(8,128)(2,1)S(1)}, u32[]{:S(2)}, u32[]{:S(2)}) %collective-permute-start.18) | collective-permute-done | bytes 65568 | tf_op jit(solution)/shard_map/ppermute | solution.py:431
  55.6 4.2 %collective-permute-start.19 = (bf16[64,128]{1,0:T(8,128)(2,1)S(1)}, bf16[64,128]{1,0:T(8,128)(2,1)S(1)}, u32[]{:S(2)}, u32[]{:S(2)}) collective-permute-start(bf16[64,128]{1,0:T(8,128)(2,1)S(1)} %get-tuple-element.49), channel_id=1, source_target_pairs={{0,16},{1,49},{2,18},{3,51},{4,20},{5,53},{6,22},{7,55},{8,24},{9,... | collective-permute-start | bytes 49160 | tf_op jit(solution)/shard_map/ppermute | solution.py:431
  59.9 2.0 %collective-permute-start.20 = (bf16[64,128]{1,0:T(8,128)(2,1)S(1)}, bf16[64,128]{1,0:T(8,128)(2,1)S(1)}, u32[]{:S(2)}, u32[]{:S(2)}) collective-permute-start(bf16[64,128]{1,0:T(8,128)(2,1)S(1)} %get-tuple-element.50), channel_id=1, source_target_pairs={{0,48},{1,17},{2,50},{3,19},{4,52},{5,21},{6,54},{7,23},{8,56},{9,... | collective-permute-start | bytes 49160 | tf_op jit(solution)/shard_map/ppermute | solution.py:431
  61.8 4.8 %collective-permute-start.21 = (bf16[64,128]{1,0:T(8,128)(2,1)S(1)}, bf16[64,128]{1,0:T(8,128)(2,1)S(1)}, u32[]{:S(2)}, u32[]{:S(2)}) collective-permute-start(bf16[64,128]{1,0:T(8,128)(2,1)S(1)} %get-tuple-element.51), channel_id=1, source_target_pairs={{0,32},{1,33},{2,34},{3,35},{4,36},{5,37},{6,38},{7,39},{8,40},{9,... | collective-permute-start | bytes 49160 | tf_op jit(solution)/shard_map/ppermute | solution.py:431
  66.6 2.9 %collective-permute-done.21.g2 = bf16[64,128]{1,0:T(8,128)(2,1)S(1)} collective-permute-done((bf16[64,128]{1,0:T(8,128)(2,1)S(1)}, bf16[64,128]{1,0:T(8,128)(2,1)S(1)}, u32[]{:S(2)}, u32[]{:S(2)}) %collective-permute-start.21) | collective-permute-done | bytes 16416 | tf_op jit(solution)/shard_map/ppermute | solution.py:431
  (22 shorter events, 2.9 us)
Async XLA Ops:
  4.8 2.6 %collective-permute-start = (bf16[3584,128]{1,0:T(8,128)(2,1)S(1)}, bf16[3584,128]{1,0:T(8,128)(2,1)S(1)}, u32[]{:S(2)}, u32[]{:S(2)}) collective-permute-start(bf16[3584,128]{1,0:T(8,128)(2,1)S(1)} %get-tuple-element.31), channel_id=1, source_target_pairs={{0,1},{1,0},{2,3},{3,2},{4,5},{5,4},{6,7},{7,6},{8,9},{9,8},{10,11... | collective-permute-start | bytes 2752520 | tf_op jit(solution)/shard_map/ppermute | solution.py:438
  7.6 11.8 %collective-permute-start.1 = (bf16[448,128]{1,0:T(8,128)(2,1)S(1)}, bf16[448,128]{1,0:T(8,128)(2,1)S(1)}, u32[]{:S(2)}, u32[]{:S(2)}) collective-permute-start(bf16[448,128]{1,0:T(8,128)(2,1)S(1)} %get-tuple-element.36), channel_id=1, source_target_pairs={{0,12},{1,13},{2,14},{3,15},{4,8},{5,9},{6,10},{7,11},{8,4},{9,5},... | collective-permute-start | bytes 344072 | tf_op jit(solution)/shard_map/ppermute | solution.py:443
  12.1 8.1 %collective-permute-start.2 = (bf16[448,128]{1,0:T(8,128)(2,1)S(1)}, bf16[448,128]{1,0:T(8,128)(2,1)S(1)}, u32[]{:S(2)}, u32[]{:S(2)}) collective-permute-start(bf16[448,128]{1,0:T(8,128)(2,1)S(1)} %get-tuple-element.37), channel_id=1, source_target_pairs={{0,10},{1,7},{2,12},{3,1},{4,14},{5,3},{6,8},{7,5},{8,2},{9,15},{1... | collective-permute-start | bytes 344072 | tf_op jit(solution)/shard_map/ppermute | solution.py:443
  13.6 9.3 %collective-permute-start.3 = (bf16[448,128]{1,0:T(8,128)(2,1)S(1)}, bf16[448,128]{1,0:T(8,128)(2,1)S(1)}, u32[]{:S(2)}, u32[]{:S(2)}) collective-permute-start(bf16[448,128]{1,0:T(8,128)(2,1)S(1)} %get-tuple-element.38), channel_id=1, source_target_pairs={{0,6},{1,11},{2,0},{3,13},{4,2},{5,15},{6,4},{7,9},{8,14},{9,3},{1... | collective-permute-start | bytes 344072 | tf_op jit(solution)/shard_map/ppermute | solution.py:443
  14.8 8.1 %collective-permute-start.4 = (bf16[448,128]{1,0:T(8,128)(2,1)S(1)}, bf16[448,128]{1,0:T(8,128)(2,1)S(1)}, u32[]{:S(2)}, u32[]{:S(2)}) collective-permute-start(bf16[448,128]{1,0:T(8,128)(2,1)S(1)} %get-tuple-element.39), channel_id=1, source_target_pairs={{0,2},{1,15},{2,4},{3,9},{4,6},{5,11},{6,0},{7,13},{8,10},{9,7},{1... | collective-permute-start | bytes 344072 | tf_op jit(solution)/shard_map/ppermute | solution.py:443
  15.6 7.3 %collective-permute-start.5 = (bf16[448,128]{1,0:T(8,128)(2,1)S(1)}, bf16[448,128]{1,0:T(8,128)(2,1)S(1)}, u32[]{:S(2)}, u32[]{:S(2)}) collective-permute-start(bf16[448,128]{1,0:T(8,128)(2,1)S(1)} %get-tuple-element.40), channel_id=1, source_target_pairs={{0,14},{1,3},{2,8},{3,5},{4,10},{5,7},{6,12},{7,1},{8,6},{9,11},{1... | collective-permute-start | bytes 344072 | tf_op jit(solution)/shard_map/ppermute | solution.py:443
  19.4 6.3 %collective-permute-start.6 = (bf16[448,128]{1,0:T(8,128)(2,1)S(1)}, bf16[448,128]{1,0:T(8,128)(2,1)S(1)}, u32[]{:S(2)}, u32[]{:S(2)}) collective-permute-start(bf16[448,128]{1,0:T(8,128)(2,1)S(1)} %get-tuple-element.41), channel_id=1, source_target_pairs={{0,4},{1,9},{2,6},{3,11},{4,0},{5,13},{6,2},{7,15},{8,12},{9,1},{1... | collective-permute-start | bytes 344072 | tf_op jit(solution)/shard_map/ppermute | solution.py:443
  20.2 5.5 %collective-permute-start.7 = (bf16[448,128]{1,0:T(8,128)(2,1)S(1)}, bf16[448,128]{1,0:T(8,128)(2,1)S(1)}, u32[]{:S(2)}, u32[]{:S(2)}) collective-permute-start(bf16[448,128]{1,0:T(8,128)(2,1)S(1)} %get-tuple-element.42), channel_id=1, source_target_pairs={{0,8},{1,5},{2,10},{3,7},{4,12},{5,1},{6,14},{7,3},{8,0},{9,13},{1... | collective-permute-start | bytes 344072 | tf_op jit(solution)/shard_map/ppermute | solution.py:443
  25.9 7.6 %collective-permute-start.14 = (bf16[448,128]{1,0:T(8,128)(2,1)S(1)}, bf16[448,128]{1,0:T(8,128)(2,1)S(1)}, u32[]{:S(2)}, u32[]{:S(2)}) collective-permute-start(bf16[448,128]{1,0:T(8,128)(2,1)S(1)} %chunk_sum.1.refs_0_), channel_id=1, source_target_pairs={{0,8},{1,5},{2,10},{3,7},{4,12},{5,1},{6,14},{7,3},{8,0},{9,13},{1... | collective-permute-start | bytes 344072 | tf_op jit(solution)/shard_map/ppermute | solution.py:446
  26.8 7.4 %collective-permute-start.13 = (bf16[448,128]{1,0:T(8,128)(2,1)S(1)}, bf16[448,128]{1,0:T(8,128)(2,1)S(1)}, u32[]{:S(2)}, u32[]{:S(2)}) collective-permute-start(bf16[448,128]{1,0:T(8,128)(2,1)S(1)} %chunk_sum.1.refs_0_), channel_id=1, source_target_pairs={{0,4},{1,9},{2,6},{3,11},{4,0},{5,13},{6,2},{7,15},{8,12},{9,1},{1... | collective-permute-start | bytes 344072 | tf_op jit(solution)/shard_map/ppermute | solution.py:446
  29.2 7.6 %collective-permute-start.12 = (bf16[448,128]{1,0:T(8,128)(2,1)S(1)}, bf16[448,128]{1,0:T(8,128)(2,1)S(1)}, u32[]{:S(2)}, u32[]{:S(2)}) collective-permute-start(bf16[448,128]{1,0:T(8,128)(2,1)S(1)} %chunk_sum.1.refs_0_), channel_id=1, source_target_pairs={{0,14},{1,3},{2,8},{3,5},{4,10},{5,7},{6,12},{7,1},{8,6},{9,11},{1... | collective-permute-start | bytes 344072 | tf_op jit(solution)/shard_map/ppermute | solution.py:446
  30.2 7.2 %collective-permute-start.11 = (bf16[448,128]{1,0:T(8,128)(2,1)S(1)}, bf16[448,128]{1,0:T(8,128)(2,1)S(1)}, u32[]{:S(2)}, u32[]{:S(2)}) collective-permute-start(bf16[448,128]{1,0:T(8,128)(2,1)S(1)} %chunk_sum.1.refs_0_), channel_id=1, source_target_pairs={{0,2},{1,15},{2,4},{3,9},{4,6},{5,11},{6,0},{7,13},{8,10},{9,7},{1... | collective-permute-start | bytes 344072 | tf_op jit(solution)/shard_map/ppermute | solution.py:446
  31.5 6.1 %collective-permute-start.10 = (bf16[448,128]{1,0:T(8,128)(2,1)S(1)}, bf16[448,128]{1,0:T(8,128)(2,1)S(1)}, u32[]{:S(2)}, u32[]{:S(2)}) collective-permute-start(bf16[448,128]{1,0:T(8,128)(2,1)S(1)} %chunk_sum.1.refs_0_), channel_id=1, source_target_pairs={{0,6},{1,11},{2,0},{3,13},{4,2},{5,15},{6,4},{7,9},{8,14},{9,3},{1... | collective-permute-start | bytes 344072 | tf_op jit(solution)/shard_map/ppermute | solution.py:446
  33.5 7.2 %collective-permute-start.9 = (bf16[448,128]{1,0:T(8,128)(2,1)S(1)}, bf16[448,128]{1,0:T(8,128)(2,1)S(1)}, u32[]{:S(2)}, u32[]{:S(2)}) collective-permute-start(bf16[448,128]{1,0:T(8,128)(2,1)S(1)} %chunk_sum.1.refs_0_), channel_id=1, source_target_pairs={{0,10},{1,7},{2,12},{3,1},{4,14},{5,3},{6,8},{7,5},{8,2},{9,15},{1... | collective-permute-start | bytes 344072 | tf_op jit(solution)/shard_map/ppermute | solution.py:446
  34.1 8.7 %collective-permute-start.8 = (bf16[448,128]{1,0:T(8,128)(2,1)S(1)}, bf16[448,128]{1,0:T(8,128)(2,1)S(1)}, u32[]{:S(2)}, u32[]{:S(2)}) collective-permute-start(bf16[448,128]{1,0:T(8,128)(2,1)S(1)} %chunk_sum.1.refs_0_), channel_id=1, source_target_pairs={{0,12},{1,13},{2,14},{3,15},{4,8},{5,9},{6,10},{7,11},{8,4},{9,5},... | collective-permute-start | bytes 344072 | tf_op jit(solution)/shard_map/ppermute | solution.py:446
  42.9 2.7 %collective-permute-start.15 = (bf16[3584,128]{1,0:T(8,128)(2,1)S(1)}, bf16[3584,128]{1,0:T(8,128)(2,1)S(1)}, u32[]{:S(2)}, u32[]{:S(2)}) collective-permute-start(bf16[3584,128]{1,0:T(8,128)(2,1)S(1)} %gather_half.1.table.own), channel_id=1, source_target_pairs={{0,1},{1,0},{2,3},{3,2},{4,5},{5,4},{6,7},{7,6},{8,9},{9,8},{10,11... | collective-permute-start | bytes 2752520 | tf_op jit(solution)/shard_map/ppermute | solution.py:448
  47.2 4.3 %collective-permute-start.16 = (bf16[256,128]{1,0:T(8,128)(2,1)S(1)}, bf16[256,128]{1,0:T(8,128)(2,1)S(1)}, u32[]{:S(2)}, u32[]{:S(2)}) collective-permute-start(bf16[256,128]{1,0:T(8,128)(2,1)S(1)} %get-tuple-element.45), channel_id=1, source_target_pairs={{0,64},{1,193},{2,66},{3,195},{4,68},{5,197},{6,70},{7,199},{8,72}... | collective-permute-start | bytes 196616 | tf_op jit(solution)/shard_map/ppermute | solution.py:431
  47.7 5.5 %collective-permute-start.17 = (bf16[256,128]{1,0:T(8,128)(2,1)S(1)}, bf16[256,128]{1,0:T(8,128)(2,1)S(1)}, u32[]{:S(2)}, u32[]{:S(2)}) collective-permute-start(bf16[256,128]{1,0:T(8,128)(2,1)S(1)} %get-tuple-element.46), channel_id=1, source_target_pairs={{0,192},{1,65},{2,194},{3,67},{4,196},{5,69},{6,198},{7,71},{8,200... | collective-permute-start | bytes 196616 | tf_op jit(solution)/shard_map/ppermute | solution.py:431
  49.3 6.3 %collective-permute-start.18 = (bf16[256,128]{1,0:T(8,128)(2,1)S(1)}, bf16[256,128]{1,0:T(8,128)(2,1)S(1)}, u32[]{:S(2)}, u32[]{:S(2)}) collective-permute-start(bf16[256,128]{1,0:T(8,128)(2,1)S(1)} %get-tuple-element.47), channel_id=1, source_target_pairs={{0,128},{1,129},{2,130},{3,131},{4,132},{5,133},{6,134},{7,135},{8... | collective-permute-start | bytes 196616 | tf_op jit(solution)/shard_map/ppermute | solution.py:431
  55.6 11.0 %collective-permute-start.19 = (bf16[64,128]{1,0:T(8,128)(2,1)S(1)}, bf16[64,128]{1,0:T(8,128)(2,1)S(1)}, u32[]{:S(2)}, u32[]{:S(2)}) collective-permute-start(bf16[64,128]{1,0:T(8,128)(2,1)S(1)} %get-tuple-element.49), channel_id=1, source_target_pairs={{0,16},{1,49},{2,18},{3,51},{4,20},{5,53},{6,22},{7,55},{8,24},{9,... | collective-permute-start | bytes 49160 | tf_op jit(solution)/shard_map/ppermute | solution.py:431
  59.9 6.8 %collective-permute-start.20 = (bf16[64,128]{1,0:T(8,128)(2,1)S(1)}, bf16[64,128]{1,0:T(8,128)(2,1)S(1)}, u32[]{:S(2)}, u32[]{:S(2)}) collective-permute-start(bf16[64,128]{1,0:T(8,128)(2,1)S(1)} %get-tuple-element.50), channel_id=1, source_target_pairs={{0,48},{1,17},{2,50},{3,19},{4,52},{5,21},{6,54},{7,23},{8,56},{9,... | collective-permute-start | bytes 49160 | tf_op jit(solution)/shard_map/ppermute | solution.py:431
  61.8 7.6 %collective-permute-start.21 = (bf16[64,128]{1,0:T(8,128)(2,1)S(1)}, bf16[64,128]{1,0:T(8,128)(2,1)S(1)}, u32[]{:S(2)}, u32[]{:S(2)}) collective-permute-start(bf16[64,128]{1,0:T(8,128)(2,1)S(1)} %get-tuple-element.51), channel_id=1, source_target_pairs={{0,32},{1,33},{2,34},{3,35},{4,36},{5,37},{6,38},{7,39},{8,40},{9,... | collective-permute-start | bytes 49160 | tf_op jit(solution)/shard_map/ppermute | solution.py:431

commit v3 on v2

--- a/solution.py
+++ b/solution.py
@@ -12,22 +12,21 @@
 SB_DEV = 8
 HALF_BLOCKS = KB_DEV // 2
 HALF = HALF_BLOCKS * TILE
-CHUNK = HALF // 8
+CHUNK_BLOCKS = KB_DEV // 8
+CHUNK = CHUNK_BLOCKS * TILE
 UNROLL = 12
 LIST = 128
 VMEM_LIMIT = 48 * 1024 * 1024
 
 ROUNDS = (
-    ((2, 1), (2, 1)),
-    ((1, 1), (3, 0)),
+    ((2, 0), (2, 1)),
+    ((1, 0), (3, 1)),
     ((3, 0), (1, 1)),
-    ((1, 0), (3, 1)),
-    ((3, 1), (1, 0)),
-    ((2, 0), (0, 1)),
-    ((0, 1), (2, 0)),
+    ((0, 1), (0, 0)),
 )
-
-LINE = ((1, 3), (3, 1), (2, 2))
+BACK = (0, 2, 1, 3)
+
+LINE = ((2, 2), (1, 3), (3, 1))
 
 
 def vm():
@@ -56,15 +55,6 @@
     return out
 
 
-def peer_chunk(r, sign):
-    z, x, c = place()
-    (dx0, dz0), (dx1, dz1) = ROUNDS[r]
-    dx = jnp.where(c == 0, dx0, dx1) * sign
-    dz = jnp.where(c == 0, dz0, dz1)
-    zz = z + dz - 2 * z * dz
-    return zz * 4 + (x + dx + 4) % 4
-
-
 def block(i):
     return pl.ds(pl.multiple_of(i * TILE, TILE), TILE)
 
@@ -73,20 +63,29 @@
     return lax.rem(word, 128), lax.rem(lax.div(word, 128), 64), lax.div(word, 8192)
 
 
-def list_slots(rows, cols, count, base, far, near):
+def list_slots(rows, cols, count, far, near, shift, owner):
     cap = rows.shape[0]
+    z, x, c = place()
+    for m in range(8):
+        dx = lax.rem(m % 4 + 4 - x, 4)
+        same_z = z == m // 4
+        for_core0 = jnp.where(dx == 0, jnp.logical_not(same_z), same_z)
+        core = 1 - for_core0.astype(jnp.int32)
+        d = jnp.where(core == 0, dx, lax.rem(4 - dx, 4))
+        q = jnp.where(d == 0, 3, jnp.where(d == 2, 0, jnp.where(d == 1, 1, 2)))
+        shift[m] = (q - m) * CHUNK_BLOCKS
+        owner[m] = (core == c).astype(jnp.int32)
 
     def visit(s, carry):
         n_far, n_near = carry
-        row = rows[s] - base
-        inside = jnp.logical_and(row >= 0, row < HALF_BLOCKS)
-        within = jnp.where(inside, row, rows[s] - (HALF_BLOCKS - base))
-        word = s + within * 128 + cols[s] * 8192
+        row = rows[s]
+        m = (row * 37) >> 8
+        word = s + (row + shift[m]) * 128 + cols[s] * 8192
         far[n_far] = word
         near[n_near] = word
         used = (s < count).astype(jnp.int32)
-        here = inside.astype(jnp.int32)
-        return n_far + used * (1 - here), n_near + used * here
+        here = used * owner[m]
+        return n_far + used - here, n_near + here
 
     n_far, n_near = lax.fori_loop(0, cap, visit, (jnp.int32(0), jnp.int32(0)), unroll=8)
     pad = HALF_BLOCKS * 128 + SB_DEV * 8192
@@ -120,7 +119,7 @@
 
 
 def forward_far_kernel(
-    rows, cols, count, tiles, omega, out, held, table, far, near, acc, s_rows, s_cols, sems
+    rows, cols, count, tiles, omega, out, held, table, far, near, acc, s_rows, s_cols, shift, owner, sems
 ):
     small = [
         pltpu.make_async_copy(rows, s_rows, sems.at[0]),
@@ -132,8 +131,7 @@
     fetch_omega.start()
     for copy in small:
         copy.wait()
-    _, _, c = place()
-    n_far, n_near = list_slots(s_rows, s_cols, count[0], c * HALF_BLOCKS, far, near)
+    n_far, n_near = list_slots(s_rows, s_cols, count[0], far, near, shift, owner)
 
     def fetch(entries, sem, k):
         slot = lax.rem(entries[k], 128)
@@ -180,6 +178,8 @@
             pltpu.VMEM((HALF + TILE, TILE), jnp.float32),
             pltpu.SMEM((cap,), jnp.int32),
             pltpu.SMEM((cap,), jnp.int32),
+            pltpu.SMEM((8,), jnp.int32),
+            pltpu.SMEM((8,), jnp.int32),
             pltpu.SemaphoreType.DMA((5,)),
         ],
         compiler_params=params(),
@@ -224,34 +224,29 @@
     )(far, near, tiles)
 
 
-def chunk_at(i):
-    return pl.ds(pl.multiple_of(i * CHUNK, CHUNK), CHUNK)
-
-
-def pair_kernel(a, b, own, *sends):
-    def total(i):
-        at = chunk_at(i)
-        return (a[at, :].astype(jnp.float32) + b[at, :].astype(jnp.float32)).astype(jnp.bfloat16)
-
-    z, x, _ = place()
-    for r, send in enumerate(sends):
-        send[...] = total(peer_chunk(r, 1))
-    own[...] = total(z * 4 + x)
+def chunk_at(q):
+    return pl.ds(q * CHUNK, CHUNK)
+
+
+def pair_kernel(a, b, *sends):
+    for q, send in enumerate(sends):
+        at = chunk_at(q)
+        send[...] = (a[at, :].astype(jnp.float32) + b[at, :].astype(jnp.float32)).astype(jnp.bfloat16)
 
 
 def pair_sum(a, b):
     shape = jax.ShapeDtypeStruct((CHUNK, TILE), jnp.bfloat16)
     return pl.pallas_call(
         pair_kernel,
-        out_shape=[shape] * 8,
+        out_shape=[shape] * 4,
         in_specs=[vm(), vm()],
-        out_specs=[vm()] * 8,
+        out_specs=[vm()] * 4,
         compiler_params=params(),
         name="pair_sum",
     )(a, b)
 
 
-def chunk_kernel(*refs):
+def part_kernel(*refs):
     out = refs[-1]
     total = refs[0][...].astype(jnp.float32)
     for ref in refs[1:-1]:
@@ -259,34 +254,52 @@
     out[...] = total.astype(jnp.bfloat16)
 
 
-def chunk_sum(parts):
-    return pl.pallas_call(
-        chunk_kernel,
+def part_sum(parts):
+    return pl.pallas_call(
+        part_kernel,
         out_shape=jax.ShapeDtypeStruct((CHUNK, TILE), jnp.bfloat16),
         in_specs=[vm()] * len(parts),
         out_specs=vm(),
         compiler_params=params(),
+        name="part_sum",
+    )(*parts)
+
+
+def chunk_kernel(mine, got, out, sketch):
+    out[...] = (mine[...].astype(jnp.float32) + got[...].astype(jnp.float32)).astype(jnp.bfloat16)
+    _, _, c = place()
+    size = sketch.shape[0]
+    sketch[...] = out[pl.ds(pl.multiple_of(c * size, size), size), :]
+
+
+def chunk_sum(mine, got):
+    return pl.pallas_call(
+        chunk_kernel,
+        out_shape=[
+            jax.ShapeDtypeStruct((CHUNK, TILE), jnp.bfloat16),
+            jax.ShapeDtypeStruct((CHUNK // 2, TILE), jnp.bfloat16),
+        ],
+        in_specs=[vm(), vm()],
+        out_specs=[vm(), vm()],
+        compiler_params=params(),
         name="chunk_sum",
-    )(*parts)
+    )(mine, got)
 
 
 def gather_kernel(*refs):
-    z, x, _ = place()
-    out = refs[-1]
-    out[chunk_at(z * 4 + x), :] = refs[0][...]
-    for r, ref in enumerate(refs[1:-1]):
-        out[chunk_at(peer_chunk(r, -1)), :] = ref[...]
-
-
-def gather_half(own, got):
+    for q in range(4):
+        refs[-1][chunk_at(q), :] = refs[BACK[q]][...]
+
+
+def gather_half(got):
     return pl.pallas_call(
         gather_kernel,
         out_shape=jax.ShapeDtypeStruct((HALF, TILE), jnp.bfloat16),
-        in_specs=[vm()] * 8,
+        in_specs=[vm()] * 4,
         out_specs=vm(),
         compiler_params=params(),
         name="gather_half",
-    )(own, *got)
+    )(*got)
 
 
 def backward_slots(n, entries, turned, table, acc):
@@ -322,9 +335,9 @@
     )(near, turned, table)
 
 
-def line_offset(r, sign):
+def line_offset(r):
     _, _, c = place()
-    return jnp.where(c == 0, LINE[r][0], LINE[r][1]) * sign
+    return jnp.where(c == 0, LINE[r][0], LINE[r][1])
 
 
 def share_at(i, size):
@@ -336,99 +349,103 @@
     return i // 4, i % 4
 
 
-def backward_far_kernel(far, turned, first, own, table, keep, s0, s1, s2, sketch, acc):
+def backward_far_kernel(far, turned, first, table, keep, s0, s1, s2, acc):
     acc[...] = first[...]
     backward_slots(far[LIST - 1], far, turned, table, acc)
     y, _ = kmer_place()
     size = keep.shape[0]
     for r, send in enumerate((s0, s1, s2)):
-        send[...] = acc[share_at(y + line_offset(r, 1), size), :].astype(jnp.bfloat16)
+        send[...] = acc[share_at(y + line_offset(r), size), :].astype(jnp.bfloat16)
     keep[...] = acc[share_at(y, size), :]
-    z, x, c = place()
-    at = chunk_at(x * 2 + c)
-
-    @pl.when(z == c)
-    def _():
-        sketch[...] = own[at, :]
-
-    @pl.when(z != c)
-    def _():
-        sketch[...] = table[at, :]
-
-
-def backward_far(far, turned, first, own, table):
+
+
+def backward_far(far, turned, first, table):
     share = SB_DEV * TILE // 4
     send = jax.ShapeDtypeStruct((share, TILE), jnp.bfloat16)
     return pl.pallas_call(
         backward_far_kernel,
-        out_shape=[
-            jax.ShapeDtypeStruct((share, TILE), jnp.float32),
-            send,
-            send,
-            send,
-            jax.ShapeDtypeStruct((CHUNK, TILE), jnp.bfloat16),
-        ],
-        in_specs=[sm(), vm(), vm(), vm(), vm()],
-        out_specs=[vm()] * 5,
+        out_shape=[jax.ShapeDtypeStruct((share, TILE), jnp.float32), send, send, send],
+        in_specs=[sm(), vm(), vm(), vm()],
+        out_specs=[vm()] * 4,
         scratch_shapes=[pltpu.VMEM(((SB_DEV + 1) * TILE, TILE), jnp.float32)],
         compiler_params=params(),
         name="backward_far",
-    )(far, turned, first, own, table)
-
-
-def line_kernel(own, g0, g1, g2, keep, s0, s1, s2, acc):
+    )(far, turned, first, table)
+
+
+def line_kernel(own, g0, g1, g2, keep, send, acc):
     total = own[...]
     for got in (g0, g1, g2):
         total = total + got[...].astype(jnp.float32)
     acc[...] = total
     _, zh = kmer_place()
-    size = keep.shape[0]
-    for r, send in enumerate((s0, s1, s2)):
-        send[...] = acc[share_at(zh + line_offset(r, 1), size), :].astype(jnp.bfloat16)
-    keep[...] = acc[share_at(zh, size), :]
+    size = keep.shape[0] // 2
+    peer = zh + 1 - 2 * lax.rem(zh, 2)
+    for k, (mine, theirs) in enumerate(((zh, peer), (3 - zh, 3 - peer))):
+        keep[pl.ds(k * size, size), :] = acc[share_at(mine, size), :]
+        send[pl.ds(k * size, size), :] = acc[share_at(theirs, size), :].astype(jnp.bfloat16)
 
 
 def line_sum(own, got):
-    share = own.shape[0] // 4
-    send = jax.ShapeDtypeStruct((share, TILE), jnp.bfloat16)
+    half = own.shape[0] // 2
     return pl.pallas_call(
         line_kernel,
-        out_shape=[jax.ShapeDtypeStruct((share, TILE), jnp.float32), send, send, send],
+        out_shape=[
+            jax.ShapeDtypeStruct((half, TILE), jnp.float32),
+            jax.ShapeDtypeStruct((half, TILE), jnp.bfloat16),
+        ],
         in_specs=[vm()] * 4,
-        out_specs=[vm()] * 4,
+        out_specs=[vm()] * 2,
         scratch_shapes=[pltpu.VMEM(own.shape, jnp.float32)],
         compiler_params=params(),
         name="line_sum",
     )(own, *got)
 
 
-def last_kernel(factor, own, g0, g1, g2, out):
-    total = own[...]
-    for got in (g0, g1, g2):
-        total = total + got[...].astype(jnp.float32)
-    out[...] = total * factor
+def halve_kernel(own, got, keep, send):
+    size = keep.shape[0]
+    total = own[...] + got[...].astype(jnp.float32)
+    keep[...] = total[:size]
+    send[...] = total[size:].astype(jnp.bfloat16)
+
+
+def halve_sum(own, got):
+    half = own.shape[0] // 2
+    return pl.pallas_call(
+        halve_kernel,
+        out_shape=[
+            jax.ShapeDtypeStruct((half, TILE), jnp.float32),
+            jax.ShapeDtypeStruct((half, TILE), jnp.bfloat16),
+        ],
+        in_specs=[vm()] * 2,
+        out_specs=[vm()] * 2,
+        compiler_params=params(),
+        name="halve_sum",
+    )(own, got)
+
+
+def last_kernel(factor, own, got, out):
+    out[...] = (own[...] + got[...].astype(jnp.float32)) * factor
 
 
 def last_sum(factor, own, got):
     return pl.pallas_call(
         functools.partial(last_kernel, factor),
         out_shape=jax.ShapeDtypeStruct(own.shape, jnp.float32),
-        in_specs=[vm()] * 4,
+        in_specs=[vm()] * 2,
         out_specs=vm(),
         compiler_params=params(),
         name="last_sum",
-    )(own, *got)
-
-
-def line_permute(value, r, along_y):
+    )(own, got)
+
+
+def y_pairs(r):
     out = []
     for i in range(16):
         for j in range(16):
-            y, zh = i // 4, i % 4
-            off = LINE[r][j % 2]
-            to = ((y + off) % 4) * 4 + zh if along_y else y * 4 + (zh + off) % 4
+            to = ((i // 4 + LINE[r][j % 2]) % 4) * 4 + i % 4
             out.append((i * 16 + j, to * 16 + j))
-    return lax.ppermute(value, ("kmer", "samp"), out)
+    return out
 
 
 def shards(tiles, omega, tile_rows, tile_cols, tile_count):
@@ -437,20 +454,21 @@
     other, held, table, far, near = forward_far(tile_rows, tile_cols, tile_count, tiles, omega)
     got = lax.ppermute(other, "samp", swap)
     mine = forward_near(near, held, table)
-    own, *sends = pair_sum(mine, got)
-    held, _ = lax.optimization_barrier((held, own))
+    sends = pair_sum(mine, got)
+    held, *_ = lax.optimization_barrier((held, *sends))
     turned = turn(far, near, held)
     parts = [lax.ppermute(s, "samp", pairs(r)) for r, s in enumerate(sends)]
-    own, turned = lax.optimization_barrier((own, turned))
-    chunk = chunk_sum([own, *parts])
-    pieces = [lax.ppermute(chunk, "samp", pairs(r)) for r in range(7)]
-    own_half = gather_half(chunk, pieces)
-    other_half = lax.ppermute(own_half, "samp", swap)
-    first = backward_near(near, turned, own_half)
-    keep, *shares, sketch = backward_far(far, turned, first, own_half, other_half)
-    got = [line_permute(s, r, True) for r, s in enumerate(shares)]
-    keep, *shares = line_sum(keep, got)
-    got = [line_permute(s, r, False) for r, s in enumerate(shares)]
+    *parts, turned = lax.optimization_barrier((*parts, turned))
+    part = part_sum(parts)
+    chunk, sketch = chunk_sum(part, lax.ppermute(part, "samp", swap))
+    half = gather_half([lax.ppermute(chunk, "samp", pairs(r)) for r in (3, 2, 1, 0)][::-1])
+    rest = lax.ppermute(half, "samp", swap)
+    first = backward_near(near, turned, half)
+    keep, *shares = backward_far(far, turned, first, rest)
+    got = [lax.ppermute(s, ("kmer", "samp"), y_pairs(r)) for r, s in enumerate(shares)]
+    keep, share = line_sum(keep, got)
+    keep, share = halve_sum(keep, lax.ppermute(share, "kmer", [(i, i ^ 1) for i in range(16)]))
+    got = lax.ppermute(share, "kmer", [(i, i // 4 * 4 + 3 - i % 4) for i in range(16)])
     factor = 1.0 / (KB_DEV * TILE * kmers) ** 0.5
     return sketch, last_sum(factor, keep, got)
 

time: 71.5 us -> 71 us (level); the launches traced: 70.1 us -> 70.7 us
  waiting for transfers between devices: 19.8 us -> 28.8 us
  starting transfers between devices: 39.7 us -> 31.5 us
    ppermute x14 -> x11, waiting for transfers between devices: 14.7 us -> 23.1 us  [the longest x4 10.7 us: shards(): lax.ppermute(chunk, 'samp', pairs(r))]
    ppermute x14 -> x11, starting transfers between devices: 26.2 us -> 21.3 us  [the longest x1 6.03 us: shards(): lax.ppermute(share, 'kmer', [(i, i // 4 * 4 + 3 - i % 4) for i in range(1...]
    ppermute x7 -> x4, starting transfers between devices: 13.4 us -> 10.1 us  [shards(): parts = [lax.ppermute(s, 'samp', pairs(r)) for r, s in enumerate(sends)]]
    pallas_call x3 -> x5, Pallas kernels: 0.41 us -> 1.15 us  [the longest x1 0.75 us: chunk_sum(): pl.pallas_call(chunk_kernel, out_shape=[jax.ShapeDtypeStruct((CHUNK, TILE...]
    ppermute x7 -> x4, waiting for transfers between devices: 3.61 us -> 4.26 us  [shards(): parts = [lax.ppermute(s, 'samp', pairs(r)) for r, s in enumerate(sends)]]
  transfers between devices with their start and end apart: 22 -> 16, of which waited for: 12 -> 12; matrix products, arithmetic and copies ran while one was open for 0% -> 0% of each run, Pallas kernels for 4% -> 4%
where the time goes in v3:
time: 71 us; the launch traced here: 70.7 us
  starting transfers between devices  31.5 us (44%)
  waiting for transfers between devices  28.8 us (41%)
  Pallas kernels  8.98 us (13%)
  between operations  1.39 us (2%)
    ppermute x4, waiting for transfers between devices, shards(): lax.ppermute(chunk, 'samp', pairs(r))  10.7 us
    ppermute x4, starting transfers between devices, shards(): parts = [lax.ppermute(s, 'samp', pairs(r)) for r, s in enumerate(sends)]  10.1 us
    ppermute x1, starting transfers between devices, shards(): lax.ppermute(share, 'kmer', [(i, i // 4 * 4 + 3 - i % 4) for i in range(1...  6.03 us
    ppermute x4, starting transfers between devices, shards(): lax.ppermute(chunk, 'samp', pairs(r))  5.96 us
    ppermute x3, waiting for transfers between devices, shards(): lax.ppermute(s, ('kmer', 'samp'), y_pairs(r))  5.47 us
    ppermute x4, waiting for transfers between devices, shards(): parts = [lax.ppermute(s, 'samp', pairs(r)) for r, s in enumerate(sends)]  4.26 us
    ppermute x1, starting transfers between devices, shards(): chunk, sketch = chunk_sum(part, lax.ppermute(part, 'samp', swap))  3.72 us
    pallas_call x1, Pallas kernels, forward_far(): pl.pallas_call(forward_far_kernel, out_shape=[jax.ShapeDtypeStruct((HALF,...  3.42 us
  transfers between devices with their start and end apart: 16, of which 12 were waited for; matrix products, arithmetic and copies ran while one was open for 0% of the time, Pallas kernels for 4%

profile of v3, /device:TPU:24, one launch (start us, length us, event | category | flops | bytes accessed | tf_op | source)
XLA Modules:
  0.0 70.7 jit_solution(17051949731174383622)
XLA Ops:
  1.3 3.4 %forward_far.1 = (bf16[3584,128]{1,0:T(8,128)(2,1)S(1)}, bf16[88,128,128]{2,1,0:T(8,128)(2,1)S(1)}, bf16[1024,128]{1,0:T(8,128)(2,1)S(1)}, s32[128]{0:T(128)S(1)}, s32[128]{0:T(128)S(1)}) custom-call(s32[88]{0:T(128)} %rows.1, s32[88]{0:T(128)} %cols.1, s32[1]{0:T(128)S(6)} %copy.7.count, bf16[88,128,128]{2,1,0:T(8,128)(2,1)} %tiles.1, bf16[1024,128]{1,0:T(8,128)(2,1)} %omega.1), custom_call_target="tpu_custom_call" | custom-call | tf_op jit(solution)/shard_map/forward_far/pallas_call | solution.py:166
  4.8 1.0 %forward_near.1.a = bf16[3584,128]{1,0:T(8,128)(2,1)S(1)} custom-call(s32[128]{0:T(128)S(1)} %get-tuple-element.27.near, bf16[88,128,128]{2,1,0:T(8,128)(2,1)S(1)} %get-tuple-element.36.held.tiles, bf16[1024,128]{1,0:T(8,128)(2,1)S(1)} %get-tuple-element.29.table), custom_call_target="tpu_custom_call" | custom-call | tf_op jit(solution)/shard_map/forward_near/pallas_call | solution.py:196
  5.9 1.4 %collective-permute-done.b = bf16[3584,128]{1,0:T(8,128)(2,1)S(1)} collective-permute-done((bf16[3584,128]{1,0:T(8,128)(2,1)S(1)}, bf16[3584,128]{1,0:T(8,128)(2,1)S(1)}, u32[]{:S(2)}, u32[]{:S(2)}) %collective-permute-start) | collective-permute-done | bytes 917536 | tf_op jit(solution)/shard_map/ppermute | solution.py:455
  7.3 0.2 pair_sum.1
  7.5 3.1 %collective-permute-start.1 = (bf16[896,128]{1,0:T(8,128)(2,1)S(1)}, bf16[896,128]{1,0:T(8,128)(2,1)S(1)}, u32[]{:S(2)}, u32[]{:S(2)}) collective-permute-start(bf16[896,128]{1,0:T(8,128)(2,1)S(1)} %get-tuple-element.31), channel_id=1, source_target_pairs={{0,4},{1,13},{2,6},{3,15},{4,0},{5,9},{6,2},{7,11},{8,12},{9,5},{1... | collective-permute-start | bytes 688136 | tf_op jit(solution)/shard_map/ppermute | solution.py:460
  10.6 0.6 collective-permute-start.2
  11.2 2.7 %collective-permute-start.3 = (bf16[896,128]{1,0:T(8,128)(2,1)S(1)}, bf16[896,128]{1,0:T(8,128)(2,1)S(1)}, u32[]{:S(2)}, u32[]{:S(2)}) collective-permute-start(bf16[896,128]{1,0:T(8,128)(2,1)S(1)} %get-tuple-element.33), channel_id=1, source_target_pairs={{0,6},{1,11},{2,0},{3,13},{4,2},{5,15},{6,4},{7,9},{8,14},{9,3},{1... | collective-permute-start | bytes 688136 | tf_op jit(solution)/shard_map/ppermute | solution.py:460
  13.9 3.8 %collective-permute-start.4 = (bf16[896,128]{1,0:T(8,128)(2,1)S(1)}, bf16[896,128]{1,0:T(8,128)(2,1)S(1)}, u32[]{:S(2)}, u32[]{:S(2)}) collective-permute-start(bf16[896,128]{1,0:T(8,128)(2,1)S(1)} %get-tuple-element.34), channel_id=1, source_target_pairs={{0,8},{1,1},{2,10},{3,3},{4,12},{5,5},{6,14},{7,7},{8,0},{9,9},{10... | collective-permute-start | bytes 688136 | tf_op jit(solution)/shard_map/ppermute | solution.py:460
  17.7 0.9 %turn_tiles.1.turned = bf16[88,128,128]{2,1,0:T(8,128)(2,1)S(1)} custom-call(s32[128]{0:T(128)S(1)} %get-tuple-element.35.far, s32[128]{0:T(128)S(1)} %get-tuple-element.27.near, bf16[88,128,128]{2,1,0:T(8,128)(2,1)S(1)} %get-tuple-element.36.held.tiles), custom_call_target="tpu_custom_call" | custom-call | tf_op jit(solution)/shard_map/turn_tiles/pallas_call | solution.py:217
  18.6 3.0 %collective-permute-done.2.refs_1_ = bf16[896,128]{1,0:T(8,128)(2,1)S(1)} collective-permute-done((bf16[896,128]{1,0:T(8,128)(2,1)S(1)}, bf16[896,128]{1,0:T(8,128)(2,1)S(1)}, u32[]{:S(2)}, u32[]{:S(2)}) %collective-permute-start.2) | collective-permute-done | bytes 229408 | tf_op jit(solution)/shard_map/ppermute | solution.py:460
  21.6 1.0 %collective-permute-done.3.refs_2_ = bf16[896,128]{1,0:T(8,128)(2,1)S(1)} collective-permute-done((bf16[896,128]{1,0:T(8,128)(2,1)S(1)}, bf16[896,128]{1,0:T(8,128)(2,1)S(1)}, u32[]{:S(2)}, u32[]{:S(2)}) %collective-permute-start.3) | collective-permute-done | bytes 229408 | tf_op jit(solution)/shard_map/ppermute | solution.py:460
  23.0 3.7 %collective-permute-start.5 = (bf16[896,128]{1,0:T(8,128)(2,1)S(1)}, bf16[896,128]{1,0:T(8,128)(2,1)S(1)}, u32[]{:S(2)}, u32[]{:S(2)}) collective-permute-start(bf16[896,128]{1,0:T(8,128)(2,1)S(1)} %part_sum.1.mine), channel_id=1, source_target_pairs={{0,1},{1,0},{2,3},{3,2},{4,5},{5,4},{6,7},{7,6},{8,9},{9,8},{10,11... | collective-permute-start | bytes 688136 | tf_op jit(solution)/shard_map/ppermute | solution.py:463
  26.7 1.1 %collective-permute-done.5.got = bf16[896,128]{1,0:T(8,128)(2,1)S(1)} collective-permute-done((bf16[896,128]{1,0:T(8,128)(2,1)S(1)}, bf16[896,128]{1,0:T(8,128)(2,1)S(1)}, u32[]{:S(2)}, u32[]{:S(2)}) %collective-permute-start.5) | collective-permute-done | bytes 229408 | tf_op jit(solution)/shard_map/ppermute | solution.py:463
  27.8 0.7 %chunk_sum.1 = (bf16[896,128]{1,0:T(8,128)(2,1)S(1)}, bf16[448,128]{1,0:T(8,128)(2,1)}) custom-call(bf16[896,128]{1,0:T(8,128)(2,1)S(1)} %part_sum.1.mine, bf16[896,128]{1,0:T(8,128)(2,1)S(1)} %collective-permute-done.5.got), custom_call_target="tpu_custom_call" | custom-call | tf_op jit(solution)/shard_map/chunk_sum/pallas_call | solution.py:276
  28.5 1.9 %collective-permute-start.9 = (bf16[896,128]{1,0:T(8,128)(2,1)S(1)}, bf16[896,128]{1,0:T(8,128)(2,1)S(1)}, u32[]{:S(2)}, u32[]{:S(2)}) collective-permute-start(bf16[896,128]{1,0:T(8,128)(2,1)S(1)} %get-tuple-element.43), channel_id=1, source_target_pairs={{0,8},{1,1},{2,10},{3,3},{4,12},{5,5},{6,14},{7,7},{8,0},{9,9},{10... | collective-permute-start | bytes 688136 | tf_op jit(solution)/shard_map/ppermute | solution.py:464
  30.5 1.2 %collective-permute-start.8 = (bf16[896,128]{1,0:T(8,128)(2,1)S(1)}, bf16[896,128]{1,0:T(8,128)(2,1)S(1)}, u32[]{:S(2)}, u32[]{:S(2)}) collective-permute-start(bf16[896,128]{1,0:T(8,128)(2,1)S(1)} %get-tuple-element.43), channel_id=1, source_target_pairs={{0,6},{1,11},{2,0},{3,13},{4,2},{5,15},{6,4},{7,9},{8,14},{9,3},{1... | collective-permute-start | bytes 688136 | tf_op jit(solution)/shard_map/ppermute | solution.py:464
  31.6 0.9 %collective-permute-start.7 = (bf16[896,128]{1,0:T(8,128)(2,1)S(1)}, bf16[896,128]{1,0:T(8,128)(2,1)S(1)}, u32[]{:S(2)}, u32[]{:S(2)}) collective-permute-start(bf16[896,128]{1,0:T(8,128)(2,1)S(1)} %get-tuple-element.43), channel_id=1, source_target_pairs={{0,2},{1,15},{2,4},{3,9},{4,6},{5,11},{6,0},{7,13},{8,10},{9,7},{1... | collective-permute-start | bytes 688136 | tf_op jit(solution)/shard_map/ppermute | solution.py:464
  32.6 2.0 %collective-permute-start.6 = (bf16[896,128]{1,0:T(8,128)(2,1)S(1)}, bf16[896,128]{1,0:T(8,128)(2,1)S(1)}, u32[]{:S(2)}, u32[]{:S(2)}) collective-permute-start(bf16[896,128]{1,0:T(8,128)(2,1)S(1)} %get-tuple-element.43), channel_id=1, source_target_pairs={{0,4},{1,13},{2,6},{3,15},{4,0},{5,9},{6,2},{7,11},{8,12},{9,5},{1... | collective-permute-start | bytes 688136 | tf_op jit(solution)/shard_map/ppermute | solution.py:464
  34.5 4.4 %collective-permute-done.9.refs_3_ = bf16[896,128]{1,0:T(8,128)(2,1)S(1)} collective-permute-done((bf16[896,128]{1,0:T(8,128)(2,1)S(1)}, bf16[896,128]{1,0:T(8,128)(2,1)S(1)}, u32[]{:S(2)}, u32[]{:S(2)}) %collective-permute-start.9) | collective-permute-done | bytes 229408 | tf_op jit(solution)/shard_map/ppermute | solution.py:464
  39.0 6.3 %collective-permute-done.7.refs_1_ = bf16[896,128]{1,0:T(8,128)(2,1)S(1)} collective-permute-done((bf16[896,128]{1,0:T(8,128)(2,1)S(1)}, bf16[896,128]{1,0:T(8,128)(2,1)S(1)}, u32[]{:S(2)}, u32[]{:S(2)}) %collective-permute-start.7) | collective-permute-done | bytes 229408 | tf_op jit(solution)/shard_map/ppermute | solution.py:464
  45.4 0.9 %backward_near.1.first = f32[1152,128]{1,0:T(8,128)S(1)} custom-call(s32[128]{0:T(128)S(1)} %get-tuple-element.27.near, bf16[88,128,128]{2,1,0:T(8,128)(2,1)S(1)} %turn_tiles.1.turned, bf16[3584,128]{1,0:T(8,128)(2,1)S(1)} %gather_half.1.table), custom_call_target="tpu_custom_call" | custom-call | tf_op jit(solution)/shard_map/backward_near/pallas_call | solution.py:328
  46.3 1.6 %collective-permute-done.10.table = bf16[3584,128]{1,0:T(8,128)(2,1)S(1)} collective-permute-done((bf16[3584,128]{1,0:T(8,128)(2,1)S(1)}, bf16[3584,128]{1,0:T(8,128)(2,1)S(1)}, u32[]{:S(2)}, u32[]{:S(2)}) %collective-permute-start.10) | collective-permute-done | bytes 917536 | tf_op jit(solution)/shard_map/ppermute | solution.py:465
  47.8 0.9 %backward_far.1 = (f32[256,128]{1,0:T(8,128)S(1)}, bf16[256,128]{1,0:T(8,128)(2,1)S(1)}, bf16[256,128]{1,0:T(8,128)(2,1)S(1)}, bf16[256,128]{1,0:T(8,128)(2,1)S(1)}) custom-call(s32[128]{0:T(128)S(1)} %get-tuple-element.35.far, bf16[88,128,128]{2,1,0:T(8,128)(2,1)S(1)} %turn_tiles.1.turned, f32[1152,128]{1,0:T(8,128)S(1)} %backward_near.1.first, ...), custom_call_target="tpu_custom_call" | custom-call | tf_op jit(solution)/shard_map/backward_far/pallas_call | solution.py:365
  48.8 0.8 %collective-permute-start.11 = (bf16[256,128]{1,0:T(8,128)(2,1)S(1)}, bf16[256,128]{1,0:T(8,128)(2,1)S(1)}, u32[]{:S(2)}, u32[]{:S(2)}) collective-permute-start(bf16[256,128]{1,0:T(8,128)(2,1)S(1)} %get-tuple-element.45), channel_id=1, source_target_pairs={{0,128},{1,129},{2,130},{3,131},{4,132},{5,133},{6,134},{7,135},{8... | collective-permute-start | bytes 196616 | tf_op jit(solution)/shard_map/ppermute | solution.py:468
  49.6 2.3 %collective-permute-start.12 = (bf16[256,128]{1,0:T(8,128)(2,1)S(1)}, bf16[256,128]{1,0:T(8,128)(2,1)S(1)}, u32[]{:S(2)}, u32[]{:S(2)}) collective-permute-start(bf16[256,128]{1,0:T(8,128)(2,1)S(1)} %get-tuple-element.46), channel_id=1, source_target_pairs={{0,64},{1,193},{2,66},{3,195},{4,68},{5,197},{6,70},{7,199},{8,72}... | collective-permute-start | bytes 196616 | tf_op jit(solution)/shard_map/ppermute | solution.py:468
  51.8 3.2 %collective-permute-done.11.g0 = bf16[256,128]{1,0:T(8,128)(2,1)S(1)} collective-permute-done((bf16[256,128]{1,0:T(8,128)(2,1)S(1)}, bf16[256,128]{1,0:T(8,128)(2,1)S(1)}, u32[]{:S(2)}, u32[]{:S(2)}) %collective-permute-start.11) | collective-permute-done | bytes 65568 | tf_op jit(solution)/shard_map/ppermute | solution.py:468
  55.0 2.3 %collective-permute-done.13.g2 = bf16[256,128]{1,0:T(8,128)(2,1)S(1)} collective-permute-done((bf16[256,128]{1,0:T(8,128)(2,1)S(1)}, bf16[256,128]{1,0:T(8,128)(2,1)S(1)}, u32[]{:S(2)}, u32[]{:S(2)}) %collective-permute-start.13) | collective-permute-done | bytes 65568 | tf_op jit(solution)/shard_map/ppermute | solution.py:468
  57.4 2.4 %collective-permute-start.14 = (bf16[128,128]{1,0:T(8,128)(2,1)S(1)}, bf16[128,128]{1,0:T(8,128)(2,1)S(1)}, u32[]{:S(2)}, u32[]{:S(2)}) collective-permute-start(bf16[128,128]{1,0:T(8,128)(2,1)S(1)} %get-tuple-element.49), channel_id=1, source_target_pairs={{0,16},{16,0},{32,48},{48,32},{64,80},{80,64},{96,112},{112,96},{1... | collective-permute-start | bytes 98312 | tf_op jit(solution)/shard_map/ppermute | solution.py:470
  59.7 2.5 %collective-permute-done.14.got = bf16[128,128]{1,0:T(8,128)(2,1)S(1)} collective-permute-done((bf16[128,128]{1,0:T(8,128)(2,1)S(1)}, bf16[128,128]{1,0:T(8,128)(2,1)S(1)}, u32[]{:S(2)}, u32[]{:S(2)}) %collective-permute-start.14) | collective-permute-done | bytes 32800 | tf_op jit(solution)/shard_map/ppermute | solution.py:470
  62.3 6.0 %collective-permute-start.15 = (bf16[64,128]{1,0:T(8,128)(2,1)S(1)}, bf16[64,128]{1,0:T(8,128)(2,1)S(1)}, u32[]{:S(2)}, u32[]{:S(2)}) collective-permute-start(bf16[64,128]{1,0:T(8,128)(2,1)S(1)} %get-tuple-element.51), channel_id=1, source_target_pairs={{0,48},{16,32},{32,16},{48,0},{64,112},{80,96},{96,80},{112,64},{1... | collective-permute-start | bytes 49160 | tf_op jit(solution)/shard_map/ppermute | solution.py:471
  68.3 1.7 %collective-permute-done.15.got = bf16[64,128]{1,0:T(8,128)(2,1)S(1)} collective-permute-done((bf16[64,128]{1,0:T(8,128)(2,1)S(1)}, bf16[64,128]{1,0:T(8,128)(2,1)S(1)}, u32[]{:S(2)}, u32[]{:S(2)}) %collective-permute-start.15) | collective-permute-done | bytes 16416 | tf_op jit(solution)/shard_map/ppermute | solution.py:471
  70.0 0.6 last_sum.1
  (12 shorter events, 0.6 us)
Async XLA Ops:
  4.7 2.6 %collective-permute-start = (bf16[3584,128]{1,0:T(8,128)(2,1)S(1)}, bf16[3584,128]{1,0:T(8,128)(2,1)S(1)}, u32[]{:S(2)}, u32[]{:S(2)}) collective-permute-start(bf16[3584,128]{1,0:T(8,128)(2,1)S(1)} %get-tuple-element.30), channel_id=1, source_target_pairs={{0,1},{1,0},{2,3},{3,2},{4,5},{5,4},{6,7},{7,6},{8,9},{9,8},{10,11... | collective-permute-start | bytes 2752520 | tf_op jit(solution)/shard_map/ppermute | solution.py:455
  7.5 11.1 %collective-permute-start.1 = (bf16[896,128]{1,0:T(8,128)(2,1)S(1)}, bf16[896,128]{1,0:T(8,128)(2,1)S(1)}, u32[]{:S(2)}, u32[]{:S(2)}) collective-permute-start(bf16[896,128]{1,0:T(8,128)(2,1)S(1)} %get-tuple-element.31), channel_id=1, source_target_pairs={{0,4},{1,13},{2,6},{3,15},{4,0},{5,9},{6,2},{7,11},{8,12},{9,5},{1... | collective-permute-start | bytes 688136 | tf_op jit(solution)/shard_map/ppermute | solution.py:460
  10.6 11.0 %collective-permute-start.2 = (bf16[896,128]{1,0:T(8,128)(2,1)S(1)}, bf16[896,128]{1,0:T(8,128)(2,1)S(1)}, u32[]{:S(2)}, u32[]{:S(2)}) collective-permute-start(bf16[896,128]{1,0:T(8,128)(2,1)S(1)} %get-tuple-element.32), channel_id=1, source_target_pairs={{0,2},{1,15},{2,4},{3,9},{4,6},{5,11},{6,0},{7,13},{8,10},{9,7},{1... | collective-permute-start | bytes 688136 | tf_op jit(solution)/shard_map/ppermute | solution.py:460
  11.2 11.4 %collective-permute-start.3 = (bf16[896,128]{1,0:T(8,128)(2,1)S(1)}, bf16[896,128]{1,0:T(8,128)(2,1)S(1)}, u32[]{:S(2)}, u32[]{:S(2)}) collective-permute-start(bf16[896,128]{1,0:T(8,128)(2,1)S(1)} %get-tuple-element.33), channel_id=1, source_target_pairs={{0,6},{1,11},{2,0},{3,13},{4,2},{5,15},{6,4},{7,9},{8,14},{9,3},{1... | collective-permute-start | bytes 688136 | tf_op jit(solution)/shard_map/ppermute | solution.py:460
  13.9 9.0 %collective-permute-start.4 = (bf16[896,128]{1,0:T(8,128)(2,1)S(1)}, bf16[896,128]{1,0:T(8,128)(2,1)S(1)}, u32[]{:S(2)}, u32[]{:S(2)}) collective-permute-start(bf16[896,128]{1,0:T(8,128)(2,1)S(1)} %get-tuple-element.34), channel_id=1, source_target_pairs={{0,8},{1,1},{2,10},{3,3},{4,12},{5,5},{6,14},{7,7},{8,0},{9,9},{10... | collective-permute-start | bytes 688136 | tf_op jit(solution)/shard_map/ppermute | solution.py:460
  23.0 4.8 %collective-permute-start.5 = (bf16[896,128]{1,0:T(8,128)(2,1)S(1)}, bf16[896,128]{1,0:T(8,128)(2,1)S(1)}, u32[]{:S(2)}, u32[]{:S(2)}) collective-permute-start(bf16[896,128]{1,0:T(8,128)(2,1)S(1)} %part_sum.1.mine), channel_id=1, source_target_pairs={{0,1},{1,0},{2,3},{3,2},{4,5},{5,4},{6,7},{7,6},{8,9},{9,8},{10,11... | collective-permute-start | bytes 688136 | tf_op jit(solution)/shard_map/ppermute | solution.py:463
  28.5 10.4 %collective-permute-start.9 = (bf16[896,128]{1,0:T(8,128)(2,1)S(1)}, bf16[896,128]{1,0:T(8,128)(2,1)S(1)}, u32[]{:S(2)}, u32[]{:S(2)}) collective-permute-start(bf16[896,128]{1,0:T(8,128)(2,1)S(1)} %get-tuple-element.43), channel_id=1, source_target_pairs={{0,8},{1,1},{2,10},{3,3},{4,12},{5,5},{6,14},{7,7},{8,0},{9,9},{10... | collective-permute-start | bytes 688136 | tf_op jit(solution)/shard_map/ppermute | solution.py:464
  30.5 8.5 %collective-permute-start.8 = (bf16[896,128]{1,0:T(8,128)(2,1)S(1)}, bf16[896,128]{1,0:T(8,128)(2,1)S(1)}, u32[]{:S(2)}, u32[]{:S(2)}) collective-permute-start(bf16[896,128]{1,0:T(8,128)(2,1)S(1)} %get-tuple-element.43), channel_id=1, source_target_pairs={{0,6},{1,11},{2,0},{3,13},{4,2},{5,15},{6,4},{7,9},{8,14},{9,3},{1... | collective-permute-start | bytes 688136 | tf_op jit(solution)/shard_map/ppermute | solution.py:464
  31.6 13.6 %collective-permute-start.7 = (bf16[896,128]{1,0:T(8,128)(2,1)S(1)}, bf16[896,128]{1,0:T(8,128)(2,1)S(1)}, u32[]{:S(2)}, u32[]{:S(2)}) collective-permute-start(bf16[896,128]{1,0:T(8,128)(2,1)S(1)} %get-tuple-element.43), channel_id=1, source_target_pairs={{0,2},{1,15},{2,4},{3,9},{4,6},{5,11},{6,0},{7,13},{8,10},{9,7},{1... | collective-permute-start | bytes 688136 | tf_op jit(solution)/shard_map/ppermute | solution.py:464
  32.6 12.7 %collective-permute-start.6 = (bf16[896,128]{1,0:T(8,128)(2,1)S(1)}, bf16[896,128]{1,0:T(8,128)(2,1)S(1)}, u32[]{:S(2)}, u32[]{:S(2)}) collective-permute-start(bf16[896,128]{1,0:T(8,128)(2,1)S(1)} %get-tuple-element.43), channel_id=1, source_target_pairs={{0,4},{1,13},{2,6},{3,15},{4,0},{5,9},{6,2},{7,11},{8,12},{9,5},{1... | collective-permute-start | bytes 688136 | tf_op jit(solution)/shard_map/ppermute | solution.py:464
  45.3 2.6 %collective-permute-start.10 = (bf16[3584,128]{1,0:T(8,128)(2,1)S(1)}, bf16[3584,128]{1,0:T(8,128)(2,1)S(1)}, u32[]{:S(2)}, u32[]{:S(2)}) collective-permute-start(bf16[3584,128]{1,0:T(8,128)(2,1)S(1)} %gather_half.1.table), channel_id=1, source_target_pairs={{0,1},{1,0},{2,3},{3,2},{4,5},{5,4},{6,7},{7,6},{8,9},{9,8},{10,11... | collective-permute-start | bytes 2752520 | tf_op jit(solution)/shard_map/ppermute | solution.py:465
  48.8 6.3 %collective-permute-start.11 = (bf16[256,128]{1,0:T(8,128)(2,1)S(1)}, bf16[256,128]{1,0:T(8,128)(2,1)S(1)}, u32[]{:S(2)}, u32[]{:S(2)}) collective-permute-start(bf16[256,128]{1,0:T(8,128)(2,1)S(1)} %get-tuple-element.45), channel_id=1, source_target_pairs={{0,128},{1,129},{2,130},{3,131},{4,132},{5,133},{6,134},{7,135},{8... | collective-permute-start | bytes 196616 | tf_op jit(solution)/shard_map/ppermute | solution.py:468
  49.6 5.5 %collective-permute-start.12 = (bf16[256,128]{1,0:T(8,128)(2,1)S(1)}, bf16[256,128]{1,0:T(8,128)(2,1)S(1)}, u32[]{:S(2)}, u32[]{:S(2)}) collective-permute-start(bf16[256,128]{1,0:T(8,128)(2,1)S(1)} %get-tuple-element.46), channel_id=1, source_target_pairs={{0,64},{1,193},{2,66},{3,195},{4,68},{5,197},{6,70},{7,199},{8,72}... | collective-permute-start | bytes 196616 | tf_op jit(solution)/shard_map/ppermute | solution.py:468
  51.8 5.5 %collective-permute-start.13 = (bf16[256,128]{1,0:T(8,128)(2,1)S(1)}, bf16[256,128]{1,0:T(8,128)(2,1)S(1)}, u32[]{:S(2)}, u32[]{:S(2)}) collective-permute-start(bf16[256,128]{1,0:T(8,128)(2,1)S(1)} %get-tuple-element.47), channel_id=1, source_target_pairs={{0,192},{1,65},{2,194},{3,67},{4,196},{5,69},{6,198},{7,71},{8,200... | collective-permute-start | bytes 196616 | tf_op jit(solution)/shard_map/ppermute | solution.py:468
  57.4 4.9 %collective-permute-start.14 = (bf16[128,128]{1,0:T(8,128)(2,1)S(1)}, bf16[128,128]{1,0:T(8,128)(2,1)S(1)}, u32[]{:S(2)}, u32[]{:S(2)}) collective-permute-start(bf16[128,128]{1,0:T(8,128)(2,1)S(1)} %get-tuple-element.49), channel_id=1, source_target_pairs={{0,16},{16,0},{32,48},{48,32},{64,80},{80,64},{96,112},{112,96},{1... | collective-permute-start | bytes 98312 | tf_op jit(solution)/shard_map/ppermute | solution.py:470
  62.3 7.8 %collective-permute-start.15 = (bf16[64,128]{1,0:T(8,128)(2,1)S(1)}, bf16[64,128]{1,0:T(8,128)(2,1)S(1)}, u32[]{:S(2)}, u32[]{:S(2)}) collective-permute-start(bf16[64,128]{1,0:T(8,128)(2,1)S(1)} %get-tuple-element.51), channel_id=1, source_target_pairs={{0,48},{16,32},{32,16},{48,0},{64,112},{80,96},{96,80},{112,64},{1... | collective-permute-start | bytes 49160 | tf_op jit(solution)/shard_map/ppermute | solution.py:471

commit v4 on v3

v4 whole, which is shorter than its diff:
```python
import functools

import jax
import jax.numpy as jnp
from jax import lax
from jax.experimental import pallas as pl
from jax.experimental.pallas import tpu as pltpu
from jax.sharding import PartitionSpec as P

TILE = 128
KB_DEV = 56
SB_DEV = 8
CHUNK_BLOCKS = KB_DEV // 8
CHUNK = CHUNK_BLOCKS * TILE
PART_BLOCKS = 2 * CHUNK_BLOCKS
PART = PART_BLOCKS * TILE
UNROLL = 12
LIST = 128
FETCH = 8
VMEM_LIMIT = 48 * 1024 * 1024
COST = pl.CostEstimate(flops=200 * 44 * TILE**3, bytes_accessed=200 * 44 * TILE**2, transcendentals=0)

ROUNDS = (
    ((1, 0), (3, 1)),
    ((3, 0), (1, 1)),
    ((2, 0), (2, 1)),
    ((0, 1), (0, 0)),
)
NEAR_EARLY, NEAR_LATE, FAR_EARLY, FAR_LATE = range(4)
LINE = ((2, 2), (1, 3), (3, 1))


def vm():
    return pl.BlockSpec(memory_space=pltpu.VMEM)


def sm():
    return pl.BlockSpec(memory_space=pltpu.SMEM)


def params():
    return pltpu.CompilerParams(vmem_limit_bytes=VMEM_LIMIT)


def place():
    j = lax.axis_index("samp")
    return j // 8, (j // 2) % 4, j % 2


def kmer_place():
    i = lax.axis_index("kmer")
    return i // 4, i % 4


def round_pairs(p):
    out = []
    for s in range(16):
        z, x, c = s // 8, (s // 2) % 4, s % 2
        dx, dz = ROUNDS[p][c]
        out.append((s, (z ^ dz) * 8 + (x ^ dx) * 2 + c))
    return out


def y_pairs(r):
    out = []
    for i in range(16):
        for j in range(16):
            to = ((i // 4 + LINE[r][j % 2]) % 4) * 4 + i % 4
            out.append((i * 16 + j, to * 16 + j))
    return out


def block(i):
    return pl.ds(pl.multiple_of(i * TILE, TILE), TILE)


def chunk_at(q):
    return pl.ds(q * CHUNK, CHUNK)


def unpack(word):
    return lax.rem(word, 128), lax.rem(lax.div(word, 128), 64), lax.div(word, 8192)


def size_of(lists, which):
    return lists[which * LIST + LIST - 1]


def list_slots(rows, cols, count, lists, shift, owner):
    cap = rows.shape[0]
    z, x, c = place()
    for m in range(8):
        mx = m % 4
        e = jnp.bitwise_xor(x, mx)
        same_z = (z == m // 4).astype(jnp.int32)
        core = jnp.where(e == 0, same_z, 1 - same_z)
        odd = jnp.where(core == 0, e == 3, e == 1).astype(jnp.int32)
        p = jnp.where(e == 0, 3, jnp.where(e == 2, 2, odd))
        late = (p >= 2).astype(jnp.int32)
        shift[m] = (p - 2 * late - m) * CHUNK_BLOCKS
        owner[m] = jnp.where(core == c, 0, 2) + late

    def visit(s, sizes):
        row = rows[s]
        m = (row * 37) >> 8
        word = s + (row + shift[m]) * 128 + cols[s] * 8192
        which = jnp.where(s < count, owner[m], 4)
        for k, n in enumerate(sizes):
            lists[k * LIST + n] = word
        return tuple(n + (which == k).astype(jnp.int32) for k, n in enumerate(sizes))

    sizes = lax.fori_loop(0, cap, visit, (jnp.int32(0),) * 4, unroll=8)
    for k, n in enumerate(sizes):
        pad = lax.rem(lists[k * LIST], 128) + PART_BLOCKS * 128 + SB_DEV * 8192
        for u in range(UNROLL):
            lists[k * LIST + n + u] = pad
        lists[k * LIST + LIST - 1] = n


def forward_slots(lists, which, tiles, omega, acc, out):
    acc[...] = jnp.zeros_like(acc)

    def step(g, carry):
        prods, where = [], []
        for u in range(UNROLL):
            slot, row, col = unpack(lists[which * LIST + g * UNROLL + u])
            col = jnp.minimum(col, SB_DEV - 1)
            where.append(block(row))
            prods.append(
                jnp.dot(tiles[slot], omega[block(col), :], preferred_element_type=jnp.float32)
            )
        for at, prod in zip(where, prods):
            acc[at, :] = acc[at, :] + prod
        return carry

    lax.fori_loop(0, (size_of(lists, which) + UNROLL - 1) // UNROLL, step, 0)
    out[...] = acc[pl.ds(0, PART), :].astype(jnp.bfloat16)


def forward_first_kernel(
    rows, cols, count, tiles, omega, out, held, table, lists, acc, s_rows, s_cols, shift, owner, sems, tile_sems
):
    small = [
        pltpu.make_async_copy(rows, s_rows, sems.at[0]),
        pltpu.make_async_copy(cols, s_cols, sems.at[1]),
    ]
    for copy in small:
        copy.start()
    used = count[0]

    def fetch(g):
        at = pl.ds(g * FETCH, FETCH)
        return pltpu.make_async_copy(tiles.at[at], held.at[at], tile_sems.at[g])

    fetches = tiles.shape[0] // FETCH
    for g in range(fetches):
        pl.when(g * FETCH < used)(fetch(g).start)
    fetch_omega = pltpu.make_async_copy(omega, table, sems.at[2])
    fetch_omega.start()
    for copy in small:
        copy.wait()
    list_slots(s_rows, s_cols, used, lists, shift, owner)
    for g in range(fetches):
        pl.when(g * FETCH < used)(fetch(g).wait)
    fetch_omega.wait()
    forward_slots(lists, FAR_EARLY, held, table, acc, out)


def in_hbm(value):
    return pltpu.with_memory_space_constraint(value, pltpu.HBM)


def forward_first(rows, cols, count, tiles, omega):
    cap = tiles.shape[0]
    anywhere = pl.BlockSpec(memory_space=pltpu.HBM)
    return pl.pallas_call(
        forward_first_kernel,
        out_shape=[
            jax.ShapeDtypeStruct((PART, TILE), jnp.bfloat16),
            jax.ShapeDtypeStruct(tiles.shape, tiles.dtype),
            jax.ShapeDtypeStruct(omega.shape, omega.dtype),
            jax.ShapeDtypeStruct((4 * LIST,), jnp.int32),
        ],
        in_specs=[anywhere, anywhere, sm(), anywhere, anywhere],
        out_specs=[vm(), vm(), vm(), sm()],
        scratch_shapes=[
            pltpu.VMEM((PART + TILE, TILE), jnp.float32),
            pltpu.SMEM((cap,), jnp.int32),
            pltpu.SMEM((cap,), jnp.int32),
            pltpu.SMEM((8,), jnp.int32),
            pltpu.SMEM((8,), jnp.int32),
            pltpu.SemaphoreType.DMA((3,)),
            pltpu.SemaphoreType.DMA((cap // FETCH,)),
        ],
        compiler_params=params(),
        name="forward_first",
    )(in_hbm(rows), in_hbm(cols), count, in_hbm(tiles), in_hbm(omega))


def forward_next_kernel(which, lists, held, table, out, acc):
    forward_slots(lists, which, held, table, acc, out)


def forward_next(which, lists, held, table):
    return pl.pallas_call(
        functools.partial(forward_next_kernel, which),
        out_shape=jax.ShapeDtypeStruct((PART, TILE), jnp.bfloat16),
        in_specs=[sm(), vm(), vm()],
        out_specs=vm(),
        scratch_shapes=[pltpu.VMEM((PART + TILE, TILE), jnp.float32)],
        compiler_params=params(),
        cost_estimate=COST,
        name=f"forward_next{which}",
    )(lists, held, table)


def turn_kernel(count, tiles, out):
    def one(g, carry):
        for u in range(4):
            out[g * 4 + u] = tiles[g * 4 + u].T
        return carry

    lax.fori_loop(0, (count[0] + 3) // 4, one, 0)


def turn(count, tiles):
    return pl.pallas_call(
        turn_kernel,
        out_shape=jax.ShapeDtypeStruct(tiles.shape, tiles.dtype),
        in_specs=[sm(), vm()],
        out_specs=vm(),
        compiler_params=params(),
        name="turn_tiles",
    )(count, tiles)


def pair_kernel(a, b, *sends):
    for q, send in enumerate(sends):
        at = chunk_at(q)
        send[...] = (a[at, :].astype(jnp.float32) + b[at, :].astype(jnp.float32)).astype(jnp.bfloat16)


def pair_sum(a, b):
    shape = jax.ShapeDtypeStruct((CHUNK, TILE), jnp.bfloat16)
    return pl.pallas_call(
        pair_kernel,
        out_shape=[shape] * 2,
        in_specs=[vm(), vm()],
        out_specs=[vm()] * 2,
        compiler_params=params(),
        name="pair_sum",
    )(a, b)


def part_kernel(*refs):
    out = refs[-1]
    total = refs[0][...].astype(jnp.float32)
    for ref in refs[1:-1]:
        total = total + ref[...].astype(jnp.float32)
    out[...] = total.astype(jnp.bfloat16)


def part_sum(name, *parts):
    return pl.pallas_call(
        part_kernel,
        out_shape=jax.ShapeDtypeStruct((CHUNK, TILE), jnp.bfloat16),
        in_specs=[vm()] * len(parts),
        out_specs=vm(),
        compiler_params=params(),
        name=name,
    )(*parts)


def backward_slots(lists, which, turned, table, acc):
    def step(g, carry):
        prods, where = [], []
        for u in range(UNROLL):
            slot, row, col = unpack(lists[which * LIST + g * UNROLL + u])
            row = jnp.minimum(row, PART_BLOCKS - 1)
            where.append(block(col))
            prods.append(
                jnp.dot(turned[slot], table[block(row), :], preferred_element_type=jnp.float32)
            )
        for at, prod in zip(where, prods):
            acc[at, :] = acc[at, :] + prod
        return carry

    lax.fori_loop(0, (size_of(lists, which) + UNROLL - 1) // UNROLL, step, 0)


def backward_part(lists, kinds, turned, near, far, table, acc):
    for kind, pieces in zip(kinds, (near, far)):
        for q, piece in enumerate(pieces):
            table[chunk_at(q), :] = piece[...]
        backward_slots(lists, kind, turned, table, acc)


def backward_early_kernel(lists, turned, chunk, n0, n1, f0, f1, out, sketch, table):
    out[...] = jnp.zeros_like(out)
    backward_part(lists, (NEAR_EARLY, FAR_EARLY), turned, (n0, n1), (f0, f1), table, out)
    _, _, c = place()
    size = sketch.shape[0]
    sketch[...] = chunk[pl.ds(pl.multiple_of(c * size, size), size), :]


def backward_early(lists, turned, chunk, near, far):
    return pl.pallas_call(
        backward_early_kernel,
        out_shape=[
            jax.ShapeDtypeStruct(((SB_DEV + 1) * TILE, TILE), jnp.float32),
            jax.ShapeDtypeStruct((CHUNK // 2, TILE), jnp.bfloat16),
        ],
        in_specs=[sm()] + [vm()] * 6,
        out_specs=[vm()] * 2,
        scratch_shapes=[pltpu.VMEM((PART, TILE), jnp.bfloat16)],
        compiler_params=params(),
        cost_estimate=COST,
        name="backward_early",
    )(lists, turned, chunk, *near, *far)


def line_offset(r):
    _, _, c = place()
    return jnp.where(c == 0, LINE[r][0], LINE[r][1])


def share_at(i, size):
    return pl.ds(pl.multiple_of(lax.rem(i + 4, 4) * size, size), size)


def backward_late_kernel(lists, turned, first, n2, n3, f2, f3, keep, s0, s1, s2, acc, table):
    acc[...] = first[...]
    backward_part(lists, (NEAR_LATE, FAR_LATE), turned, (n2, n3), (f2, f3), table, acc)
    y, _ = kmer_place()
    size = keep.shape[0]
    for r, send in enumerate((s0, s1, s2)):
        send[...] = acc[share_at(y + line_offset(r), size), :].astype(jnp.bfloat16)
    keep[...] = acc[share_at(y, size), :]


def backward_late(lists, turned, first, near, far):
    share = SB_DEV * TILE // 4
    send = jax.ShapeDtypeStruct((share, TILE), jnp.bfloat16)
    return pl.pallas_call(
        backward_late_kernel,
        out_shape=[jax.ShapeDtypeStruct((share, TILE), jnp.float32), send, send, send],
        in_specs=[sm()] + [vm()] * 6,
        out_specs=[vm()] * 4,
        scratch_shapes=[
            pltpu.VMEM(((SB_DEV + 1) * TILE, TILE), jnp.float32),
            pltpu.VMEM((PART, TILE), jnp.bfloat16),
        ],
        compiler_params=params(),
        name="backward_late",
    )(lists, turned, first, *near, *far)


def line_kernel(own, g0, g1, g2, keep, send, acc):
    total = own[...]
    for got in (g0, g1, g2):
        total = total + got[...].astype(jnp.float32)
    acc[...] = total
    _, zh = kmer_place()
    size = keep.shape[0] // 2
    peer = zh + 1 - 2 * lax.rem(zh, 2)
    for k, (mine, theirs) in enumerate(((zh, peer), (3 - zh, 3 - peer))):
        keep[pl.ds(k * size, size), :] = acc[share_at(mine, size), :]
        send[pl.ds(k * size, size), :] = acc[share_at(theirs, size), :].astype(jnp.bfloat16)


def line_sum(own, got):
    half = own.shape[0] // 2
    return pl.pallas_call(
        line_kernel,
        out_shape=[
            jax.ShapeDtypeStruct((half, TILE), jnp.float32),
            jax.ShapeDtypeStruct((half, TILE), jnp.bfloat16),
        ],
        in_specs=[vm()] * 4,
        out_specs=[vm()] * 2,
        scratch_shapes=[pltpu.VMEM(own.shape, jnp.float32)],
        compiler_params=params(),
        name="line_sum",
    )(own, *got)


def halve_kernel(own, got, keep, send):
    size = keep.shape[0]
    total = own[...] + got[...].astype(jnp.float32)
    keep[...] = total[:size]
    send[...] = total[size:].astype(jnp.bfloat16)


def halve_sum(own, got):
    half = own.shape[0] // 2
    return pl.pallas_call(
        halve_kernel,
        out_shape=[
            jax.ShapeDtypeStruct((half, TILE), jnp.float32),
            jax.ShapeDtypeStruct((half, TILE), jnp.bfloat16),
        ],
        in_specs=[vm()] * 2,
        out_specs=[vm()] * 2,
        compiler_params=params(),
        name="halve_sum",
    )(own, got)


def last_kernel(factor, own, got, out):
    out[...] = (own[...] + got[...].astype(jnp.float32)) * factor


def last_sum(factor, own, got):
    return pl.pallas_call(
        functools.partial(last_kernel, factor),
        out_shape=jax.ShapeDtypeStruct(own.shape, jnp.float32),
        in_specs=[vm()] * 2,
        out_specs=vm(),
        compiler_params=params(),
        name="last_sum",
    )(own, got)


def swap(value):
    return lax.ppermute(value, "samp", [(s, s ^ 1) for s in range(16)])


def trade(value, p):
    return lax.ppermute(value, "samp", round_pairs(p))


def after(value, *first):
    return lax.optimization_barrier((value, *first))[0]


def shards(tiles, omega, tile_rows, tile_cols, tile_count):
    kmers = lax.axis_size("kmer")
    other, held, table, lists = forward_first(tile_rows, tile_cols, tile_count, tiles, omega)
    sends = pair_sum(forward_next(NEAR_EARLY, lists, held, table), swap(other))
    held_late = after(held, *sends)
    parts = [trade(s, p) for p, s in enumerate(sends)]
    other = forward_next(FAR_LATE, lists, held_late, table)
    sends = pair_sum(forward_next(NEAR_LATE, lists, held_late, table), swap(other))
    parts += [trade(s, p + 2) for p, s in enumerate(sends)]
    turned = turn(tile_count, after(held, *sends))
    part = part_sum("part_sum", *parts)
    part, turned = lax.optimization_barrier((part, turned))
    chunk = part_sum("chunk_sum", part, swap(part))
    near = [trade(chunk, p) for p in range(4)]
    far = [swap(piece) for piece in near]
    first, sketch = backward_early(lists, turned, chunk, near[:2], far[:2])
    keep, *shares = backward_late(lists, turned, first, near[2:], far[2:])
    got = [lax.ppermute(s, ("kmer", "samp"), y_pairs(r)) for r, s in enumerate(shares)]
    keep, share = line_sum(keep, got)
    keep, share = halve_sum(keep, lax.ppermute(share, "kmer", [(i, i ^ 1) for i in range(16)]))
    got = lax.ppermute(share, "kmer", [(i, i // 4 * 4 + 3 - i % 4) for i in range(16)])
    factor = 1.0 / (KB_DEV * TILE * kmers) ** 0.5
    return sketch, last_sum(factor, keep, got)


def solution(mesh):
    placed = (
        P(("kmer", "samp"), None, None),
        P("samp", None),
        P(("kmer", "samp")),
        P(("kmer", "samp")),
        P(("kmer", "samp")),
    )
    return jax.shard_map(
        shards,
        mesh=mesh,
        in_specs=placed,
        out_specs=(P(("kmer", "samp"), None), P(("samp", "kmer"), None)),
        check_vma=False,
    )
```

time: 71 us -> 67.7 us (0.954)
  starting transfers between devices: 31.5 us -> 28.7 us
  waiting for transfers between devices: 28.8 us -> 26.5 us
  Pallas kernels: 8.98 us -> 10.7 us
    ppermute x11 -> x15, waiting for transfers between devices: 19.1 us -> 16 us  [the longest x8 12 us: trade(): return lax.ppermute(value, 'samp', round_pairs(p))]
    ppermute x11 -> x15, starting transfers between devices: 20 us -> 17.5 us  [the longest x8 16.5 us: trade(): return lax.ppermute(value, 'samp', round_pairs(p))]
    pallas_call x7 -> x8, Pallas kernels: 7.28 us -> 9.36 us  [the longest x1 3.09 us: forward_first(): pl.pallas_call(forward_first_kernel, out_shape=[jax.ShapeDtypeStruct((PAR...]
    ppermute x3, starting transfers between devices: 3.08 us -> 3.98 us  [shards(): lax.ppermute(s, ('kmer', 'samp'), y_pairs(r))]
    ppermute x1, waiting for transfers between devices: 2.53 us -> 3.33 us  [shards(): lax.ppermute(share, 'kmer', [(i, i ^ 1) for i in range(16)])]
  transfers between devices with their start and end apart: 16 -> 20, of which waited for: 12 -> 10; matrix products, arithmetic and copies ran while one was open for 0% -> 0% of each run, Pallas kernels for 4% -> 8%
where the time goes in v4:
time: 67.7 us; the launch traced here: 67.3 us
  starting transfers between devices  28.7 us (42%)
  waiting for transfers between devices  26.5 us (39%)
  Pallas kernels  10.7 us (16%)
  between operations  1.43 us (2%)
    ppermute x8, starting transfers between devices, trade(): return lax.ppermute(value, 'samp', round_pairs(p))  16.5 us
    ppermute x8, waiting for transfers between devices, trade(): return lax.ppermute(value, 'samp', round_pairs(p))  12 us
    ppermute x1, starting transfers between devices, shards(): lax.ppermute(share, 'kmer', [(i, i // 4 * 4 + 3 - i % 4) for i in range(1...  5.53 us
    ppermute x3, waiting for transfers between devices, shards(): lax.ppermute(s, ('kmer', 'samp'), y_pairs(r))  5.47 us
    ppermute x7, waiting for transfers between devices, swap(): return lax.ppermute(value, 'samp', [(s, s ^ 1) for s in range(16)])  4.04 us
    ppermute x3, starting transfers between devices, shards(): lax.ppermute(s, ('kmer', 'samp'), y_pairs(r))  3.98 us
    ppermute x1, waiting for transfers between devices, shards(): lax.ppermute(share, 'kmer', [(i, i ^ 1) for i in range(16)])  3.33 us
    pallas_call x1, Pallas kernels, forward_first(): pl.pallas_call(forward_first_kernel, out_shape=[jax.ShapeDtypeStruct((PAR...  3.09 us
  transfers between devices with their start and end apart: 20, of which 10 were waited for; matrix products, arithmetic and copies ran while one was open for 0% of the time, Pallas kernels for 8%

profile of v4, /device:TPU:24, one launch (start us, length us, event | category | flops | bytes accessed | tf_op | source)
XLA Modules:
  0.0 67.3 jit_solution(4919296340294709053)
XLA Ops:
  1.3 3.1 %forward_first.1 = (bf16[1792,128]{1,0:T(8,128)(2,1)S(1)}, bf16[88,128,128]{2,1,0:T(8,128)(2,1)S(1)}, bf16[1024,128]{1,0:T(8,128)(2,1)S(1)}, s32[512]{0:T(512)S(1)}) custom-call(s32[88]{0:T(128)} %rows.1, s32[88]{0:T(128)} %cols.1, s32[1]{0:T(128)S(6)} %copy.7.count, bf16[88,128,128]{2,1,0:T(8,128)(2,1)} %tiles.1, bf16[1024,128]{1,0:T(8,128)(2,1)} %omega.1), custom_call_target="tpu_custom_call" | custom-call | tf_op jit(solution)/shard_map/forward_first/pallas_call | solution.py:176
  4.5 1.0 %forward_next0.1.a = bf16[1792,128]{1,0:T(8,128)(2,1)S(1)} custom-call(s32[512]{0:T(512)S(1)} %get-tuple-element.24.lists, bf16[88,128,128]{2,1,0:T(8,128)(2,1)S(1)} %get-tuple-element.33.held.tiles, bf16[1024,128]{1,0:T(8,128)(2,1)S(1)} %get-tuple-element.26.table), custom_call_target="tpu_custom_call" | custom-call | flops 18454937600 | bytes 144179200 | tf_op jit(solution)/shard_map/forward_next0/pallas_call | solution.py:205
  5.4 0.8 %collective-permute-done.b = bf16[1792,128]{1,0:T(8,128)(2,1)S(1)} collective-permute-done((bf16[1792,128]{1,0:T(8,128)(2,1)S(1)}, bf16[1792,128]{1,0:T(8,128)(2,1)S(1)}, u32[]{:S(2)}, u32[]{:S(2)}) %collective-permute-start) | collective-permute-done | bytes 458784 | tf_op jit(solution)/shard_map/ppermute | solution.py:425
  6.4 1.6 %collective-permute-start.1 = (bf16[896,128]{1,0:T(8,128)(2,1)S(1)}, bf16[896,128]{1,0:T(8,128)(2,1)S(1)}, u32[]{:S(2)}, u32[]{:S(2)}) collective-permute-start(bf16[896,128]{1,0:T(8,128)(2,1)S(1)} %get-tuple-element.28), channel_id=1, source_target_pairs={{0,2},{1,15},{2,0},{3,13},{4,6},{5,11},{6,4},{7,9},{8,10},{9,7},{1... | collective-permute-start | bytes 688136 | tf_op jit(solution)/shard_map/ppermute | solution.py:429
  8.0 2.6 %collective-permute-start.2 = (bf16[896,128]{1,0:T(8,128)(2,1)S(1)}, bf16[896,128]{1,0:T(8,128)(2,1)S(1)}, u32[]{:S(2)}, u32[]{:S(2)}) collective-permute-start(bf16[896,128]{1,0:T(8,128)(2,1)S(1)} %get-tuple-element.29), channel_id=1, source_target_pairs={{0,6},{1,11},{2,4},{3,9},{4,2},{5,15},{6,0},{7,13},{8,14},{9,3},{1... | collective-permute-start | bytes 688136 | tf_op jit(solution)/shard_map/ppermute | solution.py:429
  10.6 1.0 %forward_next3.1 = bf16[1792,128]{1,0:T(8,128)(2,1)S(1)} custom-call(s32[512]{0:T(512)S(1)} %get-tuple-element.24.lists, bf16[88,128,128]{2,1,0:T(8,128)(2,1)S(1)} %get-tuple-element.33.held.tiles, bf16[1024,128]{1,0:T(8,128)(2,1)S(1)} %get-tuple-element.26.table), custom_call_target="tpu_custom_call" | custom-call | flops 18454937600 | bytes 144179200 | tf_op jit(solution)/shard_map/forward_next3/pallas_call | solution.py:205
  11.7 1.0 %forward_next1.1.a = bf16[1792,128]{1,0:T(8,128)(2,1)S(1)} custom-call(s32[512]{0:T(512)S(1)} %get-tuple-element.24.lists, bf16[88,128,128]{2,1,0:T(8,128)(2,1)S(1)} %get-tuple-element.33.held.tiles, bf16[1024,128]{1,0:T(8,128)(2,1)S(1)} %get-tuple-element.26.table), custom_call_target="tpu_custom_call" | custom-call | flops 18454937600 | bytes 144179200 | tf_op jit(solution)/shard_map/forward_next1/pallas_call | solution.py:205
  12.7 0.8 %collective-permute-done.3.b = bf16[1792,128]{1,0:T(8,128)(2,1)S(1)} collective-permute-done((bf16[1792,128]{1,0:T(8,128)(2,1)S(1)}, bf16[1792,128]{1,0:T(8,128)(2,1)S(1)}, u32[]{:S(2)}, u32[]{:S(2)}) %collective-permute-start.3) | collective-permute-done | bytes 458784 | tf_op jit(solution)/shard_map/ppermute | solution.py:425
  13.6 1.1 %collective-permute-start.4 = (bf16[896,128]{1,0:T(8,128)(2,1)S(1)}, bf16[896,128]{1,0:T(8,128)(2,1)S(1)}, u32[]{:S(2)}, u32[]{:S(2)}) collective-permute-start(bf16[896,128]{1,0:T(8,128)(2,1)S(1)} %get-tuple-element.31), channel_id=1, source_target_pairs={{0,4},{1,13},{2,6},{3,15},{4,0},{5,9},{6,2},{7,11},{8,12},{9,5},{1... | collective-permute-start | bytes 688136 | tf_op jit(solution)/shard_map/ppermute | solution.py:429
  14.7 3.7 %collective-permute-start.5 = (bf16[896,128]{1,0:T(8,128)(2,1)S(1)}, bf16[896,128]{1,0:T(8,128)(2,1)S(1)}, u32[]{:S(2)}, u32[]{:S(2)}) collective-permute-start(bf16[896,128]{1,0:T(8,128)(2,1)S(1)} %get-tuple-element.32), channel_id=1, source_target_pairs={{0,8},{1,1},{2,10},{3,3},{4,12},{5,5},{6,14},{7,7},{8,0},{9,9},{10... | collective-permute-start | bytes 688136 | tf_op jit(solution)/shard_map/ppermute | solution.py:429
  18.4 0.5 turn_tiles.1.turned
  18.9 4.7 %collective-permute-done.4.refs_2_ = bf16[896,128]{1,0:T(8,128)(2,1)S(1)} collective-permute-done((bf16[896,128]{1,0:T(8,128)(2,1)S(1)}, bf16[896,128]{1,0:T(8,128)(2,1)S(1)}, u32[]{:S(2)}, u32[]{:S(2)}) %collective-permute-start.4) | collective-permute-done | bytes 229408 | tf_op jit(solution)/shard_map/ppermute | solution.py:429
  23.7 0.1 part_sum.1.refs_0_
  23.9 1.5 %collective-permute-done.6.refs_1_ = bf16[896,128]{1,0:T(8,128)(2,1)S(1)} collective-permute-done((bf16[896,128]{1,0:T(8,128)(2,1)S(1)}, bf16[896,128]{1,0:T(8,128)(2,1)S(1)}, u32[]{:S(2)}, u32[]{:S(2)}) %collective-permute-start.6) | collective-permute-done | bytes 229408 | tf_op jit(solution)/shard_map/ppermute | solution.py:425
  25.4 0.8 %collective-permute-start.7 = (bf16[896,128]{1,0:T(8,128)(2,1)S(1)}, bf16[896,128]{1,0:T(8,128)(2,1)S(1)}, u32[]{:S(2)}, u32[]{:S(2)}) collective-permute-start(bf16[896,128]{1,0:T(8,128)(2,1)S(1)} %chunk_sum.1.chunk), channel_id=1, source_target_pairs={{0,2},{1,15},{2,0},{3,13},{4,6},{5,11},{6,4},{7,9},{8,10},{9,7},{1... | collective-permute-start | bytes 688136 | tf_op jit(solution)/shard_map/ppermute | solution.py:429
  26.3 1.3 %collective-permute-start.8 = (bf16[896,128]{1,0:T(8,128)(2,1)S(1)}, bf16[896,128]{1,0:T(8,128)(2,1)S(1)}, u32[]{:S(2)}, u32[]{:S(2)}) collective-permute-start(bf16[896,128]{1,0:T(8,128)(2,1)S(1)} %chunk_sum.1.chunk), channel_id=1, source_target_pairs={{0,6},{1,11},{2,4},{3,9},{4,2},{5,15},{6,0},{7,13},{8,14},{9,3},{1... | collective-permute-start | bytes 688136 | tf_op jit(solution)/shard_map/ppermute | solution.py:429
  27.5 2.1 %collective-permute-start.11 = (bf16[896,128]{1,0:T(8,128)(2,1)S(1)}, bf16[896,128]{1,0:T(8,128)(2,1)S(1)}, u32[]{:S(2)}, u32[]{:S(2)}) collective-permute-start(bf16[896,128]{1,0:T(8,128)(2,1)S(1)} %chunk_sum.1.chunk), channel_id=1, source_target_pairs={{0,4},{1,13},{2,6},{3,15},{4,0},{5,9},{6,2},{7,11},{8,12},{9,5},{1... | collective-permute-start | bytes 688136 | tf_op jit(solution)/shard_map/ppermute | solution.py:429
  29.6 3.3 %collective-permute-start.12 = (bf16[896,128]{1,0:T(8,128)(2,1)S(1)}, bf16[896,128]{1,0:T(8,128)(2,1)S(1)}, u32[]{:S(2)}, u32[]{:S(2)}) collective-permute-start(bf16[896,128]{1,0:T(8,128)(2,1)S(1)} %chunk_sum.1.chunk), channel_id=1, source_target_pairs={{0,8},{1,1},{2,10},{3,3},{4,12},{5,5},{6,14},{7,7},{8,0},{9,9},{10... | collective-permute-start | bytes 688136 | tf_op jit(solution)/shard_map/ppermute | solution.py:429
  33.0 7.2 %collective-permute-done.8.n1 = bf16[896,128]{1,0:T(8,128)(2,1)S(1)} collective-permute-done((bf16[896,128]{1,0:T(8,128)(2,1)S(1)}, bf16[896,128]{1,0:T(8,128)(2,1)S(1)}, u32[]{:S(2)}, u32[]{:S(2)}) %collective-permute-start.8) | collective-permute-done | bytes 229408 | tf_op jit(solution)/shard_map/ppermute | solution.py:429
  40.2 0.5 collective-permute-start.13
  40.8 0.9 %collective-permute-done.10.f1 = bf16[896,128]{1,0:T(8,128)(2,1)S(1)} collective-permute-done((bf16[896,128]{1,0:T(8,128)(2,1)S(1)}, bf16[896,128]{1,0:T(8,128)(2,1)S(1)}, u32[]{:S(2)}, u32[]{:S(2)}) %collective-permute-start.10) | collective-permute-done | bytes 229408 | tf_op jit(solution)/shard_map/ppermute | solution.py:425
  41.7 1.9 %backward_early.1 = (f32[1152,128]{1,0:T(8,128)S(1)}, bf16[448,128]{1,0:T(8,128)(2,1)}) custom-call(s32[512]{0:T(512)S(1)} %get-tuple-element.24.lists, bf16[88,128,128]{2,1,0:T(8,128)(2,1)S(1)} %turn_tiles.1.turned, bf16[896,128]{1,0:T(8,128)(2,1)S(1)} %chunk_sum.1.chunk, bf16[896,128]{1,0:T(8,128)(2,1)S(1)} %collective-permute-done.7.n0, ...), custom_call_target="tpu_custom_call" | custom-call | flops 18454937600 | bytes 144179200 | tf_op jit(solution)/shard_map/backward_early/pallas_call | solution.py:307
  43.6 1.3 %backward_late.1 = (f32[256,128]{1,0:T(8,128)S(1)}, bf16[256,128]{1,0:T(8,128)(2,1)S(1)}, bf16[256,128]{1,0:T(8,128)(2,1)S(1)}, bf16[256,128]{1,0:T(8,128)(2,1)S(1)}) custom-call(s32[512]{0:T(512)S(1)} %get-tuple-element.24.lists, bf16[88,128,128]{2,1,0:T(8,128)(2,1)S(1)} %turn_tiles.1.turned, f32[1152,128]{1,0:T(8,128)S(1)} %get-tuple-element.37.first, ...), custom_call_target="tpu_custom_call" | custom-call | tf_op jit(solution)/shard_map/backward_late/pallas_call | solution.py:344
  44.9 1.7 %collective-permute-start.15 = (bf16[256,128]{1,0:T(8,128)(2,1)S(1)}, bf16[256,128]{1,0:T(8,128)(2,1)S(1)}, u32[]{:S(2)}, u32[]{:S(2)}) collective-permute-start(bf16[256,128]{1,0:T(8,128)(2,1)S(1)} %get-tuple-element.39), channel_id=1, source_target_pairs={{0,128},{1,129},{2,130},{3,131},{4,132},{5,133},{6,134},{7,135},{8... | collective-permute-start | bytes 196616 | tf_op jit(solution)/shard_map/ppermute | solution.py:453
  46.6 2.3 %collective-permute-start.16 = (bf16[256,128]{1,0:T(8,128)(2,1)S(1)}, bf16[256,128]{1,0:T(8,128)(2,1)S(1)}, u32[]{:S(2)}, u32[]{:S(2)}) collective-permute-start(bf16[256,128]{1,0:T(8,128)(2,1)S(1)} %get-tuple-element.40), channel_id=1, source_target_pairs={{0,64},{1,193},{2,66},{3,195},{4,68},{5,197},{6,70},{7,199},{8,72}... | collective-permute-start | bytes 196616 | tf_op jit(solution)/shard_map/ppermute | solution.py:453
  48.8 2.1 %collective-permute-done.15.g0 = bf16[256,128]{1,0:T(8,128)(2,1)S(1)} collective-permute-done((bf16[256,128]{1,0:T(8,128)(2,1)S(1)}, bf16[256,128]{1,0:T(8,128)(2,1)S(1)}, u32[]{:S(2)}, u32[]{:S(2)}) %collective-permute-start.15) | collective-permute-done | bytes 65568 | tf_op jit(solution)/shard_map/ppermute | solution.py:453
  50.9 3.4 %collective-permute-done.17.g2 = bf16[256,128]{1,0:T(8,128)(2,1)S(1)} collective-permute-done((bf16[256,128]{1,0:T(8,128)(2,1)S(1)}, bf16[256,128]{1,0:T(8,128)(2,1)S(1)}, u32[]{:S(2)}, u32[]{:S(2)}) %collective-permute-start.17) | collective-permute-done | bytes 65568 | tf_op jit(solution)/shard_map/ppermute | solution.py:453
  54.4 1.7 %collective-permute-start.18 = (bf16[128,128]{1,0:T(8,128)(2,1)S(1)}, bf16[128,128]{1,0:T(8,128)(2,1)S(1)}, u32[]{:S(2)}, u32[]{:S(2)}) collective-permute-start(bf16[128,128]{1,0:T(8,128)(2,1)S(1)} %get-tuple-element.43), channel_id=1, source_target_pairs={{0,16},{16,0},{32,48},{48,32},{64,80},{80,64},{96,112},{112,96},{1... | collective-permute-start | bytes 98312 | tf_op jit(solution)/shard_map/ppermute | solution.py:455
  56.0 3.3 %collective-permute-done.18.got = bf16[128,128]{1,0:T(8,128)(2,1)S(1)} collective-permute-done((bf16[128,128]{1,0:T(8,128)(2,1)S(1)}, bf16[128,128]{1,0:T(8,128)(2,1)S(1)}, u32[]{:S(2)}, u32[]{:S(2)}) %collective-permute-start.18) | collective-permute-done | bytes 32800 | tf_op jit(solution)/shard_map/ppermute | solution.py:455
  59.4 5.5 %collective-permute-start.19 = (bf16[64,128]{1,0:T(8,128)(2,1)S(1)}, bf16[64,128]{1,0:T(8,128)(2,1)S(1)}, u32[]{:S(2)}, u32[]{:S(2)}) collective-permute-start(bf16[64,128]{1,0:T(8,128)(2,1)S(1)} %get-tuple-element.45), channel_id=1, source_target_pairs={{0,48},{16,32},{32,16},{48,0},{64,112},{80,96},{96,80},{112,64},{1... | collective-permute-start | bytes 49160 | tf_op jit(solution)/shard_map/ppermute | solution.py:456
  64.9 1.7 %collective-permute-done.19.got = bf16[64,128]{1,0:T(8,128)(2,1)S(1)} collective-permute-done((bf16[64,128]{1,0:T(8,128)(2,1)S(1)}, bf16[64,128]{1,0:T(8,128)(2,1)S(1)}, u32[]{:S(2)}, u32[]{:S(2)}) %collective-permute-start.19) | collective-permute-done | bytes 16416 | tf_op jit(solution)/shard_map/ppermute | solution.py:456
  66.6 0.6 last_sum.1
  (22 shorter events, 0.8 us)
Async XLA Ops:
  4.4 1.9 %collective-permute-start = (bf16[1792,128]{1,0:T(8,128)(2,1)S(1)}, bf16[1792,128]{1,0:T(8,128)(2,1)S(1)}, u32[]{:S(2)}, u32[]{:S(2)}) collective-permute-start(bf16[1792,128]{1,0:T(8,128)(2,1)S(1)} %get-tuple-element.27), channel_id=1, source_target_pairs={{0,1},{1,0},{2,3},{3,2},{4,5},{5,4},{6,7},{7,6},{8,9},{9,8},{10,11... | collective-permute-start | bytes 1376264 | tf_op jit(solution)/shard_map/ppermute | solution.py:425
  6.4 12.5 %collective-permute-start.1 = (bf16[896,128]{1,0:T(8,128)(2,1)S(1)}, bf16[896,128]{1,0:T(8,128)(2,1)S(1)}, u32[]{:S(2)}, u32[]{:S(2)}) collective-permute-start(bf16[896,128]{1,0:T(8,128)(2,1)S(1)} %get-tuple-element.28), channel_id=1, source_target_pairs={{0,2},{1,15},{2,0},{3,13},{4,6},{5,11},{6,4},{7,9},{8,10},{9,7},{1... | collective-permute-start | bytes 688136 | tf_op jit(solution)/shard_map/ppermute | solution.py:429
  8.0 10.9 %collective-permute-start.2 = (bf16[896,128]{1,0:T(8,128)(2,1)S(1)}, bf16[896,128]{1,0:T(8,128)(2,1)S(1)}, u32[]{:S(2)}, u32[]{:S(2)}) collective-permute-start(bf16[896,128]{1,0:T(8,128)(2,1)S(1)} %get-tuple-element.29), channel_id=1, source_target_pairs={{0,6},{1,11},{2,4},{3,9},{4,2},{5,15},{6,0},{7,13},{8,14},{9,3},{1... | collective-permute-start | bytes 688136 | tf_op jit(solution)/shard_map/ppermute | solution.py:429
  11.6 1.9 %collective-permute-start.3 = (bf16[1792,128]{1,0:T(8,128)(2,1)S(1)}, bf16[1792,128]{1,0:T(8,128)(2,1)S(1)}, u32[]{:S(2)}, u32[]{:S(2)}) collective-permute-start(bf16[1792,128]{1,0:T(8,128)(2,1)S(1)} %forward_next3.1), channel_id=1, source_target_pairs={{0,1},{1,0},{2,3},{3,2},{4,5},{5,4},{6,7},{7,6},{8,9},{9,8},{10,11... | collective-permute-start | bytes 1376264 | tf_op jit(solution)/shard_map/ppermute | solution.py:425
  13.6 10.1 %collective-permute-start.4 = (bf16[896,128]{1,0:T(8,128)(2,1)S(1)}, bf16[896,128]{1,0:T(8,128)(2,1)S(1)}, u32[]{:S(2)}, u32[]{:S(2)}) collective-permute-start(bf16[896,128]{1,0:T(8,128)(2,1)S(1)} %get-tuple-element.31), channel_id=1, source_target_pairs={{0,4},{1,13},{2,6},{3,15},{4,0},{5,9},{6,2},{7,11},{8,12},{9,5},{1... | collective-permute-start | bytes 688136 | tf_op jit(solution)/shard_map/ppermute | solution.py:429
  14.7 9.0 %collective-permute-start.5 = (bf16[896,128]{1,0:T(8,128)(2,1)S(1)}, bf16[896,128]{1,0:T(8,128)(2,1)S(1)}, u32[]{:S(2)}, u32[]{:S(2)}) collective-permute-start(bf16[896,128]{1,0:T(8,128)(2,1)S(1)} %get-tuple-element.32), channel_id=1, source_target_pairs={{0,8},{1,1},{2,10},{3,3},{4,12},{5,5},{6,14},{7,7},{8,0},{9,9},{10... | collective-permute-start | bytes 688136 | tf_op jit(solution)/shard_map/ppermute | solution.py:429
  23.8 1.6 %collective-permute-start.6 = (bf16[896,128]{1,0:T(8,128)(2,1)S(1)}, bf16[896,128]{1,0:T(8,128)(2,1)S(1)}, u32[]{:S(2)}, u32[]{:S(2)}) collective-permute-start(bf16[896,128]{1,0:T(8,128)(2,1)S(1)} %part_sum.1.refs_0_), channel_id=1, source_target_pairs={{0,1},{1,0},{2,3},{3,2},{4,5},{5,4},{6,7},{7,6},{8,9},{9,8},{10,11... | collective-permute-start | bytes 688136 | tf_op jit(solution)/shard_map/ppermute | solution.py:425
  25.4 7.5 %collective-permute-start.7 = (bf16[896,128]{1,0:T(8,128)(2,1)S(1)}, bf16[896,128]{1,0:T(8,128)(2,1)S(1)}, u32[]{:S(2)}, u32[]{:S(2)}) collective-permute-start(bf16[896,128]{1,0:T(8,128)(2,1)S(1)} %chunk_sum.1.chunk), channel_id=1, source_target_pairs={{0,2},{1,15},{2,0},{3,13},{4,6},{5,11},{6,4},{7,9},{8,10},{9,7},{1... | collective-permute-start | bytes 688136 | tf_op jit(solution)/shard_map/ppermute | solution.py:429
  26.3 13.9 %collective-permute-start.8 = (bf16[896,128]{1,0:T(8,128)(2,1)S(1)}, bf16[896,128]{1,0:T(8,128)(2,1)S(1)}, u32[]{:S(2)}, u32[]{:S(2)}) collective-permute-start(bf16[896,128]{1,0:T(8,128)(2,1)S(1)} %chunk_sum.1.chunk), channel_id=1, source_target_pairs={{0,6},{1,11},{2,4},{3,9},{4,2},{5,15},{6,0},{7,13},{8,14},{9,3},{1... | collective-permute-start | bytes 688136 | tf_op jit(solution)/shard_map/ppermute | solution.py:429
  27.5 12.7 %collective-permute-start.11 = (bf16[896,128]{1,0:T(8,128)(2,1)S(1)}, bf16[896,128]{1,0:T(8,128)(2,1)S(1)}, u32[]{:S(2)}, u32[]{:S(2)}) collective-permute-start(bf16[896,128]{1,0:T(8,128)(2,1)S(1)} %chunk_sum.1.chunk), channel_id=1, source_target_pairs={{0,4},{1,13},{2,6},{3,15},{4,0},{5,9},{6,2},{7,11},{8,12},{9,5},{1... | collective-permute-start | bytes 688136 | tf_op jit(solution)/shard_map/ppermute | solution.py:429
  29.6 11.1 %collective-permute-start.12 = (bf16[896,128]{1,0:T(8,128)(2,1)S(1)}, bf16[896,128]{1,0:T(8,128)(2,1)S(1)}, u32[]{:S(2)}, u32[]{:S(2)}) collective-permute-start(bf16[896,128]{1,0:T(8,128)(2,1)S(1)} %chunk_sum.1.chunk), channel_id=1, source_target_pairs={{0,8},{1,1},{2,10},{3,3},{4,12},{5,5},{6,14},{7,7},{8,0},{9,9},{10... | collective-permute-start | bytes 688136 | tf_op jit(solution)/shard_map/ppermute | solution.py:429
  32.9 7.9 %collective-permute-start.9 = (bf16[896,128]{1,0:T(8,128)(2,1)S(1)}, bf16[896,128]{1,0:T(8,128)(2,1)S(1)}, u32[]{:S(2)}, u32[]{:S(2)}) collective-permute-start(bf16[896,128]{1,0:T(8,128)(2,1)S(1)} %collective-permute-done.7.n0), channel_id=1, source_target_pairs={{0,1},{1,0},{2,3},{3,2},{4,5},{5,4},{6,7},{7,6},{8,9},{9,8},{10,11... | collective-permute-start | bytes 688136 | tf_op jit(solution)/shard_map/ppermute | solution.py:425
  40.2 1.5 %collective-permute-start.10 = (bf16[896,128]{1,0:T(8,128)(2,1)S(1)}, bf16[896,128]{1,0:T(8,128)(2,1)S(1)}, u32[]{:S(2)}, u32[]{:S(2)}) collective-permute-start(bf16[896,128]{1,0:T(8,128)(2,1)S(1)} %collective-permute-done.8.n1), channel_id=1, source_target_pairs={{0,1},{1,0},{2,3},{3,2},{4,5},{5,4},{6,7},{7,6},{8,9},{9,8},{10,11... | collective-permute-start | bytes 688136 | tf_op jit(solution)/shard_map/ppermute | solution.py:425
  40.2 3.4 %collective-permute-start.13 = (bf16[896,128]{1,0:T(8,128)(2,1)S(1)}, bf16[896,128]{1,0:T(8,128)(2,1)S(1)}, u32[]{:S(2)}, u32[]{:S(2)}) collective-permute-start(bf16[896,128]{1,0:T(8,128)(2,1)S(1)} %collective-permute-done.11.n2), channel_id=1, source_target_pairs={{0,1},{1,0},{2,3},{3,2},{4,5},{5,4},{6,7},{7,6},{8,9},{9,8},{10,11... | collective-permute-start | bytes 688136 | tf_op jit(solution)/shard_map/ppermute | solution.py:425
  40.7 2.9 %collective-permute-start.14 = (bf16[896,128]{1,0:T(8,128)(2,1)S(1)}, bf16[896,128]{1,0:T(8,128)(2,1)S(1)}, u32[]{:S(2)}, u32[]{:S(2)}) collective-permute-start(bf16[896,128]{1,0:T(8,128)(2,1)S(1)} %collective-permute-done.12.n3), channel_id=1, source_target_pairs={{0,1},{1,0},{2,3},{3,2},{4,5},{5,4},{6,7},{7,6},{8,9},{9,8},{10,11... | collective-permute-start | bytes 688136 | tf_op jit(solution)/shard_map/ppermute | solution.py:425
  44.9 6.0 %collective-permute-start.15 = (bf16[256,128]{1,0:T(8,128)(2,1)S(1)}, bf16[256,128]{1,0:T(8,128)(2,1)S(1)}, u32[]{:S(2)}, u32[]{:S(2)}) collective-permute-start(bf16[256,128]{1,0:T(8,128)(2,1)S(1)} %get-tuple-element.39), channel_id=1, source_target_pairs={{0,128},{1,129},{2,130},{3,131},{4,132},{5,133},{6,134},{7,135},{8... | collective-permute-start | bytes 196616 | tf_op jit(solution)/shard_map/ppermute | solution.py:453
  46.6 4.3 %collective-permute-start.16 = (bf16[256,128]{1,0:T(8,128)(2,1)S(1)}, bf16[256,128]{1,0:T(8,128)(2,1)S(1)}, u32[]{:S(2)}, u32[]{:S(2)}) collective-permute-start(bf16[256,128]{1,0:T(8,128)(2,1)S(1)} %get-tuple-element.40), channel_id=1, source_target_pairs={{0,64},{1,193},{2,66},{3,195},{4,68},{5,197},{6,70},{7,199},{8,72}... | collective-permute-start | bytes 196616 | tf_op jit(solution)/shard_map/ppermute | solution.py:453
  48.8 5.5 %collective-permute-start.17 = (bf16[256,128]{1,0:T(8,128)(2,1)S(1)}, bf16[256,128]{1,0:T(8,128)(2,1)S(1)}, u32[]{:S(2)}, u32[]{:S(2)}) collective-permute-start(bf16[256,128]{1,0:T(8,128)(2,1)S(1)} %get-tuple-element.41), channel_id=1, source_target_pairs={{0,192},{1,65},{2,194},{3,67},{4,196},{5,69},{6,198},{7,71},{8,200... | collective-permute-start | bytes 196616 | tf_op jit(solution)/shard_map/ppermute | solution.py:453
  54.4 5.0 %collective-permute-start.18 = (bf16[128,128]{1,0:T(8,128)(2,1)S(1)}, bf16[128,128]{1,0:T(8,128)(2,1)S(1)}, u32[]{:S(2)}, u32[]{:S(2)}) collective-permute-start(bf16[128,128]{1,0:T(8,128)(2,1)S(1)} %get-tuple-element.43), channel_id=1, source_target_pairs={{0,16},{16,0},{32,48},{48,32},{64,80},{80,64},{96,112},{112,96},{1... | collective-permute-start | bytes 98312 | tf_op jit(solution)/shard_map/ppermute | solution.py:455
  59.4 7.2 %collective-permute-start.19 = (bf16[64,128]{1,0:T(8,128)(2,1)S(1)}, bf16[64,128]{1,0:T(8,128)(2,1)S(1)}, u32[]{:S(2)}, u32[]{:S(2)}) collective-permute-start(bf16[64,128]{1,0:T(8,128)(2,1)S(1)} %get-tuple-element.45), channel_id=1, source_target_pairs={{0,48},{16,32},{32,16},{48,0},{64,112},{80,96},{96,80},{112,64},{1... | collective-permute-start | bytes 49160 | tf_op jit(solution)/shard_map/ppermute | solution.py:456

commit v5 on v4

--- a/solution.py
+++ b/solution.py
@@ -24,7 +24,7 @@
     ((1, 0), (3, 1)),
     ((3, 0), (1, 1)),
     ((2, 0), (2, 1)),
-    ((0, 1), (0, 0)),
+    ((0, 0), (0, 1)),
 )
 NEAR_EARLY, NEAR_LATE, FAR_EARLY, FAR_LATE = range(4)
 LINE = ((2, 2), (1, 3), (3, 1))
@@ -93,7 +93,7 @@
         mx = m % 4
         e = jnp.bitwise_xor(x, mx)
         same_z = (z == m // 4).astype(jnp.int32)
-        core = jnp.where(e == 0, same_z, 1 - same_z)
+        core = 1 - same_z
         odd = jnp.where(core == 0, e == 3, e == 1).astype(jnp.int32)
         p = jnp.where(e == 0, 3, jnp.where(e == 2, 2, odd))
         late = (p >= 2).astype(jnp.int32)
@@ -295,28 +295,39 @@
         backward_slots(lists, kind, turned, table, acc)
 
 
-def backward_early_kernel(lists, turned, chunk, n0, n1, f0, f1, out, sketch, table):
+def sketch_kernel(chunk, out):
+    _, _, c = place()
+    size = out.shape[0]
+    out[...] = chunk[pl.ds(pl.multiple_of(c * size, size), size), :]
+
+
+def sketch_rows(chunk):
+    return pl.pallas_call(
+        sketch_kernel,
+        out_shape=jax.ShapeDtypeStruct((CHUNK // 2, TILE), jnp.bfloat16),
+        in_specs=[vm()],
+        out_specs=vm(),
+        compiler_params=params(),
+        name="sketch_rows",
+    )(chunk)
+
+
+def backward_early_kernel(lists, turned, n0, n1, f0, f1, out, table):
     out[...] = jnp.zeros_like(out)
     backward_part(lists, (NEAR_EARLY, FAR_EARLY), turned, (n0, n1), (f0, f1), table, out)
-    _, _, c = place()
-    size = sketch.shape[0]
-    sketch[...] = chunk[pl.ds(pl.multiple_of(c * size, size), size), :]
-
-
-def backward_early(lists, turned, chunk, near, far):
+
+
+def backward_early(lists, turned, near, far):
     return pl.pallas_call(
         backward_early_kernel,
-        out_shape=[
-            jax.ShapeDtypeStruct(((SB_DEV + 1) * TILE, TILE), jnp.float32),
-            jax.ShapeDtypeStruct((CHUNK // 2, TILE), jnp.bfloat16),
-        ],
-        in_specs=[sm()] + [vm()] * 6,
-        out_specs=[vm()] * 2,
+        out_shape=jax.ShapeDtypeStruct(((SB_DEV + 1) * TILE, TILE), jnp.float32),
+        in_specs=[sm()] + [vm()] * 5,
+        out_specs=vm(),
         scratch_shapes=[pltpu.VMEM((PART, TILE), jnp.bfloat16)],
         compiler_params=params(),
         cost_estimate=COST,
         name="backward_early",
-    )(lists, turned, chunk, *near, *far)
+    )(lists, turned, *near, *far)
 
 
 def line_offset(r):
@@ -448,8 +459,9 @@
     chunk = part_sum("chunk_sum", part, swap(part))
     near = [trade(chunk, p) for p in range(4)]
     far = [swap(piece) for piece in near]
-    first, sketch = backward_early(lists, turned, chunk, near[:2], far[:2])
+    first = backward_early(lists, turned, near[:2], far[:2])
     keep, *shares = backward_late(lists, turned, first, near[2:], far[2:])
+    sketch = sketch_rows(after(chunk, *shares))
     got = [lax.ppermute(s, ("kmer", "samp"), y_pairs(r)) for r, s in enumerate(shares)]
     keep, share = line_sum(keep, got)
     keep, share = halve_sum(keep, lax.ppermute(share, "kmer", [(i, i ^ 1) for i in range(16)]))

time: 67.7 us -> 66.5 us (0.982)
    ppermute x8, starting transfers between devices: 16.5 us -> 10.8 us  [trade(): return lax.ppermute(value, 'samp', round_pairs(p))]
    ppermute x8, waiting for transfers between devices: 12 us -> 15.1 us  [trade(): return lax.ppermute(value, 'samp', round_pairs(p))]
    ppermute x7, starting transfers between devices: 0.97 us -> 3.4 us  [swap(): return lax.ppermute(value, 'samp', [(s, s ^ 1) for s in range(16)])]
    ppermute x1, starting transfers between devices: 1.68 us -> 3.83 us  [shards(): lax.ppermute(share, 'kmer', [(i, i ^ 1) for i in range(16)])]
    ppermute x1, waiting for transfers between devices: 3.33 us -> 1.89 us  [shards(): lax.ppermute(share, 'kmer', [(i, i ^ 1) for i in range(16)])]
    ppermute x7, waiting for transfers between devices: 4.04 us -> 2.85 us  [swap(): return lax.ppermute(value, 'samp', [(s, s ^ 1) for s in range(16)])]
    ppermute x1, starting transfers between devices: 5.53 us -> 6.49 us  [shards(): lax.ppermute(share, 'kmer', [(i, i // 4 * 4 + 3 - i % 4) for i in range(1...]
    pallas_call x1 -> x2, Pallas kernels: 1.9 us -> 1.88 us  [the longest x1 1.23 us: backward_early(): pl.pallas_call(backward_early_kernel, out_shape=jax.ShapeDtypeStruct(((SB...]
  transfers between devices with their start and end apart: 20 -> 20, of which waited for: 10 -> 12; matrix products, arithmetic and copies ran while one was open for 0% -> 0% of each run, Pallas kernels for 8% -> 8%
where the time goes in v5:
time: 66.5 us; the launch traced here: 66.3 us
  starting transfers between devices  28.2 us (42%)
  waiting for transfers between devices  26.3 us (40%)
  Pallas kernels  10.4 us (16%)
  between operations  1.42 us (2%)
    ppermute x8, waiting for transfers between devices, trade(): return lax.ppermute(value, 'samp', round_pairs(p))  15.1 us
    ppermute x8, starting transfers between devices, trade(): return lax.ppermute(value, 'samp', round_pairs(p))  10.8 us
    ppermute x1, starting transfers between devices, shards(): lax.ppermute(share, 'kmer', [(i, i // 4 * 4 + 3 - i % 4) for i in range(1...  6.49 us
    ppermute x3, waiting for transfers between devices, shards(): lax.ppermute(s, ('kmer', 'samp'), y_pairs(r))  5.36 us
    ppermute x1, starting transfers between devices, shards(): lax.ppermute(share, 'kmer', [(i, i ^ 1) for i in range(16)])  3.83 us
    ppermute x3, starting transfers between devices, shards(): lax.ppermute(s, ('kmer', 'samp'), y_pairs(r))  3.62 us
    ppermute x7, starting transfers between devices, swap(): return lax.ppermute(value, 'samp', [(s, s ^ 1) for s in range(16)])  3.4 us
    pallas_call x1, Pallas kernels, forward_first(): pl.pallas_call(forward_first_kernel, out_shape=[jax.ShapeDtypeStruct((PAR...  3.09 us
  transfers between devices with their start and end apart: 20, of which 12 were waited for; matrix products, arithmetic and copies ran while one was open for 0% of the time, Pallas kernels for 8%

profile of v5, /device:TPU:24, one launch (start us, length us, event | category | flops | bytes accessed | tf_op | source)
XLA Modules:
  0.0 66.3 jit_solution(666868283913263977)
XLA Ops:
  1.3 3.1 %forward_first.1 = (bf16[1792,128]{1,0:T(8,128)(2,1)S(1)}, bf16[88,128,128]{2,1,0:T(8,128)(2,1)S(1)}, bf16[1024,128]{1,0:T(8,128)(2,1)S(1)}, s32[512]{0:T(512)S(1)}) custom-call(s32[88]{0:T(128)} %rows.1, s32[88]{0:T(128)} %cols.1, s32[1]{0:T(128)S(6)} %copy.7.count, bf16[88,128,128]{2,1,0:T(8,128)(2,1)} %tiles.1, bf16[1024,128]{1,0:T(8,128)(2,1)} %omega.1), custom_call_target="tpu_custom_call" | custom-call | tf_op jit(solution)/shard_map/forward_first/pallas_call | solution.py:176
  4.5 1.0 %forward_next0.1.a = bf16[1792,128]{1,0:T(8,128)(2,1)S(1)} custom-call(s32[512]{0:T(512)S(1)} %get-tuple-element.23.lists, bf16[88,128,128]{2,1,0:T(8,128)(2,1)S(1)} %get-tuple-element.32.held.tiles, bf16[1024,128]{1,0:T(8,128)(2,1)S(1)} %get-tuple-element.25.table), custom_call_target="tpu_custom_call" | custom-call | flops 18454937600 | bytes 144179200 | tf_op jit(solution)/shard_map/forward_next0/pallas_call | solution.py:205
  5.4 0.8 %collective-permute-done.b = bf16[1792,128]{1,0:T(8,128)(2,1)S(1)} collective-permute-done((bf16[1792,128]{1,0:T(8,128)(2,1)S(1)}, bf16[1792,128]{1,0:T(8,128)(2,1)S(1)}, u32[]{:S(2)}, u32[]{:S(2)}) %collective-permute-start) | collective-permute-done | bytes 458784 | tf_op jit(solution)/shard_map/ppermute | solution.py:436
  6.4 1.6 %collective-permute-start.1 = (bf16[896,128]{1,0:T(8,128)(2,1)S(1)}, bf16[896,128]{1,0:T(8,128)(2,1)S(1)}, u32[]{:S(2)}, u32[]{:S(2)}) collective-permute-start(bf16[896,128]{1,0:T(8,128)(2,1)S(1)} %get-tuple-element.27), channel_id=1, source_target_pairs={{0,2},{1,15},{2,0},{3,13},{4,6},{5,11},{6,4},{7,9},{8,10},{9,7},{1... | collective-permute-start | bytes 688136 | tf_op jit(solution)/shard_map/ppermute | solution.py:440
  8.0 2.1 %collective-permute-start.2 = (bf16[896,128]{1,0:T(8,128)(2,1)S(1)}, bf16[896,128]{1,0:T(8,128)(2,1)S(1)}, u32[]{:S(2)}, u32[]{:S(2)}) collective-permute-start(bf16[896,128]{1,0:T(8,128)(2,1)S(1)} %get-tuple-element.28), channel_id=1, source_target_pairs={{0,6},{1,11},{2,4},{3,9},{4,2},{5,15},{6,0},{7,13},{8,14},{9,3},{1... | collective-permute-start | bytes 688136 | tf_op jit(solution)/shard_map/ppermute | solution.py:440
  10.1 1.0 %forward_next3.1 = bf16[1792,128]{1,0:T(8,128)(2,1)S(1)} custom-call(s32[512]{0:T(512)S(1)} %get-tuple-element.23.lists, bf16[88,128,128]{2,1,0:T(8,128)(2,1)S(1)} %get-tuple-element.32.held.tiles, bf16[1024,128]{1,0:T(8,128)(2,1)S(1)} %get-tuple-element.25.table), custom_call_target="tpu_custom_call" | custom-call | flops 18454937600 | bytes 144179200 | tf_op jit(solution)/shard_map/forward_next3/pallas_call | solution.py:205
  11.5 1.0 %forward_next1.1.a = bf16[1792,128]{1,0:T(8,128)(2,1)S(1)} custom-call(s32[512]{0:T(512)S(1)} %get-tuple-element.23.lists, bf16[88,128,128]{2,1,0:T(8,128)(2,1)S(1)} %get-tuple-element.32.held.tiles, bf16[1024,128]{1,0:T(8,128)(2,1)S(1)} %get-tuple-element.25.table), custom_call_target="tpu_custom_call" | custom-call | flops 18454937600 | bytes 144179200 | tf_op jit(solution)/shard_map/forward_next1/pallas_call | solution.py:205
  13.0 1.6 %collective-permute-start.4 = (bf16[896,128]{1,0:T(8,128)(2,1)S(1)}, bf16[896,128]{1,0:T(8,128)(2,1)S(1)}, u32[]{:S(2)}, u32[]{:S(2)}) collective-permute-start(bf16[896,128]{1,0:T(8,128)(2,1)S(1)} %get-tuple-element.30), channel_id=1, source_target_pairs={{0,4},{1,13},{2,6},{3,15},{4,0},{5,9},{6,2},{7,11},{8,12},{9,5},{1... | collective-permute-start | bytes 688136 | tf_op jit(solution)/shard_map/ppermute | solution.py:440
  14.7 0.7 collective-permute-start.5
  15.7 0.8 %collective-permute-done.2.refs_1_ = bf16[896,128]{1,0:T(8,128)(2,1)S(1)} collective-permute-done((bf16[896,128]{1,0:T(8,128)(2,1)S(1)}, bf16[896,128]{1,0:T(8,128)(2,1)S(1)}, u32[]{:S(2)}, u32[]{:S(2)}) %collective-permute-start.2) | collective-permute-done | bytes 229408 | tf_op jit(solution)/shard_map/ppermute | solution.py:440
  16.5 6.6 %collective-permute-done.4.refs_2_ = bf16[896,128]{1,0:T(8,128)(2,1)S(1)} collective-permute-done((bf16[896,128]{1,0:T(8,128)(2,1)S(1)}, bf16[896,128]{1,0:T(8,128)(2,1)S(1)}, u32[]{:S(2)}, u32[]{:S(2)}) %collective-permute-start.4) | collective-permute-done | bytes 229408 | tf_op jit(solution)/shard_map/ppermute | solution.py:440
  23.3 1.5 %collective-permute-done.6.refs_1_ = bf16[896,128]{1,0:T(8,128)(2,1)S(1)} collective-permute-done((bf16[896,128]{1,0:T(8,128)(2,1)S(1)}, bf16[896,128]{1,0:T(8,128)(2,1)S(1)}, u32[]{:S(2)}, u32[]{:S(2)}) %collective-permute-start.6) | collective-permute-done | bytes 229408 | tf_op jit(solution)/shard_map/ppermute | solution.py:436
  24.9 1.4 %collective-permute-start.7 = (bf16[896,128]{1,0:T(8,128)(2,1)S(1)}, bf16[896,128]{1,0:T(8,128)(2,1)S(1)}, u32[]{:S(2)}, u32[]{:S(2)}) collective-permute-start(bf16[896,128]{1,0:T(8,128)(2,1)S(1)} %chunk_sum.1.chunk), channel_id=1, source_target_pairs={{0,2},{1,15},{2,0},{3,13},{4,6},{5,11},{6,4},{7,9},{8,10},{9,7},{1... | collective-permute-start | bytes 688136 | tf_op jit(solution)/shard_map/ppermute | solution.py:440
  26.2 0.8 %collective-permute-start.8 = (bf16[896,128]{1,0:T(8,128)(2,1)S(1)}, bf16[896,128]{1,0:T(8,128)(2,1)S(1)}, u32[]{:S(2)}, u32[]{:S(2)}) collective-permute-start(bf16[896,128]{1,0:T(8,128)(2,1)S(1)} %chunk_sum.1.chunk), channel_id=1, source_target_pairs={{0,6},{1,11},{2,4},{3,9},{4,2},{5,15},{6,0},{7,13},{8,14},{9,3},{1... | collective-permute-start | bytes 688136 | tf_op jit(solution)/shard_map/ppermute | solution.py:440
  27.1 2.0 %collective-permute-start.11 = (bf16[896,128]{1,0:T(8,128)(2,1)S(1)}, bf16[896,128]{1,0:T(8,128)(2,1)S(1)}, u32[]{:S(2)}, u32[]{:S(2)}) collective-permute-start(bf16[896,128]{1,0:T(8,128)(2,1)S(1)} %chunk_sum.1.chunk), channel_id=1, source_target_pairs={{0,4},{1,13},{2,6},{3,15},{4,0},{5,9},{6,2},{7,11},{8,12},{9,5},{1... | collective-permute-start | bytes 688136 | tf_op jit(solution)/shard_map/ppermute | solution.py:440
  29.1 0.7 collective-permute-start.12
  29.7 1.3 %collective-permute-done.7.n0 = bf16[896,128]{1,0:T(8,128)(2,1)S(1)} collective-permute-done((bf16[896,128]{1,0:T(8,128)(2,1)S(1)}, bf16[896,128]{1,0:T(8,128)(2,1)S(1)}, u32[]{:S(2)}, u32[]{:S(2)}) %collective-permute-start.7) | collective-permute-done | bytes 229408 | tf_op jit(solution)/shard_map/ppermute | solution.py:440
  31.0 2.2 %collective-permute-start.9 = (bf16[896,128]{1,0:T(8,128)(2,1)S(1)}, bf16[896,128]{1,0:T(8,128)(2,1)S(1)}, u32[]{:S(2)}, u32[]{:S(2)}) collective-permute-start(bf16[896,128]{1,0:T(8,128)(2,1)S(1)} %collective-permute-done.7.n0), channel_id=1, source_target_pairs={{0,1},{1,0},{2,3},{3,2},{4,5},{5,4},{6,7},{7,6},{8,9},{9,8},{10,11... | collective-permute-start | bytes 688136 | tf_op jit(solution)/shard_map/ppermute | solution.py:436
  33.2 4.8 %collective-permute-done.8.n1 = bf16[896,128]{1,0:T(8,128)(2,1)S(1)} collective-permute-done((bf16[896,128]{1,0:T(8,128)(2,1)S(1)}, bf16[896,128]{1,0:T(8,128)(2,1)S(1)}, u32[]{:S(2)}, u32[]{:S(2)}) %collective-permute-start.8) | collective-permute-done | bytes 229408 | tf_op jit(solution)/shard_map/ppermute | solution.py:440
  38.0 1.6 %collective-permute-done.11.n2 = bf16[896,128]{1,0:T(8,128)(2,1)S(1)} collective-permute-done((bf16[896,128]{1,0:T(8,128)(2,1)S(1)}, bf16[896,128]{1,0:T(8,128)(2,1)S(1)}, u32[]{:S(2)}, u32[]{:S(2)}) %collective-permute-start.11) | collective-permute-done | bytes 229408 | tf_op jit(solution)/shard_map/ppermute | solution.py:440
  40.2 1.2 %backward_early.1.first = f32[1152,128]{1,0:T(8,128)S(1)} custom-call(s32[512]{0:T(512)S(1)} %get-tuple-element.23.lists, bf16[88,128,128]{2,1,0:T(8,128)(2,1)S(1)} %turn_tiles.1.turned, bf16[896,128]{1,0:T(8,128)(2,1)S(1)} %collective-permute-done.7.n0, bf16[896,128]{1,0:T(8,128)(2,1)S(1)} %collective-permute-done.8.n1, ...), custom_call_target="tpu_custom_call" | custom-call | flops 18454937600 | bytes 144179200 | tf_op jit(solution)/shard_map/backward_early/pallas_call | solution.py:321
  41.4 1.3 %backward_late.1 = (f32[256,128]{1,0:T(8,128)S(1)}, bf16[256,128]{1,0:T(8,128)(2,1)S(1)}, bf16[256,128]{1,0:T(8,128)(2,1)S(1)}, bf16[256,128]{1,0:T(8,128)(2,1)S(1)}) custom-call(s32[512]{0:T(512)S(1)} %get-tuple-element.23.lists, bf16[88,128,128]{2,1,0:T(8,128)(2,1)S(1)} %turn_tiles.1.turned, f32[1152,128]{1,0:T(8,128)S(1)} %backward_early.1.first, ...), custom_call_target="tpu_custom_call" | custom-call | tf_op jit(solution)/shard_map/backward_late/pallas_call | solution.py:355
  42.7 1.6 %collective-permute-start.15 = (bf16[256,128]{1,0:T(8,128)(2,1)S(1)}, bf16[256,128]{1,0:T(8,128)(2,1)S(1)}, u32[]{:S(2)}, u32[]{:S(2)}) collective-permute-start(bf16[256,128]{1,0:T(8,128)(2,1)S(1)} %get-tuple-element.35), channel_id=1, source_target_pairs={{0,128},{1,129},{2,130},{3,131},{4,132},{5,133},{6,134},{7,135},{8... | collective-permute-start | bytes 196616 | tf_op jit(solution)/shard_map/ppermute | solution.py:465
  44.3 1.9 %collective-permute-start.16 = (bf16[256,128]{1,0:T(8,128)(2,1)S(1)}, bf16[256,128]{1,0:T(8,128)(2,1)S(1)}, u32[]{:S(2)}, u32[]{:S(2)}) collective-permute-start(bf16[256,128]{1,0:T(8,128)(2,1)S(1)} %get-tuple-element.36), channel_id=1, source_target_pairs={{0,64},{1,193},{2,66},{3,195},{4,68},{5,197},{6,70},{7,199},{8,72}... | collective-permute-start | bytes 196616 | tf_op jit(solution)/shard_map/ppermute | solution.py:465
  46.4 2.7 %collective-permute-done.15.g0 = bf16[256,128]{1,0:T(8,128)(2,1)S(1)} collective-permute-done((bf16[256,128]{1,0:T(8,128)(2,1)S(1)}, bf16[256,128]{1,0:T(8,128)(2,1)S(1)}, u32[]{:S(2)}, u32[]{:S(2)}) %collective-permute-start.15) | collective-permute-done | bytes 65568 | tf_op jit(solution)/shard_map/ppermute | solution.py:465
  49.0 2.7 %collective-permute-done.17.g2 = bf16[256,128]{1,0:T(8,128)(2,1)S(1)} collective-permute-done((bf16[256,128]{1,0:T(8,128)(2,1)S(1)}, bf16[256,128]{1,0:T(8,128)(2,1)S(1)}, u32[]{:S(2)}, u32[]{:S(2)}) %collective-permute-start.17) | collective-permute-done | bytes 65568 | tf_op jit(solution)/shard_map/ppermute | solution.py:465
  51.8 3.8 %collective-permute-start.18 = (bf16[128,128]{1,0:T(8,128)(2,1)S(1)}, bf16[128,128]{1,0:T(8,128)(2,1)S(1)}, u32[]{:S(2)}, u32[]{:S(2)}) collective-permute-start(bf16[128,128]{1,0:T(8,128)(2,1)S(1)} %get-tuple-element.41), channel_id=1, source_target_pairs={{0,16},{16,0},{32,48},{48,32},{64,80},{80,64},{96,112},{112,96},{1... | collective-permute-start | bytes 98312 | tf_op jit(solution)/shard_map/ppermute | solution.py:467
  55.6 1.9 %collective-permute-done.18.got = bf16[128,128]{1,0:T(8,128)(2,1)S(1)} collective-permute-done((bf16[128,128]{1,0:T(8,128)(2,1)S(1)}, bf16[128,128]{1,0:T(8,128)(2,1)S(1)}, u32[]{:S(2)}, u32[]{:S(2)}) %collective-permute-start.18) | collective-permute-done | bytes 32800 | tf_op jit(solution)/shard_map/ppermute | solution.py:467
  57.5 6.5 %collective-permute-start.19 = (bf16[64,128]{1,0:T(8,128)(2,1)S(1)}, bf16[64,128]{1,0:T(8,128)(2,1)S(1)}, u32[]{:S(2)}, u32[]{:S(2)}) collective-permute-start(bf16[64,128]{1,0:T(8,128)(2,1)S(1)} %get-tuple-element.43), channel_id=1, source_target_pairs={{0,48},{16,32},{32,16},{48,0},{64,112},{80,96},{96,80},{112,64},{1... | collective-permute-start | bytes 49160 | tf_op jit(solution)/shard_map/ppermute | solution.py:468
  64.0 0.7 sketch_rows.1
  64.6 1.1 %collective-permute-done.19.got = bf16[64,128]{1,0:T(8,128)(2,1)S(1)} collective-permute-done((bf16[64,128]{1,0:T(8,128)(2,1)S(1)}, bf16[64,128]{1,0:T(8,128)(2,1)S(1)}, u32[]{:S(2)}, u32[]{:S(2)}) %collective-permute-start.19) | collective-permute-done | bytes 16416 | tf_op jit(solution)/shard_map/ppermute | solution.py:468
  65.7 0.6 last_sum.1
  (23 shorter events, 2.5 us)
Async XLA Ops:
  4.4 1.9 %collective-permute-start = (bf16[1792,128]{1,0:T(8,128)(2,1)S(1)}, bf16[1792,128]{1,0:T(8,128)(2,1)S(1)}, u32[]{:S(2)}, u32[]{:S(2)}) collective-permute-start(bf16[1792,128]{1,0:T(8,128)(2,1)S(1)} %get-tuple-element.26), channel_id=1, source_target_pairs={{0,1},{1,0},{2,3},{3,2},{4,5},{5,4},{6,7},{7,6},{8,9},{9,8},{10,11... | collective-permute-start | bytes 1376264 | tf_op jit(solution)/shard_map/ppermute | solution.py:436
  6.4 9.3 %collective-permute-start.1 = (bf16[896,128]{1,0:T(8,128)(2,1)S(1)}, bf16[896,128]{1,0:T(8,128)(2,1)S(1)}, u32[]{:S(2)}, u32[]{:S(2)}) collective-permute-start(bf16[896,128]{1,0:T(8,128)(2,1)S(1)} %get-tuple-element.27), channel_id=1, source_target_pairs={{0,2},{1,15},{2,0},{3,13},{4,6},{5,11},{6,4},{7,9},{8,10},{9,7},{1... | collective-permute-start | bytes 688136 | tf_op jit(solution)/shard_map/ppermute | solution.py:440
  8.0 8.5 %collective-permute-start.2 = (bf16[896,128]{1,0:T(8,128)(2,1)S(1)}, bf16[896,128]{1,0:T(8,128)(2,1)S(1)}, u32[]{:S(2)}, u32[]{:S(2)}) collective-permute-start(bf16[896,128]{1,0:T(8,128)(2,1)S(1)} %get-tuple-element.28), channel_id=1, source_target_pairs={{0,6},{1,11},{2,4},{3,9},{4,2},{5,15},{6,0},{7,13},{8,14},{9,3},{1... | collective-permute-start | bytes 688136 | tf_op jit(solution)/shard_map/ppermute | solution.py:440
  11.0 1.9 %collective-permute-start.3 = (bf16[1792,128]{1,0:T(8,128)(2,1)S(1)}, bf16[1792,128]{1,0:T(8,128)(2,1)S(1)}, u32[]{:S(2)}, u32[]{:S(2)}) collective-permute-start(bf16[1792,128]{1,0:T(8,128)(2,1)S(1)} %forward_next3.1), channel_id=1, source_target_pairs={{0,1},{1,0},{2,3},{3,2},{4,5},{5,4},{6,7},{7,6},{8,9},{9,8},{10,11... | collective-permute-start | bytes 1376264 | tf_op jit(solution)/shard_map/ppermute | solution.py:436
  13.0 10.1 %collective-permute-start.4 = (bf16[896,128]{1,0:T(8,128)(2,1)S(1)}, bf16[896,128]{1,0:T(8,128)(2,1)S(1)}, u32[]{:S(2)}, u32[]{:S(2)}) collective-permute-start(bf16[896,128]{1,0:T(8,128)(2,1)S(1)} %get-tuple-element.30), channel_id=1, source_target_pairs={{0,4},{1,13},{2,6},{3,15},{4,0},{5,9},{6,2},{7,11},{8,12},{9,5},{1... | collective-permute-start | bytes 688136 | tf_op jit(solution)/shard_map/ppermute | solution.py:440
  14.7 8.4 %collective-permute-start.5 = (bf16[896,128]{1,0:T(8,128)(2,1)S(1)}, bf16[896,128]{1,0:T(8,128)(2,1)S(1)}, u32[]{:S(2)}, u32[]{:S(2)}) collective-permute-start(bf16[896,128]{1,0:T(8,128)(2,1)S(1)} %get-tuple-element.31), channel_id=1, source_target_pairs={{0,0},{1,9},{2,2},{3,11},{4,4},{5,13},{6,6},{7,15},{8,8},{9,1},{10... | collective-permute-start | bytes 688136 | tf_op jit(solution)/shard_map/ppermute | solution.py:440
  23.2 1.6 %collective-permute-start.6 = (bf16[896,128]{1,0:T(8,128)(2,1)S(1)}, bf16[896,128]{1,0:T(8,128)(2,1)S(1)}, u32[]{:S(2)}, u32[]{:S(2)}) collective-permute-start(bf16[896,128]{1,0:T(8,128)(2,1)S(1)} %part_sum.1.refs_0_), channel_id=1, source_target_pairs={{0,1},{1,0},{2,3},{3,2},{4,5},{5,4},{6,7},{7,6},{8,9},{9,8},{10,11... | collective-permute-start | bytes 688136 | tf_op jit(solution)/shard_map/ppermute | solution.py:436
  24.9 6.1 %collective-permute-start.7 = (bf16[896,128]{1,0:T(8,128)(2,1)S(1)}, bf16[896,128]{1,0:T(8,128)(2,1)S(1)}, u32[]{:S(2)}, u32[]{:S(2)}) collective-permute-start(bf16[896,128]{1,0:T(8,128)(2,1)S(1)} %chunk_sum.1.chunk), channel_id=1, source_target_pairs={{0,2},{1,15},{2,0},{3,13},{4,6},{5,11},{6,4},{7,9},{8,10},{9,7},{1... | collective-permute-start | bytes 688136 | tf_op jit(solution)/shard_map/ppermute | solution.py:440
  26.2 11.8 %collective-permute-start.8 = (bf16[896,128]{1,0:T(8,128)(2,1)S(1)}, bf16[896,128]{1,0:T(8,128)(2,1)S(1)}, u32[]{:S(2)}, u32[]{:S(2)}) collective-permute-start(bf16[896,128]{1,0:T(8,128)(2,1)S(1)} %chunk_sum.1.chunk), channel_id=1, source_target_pairs={{0,6},{1,11},{2,4},{3,9},{4,2},{5,15},{6,0},{7,13},{8,14},{9,3},{1... | collective-permute-start | bytes 688136 | tf_op jit(solution)/shard_map/ppermute | solution.py:440
  27.1 12.5 %collective-permute-start.11 = (bf16[896,128]{1,0:T(8,128)(2,1)S(1)}, bf16[896,128]{1,0:T(8,128)(2,1)S(1)}, u32[]{:S(2)}, u32[]{:S(2)}) collective-permute-start(bf16[896,128]{1,0:T(8,128)(2,1)S(1)} %chunk_sum.1.chunk), channel_id=1, source_target_pairs={{0,4},{1,13},{2,6},{3,15},{4,0},{5,9},{6,2},{7,11},{8,12},{9,5},{1... | collective-permute-start | bytes 688136 | tf_op jit(solution)/shard_map/ppermute | solution.py:440
  29.1 10.6 %collective-permute-start.12 = (bf16[896,128]{1,0:T(8,128)(2,1)S(1)}, bf16[896,128]{1,0:T(8,128)(2,1)S(1)}, u32[]{:S(2)}, u32[]{:S(2)}) collective-permute-start(bf16[896,128]{1,0:T(8,128)(2,1)S(1)} %chunk_sum.1.chunk), channel_id=1, source_target_pairs={{0,0},{1,9},{2,2},{3,11},{4,4},{5,13},{6,6},{7,15},{8,8},{9,1},{10... | collective-permute-start | bytes 688136 | tf_op jit(solution)/shard_map/ppermute | solution.py:440
  31.0 9.2 %collective-permute-start.9 = (bf16[896,128]{1,0:T(8,128)(2,1)S(1)}, bf16[896,128]{1,0:T(8,128)(2,1)S(1)}, u32[]{:S(2)}, u32[]{:S(2)}) collective-permute-start(bf16[896,128]{1,0:T(8,128)(2,1)S(1)} %collective-permute-done.7.n0), channel_id=1, source_target_pairs={{0,1},{1,0},{2,3},{3,2},{4,5},{5,4},{6,7},{7,6},{8,9},{9,8},{10,11... | collective-permute-start | bytes 688136 | tf_op jit(solution)/shard_map/ppermute | solution.py:436
  38.0 2.1 %collective-permute-start.10 = (bf16[896,128]{1,0:T(8,128)(2,1)S(1)}, bf16[896,128]{1,0:T(8,128)(2,1)S(1)}, u32[]{:S(2)}, u32[]{:S(2)}) collective-permute-start(bf16[896,128]{1,0:T(8,128)(2,1)S(1)} %collective-permute-done.8.n1), channel_id=1, source_target_pairs={{0,1},{1,0},{2,3},{3,2},{4,5},{5,4},{6,7},{7,6},{8,9},{9,8},{10,11... | collective-permute-start | bytes 688136 | tf_op jit(solution)/shard_map/ppermute | solution.py:436
  39.6 1.8 %collective-permute-start.13 = (bf16[896,128]{1,0:T(8,128)(2,1)S(1)}, bf16[896,128]{1,0:T(8,128)(2,1)S(1)}, u32[]{:S(2)}, u32[]{:S(2)}) collective-permute-start(bf16[896,128]{1,0:T(8,128)(2,1)S(1)} %collective-permute-done.11.n2), channel_id=1, source_target_pairs={{0,1},{1,0},{2,3},{3,2},{4,5},{5,4},{6,7},{7,6},{8,9},{9,8},{10,11... | collective-permute-start | bytes 688136 | tf_op jit(solution)/shard_map/ppermute | solution.py:436
  39.6 1.8 %collective-permute-start.14 = (bf16[896,128]{1,0:T(8,128)(2,1)S(1)}, bf16[896,128]{1,0:T(8,128)(2,1)S(1)}, u32[]{:S(2)}, u32[]{:S(2)}) collective-permute-start(bf16[896,128]{1,0:T(8,128)(2,1)S(1)} %collective-permute-done.12.n3), channel_id=1, source_target_pairs={{0,1},{1,0},{2,3},{3,2},{4,5},{5,4},{6,7},{7,6},{8,9},{9,8},{10,11... | collective-permute-start | bytes 688136 | tf_op jit(solution)/shard_map/ppermute | solution.py:436
  42.7 6.3 %collective-permute-start.15 = (bf16[256,128]{1,0:T(8,128)(2,1)S(1)}, bf16[256,128]{1,0:T(8,128)(2,1)S(1)}, u32[]{:S(2)}, u32[]{:S(2)}) collective-permute-start(bf16[256,128]{1,0:T(8,128)(2,1)S(1)} %get-tuple-element.35), channel_id=1, source_target_pairs={{0,128},{1,129},{2,130},{3,131},{4,132},{5,133},{6,134},{7,135},{8... | collective-permute-start | bytes 196616 | tf_op jit(solution)/shard_map/ppermute | solution.py:465
  44.3 4.7 %collective-permute-start.16 = (bf16[256,128]{1,0:T(8,128)(2,1)S(1)}, bf16[256,128]{1,0:T(8,128)(2,1)S(1)}, u32[]{:S(2)}, u32[]{:S(2)}) collective-permute-start(bf16[256,128]{1,0:T(8,128)(2,1)S(1)} %get-tuple-element.36), channel_id=1, source_target_pairs={{0,64},{1,193},{2,66},{3,195},{4,68},{5,197},{6,70},{7,199},{8,72}... | collective-permute-start | bytes 196616 | tf_op jit(solution)/shard_map/ppermute | solution.py:465
  46.2 5.5 %collective-permute-start.17 = (bf16[256,128]{1,0:T(8,128)(2,1)S(1)}, bf16[256,128]{1,0:T(8,128)(2,1)S(1)}, u32[]{:S(2)}, u32[]{:S(2)}) collective-permute-start(bf16[256,128]{1,0:T(8,128)(2,1)S(1)} %get-tuple-element.37), channel_id=1, source_target_pairs={{0,192},{1,65},{2,194},{3,67},{4,196},{5,69},{6,198},{7,71},{8,200... | collective-permute-start | bytes 196616 | tf_op jit(solution)/shard_map/ppermute | solution.py:465
  51.8 5.7 %collective-permute-start.18 = (bf16[128,128]{1,0:T(8,128)(2,1)S(1)}, bf16[128,128]{1,0:T(8,128)(2,1)S(1)}, u32[]{:S(2)}, u32[]{:S(2)}) collective-permute-start(bf16[128,128]{1,0:T(8,128)(2,1)S(1)} %get-tuple-element.41), channel_id=1, source_target_pairs={{0,16},{16,0},{32,48},{48,32},{64,80},{80,64},{96,112},{112,96},{1... | collective-permute-start | bytes 98312 | tf_op jit(solution)/shard_map/ppermute | solution.py:467
  57.5 8.2 %collective-permute-start.19 = (bf16[64,128]{1,0:T(8,128)(2,1)S(1)}, bf16[64,128]{1,0:T(8,128)(2,1)S(1)}, u32[]{:S(2)}, u32[]{:S(2)}) collective-permute-start(bf16[64,128]{1,0:T(8,128)(2,1)S(1)} %get-tuple-element.43), channel_id=1, source_target_pairs={{0,48},{16,32},{32,16},{48,0},{64,112},{80,96},{96,80},{112,64},{1... | collective-permute-start | bytes 49160 | tf_op jit(solution)/shard_map/ppermute | solution.py:468

commit v6 on v5

--- a/solution.py
+++ b/solution.py
@@ -26,6 +26,7 @@
     ((2, 0), (2, 1)),
     ((0, 0), (0, 1)),
 )
+RELAYS = (((1, 0), (3, 0)), ((3, 0), (1, 0)))
 NEAR_EARLY, NEAR_LATE, FAR_EARLY, FAR_LATE = range(4)
 LINE = ((2, 2), (1, 3), (3, 1))
 
@@ -52,11 +53,11 @@
     return i // 4, i % 4
 
 
-def round_pairs(p):
+def pairs(moves):
     out = []
     for s in range(16):
         z, x, c = s // 8, (s // 2) % 4, s % 2
-        dx, dz = ROUNDS[p][c]
+        dx, dz = moves[c]
         out.append((s, (z ^ dz) * 8 + (x ^ dx) * 2 + c))
     return out
 
@@ -72,10 +73,6 @@
 
 def block(i):
     return pl.ds(pl.multiple_of(i * TILE, TILE), TILE)
-
-
-def chunk_at(q):
-    return pl.ds(q * CHUNK, CHUNK)
 
 
 def unpack(word):
@@ -163,7 +160,7 @@
     for g in range(fetches):
         pl.when(g * FETCH < used)(fetch(g).wait)
     fetch_omega.wait()
-    forward_slots(lists, FAR_EARLY, held, table, acc, out)
+    forward_slots(lists, FAR_LATE, held, table, acc, out)
 
 
 def in_hbm(value):
@@ -234,22 +231,49 @@
     )(count, tiles)
 
 
-def pair_kernel(a, b, *sends):
-    for q, send in enumerate(sends):
-        at = chunk_at(q)
-        send[...] = (a[at, :].astype(jnp.float32) + b[at, :].astype(jnp.float32)).astype(jnp.bfloat16)
-
-
-def pair_sum(a, b):
+def pair_chunk(a, b, start, rows):
+    at = pl.ds(start, rows)
+    return a[at, :].astype(jnp.float32) + b[at, :].astype(jnp.float32)
+
+
+def pair_late_kernel(a, b, low, high, last):
+    half = CHUNK // 2
+    for q, send in enumerate((low, high)):
+        send[...] = pair_chunk(a, b, q * half, half).astype(jnp.bfloat16)
+    last[...] = pair_chunk(a, b, CHUNK, CHUNK).astype(jnp.bfloat16)
+
+
+def pair_late(a, b):
+    half = jax.ShapeDtypeStruct((CHUNK // 2, TILE), jnp.bfloat16)
+    return pl.pallas_call(
+        pair_late_kernel,
+        out_shape=[half, half, jax.ShapeDtypeStruct((CHUNK, TILE), jnp.bfloat16)],
+        in_specs=[vm(), vm()],
+        out_specs=[vm()] * 3,
+        compiler_params=params(),
+        name="pair_late",
+    )(a, b)
+
+
+def pair_early_kernel(a, b, low, high, s0, s1):
+    half = CHUNK // 2
+    lower, upper = pl.ds(0, half), pl.ds(half, half)
+    s0[lower, :] = pair_chunk(a, b, 0, half).astype(jnp.bfloat16)
+    s0[upper, :] = (pair_chunk(a, b, half, half) + high[...].astype(jnp.float32)).astype(jnp.bfloat16)
+    s1[lower, :] = (pair_chunk(a, b, CHUNK, half) + low[...].astype(jnp.float32)).astype(jnp.bfloat16)
+    s1[upper, :] = pair_chunk(a, b, CHUNK + half, half).astype(jnp.bfloat16)
+
+
+def pair_early(a, b, low, high):
     shape = jax.ShapeDtypeStruct((CHUNK, TILE), jnp.bfloat16)
     return pl.pallas_call(
-        pair_kernel,
+        pair_early_kernel,
         out_shape=[shape] * 2,
-        in_specs=[vm(), vm()],
+        in_specs=[vm()] * 4,
         out_specs=[vm()] * 2,
         compiler_params=params(),
-        name="pair_sum",
-    )(a, b)
+        name="pair_early",
+    )(a, b, low, high)
 
 
 def part_kernel(*refs):
@@ -290,8 +314,10 @@
 
 def backward_part(lists, kinds, turned, near, far, table, acc):
     for kind, pieces in zip(kinds, (near, far)):
-        for q, piece in enumerate(pieces):
-            table[chunk_at(q), :] = piece[...]
+        start = 0
+        for piece in pieces:
+            table[pl.ds(start, piece.shape[0]), :] = piece[...]
+            start += piece.shape[0]
         backward_slots(lists, kind, turned, table, acc)
 
 
@@ -339,9 +365,11 @@
     return pl.ds(pl.multiple_of(lax.rem(i + 4, 4) * size, size), size)
 
 
-def backward_late_kernel(lists, turned, first, n2, n3, f2, f3, keep, s0, s1, s2, acc, table):
+def backward_late_kernel(
+    lists, turned, first, nl, nh, n3, fl, fh, f3, keep, s0, s1, s2, acc, table
+):
     acc[...] = first[...]
-    backward_part(lists, (NEAR_LATE, FAR_LATE), turned, (n2, n3), (f2, f3), table, acc)
+    backward_part(lists, (NEAR_LATE, FAR_LATE), turned, (nl, nh, n3), (fl, fh, f3), table, acc)
     y, _ = kmer_place()
     size = keep.shape[0]
     for r, send in enumerate((s0, s1, s2)):
@@ -355,7 +383,7 @@
     return pl.pallas_call(
         backward_late_kernel,
         out_shape=[jax.ShapeDtypeStruct((share, TILE), jnp.float32), send, send, send],
-        in_specs=[sm()] + [vm()] * 6,
+        in_specs=[sm()] + [vm()] * 8,
         out_specs=[vm()] * 4,
         scratch_shapes=[
             pltpu.VMEM(((SB_DEV + 1) * TILE, TILE), jnp.float32),
@@ -436,8 +464,8 @@
     return lax.ppermute(value, "samp", [(s, s ^ 1) for s in range(16)])
 
 
-def trade(value, p):
-    return lax.ppermute(value, "samp", round_pairs(p))
+def trade(value, moves):
+    return lax.ppermute(value, "samp", pairs(moves))
 
 
 def after(value, *first):
@@ -447,20 +475,25 @@
 def shards(tiles, omega, tile_rows, tile_cols, tile_count):
     kmers = lax.axis_size("kmer")
     other, held, table, lists = forward_first(tile_rows, tile_cols, tile_count, tiles, omega)
-    sends = pair_sum(forward_next(NEAR_EARLY, lists, held, table), swap(other))
-    held_late = after(held, *sends)
-    parts = [trade(s, p) for p, s in enumerate(sends)]
-    other = forward_next(FAR_LATE, lists, held_late, table)
-    sends = pair_sum(forward_next(NEAR_LATE, lists, held_late, table), swap(other))
-    parts += [trade(s, p + 2) for p, s in enumerate(sends)]
+    *halves, send3 = pair_late(forward_next(NEAR_LATE, lists, held, table), swap(other))
+    held_next = after(held, *halves)
+    relayed = [trade(s, m) for s, m in zip(halves, RELAYS)]
+    part3 = trade(send3, ROUNDS[3])
+    other = forward_next(FAR_EARLY, lists, held_next, table)
+    sends = pair_early(forward_next(NEAR_EARLY, lists, held_next, table), swap(other), *relayed)
+    parts = [trade(s, m) for s, m in zip(sends, ROUNDS)]
     turned = turn(tile_count, after(held, *sends))
-    part = part_sum("part_sum", *parts)
+    part = part_sum("part_sum", *parts, part3)
     part, turned = lax.optimization_barrier((part, turned))
     chunk = part_sum("chunk_sum", part, swap(part))
-    near = [trade(chunk, p) for p in range(4)]
+    n0, n1 = trade(chunk, ROUNDS[0]), trade(chunk, ROUNDS[1])
+    n3 = trade(chunk, ROUNDS[3])
+    high = trade(n0[CHUNK // 2 :], RELAYS[1])
+    low = trade(n1[: CHUNK // 2], RELAYS[0])
+    first = backward_early(lists, turned, (n0, n1), (swap(n0), swap(n1)))
+    near = (low, high, n3)
     far = [swap(piece) for piece in near]
-    first = backward_early(lists, turned, near[:2], far[:2])
-    keep, *shares = backward_late(lists, turned, first, near[2:], far[2:])
+    keep, *shares = backward_late(lists, turned, first, near, far)
     sketch = sketch_rows(after(chunk, *shares))
     got = [lax.ppermute(s, ("kmer", "samp"), y_pairs(r)) for r, s in enumerate(shares)]
     keep, share = line_sum(keep, got)

time: 66.5 us -> 68.3 us (1.027)
  starting transfers between devices: 28.2 us -> 30.1 us
    ppermute x8 -> x10, starting transfers between devices: 10.8 us -> 14.4 us  [trade(): return lax.ppermute(value, 'samp', pairs(moves))]
    ppermute x1, starting transfers between devices: 6.49 us -> 5.57 us  [shards(): lax.ppermute(share, 'kmer', [(i, i // 4 * 4 + 3 - i % 4) for i in range(1...]
    ppermute x7 -> x8, waiting for transfers between devices: 2.85 us -> 2.03 us  [swap(): return lax.ppermute(value, 'samp', [(s, s ^ 1) for s in range(16)])]
    ppermute x7 -> x8, starting transfers between devices: 3.4 us -> 3.1 us  [swap(): return lax.ppermute(value, 'samp', [(s, s ^ 1) for s in range(16)])]
    ppermute x8 -> x10, waiting for transfers between devices: 15.1 us -> 15.4 us  [trade(): return lax.ppermute(value, 'samp', pairs(moves))]
  transfers between devices with their start and end apart: 20 -> 23, of which waited for: 12 -> 14; matrix products, arithmetic and copies ran while one was open for 0% -> 0% of each run, Pallas kernels for 8% -> 8%
where the time goes in v6:
time: 68.3 us; the launch traced here: 68.1 us
  starting transfers between devices  30.1 us (44%)
  waiting for transfers between devices  25.7 us (38%)
  Pallas kernels  10.8 us (16%)
  between operations  1.45 us (2%)
    ppermute x10, waiting for transfers between devices, trade(): return lax.ppermute(value, 'samp', pairs(moves))  15.4 us
    ppermute x10, starting transfers between devices, trade(): return lax.ppermute(value, 'samp', pairs(moves))  14.4 us
    ppermute x1, starting transfers between devices, shards(): lax.ppermute(share, 'kmer', [(i, i // 4 * 4 + 3 - i % 4) for i in range(1...  5.57 us
    ppermute x3, waiting for transfers between devices, shards(): lax.ppermute(s, ('kmer', 'samp'), y_pairs(r))  5.35 us
    ppermute x1, starting transfers between devices, shards(): lax.ppermute(share, 'kmer', [(i, i ^ 1) for i in range(16)])  3.64 us
    ppermute x3, starting transfers between devices, shards(): lax.ppermute(s, ('kmer', 'samp'), y_pairs(r))  3.43 us
    ppermute x8, starting transfers between devices, swap(): return lax.ppermute(value, 'samp', [(s, s ^ 1) for s in range(16)])  3.1 us
    pallas_call x1, Pallas kernels, forward_first(): pl.pallas_call(forward_first_kernel, out_shape=[jax.ShapeDtypeStruct((PAR...  3.09 us
  transfers between devices with their start and end apart: 23, of which 14 were waited for; matrix products, arithmetic and copies ran while one was open for 0% of the time, Pallas kernels for 8%

profile of v6, /device:TPU:24, one launch (start us, length us, event | category | flops | bytes accessed | tf_op | source)
XLA Modules:
  0.0 68.1 jit_solution(54470042275851547)
XLA Ops:
  1.3 3.1 %forward_first.1 = (bf16[1792,128]{1,0:T(8,128)(2,1)S(1)}, bf16[88,128,128]{2,1,0:T(8,128)(2,1)S(1)}, bf16[1024,128]{1,0:T(8,128)(2,1)S(1)}, s32[512]{0:T(512)S(1)}) custom-call(s32[88]{0:T(128)} %rows.1, s32[88]{0:T(128)} %cols.1, s32[1]{0:T(128)S(6)} %copy.7.count, bf16[88,128,128]{2,1,0:T(8,128)(2,1)} %tiles.1, bf16[1024,128]{1,0:T(8,128)(2,1)} %omega.1), custom_call_target="tpu_custom_call" | custom-call | tf_op jit(solution)/shard_map/forward_first/pallas_call | solution.py:173
  4.5 1.0 %forward_next1.1.a = bf16[1792,128]{1,0:T(8,128)(2,1)S(1)} custom-call(s32[512]{0:T(512)S(1)} %get-tuple-element.24.lists, bf16[88,128,128]{2,1,0:T(8,128)(2,1)S(1)} %get-tuple-element.34.held.tiles, bf16[1024,128]{1,0:T(8,128)(2,1)S(1)} %get-tuple-element.26.table), custom_call_target="tpu_custom_call" | custom-call | flops 18454937600 | bytes 144179200 | tf_op jit(solution)/shard_map/forward_next1/pallas_call | solution.py:202
  5.4 0.8 %collective-permute-done.b = bf16[1792,128]{1,0:T(8,128)(2,1)S(1)} collective-permute-done((bf16[1792,128]{1,0:T(8,128)(2,1)S(1)}, bf16[1792,128]{1,0:T(8,128)(2,1)S(1)}, u32[]{:S(2)}, u32[]{:S(2)}) %collective-permute-start) | collective-permute-done | bytes 458784 | tf_op jit(solution)/shard_map/ppermute | solution.py:464
  6.4 1.6 %collective-permute-start.2 = (bf16[448,128]{1,0:T(8,128)(2,1)S(1)}, bf16[448,128]{1,0:T(8,128)(2,1)S(1)}, u32[]{:S(2)}, u32[]{:S(2)}) collective-permute-start(bf16[448,128]{1,0:T(8,128)(2,1)S(1)} %get-tuple-element.28), channel_id=1, source_target_pairs={{0,2},{1,7},{2,0},{3,5},{4,6},{5,3},{6,4},{7,1},{8,10},{9,15},{10,... | collective-permute-start | bytes 344072 | tf_op jit(solution)/shard_map/ppermute | solution.py:468
  8.0 2.6 %collective-permute-start.3 = (bf16[448,128]{1,0:T(8,128)(2,1)S(1)}, bf16[448,128]{1,0:T(8,128)(2,1)S(1)}, u32[]{:S(2)}, u32[]{:S(2)}) collective-permute-start(bf16[448,128]{1,0:T(8,128)(2,1)S(1)} %get-tuple-element.29), channel_id=1, source_target_pairs={{0,6},{1,3},{2,4},{3,1},{4,2},{5,7},{6,0},{7,5},{8,14},{9,11},{10,... | collective-permute-start | bytes 344072 | tf_op jit(solution)/shard_map/ppermute | solution.py:468
  10.6 1.0 %forward_next2.1 = bf16[1792,128]{1,0:T(8,128)(2,1)S(1)} custom-call(s32[512]{0:T(512)S(1)} %get-tuple-element.24.lists, bf16[88,128,128]{2,1,0:T(8,128)(2,1)S(1)} %get-tuple-element.34.held.tiles, bf16[1024,128]{1,0:T(8,128)(2,1)S(1)} %get-tuple-element.26.table), custom_call_target="tpu_custom_call" | custom-call | flops 18454937600 | bytes 144179200 | tf_op jit(solution)/shard_map/forward_next2/pallas_call | solution.py:202
  11.7 1.0 %forward_next0.1.a = bf16[1792,128]{1,0:T(8,128)(2,1)S(1)} custom-call(s32[512]{0:T(512)S(1)} %get-tuple-element.24.lists, bf16[88,128,128]{2,1,0:T(8,128)(2,1)S(1)} %get-tuple-element.34.held.tiles, bf16[1024,128]{1,0:T(8,128)(2,1)S(1)} %get-tuple-element.26.table), custom_call_target="tpu_custom_call" | custom-call | flops 18454937600 | bytes 144179200 | tf_op jit(solution)/shard_map/forward_next0/pallas_call | solution.py:202
  12.6 0.7 collective-permute-start.6
  14.2 2.7 %collective-permute-start.5 = (bf16[896,128]{1,0:T(8,128)(2,1)S(1)}, bf16[896,128]{1,0:T(8,128)(2,1)S(1)}, u32[]{:S(2)}, u32[]{:S(2)}) collective-permute-start(bf16[896,128]{1,0:T(8,128)(2,1)S(1)} %get-tuple-element.32), channel_id=1, source_target_pairs={{0,6},{1,11},{2,4},{3,9},{4,2},{5,15},{6,0},{7,13},{8,14},{9,3},{1... | collective-permute-start | bytes 688136 | tf_op jit(solution)/shard_map/ppermute | solution.py:468
  17.4 2.8 %collective-permute-done.4.refs_0_ = bf16[896,128]{1,0:T(8,128)(2,1)S(1)} collective-permute-done((bf16[896,128]{1,0:T(8,128)(2,1)S(1)}, bf16[896,128]{1,0:T(8,128)(2,1)S(1)}, u32[]{:S(2)}, u32[]{:S(2)}) %collective-permute-start.4) | collective-permute-done | bytes 229408 | tf_op jit(solution)/shard_map/ppermute | solution.py:468
  20.2 3.8 %collective-permute-done.5.refs_1_ = bf16[896,128]{1,0:T(8,128)(2,1)S(1)} collective-permute-done((bf16[896,128]{1,0:T(8,128)(2,1)S(1)}, bf16[896,128]{1,0:T(8,128)(2,1)S(1)}, u32[]{:S(2)}, u32[]{:S(2)}) %collective-permute-start.5) | collective-permute-done | bytes 229408 | tf_op jit(solution)/shard_map/ppermute | solution.py:468
  24.7 1.1 %collective-permute-done.7.refs_1_ = bf16[896,128]{1,0:T(8,128)(2,1)S(1)} collective-permute-done((bf16[896,128]{1,0:T(8,128)(2,1)S(1)}, bf16[896,128]{1,0:T(8,128)(2,1)S(1)}, u32[]{:S(2)}, u32[]{:S(2)}) %collective-permute-start.7) | collective-permute-done | bytes 229408 | tf_op jit(solution)/shard_map/ppermute | solution.py:464
  25.9 1.9 %collective-permute-start.8 = (bf16[896,128]{1,0:T(8,128)(2,1)S(1)}, bf16[896,128]{1,0:T(8,128)(2,1)S(1)}, u32[]{:S(2)}, u32[]{:S(2)}) collective-permute-start(bf16[896,128]{1,0:T(8,128)(2,1)S(1)} %chunk_sum.1.chunk), channel_id=1, source_target_pairs={{0,2},{1,15},{2,0},{3,13},{4,6},{5,11},{6,4},{7,9},{8,10},{9,7},{1... | collective-permute-start | bytes 688136 | tf_op jit(solution)/shard_map/ppermute | solution.py:468
  27.8 1.6 %collective-permute-start.9 = (bf16[896,128]{1,0:T(8,128)(2,1)S(1)}, bf16[896,128]{1,0:T(8,128)(2,1)S(1)}, u32[]{:S(2)}, u32[]{:S(2)}) collective-permute-start(bf16[896,128]{1,0:T(8,128)(2,1)S(1)} %chunk_sum.1.chunk), channel_id=1, source_target_pairs={{0,6},{1,11},{2,4},{3,9},{4,2},{5,15},{6,0},{7,13},{8,14},{9,3},{1... | collective-permute-start | bytes 688136 | tf_op jit(solution)/shard_map/ppermute | solution.py:468
  29.4 0.7 collective-permute-start.14
  30.0 1.9 %collective-permute-done.8.n0 = bf16[896,128]{1,0:T(8,128)(2,1)S(1)} collective-permute-done((bf16[896,128]{1,0:T(8,128)(2,1)S(1)}, bf16[896,128]{1,0:T(8,128)(2,1)S(1)}, u32[]{:S(2)}, u32[]{:S(2)}) %collective-permute-start.8) | collective-permute-done | bytes 229408 | tf_op jit(solution)/shard_map/ppermute | solution.py:468
  32.0 1.4 %collective-permute-start.10 = (bf16[896,128]{1,0:T(8,128)(2,1)S(1)}, bf16[896,128]{1,0:T(8,128)(2,1)S(1)}, u32[]{:S(2)}, u32[]{:S(2)}) collective-permute-start(bf16[896,128]{1,0:T(8,128)(2,1)S(1)} %collective-permute-done.8.n0), channel_id=1, source_target_pairs={{0,1},{1,0},{2,3},{3,2},{4,5},{5,4},{6,7},{7,6},{8,9},{9,8},{10,11... | collective-permute-start | bytes 688136 | tf_op jit(solution)/shard_map/ppermute | solution.py:464
  33.4 2.5 %collective-permute-done.9.n1 = bf16[896,128]{1,0:T(8,128)(2,1)S(1)} collective-permute-done((bf16[896,128]{1,0:T(8,128)(2,1)S(1)}, bf16[896,128]{1,0:T(8,128)(2,1)S(1)}, u32[]{:S(2)}, u32[]{:S(2)}) %collective-permute-start.9) | collective-permute-done | bytes 229408 | tf_op jit(solution)/shard_map/ppermute | solution.py:468
  36.0 0.9 %collective-permute-start.12 = (bf16[448,128]{1,0:T(8,128)(2,1)S(1)}, bf16[448,128]{1,0:T(8,128)(2,1)S(1)}, u32[]{:S(2)}, u32[]{:S(2)}) collective-permute-start(bf16[448,128]{1,0:T(8,128)(2,1)S(1)} %slice.8), channel_id=1, source_target_pairs={{0,2},{1,7},{2,0},{3,5},{4,6},{5,3},{6,4},{7,1},{8,10},{9,15},{10,... | collective-permute-start | bytes 344072 | tf_op jit(solution)/shard_map/ppermute | solution.py:468
  36.9 1.5 %collective-permute-start.13 = (bf16[448,128]{1,0:T(8,128)(2,1)S(1)}, bf16[448,128]{1,0:T(8,128)(2,1)S(1)}, u32[]{:S(2)}, u32[]{:S(2)}) collective-permute-start(bf16[448,128]{1,0:T(8,128)(2,1)S(1)} %slice.9), channel_id=1, source_target_pairs={{0,6},{1,3},{2,4},{3,1},{4,2},{5,7},{6,0},{7,5},{8,14},{9,11},{10,... | collective-permute-start | bytes 344072 | tf_op jit(solution)/shard_map/ppermute | solution.py:468
  38.7 2.1 %collective-permute-done.12.nl = bf16[448,128]{1,0:T(8,128)(2,1)S(1)} collective-permute-done((bf16[448,128]{1,0:T(8,128)(2,1)S(1)}, bf16[448,128]{1,0:T(8,128)(2,1)S(1)}, u32[]{:S(2)}, u32[]{:S(2)}) %collective-permute-start.12) | collective-permute-done | bytes 114720 | tf_op jit(solution)/shard_map/ppermute | solution.py:468
  41.4 1.6 %collective-permute-done.13.nh = bf16[448,128]{1,0:T(8,128)(2,1)S(1)} collective-permute-done((bf16[448,128]{1,0:T(8,128)(2,1)S(1)}, bf16[448,128]{1,0:T(8,128)(2,1)S(1)}, u32[]{:S(2)}, u32[]{:S(2)}) %collective-permute-start.13) | collective-permute-done | bytes 114720 | tf_op jit(solution)/shard_map/ppermute | solution.py:468
  43.0 1.2 %backward_early.1.first = f32[1152,128]{1,0:T(8,128)S(1)} custom-call(s32[512]{0:T(512)S(1)} %get-tuple-element.24.lists, bf16[88,128,128]{2,1,0:T(8,128)(2,1)S(1)} %turn_tiles.1.turned, bf16[896,128]{1,0:T(8,128)(2,1)S(1)} %collective-permute-done.8.n0, bf16[896,128]{1,0:T(8,128)(2,1)S(1)} %collective-permute-done.9.n1, ...), custom_call_target="tpu_custom_call" | custom-call | flops 18454937600 | bytes 144179200 | tf_op jit(solution)/shard_map/backward_early/pallas_call | solution.py:347
  44.3 1.5 %backward_late.1 = (f32[256,128]{1,0:T(8,128)S(1)}, bf16[256,128]{1,0:T(8,128)(2,1)S(1)}, bf16[256,128]{1,0:T(8,128)(2,1)S(1)}, bf16[256,128]{1,0:T(8,128)(2,1)S(1)}) custom-call(s32[512]{0:T(512)S(1)} %get-tuple-element.24.lists, bf16[88,128,128]{2,1,0:T(8,128)(2,1)S(1)} %turn_tiles.1.turned, f32[1152,128]{1,0:T(8,128)S(1)} %backward_early.1.first, ...), custom_call_target="tpu_custom_call" | custom-call | tf_op jit(solution)/shard_map/backward_late/pallas_call | solution.py:383
  45.8 1.4 %collective-permute-start.18 = (bf16[256,128]{1,0:T(8,128)(2,1)S(1)}, bf16[256,128]{1,0:T(8,128)(2,1)S(1)}, u32[]{:S(2)}, u32[]{:S(2)}) collective-permute-start(bf16[256,128]{1,0:T(8,128)(2,1)S(1)} %get-tuple-element.37), channel_id=1, source_target_pairs={{0,128},{1,129},{2,130},{3,131},{4,132},{5,133},{6,134},{7,135},{8... | collective-permute-start | bytes 196616 | tf_op jit(solution)/shard_map/ppermute | solution.py:498
  47.2 1.9 %collective-permute-start.19 = (bf16[256,128]{1,0:T(8,128)(2,1)S(1)}, bf16[256,128]{1,0:T(8,128)(2,1)S(1)}, u32[]{:S(2)}, u32[]{:S(2)}) collective-permute-start(bf16[256,128]{1,0:T(8,128)(2,1)S(1)} %get-tuple-element.38), channel_id=1, source_target_pairs={{0,64},{1,193},{2,66},{3,195},{4,68},{5,197},{6,70},{7,199},{8,72}... | collective-permute-start | bytes 196616 | tf_op jit(solution)/shard_map/ppermute | solution.py:498
  49.2 3.0 %collective-permute-done.18.g0 = bf16[256,128]{1,0:T(8,128)(2,1)S(1)} collective-permute-done((bf16[256,128]{1,0:T(8,128)(2,1)S(1)}, bf16[256,128]{1,0:T(8,128)(2,1)S(1)}, u32[]{:S(2)}, u32[]{:S(2)}) %collective-permute-start.18) | collective-permute-done | bytes 65568 | tf_op jit(solution)/shard_map/ppermute | solution.py:498
  52.3 2.3 %collective-permute-done.20.g2 = bf16[256,128]{1,0:T(8,128)(2,1)S(1)} collective-permute-done((bf16[256,128]{1,0:T(8,128)(2,1)S(1)}, bf16[256,128]{1,0:T(8,128)(2,1)S(1)}, u32[]{:S(2)}, u32[]{:S(2)}) %collective-permute-start.20) | collective-permute-done | bytes 65568 | tf_op jit(solution)/shard_map/ppermute | solution.py:498
  54.6 3.6 %collective-permute-start.21 = (bf16[128,128]{1,0:T(8,128)(2,1)S(1)}, bf16[128,128]{1,0:T(8,128)(2,1)S(1)}, u32[]{:S(2)}, u32[]{:S(2)}) collective-permute-start(bf16[128,128]{1,0:T(8,128)(2,1)S(1)} %get-tuple-element.43), channel_id=1, source_target_pairs={{0,16},{16,0},{32,48},{48,32},{64,80},{80,64},{96,112},{112,96},{1... | collective-permute-start | bytes 98312 | tf_op jit(solution)/shard_map/ppermute | solution.py:500
  58.3 1.9 %collective-permute-done.21.got = bf16[128,128]{1,0:T(8,128)(2,1)S(1)} collective-permute-done((bf16[128,128]{1,0:T(8,128)(2,1)S(1)}, bf16[128,128]{1,0:T(8,128)(2,1)S(1)}, u32[]{:S(2)}, u32[]{:S(2)}) %collective-permute-start.21) | collective-permute-done | bytes 32800 | tf_op jit(solution)/shard_map/ppermute | solution.py:500
  60.2 5.6 %collective-permute-start.22 = (bf16[64,128]{1,0:T(8,128)(2,1)S(1)}, bf16[64,128]{1,0:T(8,128)(2,1)S(1)}, u32[]{:S(2)}, u32[]{:S(2)}) collective-permute-start(bf16[64,128]{1,0:T(8,128)(2,1)S(1)} %get-tuple-element.45), channel_id=1, source_target_pairs={{0,48},{16,32},{32,16},{48,0},{64,112},{80,96},{96,80},{112,64},{1... | collective-permute-start | bytes 49160 | tf_op jit(solution)/shard_map/ppermute | solution.py:501
  66.4 1.1 %collective-permute-done.22.got = bf16[64,128]{1,0:T(8,128)(2,1)S(1)} collective-permute-done((bf16[64,128]{1,0:T(8,128)(2,1)S(1)}, bf16[64,128]{1,0:T(8,128)(2,1)S(1)}, u32[]{:S(2)}, u32[]{:S(2)}) %collective-permute-start.22) | collective-permute-done | bytes 16416 | tf_op jit(solution)/shard_map/ppermute | solution.py:501
  (31 shorter events, 4.8 us)
Async XLA Ops:
  4.4 1.9 %collective-permute-start = (bf16[1792,128]{1,0:T(8,128)(2,1)S(1)}, bf16[1792,128]{1,0:T(8,128)(2,1)S(1)}, u32[]{:S(2)}, u32[]{:S(2)}) collective-permute-start(bf16[1792,128]{1,0:T(8,128)(2,1)S(1)} %get-tuple-element.27), channel_id=1, source_target_pairs={{0,1},{1,0},{2,3},{3,2},{4,5},{5,4},{6,7},{7,6},{8,9},{9,8},{10,11... | collective-permute-start | bytes 1376264 | tf_op jit(solution)/shard_map/ppermute | solution.py:464
  6.4 6.9 %collective-permute-start.2 = (bf16[448,128]{1,0:T(8,128)(2,1)S(1)}, bf16[448,128]{1,0:T(8,128)(2,1)S(1)}, u32[]{:S(2)}, u32[]{:S(2)}) collective-permute-start(bf16[448,128]{1,0:T(8,128)(2,1)S(1)} %get-tuple-element.28), channel_id=1, source_target_pairs={{0,2},{1,7},{2,0},{3,5},{4,6},{5,3},{6,4},{7,1},{8,10},{9,15},{10,... | collective-permute-start | bytes 344072 | tf_op jit(solution)/shard_map/ppermute | solution.py:468
  8.0 6.0 %collective-permute-start.3 = (bf16[448,128]{1,0:T(8,128)(2,1)S(1)}, bf16[448,128]{1,0:T(8,128)(2,1)S(1)}, u32[]{:S(2)}, u32[]{:S(2)}) collective-permute-start(bf16[448,128]{1,0:T(8,128)(2,1)S(1)} %get-tuple-element.29), channel_id=1, source_target_pairs={{0,6},{1,3},{2,4},{3,1},{4,2},{5,7},{6,0},{7,5},{8,14},{9,11},{10,... | collective-permute-start | bytes 344072 | tf_op jit(solution)/shard_map/ppermute | solution.py:468
  11.6 2.4 %collective-permute-start.1 = (bf16[1792,128]{1,0:T(8,128)(2,1)S(1)}, bf16[1792,128]{1,0:T(8,128)(2,1)S(1)}, u32[]{:S(2)}, u32[]{:S(2)}) collective-permute-start(bf16[1792,128]{1,0:T(8,128)(2,1)S(1)} %forward_next2.1), channel_id=1, source_target_pairs={{0,1},{1,0},{2,3},{3,2},{4,5},{5,4},{6,7},{7,6},{8,9},{9,8},{10,11... | collective-permute-start | bytes 1376264 | tf_op jit(solution)/shard_map/ppermute | solution.py:464
  12.6 4.7 %collective-permute-start.6 = (bf16[896,128]{1,0:T(8,128)(2,1)S(1)}, bf16[896,128]{1,0:T(8,128)(2,1)S(1)}, u32[]{:S(2)}, u32[]{:S(2)}) collective-permute-start(bf16[896,128]{1,0:T(8,128)(2,1)S(1)} %get-tuple-element.33), channel_id=1, source_target_pairs={{0,0},{1,9},{2,2},{3,11},{4,4},{5,13},{6,6},{7,15},{8,8},{9,1},{10... | collective-permute-start | bytes 688136 | tf_op jit(solution)/shard_map/ppermute | solution.py:468
  14.1 6.1 %collective-permute-start.4 = (bf16[896,128]{1,0:T(8,128)(2,1)S(1)}, bf16[896,128]{1,0:T(8,128)(2,1)S(1)}, u32[]{:S(2)}, u32[]{:S(2)}) collective-permute-start(bf16[896,128]{1,0:T(8,128)(2,1)S(1)} %get-tuple-element.31), channel_id=1, source_target_pairs={{0,2},{1,15},{2,0},{3,13},{4,6},{5,11},{6,4},{7,9},{8,10},{9,7},{1... | collective-permute-start | bytes 688136 | tf_op jit(solution)/shard_map/ppermute | solution.py:468
  14.2 9.8 %collective-permute-start.5 = (bf16[896,128]{1,0:T(8,128)(2,1)S(1)}, bf16[896,128]{1,0:T(8,128)(2,1)S(1)}, u32[]{:S(2)}, u32[]{:S(2)}) collective-permute-start(bf16[896,128]{1,0:T(8,128)(2,1)S(1)} %get-tuple-element.32), channel_id=1, source_target_pairs={{0,6},{1,11},{2,4},{3,9},{4,2},{5,15},{6,0},{7,13},{8,14},{9,3},{1... | collective-permute-start | bytes 688136 | tf_op jit(solution)/shard_map/ppermute | solution.py:468
  24.1 1.7 %collective-permute-start.7 = (bf16[896,128]{1,0:T(8,128)(2,1)S(1)}, bf16[896,128]{1,0:T(8,128)(2,1)S(1)}, u32[]{:S(2)}, u32[]{:S(2)}) collective-permute-start(bf16[896,128]{1,0:T(8,128)(2,1)S(1)} %part_sum.1.refs_0_), channel_id=1, source_target_pairs={{0,1},{1,0},{2,3},{3,2},{4,5},{5,4},{6,7},{7,6},{8,9},{9,8},{10,11... | collective-permute-start | bytes 688136 | tf_op jit(solution)/shard_map/ppermute | solution.py:464
  25.9 6.1 %collective-permute-start.8 = (bf16[896,128]{1,0:T(8,128)(2,1)S(1)}, bf16[896,128]{1,0:T(8,128)(2,1)S(1)}, u32[]{:S(2)}, u32[]{:S(2)}) collective-permute-start(bf16[896,128]{1,0:T(8,128)(2,1)S(1)} %chunk_sum.1.chunk), channel_id=1, source_target_pairs={{0,2},{1,15},{2,0},{3,13},{4,6},{5,11},{6,4},{7,9},{8,10},{9,7},{1... | collective-permute-start | bytes 688136 | tf_op jit(solution)/shard_map/ppermute | solution.py:468
  27.8 8.2 %collective-permute-start.9 = (bf16[896,128]{1,0:T(8,128)(2,1)S(1)}, bf16[896,128]{1,0:T(8,128)(2,1)S(1)}, u32[]{:S(2)}, u32[]{:S(2)}) collective-permute-start(bf16[896,128]{1,0:T(8,128)(2,1)S(1)} %chunk_sum.1.chunk), channel_id=1, source_target_pairs={{0,6},{1,11},{2,4},{3,9},{4,2},{5,15},{6,0},{7,13},{8,14},{9,3},{1... | collective-permute-start | bytes 688136 | tf_op jit(solution)/shard_map/ppermute | solution.py:468
  29.4 9.1 %collective-permute-start.14 = (bf16[896,128]{1,0:T(8,128)(2,1)S(1)}, bf16[896,128]{1,0:T(8,128)(2,1)S(1)}, u32[]{:S(2)}, u32[]{:S(2)}) collective-permute-start(bf16[896,128]{1,0:T(8,128)(2,1)S(1)} %chunk_sum.1.chunk), channel_id=1, source_target_pairs={{0,0},{1,9},{2,2},{3,11},{4,4},{5,13},{6,6},{7,15},{8,8},{9,1},{10... | collective-permute-start | bytes 688136 | tf_op jit(solution)/shard_map/ppermute | solution.py:468
  32.0 11.0 %collective-permute-start.10 = (bf16[896,128]{1,0:T(8,128)(2,1)S(1)}, bf16[896,128]{1,0:T(8,128)(2,1)S(1)}, u32[]{:S(2)}, u32[]{:S(2)}) collective-permute-start(bf16[896,128]{1,0:T(8,128)(2,1)S(1)} %collective-permute-done.8.n0), channel_id=1, source_target_pairs={{0,1},{1,0},{2,3},{3,2},{4,5},{5,4},{6,7},{7,6},{8,9},{9,8},{10,11... | collective-permute-start | bytes 688136 | tf_op jit(solution)/shard_map/ppermute | solution.py:464
  35.9 7.1 %collective-permute-start.11 = (bf16[896,128]{1,0:T(8,128)(2,1)S(1)}, bf16[896,128]{1,0:T(8,128)(2,1)S(1)}, u32[]{:S(2)}, u32[]{:S(2)}) collective-permute-start(bf16[896,128]{1,0:T(8,128)(2,1)S(1)} %collective-permute-done.9.n1), channel_id=1, source_target_pairs={{0,1},{1,0},{2,3},{3,2},{4,5},{5,4},{6,7},{7,6},{8,9},{9,8},{10,11... | collective-permute-start | bytes 688136 | tf_op jit(solution)/shard_map/ppermute | solution.py:464
  36.0 4.9 %collective-permute-start.12 = (bf16[448,128]{1,0:T(8,128)(2,1)S(1)}, bf16[448,128]{1,0:T(8,128)(2,1)S(1)}, u32[]{:S(2)}, u32[]{:S(2)}) collective-permute-start(bf16[448,128]{1,0:T(8,128)(2,1)S(1)} %slice.8), channel_id=1, source_target_pairs={{0,2},{1,7},{2,0},{3,5},{4,6},{5,3},{6,4},{7,1},{8,10},{9,15},{10,... | collective-permute-start | bytes 344072 | tf_op jit(solution)/shard_map/ppermute | solution.py:468
  36.9 6.1 %collective-permute-start.13 = (bf16[448,128]{1,0:T(8,128)(2,1)S(1)}, bf16[448,128]{1,0:T(8,128)(2,1)S(1)}, u32[]{:S(2)}, u32[]{:S(2)}) collective-permute-start(bf16[448,128]{1,0:T(8,128)(2,1)S(1)} %slice.9), channel_id=1, source_target_pairs={{0,6},{1,3},{2,4},{3,1},{4,2},{5,7},{6,0},{7,5},{8,14},{9,11},{10,... | collective-permute-start | bytes 344072 | tf_op jit(solution)/shard_map/ppermute | solution.py:468
  38.4 5.9 %collective-permute-start.17 = (bf16[896,128]{1,0:T(8,128)(2,1)S(1)}, bf16[896,128]{1,0:T(8,128)(2,1)S(1)}, u32[]{:S(2)}, u32[]{:S(2)}) collective-permute-start(bf16[896,128]{1,0:T(8,128)(2,1)S(1)} %collective-permute-done.14.n3), channel_id=1, source_target_pairs={{0,1},{1,0},{2,3},{3,2},{4,5},{5,4},{6,7},{7,6},{8,9},{9,8},{10,11... | collective-permute-start | bytes 688136 | tf_op jit(solution)/shard_map/ppermute | solution.py:464
  40.8 3.4 %collective-permute-start.15 = (bf16[448,128]{1,0:T(8,128)(2,1)S(1)}, bf16[448,128]{1,0:T(8,128)(2,1)S(1)}, u32[]{:S(2)}, u32[]{:S(2)}) collective-permute-start(bf16[448,128]{1,0:T(8,128)(2,1)S(1)} %collective-permute-done.12.nl), channel_id=1, source_target_pairs={{0,1},{1,0},{2,3},{3,2},{4,5},{5,4},{6,7},{7,6},{8,9},{9,8},{10,11... | collective-permute-start | bytes 344072 | tf_op jit(solution)/shard_map/ppermute | solution.py:464
  43.0 1.3 %collective-permute-start.16 = (bf16[448,128]{1,0:T(8,128)(2,1)S(1)}, bf16[448,128]{1,0:T(8,128)(2,1)S(1)}, u32[]{:S(2)}, u32[]{:S(2)}) collective-permute-start(bf16[448,128]{1,0:T(8,128)(2,1)S(1)} %collective-permute-done.13.nh), channel_id=1, source_target_pairs={{0,1},{1,0},{2,3},{3,2},{4,5},{5,4},{6,7},{7,6},{8,9},{9,8},{10,11... | collective-permute-start | bytes 344072 | tf_op jit(solution)/shard_map/ppermute | solution.py:464
  45.8 6.5 %collective-permute-start.18 = (bf16[256,128]{1,0:T(8,128)(2,1)S(1)}, bf16[256,128]{1,0:T(8,128)(2,1)S(1)}, u32[]{:S(2)}, u32[]{:S(2)}) collective-permute-start(bf16[256,128]{1,0:T(8,128)(2,1)S(1)} %get-tuple-element.37), channel_id=1, source_target_pairs={{0,128},{1,129},{2,130},{3,131},{4,132},{5,133},{6,134},{7,135},{8... | collective-permute-start | bytes 196616 | tf_op jit(solution)/shard_map/ppermute | solution.py:498
  47.2 5.1 %collective-permute-start.19 = (bf16[256,128]{1,0:T(8,128)(2,1)S(1)}, bf16[256,128]{1,0:T(8,128)(2,1)S(1)}, u32[]{:S(2)}, u32[]{:S(2)}) collective-permute-start(bf16[256,128]{1,0:T(8,128)(2,1)S(1)} %get-tuple-element.38), channel_id=1, source_target_pairs={{0,64},{1,193},{2,66},{3,195},{4,68},{5,197},{6,70},{7,199},{8,72}... | collective-permute-start | bytes 196616 | tf_op jit(solution)/shard_map/ppermute | solution.py:498
  49.1 5.5 %collective-permute-start.20 = (bf16[256,128]{1,0:T(8,128)(2,1)S(1)}, bf16[256,128]{1,0:T(8,128)(2,1)S(1)}, u32[]{:S(2)}, u32[]{:S(2)}) collective-permute-start(bf16[256,128]{1,0:T(8,128)(2,1)S(1)} %get-tuple-element.39), channel_id=1, source_target_pairs={{0,192},{1,65},{2,194},{3,67},{4,196},{5,69},{6,198},{7,71},{8,200... | collective-permute-start | bytes 196616 | tf_op jit(solution)/shard_map/ppermute | solution.py:498
  54.6 5.5 %collective-permute-start.21 = (bf16[128,128]{1,0:T(8,128)(2,1)S(1)}, bf16[128,128]{1,0:T(8,128)(2,1)S(1)}, u32[]{:S(2)}, u32[]{:S(2)}) collective-permute-start(bf16[128,128]{1,0:T(8,128)(2,1)S(1)} %get-tuple-element.43), channel_id=1, source_target_pairs={{0,16},{16,0},{32,48},{48,32},{64,80},{80,64},{96,112},{112,96},{1... | collective-permute-start | bytes 98312 | tf_op jit(solution)/shard_map/ppermute | solution.py:500
  60.2 7.3 %collective-permute-start.22 = (bf16[64,128]{1,0:T(8,128)(2,1)S(1)}, bf16[64,128]{1,0:T(8,128)(2,1)S(1)}, u32[]{:S(2)}, u32[]{:S(2)}) collective-permute-start(bf16[64,128]{1,0:T(8,128)(2,1)S(1)} %get-tuple-element.45), channel_id=1, source_target_pairs={{0,48},{16,32},{32,16},{48,0},{64,112},{80,96},{96,80},{112,64},{1... | collective-permute-start | bytes 49160 | tf_op jit(solution)/shard_map/ppermute | solution.py:501

commit v7 on v5

--- a/solution.py
+++ b/solution.py
@@ -163,7 +163,7 @@
     for g in range(fetches):
         pl.when(g * FETCH < used)(fetch(g).wait)
     fetch_omega.wait()
-    forward_slots(lists, FAR_EARLY, held, table, acc, out)
+    forward_slots(lists, FAR_LATE, held, table, acc, out)
 
 
 def in_hbm(value):
@@ -447,12 +447,12 @@
 def shards(tiles, omega, tile_rows, tile_cols, tile_count):
     kmers = lax.axis_size("kmer")
     other, held, table, lists = forward_first(tile_rows, tile_cols, tile_count, tiles, omega)
-    sends = pair_sum(forward_next(NEAR_EARLY, lists, held, table), swap(other))
-    held_late = after(held, *sends)
-    parts = [trade(s, p) for p, s in enumerate(sends)]
-    other = forward_next(FAR_LATE, lists, held_late, table)
-    sends = pair_sum(forward_next(NEAR_LATE, lists, held_late, table), swap(other))
-    parts += [trade(s, p + 2) for p, s in enumerate(sends)]
+    sends = pair_sum(forward_next(NEAR_LATE, lists, held, table), swap(other))
+    held_next = after(held, *sends)
+    parts = [trade(s, p + 2) for p, s in enumerate(sends)]
+    other = forward_next(FAR_EARLY, lists, held_next, table)
+    sends = pair_sum(forward_next(NEAR_EARLY, lists, held_next, table), swap(other))
+    parts += [trade(s, p) for p, s in enumerate(sends)]
     turned = turn(tile_count, after(held, *sends))
     part = part_sum("part_sum", *parts)
     part, turned = lax.optimization_barrier((part, turned))

time: 66.5 us -> 69.3 us (1.042); the launches traced: 66.3 us -> 68.3 us
  waiting for transfers between devices: 26.3 us -> 27.5 us
  starting transfers between devices: 28.2 us -> 28.9 us
    ppermute x7, starting transfers between devices: 3.4 us -> 5.65 us  [swap(): return lax.ppermute(value, 'samp', [(s, s ^ 1) for s in range(16)])]
    ppermute x1, starting transfers between devices: 6.49 us -> 5.57 us  [shards(): lax.ppermute(share, 'kmer', [(i, i // 4 * 4 + 3 - i % 4) for i in range(1...]
    ppermute x7, waiting for transfers between devices: 2.85 us -> 3.68 us  [swap(): return lax.ppermute(value, 'samp', [(s, s ^ 1) for s in range(16)])]
  transfers between devices with their start and end apart: 20 -> 20, of which waited for: 12 -> 13; matrix products, arithmetic and copies ran while one was open for 0% -> 0% of each run, Pallas kernels for 8% -> 8%
where the time goes in v7:
time: 69.3 us; the launch traced here: 68.3 us
  starting transfers between devices  28.9 us (42%)
  waiting for transfers between devices  27.5 us (40%)
  Pallas kernels  10.5 us (15%)
  between operations  1.44 us (2%)
    ppermute x8, waiting for transfers between devices, trade(): return lax.ppermute(value, 'samp', round_pairs(p))  15.4 us
    ppermute x8, starting transfers between devices, trade(): return lax.ppermute(value, 'samp', round_pairs(p))  10.5 us
    ppermute x7, starting transfers between devices, swap(): return lax.ppermute(value, 'samp', [(s, s ^ 1) for s in range(16)])  5.65 us
    ppermute x1, starting transfers between devices, shards(): lax.ppermute(share, 'kmer', [(i, i // 4 * 4 + 3 - i % 4) for i in range(1...  5.57 us
    ppermute x3, waiting for transfers between devices, shards(): lax.ppermute(s, ('kmer', 'samp'), y_pairs(r))  5.47 us
    ppermute x7, waiting for transfers between devices, swap(): return lax.ppermute(value, 'samp', [(s, s ^ 1) for s in range(16)])  3.68 us
    ppermute x1, starting transfers between devices, shards(): lax.ppermute(share, 'kmer', [(i, i ^ 1) for i in range(16)])  3.64 us
    ppermute x3, starting transfers between devices, shards(): lax.ppermute(s, ('kmer', 'samp'), y_pairs(r))  3.51 us
  transfers between devices with their start and end apart: 20, of which 13 were waited for; matrix products, arithmetic and copies ran while one was open for 0% of the time, Pallas kernels for 8%

profile of v7, /device:TPU:24, one launch (start us, length us, event | category | flops | bytes accessed | tf_op | source)
XLA Modules:
  0.0 68.3 jit_solution(9613383643862494909)
XLA Ops:
  1.3 3.1 %forward_first.1 = (bf16[1792,128]{1,0:T(8,128)(2,1)S(1)}, bf16[88,128,128]{2,1,0:T(8,128)(2,1)S(1)}, bf16[1024,128]{1,0:T(8,128)(2,1)S(1)}, s32[512]{0:T(512)S(1)}) custom-call(s32[88]{0:T(128)} %rows.1, s32[88]{0:T(128)} %cols.1, s32[1]{0:T(128)S(6)} %copy.7.count, bf16[88,128,128]{2,1,0:T(8,128)(2,1)} %tiles.1, bf16[1024,128]{1,0:T(8,128)(2,1)} %omega.1), custom_call_target="tpu_custom_call" | custom-call | tf_op jit(solution)/shard_map/forward_first/pallas_call | solution.py:176
  4.5 1.0 %forward_next1.1.a = bf16[1792,128]{1,0:T(8,128)(2,1)S(1)} custom-call(s32[512]{0:T(512)S(1)} %get-tuple-element.23.lists, bf16[88,128,128]{2,1,0:T(8,128)(2,1)S(1)} %get-tuple-element.32.held.tiles, bf16[1024,128]{1,0:T(8,128)(2,1)S(1)} %get-tuple-element.25.table), custom_call_target="tpu_custom_call" | custom-call | flops 18454937600 | bytes 144179200 | tf_op jit(solution)/shard_map/forward_next1/pallas_call | solution.py:205
  5.4 0.8 %collective-permute-done.b = bf16[1792,128]{1,0:T(8,128)(2,1)S(1)} collective-permute-done((bf16[1792,128]{1,0:T(8,128)(2,1)S(1)}, bf16[1792,128]{1,0:T(8,128)(2,1)S(1)}, u32[]{:S(2)}, u32[]{:S(2)}) %collective-permute-start) | collective-permute-done | bytes 458784 | tf_op jit(solution)/shard_map/ppermute | solution.py:436
  6.4 3.1 %collective-permute-start.1 = (bf16[896,128]{1,0:T(8,128)(2,1)S(1)}, bf16[896,128]{1,0:T(8,128)(2,1)S(1)}, u32[]{:S(2)}, u32[]{:S(2)}) collective-permute-start(bf16[896,128]{1,0:T(8,128)(2,1)S(1)} %get-tuple-element.27), channel_id=1, source_target_pairs={{0,4},{1,13},{2,6},{3,15},{4,0},{5,9},{6,2},{7,11},{8,12},{9,5},{1... | collective-permute-start | bytes 688136 | tf_op jit(solution)/shard_map/ppermute | solution.py:440
  9.5 0.7 collective-permute-start.2
  10.2 1.0 %forward_next2.1 = bf16[1792,128]{1,0:T(8,128)(2,1)S(1)} custom-call(s32[512]{0:T(512)S(1)} %get-tuple-element.23.lists, bf16[88,128,128]{2,1,0:T(8,128)(2,1)S(1)} %get-tuple-element.32.held.tiles, bf16[1024,128]{1,0:T(8,128)(2,1)S(1)} %get-tuple-element.25.table), custom_call_target="tpu_custom_call" | custom-call | flops 18454937600 | bytes 144179200 | tf_op jit(solution)/shard_map/forward_next2/pallas_call | solution.py:205
  11.1 2.5 %collective-permute-start.3 = (bf16[1792,128]{1,0:T(8,128)(2,1)S(1)}, bf16[1792,128]{1,0:T(8,128)(2,1)S(1)}, u32[]{:S(2)}, u32[]{:S(2)}) collective-permute-start(bf16[1792,128]{1,0:T(8,128)(2,1)S(1)} %forward_next2.1), channel_id=1, source_target_pairs={{0,1},{1,0},{2,3},{3,2},{4,5},{5,4},{6,7},{7,6},{8,9},{9,8},{10,11... | collective-permute-start | bytes 1376264 | tf_op jit(solution)/shard_map/ppermute | solution.py:436
  13.7 1.0 %forward_next0.1.a = bf16[1792,128]{1,0:T(8,128)(2,1)S(1)} custom-call(s32[512]{0:T(512)S(1)} %get-tuple-element.23.lists, bf16[88,128,128]{2,1,0:T(8,128)(2,1)S(1)} %get-tuple-element.32.held.tiles, bf16[1024,128]{1,0:T(8,128)(2,1)S(1)} %get-tuple-element.25.table), custom_call_target="tpu_custom_call" | custom-call | flops 18454937600 | bytes 144179200 | tf_op jit(solution)/shard_map/forward_next0/pallas_call | solution.py:205
  15.2 0.7 %collective-permute-start.4 = (bf16[896,128]{1,0:T(8,128)(2,1)S(1)}, bf16[896,128]{1,0:T(8,128)(2,1)S(1)}, u32[]{:S(2)}, u32[]{:S(2)}) collective-permute-start(bf16[896,128]{1,0:T(8,128)(2,1)S(1)} %get-tuple-element.30), channel_id=1, source_target_pairs={{0,2},{1,15},{2,0},{3,13},{4,6},{5,11},{6,4},{7,9},{8,10},{9,7},{1... | collective-permute-start | bytes 688136 | tf_op jit(solution)/shard_map/ppermute | solution.py:440
  15.9 1.2 %collective-permute-start.5 = (bf16[896,128]{1,0:T(8,128)(2,1)S(1)}, bf16[896,128]{1,0:T(8,128)(2,1)S(1)}, u32[]{:S(2)}, u32[]{:S(2)}) collective-permute-start(bf16[896,128]{1,0:T(8,128)(2,1)S(1)} %get-tuple-element.31), channel_id=1, source_target_pairs={{0,6},{1,11},{2,4},{3,9},{4,2},{5,15},{6,0},{7,13},{8,14},{9,3},{1... | collective-permute-start | bytes 688136 | tf_op jit(solution)/shard_map/ppermute | solution.py:440
  17.5 3.8 %collective-permute-done.4.refs_2_ = bf16[896,128]{1,0:T(8,128)(2,1)S(1)} collective-permute-done((bf16[896,128]{1,0:T(8,128)(2,1)S(1)}, bf16[896,128]{1,0:T(8,128)(2,1)S(1)}, u32[]{:S(2)}, u32[]{:S(2)}) %collective-permute-start.4) | collective-permute-done | bytes 229408 | tf_op jit(solution)/shard_map/ppermute | solution.py:440
  21.3 4.0 %collective-permute-done.5.refs_3_ = bf16[896,128]{1,0:T(8,128)(2,1)S(1)} collective-permute-done((bf16[896,128]{1,0:T(8,128)(2,1)S(1)}, bf16[896,128]{1,0:T(8,128)(2,1)S(1)}, u32[]{:S(2)}, u32[]{:S(2)}) %collective-permute-start.5) | collective-permute-done | bytes 229408 | tf_op jit(solution)/shard_map/ppermute | solution.py:440
  25.5 1.5 %collective-permute-done.6.refs_1_ = bf16[896,128]{1,0:T(8,128)(2,1)S(1)} collective-permute-done((bf16[896,128]{1,0:T(8,128)(2,1)S(1)}, bf16[896,128]{1,0:T(8,128)(2,1)S(1)}, u32[]{:S(2)}, u32[]{:S(2)}) %collective-permute-start.6) | collective-permute-done | bytes 229408 | tf_op jit(solution)/shard_map/ppermute | solution.py:436
  27.2 1.6 %collective-permute-start.8 = (bf16[896,128]{1,0:T(8,128)(2,1)S(1)}, bf16[896,128]{1,0:T(8,128)(2,1)S(1)}, u32[]{:S(2)}, u32[]{:S(2)}) collective-permute-start(bf16[896,128]{1,0:T(8,128)(2,1)S(1)} %chunk_sum.1.chunk), channel_id=1, source_target_pairs={{0,6},{1,11},{2,4},{3,9},{4,2},{5,15},{6,0},{7,13},{8,14},{9,3},{1... | collective-permute-start | bytes 688136 | tf_op jit(solution)/shard_map/ppermute | solution.py:440
  28.7 2.5 %collective-permute-start.11 = (bf16[896,128]{1,0:T(8,128)(2,1)S(1)}, bf16[896,128]{1,0:T(8,128)(2,1)S(1)}, u32[]{:S(2)}, u32[]{:S(2)}) collective-permute-start(bf16[896,128]{1,0:T(8,128)(2,1)S(1)} %chunk_sum.1.chunk), channel_id=1, source_target_pairs={{0,4},{1,13},{2,6},{3,15},{4,0},{5,9},{6,2},{7,11},{8,12},{9,5},{1... | collective-permute-start | bytes 688136 | tf_op jit(solution)/shard_map/ppermute | solution.py:440
  31.2 0.7 collective-permute-start.12
  31.9 1.3 %collective-permute-done.7.n0 = bf16[896,128]{1,0:T(8,128)(2,1)S(1)} collective-permute-done((bf16[896,128]{1,0:T(8,128)(2,1)S(1)}, bf16[896,128]{1,0:T(8,128)(2,1)S(1)}, u32[]{:S(2)}, u32[]{:S(2)}) %collective-permute-start.7) | collective-permute-done | bytes 229408 | tf_op jit(solution)/shard_map/ppermute | solution.py:440
  33.2 2.3 %collective-permute-start.9 = (bf16[896,128]{1,0:T(8,128)(2,1)S(1)}, bf16[896,128]{1,0:T(8,128)(2,1)S(1)}, u32[]{:S(2)}, u32[]{:S(2)}) collective-permute-start(bf16[896,128]{1,0:T(8,128)(2,1)S(1)} %collective-permute-done.7.n0), channel_id=1, source_target_pairs={{0,1},{1,0},{2,3},{3,2},{4,5},{5,4},{6,7},{7,6},{8,9},{9,8},{10,11... | collective-permute-start | bytes 688136 | tf_op jit(solution)/shard_map/ppermute | solution.py:436
  35.5 6.3 %collective-permute-done.8.n1 = bf16[896,128]{1,0:T(8,128)(2,1)S(1)} collective-permute-done((bf16[896,128]{1,0:T(8,128)(2,1)S(1)}, bf16[896,128]{1,0:T(8,128)(2,1)S(1)}, u32[]{:S(2)}, u32[]{:S(2)}) %collective-permute-start.8) | collective-permute-done | bytes 229408 | tf_op jit(solution)/shard_map/ppermute | solution.py:440
  42.4 0.9 %collective-permute-done.10.f1 = bf16[896,128]{1,0:T(8,128)(2,1)S(1)} collective-permute-done((bf16[896,128]{1,0:T(8,128)(2,1)S(1)}, bf16[896,128]{1,0:T(8,128)(2,1)S(1)}, u32[]{:S(2)}, u32[]{:S(2)}) %collective-permute-start.10) | collective-permute-done | bytes 229408 | tf_op jit(solution)/shard_map/ppermute | solution.py:436
  43.3 1.2 %backward_early.1.first = f32[1152,128]{1,0:T(8,128)S(1)} custom-call(s32[512]{0:T(512)S(1)} %get-tuple-element.23.lists, bf16[88,128,128]{2,1,0:T(8,128)(2,1)S(1)} %turn_tiles.1.turned, bf16[896,128]{1,0:T(8,128)(2,1)S(1)} %collective-permute-done.7.n0, bf16[896,128]{1,0:T(8,128)(2,1)S(1)} %collective-permute-done.8.n1, ...), custom_call_target="tpu_custom_call" | custom-call | flops 18454937600 | bytes 144179200 | tf_op jit(solution)/shard_map/backward_early/pallas_call | solution.py:321
  44.6 1.3 %backward_late.1 = (f32[256,128]{1,0:T(8,128)S(1)}, bf16[256,128]{1,0:T(8,128)(2,1)S(1)}, bf16[256,128]{1,0:T(8,128)(2,1)S(1)}, bf16[256,128]{1,0:T(8,128)(2,1)S(1)}) custom-call(s32[512]{0:T(512)S(1)} %get-tuple-element.23.lists, bf16[88,128,128]{2,1,0:T(8,128)(2,1)S(1)} %turn_tiles.1.turned, f32[1152,128]{1,0:T(8,128)S(1)} %backward_early.1.first, ...), custom_call_target="tpu_custom_call" | custom-call | tf_op jit(solution)/shard_map/backward_late/pallas_call | solution.py:355
  45.9 1.3 %collective-permute-start.15 = (bf16[256,128]{1,0:T(8,128)(2,1)S(1)}, bf16[256,128]{1,0:T(8,128)(2,1)S(1)}, u32[]{:S(2)}, u32[]{:S(2)}) collective-permute-start(bf16[256,128]{1,0:T(8,128)(2,1)S(1)} %get-tuple-element.35), channel_id=1, source_target_pairs={{0,128},{1,129},{2,130},{3,131},{4,132},{5,133},{6,134},{7,135},{8... | collective-permute-start | bytes 196616 | tf_op jit(solution)/shard_map/ppermute | solution.py:465
  47.2 2.2 %collective-permute-start.16 = (bf16[256,128]{1,0:T(8,128)(2,1)S(1)}, bf16[256,128]{1,0:T(8,128)(2,1)S(1)}, u32[]{:S(2)}, u32[]{:S(2)}) collective-permute-start(bf16[256,128]{1,0:T(8,128)(2,1)S(1)} %get-tuple-element.36), channel_id=1, source_target_pairs={{0,64},{1,193},{2,66},{3,195},{4,68},{5,197},{6,70},{7,199},{8,72}... | collective-permute-start | bytes 196616 | tf_op jit(solution)/shard_map/ppermute | solution.py:465
  49.4 2.8 %collective-permute-done.15.g0 = bf16[256,128]{1,0:T(8,128)(2,1)S(1)} collective-permute-done((bf16[256,128]{1,0:T(8,128)(2,1)S(1)}, bf16[256,128]{1,0:T(8,128)(2,1)S(1)}, u32[]{:S(2)}, u32[]{:S(2)}) %collective-permute-start.15) | collective-permute-done | bytes 65568 | tf_op jit(solution)/shard_map/ppermute | solution.py:465
  52.6 2.2 %collective-permute-done.17.g2 = bf16[256,128]{1,0:T(8,128)(2,1)S(1)} collective-permute-done((bf16[256,128]{1,0:T(8,128)(2,1)S(1)}, bf16[256,128]{1,0:T(8,128)(2,1)S(1)}, u32[]{:S(2)}, u32[]{:S(2)}) %collective-permute-start.17) | collective-permute-done | bytes 65568 | tf_op jit(solution)/shard_map/ppermute | solution.py:465
  54.9 3.6 %collective-permute-start.18 = (bf16[128,128]{1,0:T(8,128)(2,1)S(1)}, bf16[128,128]{1,0:T(8,128)(2,1)S(1)}, u32[]{:S(2)}, u32[]{:S(2)}) collective-permute-start(bf16[128,128]{1,0:T(8,128)(2,1)S(1)} %get-tuple-element.41), channel_id=1, source_target_pairs={{0,16},{16,0},{32,48},{48,32},{64,80},{80,64},{96,112},{112,96},{1... | collective-permute-start | bytes 98312 | tf_op jit(solution)/shard_map/ppermute | solution.py:467
  58.5 1.9 %collective-permute-done.18.got = bf16[128,128]{1,0:T(8,128)(2,1)S(1)} collective-permute-done((bf16[128,128]{1,0:T(8,128)(2,1)S(1)}, bf16[128,128]{1,0:T(8,128)(2,1)S(1)}, u32[]{:S(2)}, u32[]{:S(2)}) %collective-permute-start.18) | collective-permute-done | bytes 32800 | tf_op jit(solution)/shard_map/ppermute | solution.py:467
  60.4 5.6 %collective-permute-start.19 = (bf16[64,128]{1,0:T(8,128)(2,1)S(1)}, bf16[64,128]{1,0:T(8,128)(2,1)S(1)}, u32[]{:S(2)}, u32[]{:S(2)}) collective-permute-start(bf16[64,128]{1,0:T(8,128)(2,1)S(1)} %get-tuple-element.43), channel_id=1, source_target_pairs={{0,48},{16,32},{32,16},{48,0},{64,112},{80,96},{96,80},{112,64},{1... | collective-permute-start | bytes 49160 | tf_op jit(solution)/shard_map/ppermute | solution.py:468
  66.0 0.7 sketch_rows.1
  66.7 1.1 %collective-permute-done.19.got = bf16[64,128]{1,0:T(8,128)(2,1)S(1)} collective-permute-done((bf16[64,128]{1,0:T(8,128)(2,1)S(1)}, bf16[64,128]{1,0:T(8,128)(2,1)S(1)}, u32[]{:S(2)}, u32[]{:S(2)}) %collective-permute-start.19) | collective-permute-done | bytes 16416 | tf_op jit(solution)/shard_map/ppermute | solution.py:468
  67.7 0.6 last_sum.1
  (23 shorter events, 2.6 us)
Async XLA Ops:
  4.4 1.9 %collective-permute-start = (bf16[1792,128]{1,0:T(8,128)(2,1)S(1)}, bf16[1792,128]{1,0:T(8,128)(2,1)S(1)}, u32[]{:S(2)}, u32[]{:S(2)}) collective-permute-start(bf16[1792,128]{1,0:T(8,128)(2,1)S(1)} %get-tuple-element.26), channel_id=1, source_target_pairs={{0,1},{1,0},{2,3},{3,2},{4,5},{5,4},{6,7},{7,6},{8,9},{9,8},{10,11... | collective-permute-start | bytes 1376264 | tf_op jit(solution)/shard_map/ppermute | solution.py:436
  6.4 11.1 %collective-permute-start.1 = (bf16[896,128]{1,0:T(8,128)(2,1)S(1)}, bf16[896,128]{1,0:T(8,128)(2,1)S(1)}, u32[]{:S(2)}, u32[]{:S(2)}) collective-permute-start(bf16[896,128]{1,0:T(8,128)(2,1)S(1)} %get-tuple-element.27), channel_id=1, source_target_pairs={{0,4},{1,13},{2,6},{3,15},{4,0},{5,9},{6,2},{7,11},{8,12},{9,5},{1... | collective-permute-start | bytes 688136 | tf_op jit(solution)/shard_map/ppermute | solution.py:440
  9.5 8.0 %collective-permute-start.2 = (bf16[896,128]{1,0:T(8,128)(2,1)S(1)}, bf16[896,128]{1,0:T(8,128)(2,1)S(1)}, u32[]{:S(2)}, u32[]{:S(2)}) collective-permute-start(bf16[896,128]{1,0:T(8,128)(2,1)S(1)} %get-tuple-element.28), channel_id=1, source_target_pairs={{0,0},{1,9},{2,2},{3,11},{4,4},{5,13},{6,6},{7,15},{8,8},{9,1},{10... | collective-permute-start | bytes 688136 | tf_op jit(solution)/shard_map/ppermute | solution.py:440
  11.1 4.0 %collective-permute-start.3 = (bf16[1792,128]{1,0:T(8,128)(2,1)S(1)}, bf16[1792,128]{1,0:T(8,128)(2,1)S(1)}, u32[]{:S(2)}, u32[]{:S(2)}) collective-permute-start(bf16[1792,128]{1,0:T(8,128)(2,1)S(1)} %forward_next2.1), channel_id=1, source_target_pairs={{0,1},{1,0},{2,3},{3,2},{4,5},{5,4},{6,7},{7,6},{8,9},{9,8},{10,11... | collective-permute-start | bytes 1376264 | tf_op jit(solution)/shard_map/ppermute | solution.py:436
  15.2 6.1 %collective-permute-start.4 = (bf16[896,128]{1,0:T(8,128)(2,1)S(1)}, bf16[896,128]{1,0:T(8,128)(2,1)S(1)}, u32[]{:S(2)}, u32[]{:S(2)}) collective-permute-start(bf16[896,128]{1,0:T(8,128)(2,1)S(1)} %get-tuple-element.30), channel_id=1, source_target_pairs={{0,2},{1,15},{2,0},{3,13},{4,6},{5,11},{6,4},{7,9},{8,10},{9,7},{1... | collective-permute-start | bytes 688136 | tf_op jit(solution)/shard_map/ppermute | solution.py:440
  15.9 9.4 %collective-permute-start.5 = (bf16[896,128]{1,0:T(8,128)(2,1)S(1)}, bf16[896,128]{1,0:T(8,128)(2,1)S(1)}, u32[]{:S(2)}, u32[]{:S(2)}) collective-permute-start(bf16[896,128]{1,0:T(8,128)(2,1)S(1)} %get-tuple-element.31), channel_id=1, source_target_pairs={{0,6},{1,11},{2,4},{3,9},{4,2},{5,15},{6,0},{7,13},{8,14},{9,3},{1... | collective-permute-start | bytes 688136 | tf_op jit(solution)/shard_map/ppermute | solution.py:440
  25.4 1.6 %collective-permute-start.6 = (bf16[896,128]{1,0:T(8,128)(2,1)S(1)}, bf16[896,128]{1,0:T(8,128)(2,1)S(1)}, u32[]{:S(2)}, u32[]{:S(2)}) collective-permute-start(bf16[896,128]{1,0:T(8,128)(2,1)S(1)} %part_sum.1.refs_0_), channel_id=1, source_target_pairs={{0,1},{1,0},{2,3},{3,2},{4,5},{5,4},{6,7},{7,6},{8,9},{9,8},{10,11... | collective-permute-start | bytes 688136 | tf_op jit(solution)/shard_map/ppermute | solution.py:436
  27.1 6.1 %collective-permute-start.7 = (bf16[896,128]{1,0:T(8,128)(2,1)S(1)}, bf16[896,128]{1,0:T(8,128)(2,1)S(1)}, u32[]{:S(2)}, u32[]{:S(2)}) collective-permute-start(bf16[896,128]{1,0:T(8,128)(2,1)S(1)} %chunk_sum.1.chunk), channel_id=1, source_target_pairs={{0,2},{1,15},{2,0},{3,13},{4,6},{5,11},{6,4},{7,9},{8,10},{9,7},{1... | collective-permute-start | bytes 688136 | tf_op jit(solution)/shard_map/ppermute | solution.py:440
  27.2 14.7 %collective-permute-start.8 = (bf16[896,128]{1,0:T(8,128)(2,1)S(1)}, bf16[896,128]{1,0:T(8,128)(2,1)S(1)}, u32[]{:S(2)}, u32[]{:S(2)}) collective-permute-start(bf16[896,128]{1,0:T(8,128)(2,1)S(1)} %chunk_sum.1.chunk), channel_id=1, source_target_pairs={{0,6},{1,11},{2,4},{3,9},{4,2},{5,15},{6,0},{7,13},{8,14},{9,3},{1... | collective-permute-start | bytes 688136 | tf_op jit(solution)/shard_map/ppermute | solution.py:440
  28.7 13.1 %collective-permute-start.11 = (bf16[896,128]{1,0:T(8,128)(2,1)S(1)}, bf16[896,128]{1,0:T(8,128)(2,1)S(1)}, u32[]{:S(2)}, u32[]{:S(2)}) collective-permute-start(bf16[896,128]{1,0:T(8,128)(2,1)S(1)} %chunk_sum.1.chunk), channel_id=1, source_target_pairs={{0,4},{1,13},{2,6},{3,15},{4,0},{5,9},{6,2},{7,11},{8,12},{9,5},{1... | collective-permute-start | bytes 688136 | tf_op jit(solution)/shard_map/ppermute | solution.py:440
  31.2 11.1 %collective-permute-start.12 = (bf16[896,128]{1,0:T(8,128)(2,1)S(1)}, bf16[896,128]{1,0:T(8,128)(2,1)S(1)}, u32[]{:S(2)}, u32[]{:S(2)}) collective-permute-start(bf16[896,128]{1,0:T(8,128)(2,1)S(1)} %chunk_sum.1.chunk), channel_id=1, source_target_pairs={{0,0},{1,9},{2,2},{3,11},{4,4},{5,13},{6,6},{7,15},{8,8},{9,1},{10... | collective-permute-start | bytes 688136 | tf_op jit(solution)/shard_map/ppermute | solution.py:440
  33.2 9.3 %collective-permute-start.9 = (bf16[896,128]{1,0:T(8,128)(2,1)S(1)}, bf16[896,128]{1,0:T(8,128)(2,1)S(1)}, u32[]{:S(2)}, u32[]{:S(2)}) collective-permute-start(bf16[896,128]{1,0:T(8,128)(2,1)S(1)} %collective-permute-done.7.n0), channel_id=1, source_target_pairs={{0,1},{1,0},{2,3},{3,2},{4,5},{5,4},{6,7},{7,6},{8,9},{9,8},{10,11... | collective-permute-start | bytes 688136 | tf_op jit(solution)/shard_map/ppermute | solution.py:436
  41.8 1.5 %collective-permute-start.10 = (bf16[896,128]{1,0:T(8,128)(2,1)S(1)}, bf16[896,128]{1,0:T(8,128)(2,1)S(1)}, u32[]{:S(2)}, u32[]{:S(2)}) collective-permute-start(bf16[896,128]{1,0:T(8,128)(2,1)S(1)} %collective-permute-done.8.n1), channel_id=1, source_target_pairs={{0,1},{1,0},{2,3},{3,2},{4,5},{5,4},{6,7},{7,6},{8,9},{9,8},{10,11... | collective-permute-start | bytes 688136 | tf_op jit(solution)/shard_map/ppermute | solution.py:436
  41.8 2.7 %collective-permute-start.13 = (bf16[896,128]{1,0:T(8,128)(2,1)S(1)}, bf16[896,128]{1,0:T(8,128)(2,1)S(1)}, u32[]{:S(2)}, u32[]{:S(2)}) collective-permute-start(bf16[896,128]{1,0:T(8,128)(2,1)S(1)} %collective-permute-done.11.n2), channel_id=1, source_target_pairs={{0,1},{1,0},{2,3},{3,2},{4,5},{5,4},{6,7},{7,6},{8,9},{9,8},{10,11... | collective-permute-start | bytes 688136 | tf_op jit(solution)/shard_map/ppermute | solution.py:436
  42.3 2.2 %collective-permute-start.14 = (bf16[896,128]{1,0:T(8,128)(2,1)S(1)}, bf16[896,128]{1,0:T(8,128)(2,1)S(1)}, u32[]{:S(2)}, u32[]{:S(2)}) collective-permute-start(bf16[896,128]{1,0:T(8,128)(2,1)S(1)} %collective-permute-done.12.n3), channel_id=1, source_target_pairs={{0,1},{1,0},{2,3},{3,2},{4,5},{5,4},{6,7},{7,6},{8,9},{9,8},{10,11... | collective-permute-start | bytes 688136 | tf_op jit(solution)/shard_map/ppermute | solution.py:436
  45.9 6.3 %collective-permute-start.15 = (bf16[256,128]{1,0:T(8,128)(2,1)S(1)}, bf16[256,128]{1,0:T(8,128)(2,1)S(1)}, u32[]{:S(2)}, u32[]{:S(2)}) collective-permute-start(bf16[256,128]{1,0:T(8,128)(2,1)S(1)} %get-tuple-element.35), channel_id=1, source_target_pairs={{0,128},{1,129},{2,130},{3,131},{4,132},{5,133},{6,134},{7,135},{8... | collective-permute-start | bytes 196616 | tf_op jit(solution)/shard_map/ppermute | solution.py:465
  47.2 5.4 %collective-permute-start.16 = (bf16[256,128]{1,0:T(8,128)(2,1)S(1)}, bf16[256,128]{1,0:T(8,128)(2,1)S(1)}, u32[]{:S(2)}, u32[]{:S(2)}) collective-permute-start(bf16[256,128]{1,0:T(8,128)(2,1)S(1)} %get-tuple-element.36), channel_id=1, source_target_pairs={{0,64},{1,193},{2,66},{3,195},{4,68},{5,197},{6,70},{7,199},{8,72}... | collective-permute-start | bytes 196616 | tf_op jit(solution)/shard_map/ppermute | solution.py:465
  49.4 5.5 %collective-permute-start.17 = (bf16[256,128]{1,0:T(8,128)(2,1)S(1)}, bf16[256,128]{1,0:T(8,128)(2,1)S(1)}, u32[]{:S(2)}, u32[]{:S(2)}) collective-permute-start(bf16[256,128]{1,0:T(8,128)(2,1)S(1)} %get-tuple-element.37), channel_id=1, source_target_pairs={{0,192},{1,65},{2,194},{3,67},{4,196},{5,69},{6,198},{7,71},{8,200... | collective-permute-start | bytes 196616 | tf_op jit(solution)/shard_map/ppermute | solution.py:465
  54.9 5.5 %collective-permute-start.18 = (bf16[128,128]{1,0:T(8,128)(2,1)S(1)}, bf16[128,128]{1,0:T(8,128)(2,1)S(1)}, u32[]{:S(2)}, u32[]{:S(2)}) collective-permute-start(bf16[128,128]{1,0:T(8,128)(2,1)S(1)} %get-tuple-element.41), channel_id=1, source_target_pairs={{0,16},{16,0},{32,48},{48,32},{64,80},{80,64},{96,112},{112,96},{1... | collective-permute-start | bytes 98312 | tf_op jit(solution)/shard_map/ppermute | solution.py:467
  60.4 7.3 %collective-permute-start.19 = (bf16[64,128]{1,0:T(8,128)(2,1)S(1)}, bf16[64,128]{1,0:T(8,128)(2,1)S(1)}, u32[]{:S(2)}, u32[]{:S(2)}) collective-permute-start(bf16[64,128]{1,0:T(8,128)(2,1)S(1)} %get-tuple-element.43), channel_id=1, source_target_pairs={{0,48},{16,32},{32,16},{48,0},{64,112},{80,96},{96,80},{112,64},{1... | collective-permute-start | bytes 49160 | tf_op jit(solution)/shard_map/ppermute | solution.py:468

commit v8 on v5

--- a/solution.py
+++ b/solution.py
@@ -15,6 +15,7 @@
 PART_BLOCKS = 2 * CHUNK_BLOCKS
 PART = PART_BLOCKS * TILE
 UNROLL = 12
+PIECE = 448
 LIST = 128
 FETCH = 8
 VMEM_LIMIT = 48 * 1024 * 1024
@@ -288,13 +289,6 @@
     lax.fori_loop(0, (size_of(lists, which) + UNROLL - 1) // UNROLL, step, 0)
 
 
-def backward_part(lists, kinds, turned, near, far, table, acc):
-    for kind, pieces in zip(kinds, (near, far)):
-        for q, piece in enumerate(pieces):
-            table[chunk_at(q), :] = piece[...]
-        backward_slots(lists, kind, turned, table, acc)
-
-
 def sketch_kernel(chunk, out):
     _, _, c = place()
     size = out.shape[0]
@@ -312,20 +306,30 @@
     )(chunk)
 
 
-def backward_early_kernel(lists, turned, n0, n1, f0, f1, out, table):
+def backward_part(lists, which, pieces, turned, table, acc):
+    start = 0
+    for piece in pieces:
+        table[pl.ds(start, piece.shape[0]), :] = piece[...]
+        start += piece.shape[0]
+    backward_slots(lists, which, turned, table, acc)
+
+
+def backward_early_kernel(lists, turned, n0, n1, *refs):
+    *far, out, table = refs
     out[...] = jnp.zeros_like(out)
-    backward_part(lists, (NEAR_EARLY, FAR_EARLY), turned, (n0, n1), (f0, f1), table, out)
+    backward_part(lists, NEAR_EARLY, (n0, n1), turned, table, out)
+    backward_part(lists, FAR_EARLY, far, turned, table, out)
 
 
 def backward_early(lists, turned, near, far):
     return pl.pallas_call(
         backward_early_kernel,
         out_shape=jax.ShapeDtypeStruct(((SB_DEV + 1) * TILE, TILE), jnp.float32),
-        in_specs=[sm()] + [vm()] * 5,
+        in_specs=[sm()] + [vm()] * (3 + len(far)),
         out_specs=vm(),
         scratch_shapes=[pltpu.VMEM((PART, TILE), jnp.bfloat16)],
         compiler_params=params(),
-        cost_estimate=COST,
+        cost_estimate=pl.CostEstimate(flops=1, bytes_accessed=1, transcendentals=0),
         name="backward_early",
     )(lists, turned, *near, *far)
 
@@ -339,9 +343,12 @@
     return pl.ds(pl.multiple_of(lax.rem(i + 4, 4) * size, size), size)
 
 
-def backward_late_kernel(lists, turned, first, n2, n3, f2, f3, keep, s0, s1, s2, acc, table):
+def backward_late_kernel(
+    lists, turned, first, n2, n3, f2, f3, keep, s0, s1, s2, acc, table
+):
     acc[...] = first[...]
-    backward_part(lists, (NEAR_LATE, FAR_LATE), turned, (n2, n3), (f2, f3), table, acc)
+    backward_part(lists, NEAR_LATE, (n2, n3), turned, table, acc)
+    backward_part(lists, FAR_LATE, (f2, f3), turned, table, acc)
     y, _ = kmer_place()
     size = keep.shape[0]
     for r, send in enumerate((s0, s1, s2)):
@@ -349,7 +356,7 @@
     keep[...] = acc[share_at(y, size), :]
 
 
-def backward_late(lists, turned, first, near, far):
+def backward_late(lists, turned, first, *pieces):
     share = SB_DEV * TILE // 4
     send = jax.ShapeDtypeStruct((share, TILE), jnp.bfloat16)
     return pl.pallas_call(
@@ -363,7 +370,7 @@
         ],
         compiler_params=params(),
         name="backward_late",
-    )(lists, turned, first, *near, *far)
+    )(lists, turned, first, *pieces)
 
 
 def line_kernel(own, g0, g1, g2, keep, send, acc):
@@ -458,9 +465,10 @@
     part, turned = lax.optimization_barrier((part, turned))
     chunk = part_sum("chunk_sum", part, swap(part))
     near = [trade(chunk, p) for p in range(4)]
-    far = [swap(piece) for piece in near]
-    first = backward_early(lists, turned, near[:2], far[:2])
-    keep, *shares = backward_late(lists, turned, first, near[2:], far[2:])
+    far = [swap(piece[r : r + PIECE]) for piece in near[:2] for r in range(0, CHUNK, PIECE)]
+    first = backward_early(lists, turned, near[:2], far)
+    *late, first = lax.optimization_barrier((*near[2:], first))
+    keep, *shares = backward_late(lists, turned, first, *late, *(swap(piece) for piece in late))
     sketch = sketch_rows(after(chunk, *shares))
     got = [lax.ppermute(s, ("kmer", "samp"), y_pairs(r)) for r, s in enumerate(shares)]
     keep, share = line_sum(keep, got)

time: 66.5 us -> 70.2 us (1.056)
  starting transfers between devices: 28.2 us -> 30.6 us
  waiting for transfers between devices: 26.3 us -> 27.8 us
    ppermute x7 -> x9, waiting for transfers between devices: 2.85 us -> 5.18 us  [swap(): return lax.ppermute(value, 'samp', [(s, s ^ 1) for s in range(16)])]
    ppermute x1, starting transfers between devices: 6.49 us -> 8.12 us  [shards(): lax.ppermute(share, 'kmer', [(i, i // 4 * 4 + 3 - i % 4) for i in range(1...]
    ppermute x8, starting transfers between devices: 10.8 us -> 11.9 us  [trade(): return lax.ppermute(value, 'samp', round_pairs(p))]
    ppermute x8, waiting for transfers between devices: 15.1 us -> 14.2 us  [trade(): return lax.ppermute(value, 'samp', round_pairs(p))]
    ppermute x7 -> x9, starting transfers between devices: 3.4 us -> 3.93 us  [swap(): return lax.ppermute(value, 'samp', [(s, s ^ 1) for s in range(16)])]
  transfers between devices with their start and end apart: 20 -> 22, of which waited for: 12 -> 15; matrix products, arithmetic and copies ran while one was open for 0% -> 0% of each run, Pallas kernels for 8% -> 8%
where the time goes in v8:
time: 70.2 us; the launch traced here: 70.6 us
  starting transfers between devices  30.6 us (44%)
  waiting for transfers between devices  27.8 us (40%)
  Pallas kernels  10.7 us (15%)
  between operations  1.43 us (2%)
    ppermute x8, waiting for transfers between devices, trade(): return lax.ppermute(value, 'samp', round_pairs(p))  14.2 us
    ppermute x8, starting transfers between devices, trade(): return lax.ppermute(value, 'samp', round_pairs(p))  11.9 us
    ppermute x1, starting transfers between devices, shards(): lax.ppermute(share, 'kmer', [(i, i // 4 * 4 + 3 - i % 4) for i in range(1...  8.12 us
    ppermute x3, waiting for transfers between devices, shards(): lax.ppermute(s, ('kmer', 'samp'), y_pairs(r))  5.47 us
    ppermute x9, waiting for transfers between devices, swap(): return lax.ppermute(value, 'samp', [(s, s ^ 1) for s in range(16)])  5.18 us
    ppermute x9, starting transfers between devices, swap(): return lax.ppermute(value, 'samp', [(s, s ^ 1) for s in range(16)])  3.93 us
    ppermute x1, starting transfers between devices, shards(): lax.ppermute(share, 'kmer', [(i, i ^ 1) for i in range(16)])  3.35 us
    ppermute x3, starting transfers between devices, shards(): lax.ppermute(s, ('kmer', 'samp'), y_pairs(r))  3.33 us
  transfers between devices with their start and end apart: 22, of which 15 were waited for; matrix products, arithmetic and copies ran while one was open for 0% of the time, Pallas kernels for 8%

profile of v8, /device:TPU:24, one launch (start us, length us, event | category | flops | bytes accessed | tf_op | source)
XLA Modules:
  0.0 70.6 jit_solution(13928816033605715233)
XLA Ops:
  1.3 3.1 %forward_first.1 = (bf16[1792,128]{1,0:T(8,128)(2,1)S(1)}, bf16[88,128,128]{2,1,0:T(8,128)(2,1)S(1)}, bf16[1024,128]{1,0:T(8,128)(2,1)S(1)}, s32[512]{0:T(512)S(1)}) custom-call(s32[88]{0:T(128)} %rows.1, s32[88]{0:T(128)} %cols.1, s32[1]{0:T(128)S(6)} %copy.7.count, bf16[88,128,128]{2,1,0:T(8,128)(2,1)} %tiles.1, bf16[1024,128]{1,0:T(8,128)(2,1)} %omega.1), custom_call_target="tpu_custom_call" | custom-call | tf_op jit(solution)/shard_map/forward_first/pallas_call | solution.py:177
  4.5 1.0 %forward_next0.1.a = bf16[1792,128]{1,0:T(8,128)(2,1)S(1)} custom-call(s32[512]{0:T(512)S(1)} %get-tuple-element.26.lists, bf16[88,128,128]{2,1,0:T(8,128)(2,1)S(1)} %get-tuple-element.35.held.tiles, bf16[1024,128]{1,0:T(8,128)(2,1)S(1)} %get-tuple-element.28.table), custom_call_target="tpu_custom_call" | custom-call | flops 18454937600 | bytes 144179200 | tf_op jit(solution)/shard_map/forward_next0/pallas_call | solution.py:206
  5.4 0.8 %collective-permute-done.b = bf16[1792,128]{1,0:T(8,128)(2,1)S(1)} collective-permute-done((bf16[1792,128]{1,0:T(8,128)(2,1)S(1)}, bf16[1792,128]{1,0:T(8,128)(2,1)S(1)}, u32[]{:S(2)}, u32[]{:S(2)}) %collective-permute-start) | collective-permute-done | bytes 458784 | tf_op jit(solution)/shard_map/ppermute | solution.py:443
  6.4 1.6 %collective-permute-start.1 = (bf16[896,128]{1,0:T(8,128)(2,1)S(1)}, bf16[896,128]{1,0:T(8,128)(2,1)S(1)}, u32[]{:S(2)}, u32[]{:S(2)}) collective-permute-start(bf16[896,128]{1,0:T(8,128)(2,1)S(1)} %get-tuple-element.30), channel_id=1, source_target_pairs={{0,2},{1,15},{2,0},{3,13},{4,6},{5,11},{6,4},{7,9},{8,10},{9,7},{1... | collective-permute-start | bytes 688136 | tf_op jit(solution)/shard_map/ppermute | solution.py:447
  8.0 2.4 %collective-permute-start.2 = (bf16[896,128]{1,0:T(8,128)(2,1)S(1)}, bf16[896,128]{1,0:T(8,128)(2,1)S(1)}, u32[]{:S(2)}, u32[]{:S(2)}) collective-permute-start(bf16[896,128]{1,0:T(8,128)(2,1)S(1)} %get-tuple-element.31), channel_id=1, source_target_pairs={{0,6},{1,11},{2,4},{3,9},{4,2},{5,15},{6,0},{7,13},{8,14},{9,3},{1... | collective-permute-start | bytes 688136 | tf_op jit(solution)/shard_map/ppermute | solution.py:447
  10.3 1.0 %forward_next3.1 = bf16[1792,128]{1,0:T(8,128)(2,1)S(1)} custom-call(s32[512]{0:T(512)S(1)} %get-tuple-element.26.lists, bf16[88,128,128]{2,1,0:T(8,128)(2,1)S(1)} %get-tuple-element.35.held.tiles, bf16[1024,128]{1,0:T(8,128)(2,1)S(1)} %get-tuple-element.28.table), custom_call_target="tpu_custom_call" | custom-call | flops 18454937600 | bytes 144179200 | tf_op jit(solution)/shard_map/forward_next3/pallas_call | solution.py:206
  11.8 1.0 %forward_next1.1.a = bf16[1792,128]{1,0:T(8,128)(2,1)S(1)} custom-call(s32[512]{0:T(512)S(1)} %get-tuple-element.26.lists, bf16[88,128,128]{2,1,0:T(8,128)(2,1)S(1)} %get-tuple-element.35.held.tiles, bf16[1024,128]{1,0:T(8,128)(2,1)S(1)} %get-tuple-element.28.table), custom_call_target="tpu_custom_call" | custom-call | flops 18454937600 | bytes 144179200 | tf_op jit(solution)/shard_map/forward_next1/pallas_call | solution.py:206
  13.3 1.7 %collective-permute-start.4 = (bf16[896,128]{1,0:T(8,128)(2,1)S(1)}, bf16[896,128]{1,0:T(8,128)(2,1)S(1)}, u32[]{:S(2)}, u32[]{:S(2)}) collective-permute-start(bf16[896,128]{1,0:T(8,128)(2,1)S(1)} %get-tuple-element.33), channel_id=1, source_target_pairs={{0,4},{1,13},{2,6},{3,15},{4,0},{5,9},{6,2},{7,11},{8,12},{9,5},{1... | collective-permute-start | bytes 688136 | tf_op jit(solution)/shard_map/ppermute | solution.py:447
  15.1 0.7 collective-permute-start.5
  16.8 6.6 %collective-permute-done.4.refs_2_ = bf16[896,128]{1,0:T(8,128)(2,1)S(1)} collective-permute-done((bf16[896,128]{1,0:T(8,128)(2,1)S(1)}, bf16[896,128]{1,0:T(8,128)(2,1)S(1)}, u32[]{:S(2)}, u32[]{:S(2)}) %collective-permute-start.4) | collective-permute-done | bytes 229408 | tf_op jit(solution)/shard_map/ppermute | solution.py:447
  23.6 1.5 %collective-permute-done.6.refs_1_ = bf16[896,128]{1,0:T(8,128)(2,1)S(1)} collective-permute-done((bf16[896,128]{1,0:T(8,128)(2,1)S(1)}, bf16[896,128]{1,0:T(8,128)(2,1)S(1)}, u32[]{:S(2)}, u32[]{:S(2)}) %collective-permute-start.6) | collective-permute-done | bytes 229408 | tf_op jit(solution)/shard_map/ppermute | solution.py:443
  25.1 1.1 %collective-permute-start.9 = (bf16[896,128]{1,0:T(8,128)(2,1)S(1)}, bf16[896,128]{1,0:T(8,128)(2,1)S(1)}, u32[]{:S(2)}, u32[]{:S(2)}) collective-permute-start(bf16[896,128]{1,0:T(8,128)(2,1)S(1)} %chunk_sum.1.chunk), channel_id=1, source_target_pairs={{0,2},{1,15},{2,0},{3,13},{4,6},{5,11},{6,4},{7,9},{8,10},{9,7},{1... | collective-permute-start | bytes 688136 | tf_op jit(solution)/shard_map/ppermute | solution.py:447
  26.3 2.2 %collective-permute-start.7 = (bf16[896,128]{1,0:T(8,128)(2,1)S(1)}, bf16[896,128]{1,0:T(8,128)(2,1)S(1)}, u32[]{:S(2)}, u32[]{:S(2)}) collective-permute-start(bf16[896,128]{1,0:T(8,128)(2,1)S(1)} %chunk_sum.1.chunk), channel_id=1, source_target_pairs={{0,4},{1,13},{2,6},{3,15},{4,0},{5,9},{6,2},{7,11},{8,12},{9,5},{1... | collective-permute-start | bytes 688136 | tf_op jit(solution)/shard_map/ppermute | solution.py:447
  28.5 0.7 collective-permute-start.8
  29.2 1.5 %collective-permute-start.10 = (bf16[896,128]{1,0:T(8,128)(2,1)S(1)}, bf16[896,128]{1,0:T(8,128)(2,1)S(1)}, u32[]{:S(2)}, u32[]{:S(2)}) collective-permute-start(bf16[896,128]{1,0:T(8,128)(2,1)S(1)} %chunk_sum.1.chunk), channel_id=1, source_target_pairs={{0,6},{1,11},{2,4},{3,9},{4,2},{5,15},{6,0},{7,13},{8,14},{9,3},{1... | collective-permute-start | bytes 688136 | tf_op jit(solution)/shard_map/ppermute | solution.py:447
  30.7 0.6 collective-permute-done.9.n0
  31.3 2.0 %collective-permute-start.11 = (bf16[448,128]{1,0:T(8,128)(2,1)S(1)}, bf16[448,128]{1,0:T(8,128)(2,1)S(1)}, u32[]{:S(2)}, u32[]{:S(2)}) collective-permute-start(bf16[448,128]{1,0:T(8,128)(2,1)S(1)} %get-tuple-element.53), channel_id=1, source_target_pairs={{0,1},{1,0},{2,3},{3,2},{4,5},{5,4},{6,7},{7,6},{8,9},{9,8},{10,11... | collective-permute-start | bytes 344072 | tf_op jit(solution)/shard_map/ppermute | solution.py:443
  33.4 6.6 %collective-permute-done.10.n1 = bf16[896,128]{1,0:T(8,128)(2,1)S(1)} collective-permute-done((bf16[896,128]{1,0:T(8,128)(2,1)S(1)}, bf16[896,128]{1,0:T(8,128)(2,1)S(1)}, u32[]{:S(2)}, u32[]{:S(2)}) %collective-permute-start.10) | collective-permute-done | bytes 229408 | tf_op jit(solution)/shard_map/ppermute | solution.py:447
  40.5 0.8 %collective-permute-done.13.refs_2_ = bf16[448,128]{1,0:T(8,128)(2,1)S(1)} collective-permute-done((bf16[448,128]{1,0:T(8,128)(2,1)S(1)}, bf16[448,128]{1,0:T(8,128)(2,1)S(1)}, u32[]{:S(2)}, u32[]{:S(2)}) %collective-permute-start.13) | collective-permute-done | bytes 114720 | tf_op jit(solution)/shard_map/ppermute | solution.py:443
  41.6 1.2 %backward_early.1.first = f32[1152,128]{1,0:T(8,128)S(1)} custom-call(s32[512]{0:T(512)S(1)} %get-tuple-element.26.lists, bf16[88,128,128]{2,1,0:T(8,128)(2,1)S(1)} %turn_tiles.1.turned, bf16[896,128]{1,0:T(8,128)(2,1)S(1)} %collective-permute-done.9.n0, bf16[896,128]{1,0:T(8,128)(2,1)S(1)} %collective-permute-done.10.n1, ...), custom_call_target="tpu_custom_call" | custom-call | flops 1 | bytes 1 | tf_op jit(solution)/shard_map/backward_early/pallas_call | solution.py:325
  43.5 1.0 %collective-permute-done.15.f2 = bf16[896,128]{1,0:T(8,128)(2,1)S(1)} collective-permute-done((bf16[896,128]{1,0:T(8,128)(2,1)S(1)}, bf16[896,128]{1,0:T(8,128)(2,1)S(1)}, u32[]{:S(2)}, u32[]{:S(2)}) %collective-permute-start.15) | collective-permute-done | bytes 229408 | tf_op jit(solution)/shard_map/ppermute | solution.py:443
  44.8 1.3 %backward_late.1 = (f32[256,128]{1,0:T(8,128)S(1)}, bf16[256,128]{1,0:T(8,128)(2,1)S(1)}, bf16[256,128]{1,0:T(8,128)(2,1)S(1)}, bf16[256,128]{1,0:T(8,128)(2,1)S(1)}) custom-call(s32[512]{0:T(512)S(1)} %get-tuple-element.26.lists, bf16[88,128,128]{2,1,0:T(8,128)(2,1)S(1)} %turn_tiles.1.turned, f32[1152,128]{1,0:T(8,128)S(1)} %backward_early.1.first, ...), custom_call_target="tpu_custom_call" | custom-call | tf_op jit(solution)/shard_map/backward_late/pallas_call | solution.py:362
  46.1 1.1 %collective-permute-start.17 = (bf16[256,128]{1,0:T(8,128)(2,1)S(1)}, bf16[256,128]{1,0:T(8,128)(2,1)S(1)}, u32[]{:S(2)}, u32[]{:S(2)}) collective-permute-start(bf16[256,128]{1,0:T(8,128)(2,1)S(1)} %get-tuple-element.41), channel_id=1, source_target_pairs={{0,128},{1,129},{2,130},{3,131},{4,132},{5,133},{6,134},{7,135},{8... | collective-permute-start | bytes 196616 | tf_op jit(solution)/shard_map/ppermute | solution.py:473
  47.2 2.2 %collective-permute-start.18 = (bf16[256,128]{1,0:T(8,128)(2,1)S(1)}, bf16[256,128]{1,0:T(8,128)(2,1)S(1)}, u32[]{:S(2)}, u32[]{:S(2)}) collective-permute-start(bf16[256,128]{1,0:T(8,128)(2,1)S(1)} %get-tuple-element.42), channel_id=1, source_target_pairs={{0,64},{1,193},{2,66},{3,195},{4,68},{5,197},{6,70},{7,199},{8,72}... | collective-permute-start | bytes 196616 | tf_op jit(solution)/shard_map/ppermute | solution.py:473
  49.4 3.3 %collective-permute-done.17.g0 = bf16[256,128]{1,0:T(8,128)(2,1)S(1)} collective-permute-done((bf16[256,128]{1,0:T(8,128)(2,1)S(1)}, bf16[256,128]{1,0:T(8,128)(2,1)S(1)}, u32[]{:S(2)}, u32[]{:S(2)}) %collective-permute-start.17) | collective-permute-done | bytes 65568 | tf_op jit(solution)/shard_map/ppermute | solution.py:473
  52.7 2.1 %collective-permute-done.19.g2 = bf16[256,128]{1,0:T(8,128)(2,1)S(1)} collective-permute-done((bf16[256,128]{1,0:T(8,128)(2,1)S(1)}, bf16[256,128]{1,0:T(8,128)(2,1)S(1)}, u32[]{:S(2)}, u32[]{:S(2)}) %collective-permute-start.19) | collective-permute-done | bytes 65568 | tf_op jit(solution)/shard_map/ppermute | solution.py:473
  54.9 3.4 %collective-permute-start.20 = (bf16[128,128]{1,0:T(8,128)(2,1)S(1)}, bf16[128,128]{1,0:T(8,128)(2,1)S(1)}, u32[]{:S(2)}, u32[]{:S(2)}) collective-permute-start(bf16[128,128]{1,0:T(8,128)(2,1)S(1)} %get-tuple-element.47), channel_id=1, source_target_pairs={{0,16},{16,0},{32,48},{48,32},{64,80},{80,64},{96,112},{112,96},{1... | collective-permute-start | bytes 98312 | tf_op jit(solution)/shard_map/ppermute | solution.py:475
  58.3 1.9 %collective-permute-done.20.got = bf16[128,128]{1,0:T(8,128)(2,1)S(1)} collective-permute-done((bf16[128,128]{1,0:T(8,128)(2,1)S(1)}, bf16[128,128]{1,0:T(8,128)(2,1)S(1)}, u32[]{:S(2)}, u32[]{:S(2)}) %collective-permute-start.20) | collective-permute-done | bytes 32800 | tf_op jit(solution)/shard_map/ppermute | solution.py:475
  60.2 8.1 %collective-permute-start.21 = (bf16[64,128]{1,0:T(8,128)(2,1)S(1)}, bf16[64,128]{1,0:T(8,128)(2,1)S(1)}, u32[]{:S(2)}, u32[]{:S(2)}) collective-permute-start(bf16[64,128]{1,0:T(8,128)(2,1)S(1)} %get-tuple-element.49), channel_id=1, source_target_pairs={{0,48},{16,32},{32,16},{48,0},{64,112},{80,96},{96,80},{112,64},{1... | collective-permute-start | bytes 49160 | tf_op jit(solution)/shard_map/ppermute | solution.py:476
  68.3 0.7 sketch_rows.1
  68.9 1.1 %collective-permute-done.21.got = bf16[64,128]{1,0:T(8,128)(2,1)S(1)} collective-permute-done((bf16[64,128]{1,0:T(8,128)(2,1)S(1)}, bf16[64,128]{1,0:T(8,128)(2,1)S(1)}, u32[]{:S(2)}, u32[]{:S(2)}) %collective-permute-start.21) | collective-permute-done | bytes 16416 | tf_op jit(solution)/shard_map/ppermute | solution.py:476
  70.0 0.6 last_sum.1
  (29 shorter events, 4.5 us)
Async XLA Ops:
  4.4 1.9 %collective-permute-start = (bf16[1792,128]{1,0:T(8,128)(2,1)S(1)}, bf16[1792,128]{1,0:T(8,128)(2,1)S(1)}, u32[]{:S(2)}, u32[]{:S(2)}) collective-permute-start(bf16[1792,128]{1,0:T(8,128)(2,1)S(1)} %get-tuple-element.29), channel_id=1, source_target_pairs={{0,1},{1,0},{2,3},{3,2},{4,5},{5,4},{6,7},{7,6},{8,9},{9,8},{10,11... | collective-permute-start | bytes 1376264 | tf_op jit(solution)/shard_map/ppermute | solution.py:443
  6.4 9.9 %collective-permute-start.1 = (bf16[896,128]{1,0:T(8,128)(2,1)S(1)}, bf16[896,128]{1,0:T(8,128)(2,1)S(1)}, u32[]{:S(2)}, u32[]{:S(2)}) collective-permute-start(bf16[896,128]{1,0:T(8,128)(2,1)S(1)} %get-tuple-element.30), channel_id=1, source_target_pairs={{0,2},{1,15},{2,0},{3,13},{4,6},{5,11},{6,4},{7,9},{8,10},{9,7},{1... | collective-permute-start | bytes 688136 | tf_op jit(solution)/shard_map/ppermute | solution.py:447
  8.0 8.8 %collective-permute-start.2 = (bf16[896,128]{1,0:T(8,128)(2,1)S(1)}, bf16[896,128]{1,0:T(8,128)(2,1)S(1)}, u32[]{:S(2)}, u32[]{:S(2)}) collective-permute-start(bf16[896,128]{1,0:T(8,128)(2,1)S(1)} %get-tuple-element.31), channel_id=1, source_target_pairs={{0,6},{1,11},{2,4},{3,9},{4,2},{5,15},{6,0},{7,13},{8,14},{9,3},{1... | collective-permute-start | bytes 688136 | tf_op jit(solution)/shard_map/ppermute | solution.py:447
  11.3 1.9 %collective-permute-start.3 = (bf16[1792,128]{1,0:T(8,128)(2,1)S(1)}, bf16[1792,128]{1,0:T(8,128)(2,1)S(1)}, u32[]{:S(2)}, u32[]{:S(2)}) collective-permute-start(bf16[1792,128]{1,0:T(8,128)(2,1)S(1)} %forward_next3.1), channel_id=1, source_target_pairs={{0,1},{1,0},{2,3},{3,2},{4,5},{5,4},{6,7},{7,6},{8,9},{9,8},{10,11... | collective-permute-start | bytes 1376264 | tf_op jit(solution)/shard_map/ppermute | solution.py:443
  13.3 10.1 %collective-permute-start.4 = (bf16[896,128]{1,0:T(8,128)(2,1)S(1)}, bf16[896,128]{1,0:T(8,128)(2,1)S(1)}, u32[]{:S(2)}, u32[]{:S(2)}) collective-permute-start(bf16[896,128]{1,0:T(8,128)(2,1)S(1)} %get-tuple-element.33), channel_id=1, source_target_pairs={{0,4},{1,13},{2,6},{3,15},{4,0},{5,9},{6,2},{7,11},{8,12},{9,5},{1... | collective-permute-start | bytes 688136 | tf_op jit(solution)/shard_map/ppermute | solution.py:447
  15.1 8.3 %collective-permute-start.5 = (bf16[896,128]{1,0:T(8,128)(2,1)S(1)}, bf16[896,128]{1,0:T(8,128)(2,1)S(1)}, u32[]{:S(2)}, u32[]{:S(2)}) collective-permute-start(bf16[896,128]{1,0:T(8,128)(2,1)S(1)} %get-tuple-element.34), channel_id=1, source_target_pairs={{0,0},{1,9},{2,2},{3,11},{4,4},{5,13},{6,6},{7,15},{8,8},{9,1},{10... | collective-permute-start | bytes 688136 | tf_op jit(solution)/shard_map/ppermute | solution.py:447
  23.5 1.6 %collective-permute-start.6 = (bf16[896,128]{1,0:T(8,128)(2,1)S(1)}, bf16[896,128]{1,0:T(8,128)(2,1)S(1)}, u32[]{:S(2)}, u32[]{:S(2)}) collective-permute-start(bf16[896,128]{1,0:T(8,128)(2,1)S(1)} %part_sum.1.refs_0_), channel_id=1, source_target_pairs={{0,1},{1,0},{2,3},{3,2},{4,5},{5,4},{6,7},{7,6},{8,9},{9,8},{10,11... | collective-permute-start | bytes 688136 | tf_op jit(solution)/shard_map/ppermute | solution.py:443
  25.1 6.1 %collective-permute-start.9 = (bf16[896,128]{1,0:T(8,128)(2,1)S(1)}, bf16[896,128]{1,0:T(8,128)(2,1)S(1)}, u32[]{:S(2)}, u32[]{:S(2)}) collective-permute-start(bf16[896,128]{1,0:T(8,128)(2,1)S(1)} %chunk_sum.1.chunk), channel_id=1, source_target_pairs={{0,2},{1,15},{2,0},{3,13},{4,6},{5,11},{6,4},{7,9},{8,10},{9,7},{1... | collective-permute-start | bytes 688136 | tf_op jit(solution)/shard_map/ppermute | solution.py:447
  26.3 16.6 %collective-permute-start.7 = (bf16[896,128]{1,0:T(8,128)(2,1)S(1)}, bf16[896,128]{1,0:T(8,128)(2,1)S(1)}, u32[]{:S(2)}, u32[]{:S(2)}) collective-permute-start(bf16[896,128]{1,0:T(8,128)(2,1)S(1)} %chunk_sum.1.chunk), channel_id=1, source_target_pairs={{0,4},{1,13},{2,6},{3,15},{4,0},{5,9},{6,2},{7,11},{8,12},{9,5},{1... | collective-permute-start | bytes 688136 | tf_op jit(solution)/shard_map/ppermute | solution.py:447
  28.5 14.4 %collective-permute-start.8 = (bf16[896,128]{1,0:T(8,128)(2,1)S(1)}, bf16[896,128]{1,0:T(8,128)(2,1)S(1)}, u32[]{:S(2)}, u32[]{:S(2)}) collective-permute-start(bf16[896,128]{1,0:T(8,128)(2,1)S(1)} %chunk_sum.1.chunk), channel_id=1, source_target_pairs={{0,0},{1,9},{2,2},{3,11},{4,4},{5,13},{6,6},{7,15},{8,8},{9,1},{10... | collective-permute-start | bytes 688136 | tf_op jit(solution)/shard_map/ppermute | solution.py:447
  29.2 10.7 %collective-permute-start.10 = (bf16[896,128]{1,0:T(8,128)(2,1)S(1)}, bf16[896,128]{1,0:T(8,128)(2,1)S(1)}, u32[]{:S(2)}, u32[]{:S(2)}) collective-permute-start(bf16[896,128]{1,0:T(8,128)(2,1)S(1)} %chunk_sum.1.chunk), channel_id=1, source_target_pairs={{0,6},{1,11},{2,4},{3,9},{4,2},{5,15},{6,0},{7,13},{8,14},{9,3},{1... | collective-permute-start | bytes 688136 | tf_op jit(solution)/shard_map/ppermute | solution.py:447
  31.3 9.0 %collective-permute-start.11 = (bf16[448,128]{1,0:T(8,128)(2,1)S(1)}, bf16[448,128]{1,0:T(8,128)(2,1)S(1)}, u32[]{:S(2)}, u32[]{:S(2)}) collective-permute-start(bf16[448,128]{1,0:T(8,128)(2,1)S(1)} %get-tuple-element.53), channel_id=1, source_target_pairs={{0,1},{1,0},{2,3},{3,2},{4,5},{5,4},{6,7},{7,6},{8,9},{9,8},{10,11... | collective-permute-start | bytes 344072 | tf_op jit(solution)/shard_map/ppermute | solution.py:443
  33.3 7.3 %collective-permute-start.12 = (bf16[448,128]{1,0:T(8,128)(2,1)S(1)}, bf16[448,128]{1,0:T(8,128)(2,1)S(1)}, u32[]{:S(2)}, u32[]{:S(2)}) collective-permute-start(bf16[448,128]{1,0:T(8,128)(2,1)S(1)} %get-tuple-element.52), channel_id=1, source_target_pairs={{0,1},{1,0},{2,3},{3,2},{4,5},{5,4},{6,7},{7,6},{8,9},{9,8},{10,11... | collective-permute-start | bytes 344072 | tf_op jit(solution)/shard_map/ppermute | solution.py:443
  39.9 1.4 %collective-permute-start.13 = (bf16[448,128]{1,0:T(8,128)(2,1)S(1)}, bf16[448,128]{1,0:T(8,128)(2,1)S(1)}, u32[]{:S(2)}, u32[]{:S(2)}) collective-permute-start(bf16[448,128]{1,0:T(8,128)(2,1)S(1)} %get-tuple-element.51), channel_id=1, source_target_pairs={{0,1},{1,0},{2,3},{3,2},{4,5},{5,4},{6,7},{7,6},{8,9},{9,8},{10,11... | collective-permute-start | bytes 344072 | tf_op jit(solution)/shard_map/ppermute | solution.py:443
  40.3 1.3 %collective-permute-start.14 = (bf16[448,128]{1,0:T(8,128)(2,1)S(1)}, bf16[448,128]{1,0:T(8,128)(2,1)S(1)}, u32[]{:S(2)}, u32[]{:S(2)}) collective-permute-start(bf16[448,128]{1,0:T(8,128)(2,1)S(1)} %get-tuple-element.50), channel_id=1, source_target_pairs={{0,1},{1,0},{2,3},{3,2},{4,5},{5,4},{6,7},{7,6},{8,9},{9,8},{10,11... | collective-permute-start | bytes 344072 | tf_op jit(solution)/shard_map/ppermute | solution.py:443
  42.9 1.6 %collective-permute-start.15 = (bf16[896,128]{1,0:T(8,128)(2,1)S(1)}, bf16[896,128]{1,0:T(8,128)(2,1)S(1)}, u32[]{:S(2)}, u32[]{:S(2)}) collective-permute-start(bf16[896,128]{1,0:T(8,128)(2,1)S(1)} %collective-permute-done.7.n2), channel_id=1, source_target_pairs={{0,1},{1,0},{2,3},{3,2},{4,5},{5,4},{6,7},{7,6},{8,9},{9,8},{10,11... | collective-permute-start | bytes 688136 | tf_op jit(solution)/shard_map/ppermute | solution.py:443
  43.2 1.6 %collective-permute-start.16 = (bf16[896,128]{1,0:T(8,128)(2,1)S(1)}, bf16[896,128]{1,0:T(8,128)(2,1)S(1)}, u32[]{:S(2)}, u32[]{:S(2)}) collective-permute-start(bf16[896,128]{1,0:T(8,128)(2,1)S(1)} %collective-permute-done.8.n3), channel_id=1, source_target_pairs={{0,1},{1,0},{2,3},{3,2},{4,5},{5,4},{6,7},{7,6},{8,9},{9,8},{10,11... | collective-permute-start | bytes 688136 | tf_op jit(solution)/shard_map/ppermute | solution.py:443
  46.1 6.7 %collective-permute-start.17 = (bf16[256,128]{1,0:T(8,128)(2,1)S(1)}, bf16[256,128]{1,0:T(8,128)(2,1)S(1)}, u32[]{:S(2)}, u32[]{:S(2)}) collective-permute-start(bf16[256,128]{1,0:T(8,128)(2,1)S(1)} %get-tuple-element.41), channel_id=1, source_target_pairs={{0,128},{1,129},{2,130},{3,131},{4,132},{5,133},{6,134},{7,135},{8... | collective-permute-start | bytes 196616 | tf_op jit(solution)/shard_map/ppermute | solution.py:473
  47.2 5.5 %collective-permute-start.18 = (bf16[256,128]{1,0:T(8,128)(2,1)S(1)}, bf16[256,128]{1,0:T(8,128)(2,1)S(1)}, u32[]{:S(2)}, u32[]{:S(2)}) collective-permute-start(bf16[256,128]{1,0:T(8,128)(2,1)S(1)} %get-tuple-element.42), channel_id=1, source_target_pairs={{0,64},{1,193},{2,66},{3,195},{4,68},{5,197},{6,70},{7,199},{8,72}... | collective-permute-start | bytes 196616 | tf_op jit(solution)/shard_map/ppermute | solution.py:473
  49.4 5.5 %collective-permute-start.19 = (bf16[256,128]{1,0:T(8,128)(2,1)S(1)}, bf16[256,128]{1,0:T(8,128)(2,1)S(1)}, u32[]{:S(2)}, u32[]{:S(2)}) collective-permute-start(bf16[256,128]{1,0:T(8,128)(2,1)S(1)} %get-tuple-element.43), channel_id=1, source_target_pairs={{0,192},{1,65},{2,194},{3,67},{4,196},{5,69},{6,198},{7,71},{8,200... | collective-permute-start | bytes 196616 | tf_op jit(solution)/shard_map/ppermute | solution.py:473
  54.9 5.2 %collective-permute-start.20 = (bf16[128,128]{1,0:T(8,128)(2,1)S(1)}, bf16[128,128]{1,0:T(8,128)(2,1)S(1)}, u32[]{:S(2)}, u32[]{:S(2)}) collective-permute-start(bf16[128,128]{1,0:T(8,128)(2,1)S(1)} %get-tuple-element.47), channel_id=1, source_target_pairs={{0,16},{16,0},{32,48},{48,32},{64,80},{80,64},{96,112},{112,96},{1... | collective-permute-start | bytes 98312 | tf_op jit(solution)/shard_map/ppermute | solution.py:475
  60.2 9.8 %collective-permute-start.21 = (bf16[64,128]{1,0:T(8,128)(2,1)S(1)}, bf16[64,128]{1,0:T(8,128)(2,1)S(1)}, u32[]{:S(2)}, u32[]{:S(2)}) collective-permute-start(bf16[64,128]{1,0:T(8,128)(2,1)S(1)} %get-tuple-element.49), channel_id=1, source_target_pairs={{0,48},{16,32},{32,16},{48,0},{64,112},{80,96},{96,80},{112,64},{1... | collective-permute-start | bytes 49160 | tf_op jit(solution)/shard_map/ppermute | solution.py:476

commit v9 on v5

--- a/solution.py
+++ b/solution.py
@@ -22,8 +22,8 @@
 
 ROUNDS = (
     ((1, 0), (3, 1)),
+    ((2, 0), (2, 1)),
     ((3, 0), (1, 1)),
-    ((2, 0), (2, 1)),
     ((0, 0), (0, 1)),
 )
 NEAR_EARLY, NEAR_LATE, FAR_EARLY, FAR_LATE = range(4)
@@ -95,7 +95,7 @@
         same_z = (z == m // 4).astype(jnp.int32)
         core = 1 - same_z
         odd = jnp.where(core == 0, e == 3, e == 1).astype(jnp.int32)
-        p = jnp.where(e == 0, 3, jnp.where(e == 2, 2, odd))
+        p = jnp.where(e == 0, 3, jnp.where(e == 2, 1, 2 * odd))
         late = (p >= 2).astype(jnp.int32)
         shift[m] = (p - 2 * late - m) * CHUNK_BLOCKS
         owner[m] = jnp.where(core == c, 0, 2) + late

time: 66.5 us -> 66.3 us (level); the launches traced: 66.3 us -> 66.9 us
  starting transfers between devices: 28.2 us -> 29.5 us
  waiting for transfers between devices: 26.3 us -> 25.4 us
    ppermute x8, waiting for transfers between devices: 15.1 us -> 13.4 us  [trade(): return lax.ppermute(value, 'samp', round_pairs(p))]
    ppermute x8, starting transfers between devices: 10.8 us -> 12.3 us  [trade(): return lax.ppermute(value, 'samp', round_pairs(p))]
    ppermute x7, waiting for transfers between devices: 2.85 us -> 3.58 us  [swap(): return lax.ppermute(value, 'samp', [(s, s ^ 1) for s in range(16)])]
  transfers between devices with their start and end apart: 20 -> 20, of which waited for: 12 -> 11; matrix products, arithmetic and copies ran while one was open for 0% -> 0% of each run, Pallas kernels for 8% -> 8%
where the time goes in v9:
time: 66.3 us; the launch traced here: 66.9 us
  starting transfers between devices  29.5 us (44%)
  waiting for transfers between devices  25.4 us (38%)
  Pallas kernels  10.6 us (16%)
  between operations  1.42 us (2%)
    ppermute x8, waiting for transfers between devices, trade(): return lax.ppermute(value, 'samp', round_pairs(p))  13.4 us
    ppermute x8, starting transfers between devices, trade(): return lax.ppermute(value, 'samp', round_pairs(p))  12.3 us
    ppermute x1, starting transfers between devices, shards(): lax.ppermute(share, 'kmer', [(i, i // 4 * 4 + 3 - i % 4) for i in range(1...  6.97 us
    ppermute x3, waiting for transfers between devices, shards(): lax.ppermute(s, ('kmer', 'samp'), y_pairs(r))  5.47 us
    ppermute x1, starting transfers between devices, shards(): lax.ppermute(share, 'kmer', [(i, i ^ 1) for i in range(16)])  3.63 us
    ppermute x7, waiting for transfers between devices, swap(): return lax.ppermute(value, 'samp', [(s, s ^ 1) for s in range(16)])  3.58 us
    ppermute x3, starting transfers between devices, shards(): lax.ppermute(s, ('kmer', 'samp'), y_pairs(r))  3.51 us
    ppermute x7, starting transfers between devices, swap(): return lax.ppermute(value, 'samp', [(s, s ^ 1) for s in range(16)])  3.09 us
  transfers between devices with their start and end apart: 20, of which 11 were waited for; matrix products, arithmetic and copies ran while one was open for 0% of the time, Pallas kernels for 8%

profile of v9, /device:TPU:24, one launch (start us, length us, event | category | flops | bytes accessed | tf_op | source)
XLA Modules:
  0.0 66.9 jit_solution(6694062622270035084)
XLA Ops:
  1.3 3.1 %forward_first.1 = (bf16[1792,128]{1,0:T(8,128)(2,1)S(1)}, bf16[88,128,128]{2,1,0:T(8,128)(2,1)S(1)}, bf16[1024,128]{1,0:T(8,128)(2,1)S(1)}, s32[512]{0:T(512)S(1)}) custom-call(s32[88]{0:T(128)} %rows.1, s32[88]{0:T(128)} %cols.1, s32[1]{0:T(128)S(6)} %copy.7.count, bf16[88,128,128]{2,1,0:T(8,128)(2,1)} %tiles.1, bf16[1024,128]{1,0:T(8,128)(2,1)} %omega.1), custom_call_target="tpu_custom_call" | custom-call | tf_op jit(solution)/shard_map/forward_first/pallas_call | solution.py:176
  4.5 1.0 %forward_next0.1.a = bf16[1792,128]{1,0:T(8,128)(2,1)S(1)} custom-call(s32[512]{0:T(512)S(1)} %get-tuple-element.23.lists, bf16[88,128,128]{2,1,0:T(8,128)(2,1)S(1)} %get-tuple-element.32.held.tiles, bf16[1024,128]{1,0:T(8,128)(2,1)S(1)} %get-tuple-element.25.table), custom_call_target="tpu_custom_call" | custom-call | flops 18454937600 | bytes 144179200 | tf_op jit(solution)/shard_map/forward_next0/pallas_call | solution.py:205
  5.4 0.8 %collective-permute-done.b = bf16[1792,128]{1,0:T(8,128)(2,1)S(1)} collective-permute-done((bf16[1792,128]{1,0:T(8,128)(2,1)S(1)}, bf16[1792,128]{1,0:T(8,128)(2,1)S(1)}, u32[]{:S(2)}, u32[]{:S(2)}) %collective-permute-start) | collective-permute-done | bytes 458784 | tf_op jit(solution)/shard_map/ppermute | solution.py:436
  6.4 1.6 %collective-permute-start.1 = (bf16[896,128]{1,0:T(8,128)(2,1)S(1)}, bf16[896,128]{1,0:T(8,128)(2,1)S(1)}, u32[]{:S(2)}, u32[]{:S(2)}) collective-permute-start(bf16[896,128]{1,0:T(8,128)(2,1)S(1)} %get-tuple-element.27), channel_id=1, source_target_pairs={{0,2},{1,15},{2,0},{3,13},{4,6},{5,11},{6,4},{7,9},{8,10},{9,7},{1... | collective-permute-start | bytes 688136 | tf_op jit(solution)/shard_map/ppermute | solution.py:440
  8.0 2.7 %collective-permute-start.2 = (bf16[896,128]{1,0:T(8,128)(2,1)S(1)}, bf16[896,128]{1,0:T(8,128)(2,1)S(1)}, u32[]{:S(2)}, u32[]{:S(2)}) collective-permute-start(bf16[896,128]{1,0:T(8,128)(2,1)S(1)} %get-tuple-element.28), channel_id=1, source_target_pairs={{0,4},{1,13},{2,6},{3,15},{4,0},{5,9},{6,2},{7,11},{8,12},{9,5},{1... | collective-permute-start | bytes 688136 | tf_op jit(solution)/shard_map/ppermute | solution.py:440
  10.7 1.0 %forward_next3.1 = bf16[1792,128]{1,0:T(8,128)(2,1)S(1)} custom-call(s32[512]{0:T(512)S(1)} %get-tuple-element.23.lists, bf16[88,128,128]{2,1,0:T(8,128)(2,1)S(1)} %get-tuple-element.32.held.tiles, bf16[1024,128]{1,0:T(8,128)(2,1)S(1)} %get-tuple-element.25.table), custom_call_target="tpu_custom_call" | custom-call | flops 18454937600 | bytes 144179200 | tf_op jit(solution)/shard_map/forward_next3/pallas_call | solution.py:205
  11.9 1.0 %forward_next1.1.a = bf16[1792,128]{1,0:T(8,128)(2,1)S(1)} custom-call(s32[512]{0:T(512)S(1)} %get-tuple-element.23.lists, bf16[88,128,128]{2,1,0:T(8,128)(2,1)S(1)} %get-tuple-element.32.held.tiles, bf16[1024,128]{1,0:T(8,128)(2,1)S(1)} %get-tuple-element.25.table), custom_call_target="tpu_custom_call" | custom-call | flops 18454937600 | bytes 144179200 | tf_op jit(solution)/shard_map/forward_next1/pallas_call | solution.py:205
  12.8 0.7 %collective-permute-done.3.b = bf16[1792,128]{1,0:T(8,128)(2,1)S(1)} collective-permute-done((bf16[1792,128]{1,0:T(8,128)(2,1)S(1)}, bf16[1792,128]{1,0:T(8,128)(2,1)S(1)}, u32[]{:S(2)}, u32[]{:S(2)}) %collective-permute-start.3) | collective-permute-done | bytes 458784 | tf_op jit(solution)/shard_map/ppermute | solution.py:436
  13.7 1.9 %collective-permute-start.4 = (bf16[896,128]{1,0:T(8,128)(2,1)S(1)}, bf16[896,128]{1,0:T(8,128)(2,1)S(1)}, u32[]{:S(2)}, u32[]{:S(2)}) collective-permute-start(bf16[896,128]{1,0:T(8,128)(2,1)S(1)} %get-tuple-element.30), channel_id=1, source_target_pairs={{0,6},{1,11},{2,4},{3,9},{4,2},{5,15},{6,0},{7,13},{8,14},{9,3},{1... | collective-permute-start | bytes 688136 | tf_op jit(solution)/shard_map/ppermute | solution.py:440
  15.6 0.7 collective-permute-start.5
  16.7 5.4 %collective-permute-done.2.refs_1_ = bf16[896,128]{1,0:T(8,128)(2,1)S(1)} collective-permute-done((bf16[896,128]{1,0:T(8,128)(2,1)S(1)}, bf16[896,128]{1,0:T(8,128)(2,1)S(1)}, u32[]{:S(2)}, u32[]{:S(2)}) %collective-permute-start.2) | collective-permute-done | bytes 229408 | tf_op jit(solution)/shard_map/ppermute | solution.py:440
  22.7 1.1 %collective-permute-done.6.refs_1_ = bf16[896,128]{1,0:T(8,128)(2,1)S(1)} collective-permute-done((bf16[896,128]{1,0:T(8,128)(2,1)S(1)}, bf16[896,128]{1,0:T(8,128)(2,1)S(1)}, u32[]{:S(2)}, u32[]{:S(2)}) %collective-permute-start.6) | collective-permute-done | bytes 229408 | tf_op jit(solution)/shard_map/ppermute | solution.py:436
  23.9 1.6 %collective-permute-start.7 = (bf16[896,128]{1,0:T(8,128)(2,1)S(1)}, bf16[896,128]{1,0:T(8,128)(2,1)S(1)}, u32[]{:S(2)}, u32[]{:S(2)}) collective-permute-start(bf16[896,128]{1,0:T(8,128)(2,1)S(1)} %chunk_sum.1.chunk), channel_id=1, source_target_pairs={{0,2},{1,15},{2,0},{3,13},{4,6},{5,11},{6,4},{7,9},{8,10},{9,7},{1... | collective-permute-start | bytes 688136 | tf_op jit(solution)/shard_map/ppermute | solution.py:440
  25.5 2.1 %collective-permute-start.8 = (bf16[896,128]{1,0:T(8,128)(2,1)S(1)}, bf16[896,128]{1,0:T(8,128)(2,1)S(1)}, u32[]{:S(2)}, u32[]{:S(2)}) collective-permute-start(bf16[896,128]{1,0:T(8,128)(2,1)S(1)} %chunk_sum.1.chunk), channel_id=1, source_target_pairs={{0,4},{1,13},{2,6},{3,15},{4,0},{5,9},{6,2},{7,11},{8,12},{9,5},{1... | collective-permute-start | bytes 688136 | tf_op jit(solution)/shard_map/ppermute | solution.py:440
  27.6 1.0 %collective-permute-start.11 = (bf16[896,128]{1,0:T(8,128)(2,1)S(1)}, bf16[896,128]{1,0:T(8,128)(2,1)S(1)}, u32[]{:S(2)}, u32[]{:S(2)}) collective-permute-start(bf16[896,128]{1,0:T(8,128)(2,1)S(1)} %chunk_sum.1.chunk), channel_id=1, source_target_pairs={{0,6},{1,11},{2,4},{3,9},{4,2},{5,15},{6,0},{7,13},{8,14},{9,3},{1... | collective-permute-start | bytes 688136 | tf_op jit(solution)/shard_map/ppermute | solution.py:440
  28.6 0.7 collective-permute-start.12
  29.3 0.7 collective-permute-done.7.n0
  30.0 1.7 %collective-permute-start.9 = (bf16[896,128]{1,0:T(8,128)(2,1)S(1)}, bf16[896,128]{1,0:T(8,128)(2,1)S(1)}, u32[]{:S(2)}, u32[]{:S(2)}) collective-permute-start(bf16[896,128]{1,0:T(8,128)(2,1)S(1)} %collective-permute-done.7.n0), channel_id=1, source_target_pairs={{0,1},{1,0},{2,3},{3,2},{4,5},{5,4},{6,7},{7,6},{8,9},{9,8},{10,11... | collective-permute-start | bytes 688136 | tf_op jit(solution)/shard_map/ppermute | solution.py:436
  31.7 7.4 %collective-permute-done.8.n1 = bf16[896,128]{1,0:T(8,128)(2,1)S(1)} collective-permute-done((bf16[896,128]{1,0:T(8,128)(2,1)S(1)}, bf16[896,128]{1,0:T(8,128)(2,1)S(1)}, u32[]{:S(2)}, u32[]{:S(2)}) %collective-permute-start.8) | collective-permute-done | bytes 229408 | tf_op jit(solution)/shard_map/ppermute | solution.py:440
  39.6 0.9 %collective-permute-done.10.f1 = bf16[896,128]{1,0:T(8,128)(2,1)S(1)} collective-permute-done((bf16[896,128]{1,0:T(8,128)(2,1)S(1)}, bf16[896,128]{1,0:T(8,128)(2,1)S(1)}, u32[]{:S(2)}, u32[]{:S(2)}) %collective-permute-start.10) | collective-permute-done | bytes 229408 | tf_op jit(solution)/shard_map/ppermute | solution.py:436
  40.5 1.2 %backward_early.1.first = f32[1152,128]{1,0:T(8,128)S(1)} custom-call(s32[512]{0:T(512)S(1)} %get-tuple-element.23.lists, bf16[88,128,128]{2,1,0:T(8,128)(2,1)S(1)} %turn_tiles.1.turned, bf16[896,128]{1,0:T(8,128)(2,1)S(1)} %collective-permute-done.7.n0, bf16[896,128]{1,0:T(8,128)(2,1)S(1)} %collective-permute-done.8.n1, ...), custom_call_target="tpu_custom_call" | custom-call | flops 18454937600 | bytes 144179200 | tf_op jit(solution)/shard_map/backward_early/pallas_call | solution.py:321
  41.8 1.3 %backward_late.1 = (f32[256,128]{1,0:T(8,128)S(1)}, bf16[256,128]{1,0:T(8,128)(2,1)S(1)}, bf16[256,128]{1,0:T(8,128)(2,1)S(1)}, bf16[256,128]{1,0:T(8,128)(2,1)S(1)}) custom-call(s32[512]{0:T(512)S(1)} %get-tuple-element.23.lists, bf16[88,128,128]{2,1,0:T(8,128)(2,1)S(1)} %turn_tiles.1.turned, f32[1152,128]{1,0:T(8,128)S(1)} %backward_early.1.first, ...), custom_call_target="tpu_custom_call" | custom-call | tf_op jit(solution)/shard_map/backward_late/pallas_call | solution.py:355
  43.1 1.3 %collective-permute-start.15 = (bf16[256,128]{1,0:T(8,128)(2,1)S(1)}, bf16[256,128]{1,0:T(8,128)(2,1)S(1)}, u32[]{:S(2)}, u32[]{:S(2)}) collective-permute-start(bf16[256,128]{1,0:T(8,128)(2,1)S(1)} %get-tuple-element.35), channel_id=1, source_target_pairs={{0,128},{1,129},{2,130},{3,131},{4,132},{5,133},{6,134},{7,135},{8... | collective-permute-start | bytes 196616 | tf_op jit(solution)/shard_map/ppermute | solution.py:465
  44.4 2.2 %collective-permute-start.16 = (bf16[256,128]{1,0:T(8,128)(2,1)S(1)}, bf16[256,128]{1,0:T(8,128)(2,1)S(1)}, u32[]{:S(2)}, u32[]{:S(2)}) collective-permute-start(bf16[256,128]{1,0:T(8,128)(2,1)S(1)} %get-tuple-element.36), channel_id=1, source_target_pairs={{0,64},{1,193},{2,66},{3,195},{4,68},{5,197},{6,70},{7,199},{8,72}... | collective-permute-start | bytes 196616 | tf_op jit(solution)/shard_map/ppermute | solution.py:465
  46.6 2.8 %collective-permute-done.15.g0 = bf16[256,128]{1,0:T(8,128)(2,1)S(1)} collective-permute-done((bf16[256,128]{1,0:T(8,128)(2,1)S(1)}, bf16[256,128]{1,0:T(8,128)(2,1)S(1)}, u32[]{:S(2)}, u32[]{:S(2)}) %collective-permute-start.15) | collective-permute-done | bytes 65568 | tf_op jit(solution)/shard_map/ppermute | solution.py:465
  49.4 2.7 %collective-permute-done.17.g2 = bf16[256,128]{1,0:T(8,128)(2,1)S(1)} collective-permute-done((bf16[256,128]{1,0:T(8,128)(2,1)S(1)}, bf16[256,128]{1,0:T(8,128)(2,1)S(1)}, u32[]{:S(2)}, u32[]{:S(2)}) %collective-permute-start.17) | collective-permute-done | bytes 65568 | tf_op jit(solution)/shard_map/ppermute | solution.py:465
  52.1 3.6 %collective-permute-start.18 = (bf16[128,128]{1,0:T(8,128)(2,1)S(1)}, bf16[128,128]{1,0:T(8,128)(2,1)S(1)}, u32[]{:S(2)}, u32[]{:S(2)}) collective-permute-start(bf16[128,128]{1,0:T(8,128)(2,1)S(1)} %get-tuple-element.41), channel_id=1, source_target_pairs={{0,16},{16,0},{32,48},{48,32},{64,80},{80,64},{96,112},{112,96},{1... | collective-permute-start | bytes 98312 | tf_op jit(solution)/shard_map/ppermute | solution.py:467
  55.7 1.9 %collective-permute-done.18.got = bf16[128,128]{1,0:T(8,128)(2,1)S(1)} collective-permute-done((bf16[128,128]{1,0:T(8,128)(2,1)S(1)}, bf16[128,128]{1,0:T(8,128)(2,1)S(1)}, u32[]{:S(2)}, u32[]{:S(2)}) %collective-permute-start.18) | collective-permute-done | bytes 32800 | tf_op jit(solution)/shard_map/ppermute | solution.py:467
  57.6 7.0 %collective-permute-start.19 = (bf16[64,128]{1,0:T(8,128)(2,1)S(1)}, bf16[64,128]{1,0:T(8,128)(2,1)S(1)}, u32[]{:S(2)}, u32[]{:S(2)}) collective-permute-start(bf16[64,128]{1,0:T(8,128)(2,1)S(1)} %get-tuple-element.43), channel_id=1, source_target_pairs={{0,48},{16,32},{32,16},{48,0},{64,112},{80,96},{96,80},{112,64},{1... | collective-permute-start | bytes 49160 | tf_op jit(solution)/shard_map/ppermute | solution.py:468
  64.6 0.7 sketch_rows.1
  65.3 1.1 %collective-permute-done.19.got = bf16[64,128]{1,0:T(8,128)(2,1)S(1)} collective-permute-done((bf16[64,128]{1,0:T(8,128)(2,1)S(1)}, bf16[64,128]{1,0:T(8,128)(2,1)S(1)}, u32[]{:S(2)}, u32[]{:S(2)}) %collective-permute-start.19) | collective-permute-done | bytes 16416 | tf_op jit(solution)/shard_map/ppermute | solution.py:468
  66.3 0.6 last_sum.1
  (23 shorter events, 2.3 us)
Async XLA Ops:
  4.4 1.9 %collective-permute-start = (bf16[1792,128]{1,0:T(8,128)(2,1)S(1)}, bf16[1792,128]{1,0:T(8,128)(2,1)S(1)}, u32[]{:S(2)}, u32[]{:S(2)}) collective-permute-start(bf16[1792,128]{1,0:T(8,128)(2,1)S(1)} %get-tuple-element.26), channel_id=1, source_target_pairs={{0,1},{1,0},{2,3},{3,2},{4,5},{5,4},{6,7},{7,6},{8,9},{9,8},{10,11... | collective-permute-start | bytes 1376264 | tf_op jit(solution)/shard_map/ppermute | solution.py:436
  6.4 10.3 %collective-permute-start.1 = (bf16[896,128]{1,0:T(8,128)(2,1)S(1)}, bf16[896,128]{1,0:T(8,128)(2,1)S(1)}, u32[]{:S(2)}, u32[]{:S(2)}) collective-permute-start(bf16[896,128]{1,0:T(8,128)(2,1)S(1)} %get-tuple-element.27), channel_id=1, source_target_pairs={{0,2},{1,15},{2,0},{3,13},{4,6},{5,11},{6,4},{7,9},{8,10},{9,7},{1... | collective-permute-start | bytes 688136 | tf_op jit(solution)/shard_map/ppermute | solution.py:440
  8.0 14.1 %collective-permute-start.2 = (bf16[896,128]{1,0:T(8,128)(2,1)S(1)}, bf16[896,128]{1,0:T(8,128)(2,1)S(1)}, u32[]{:S(2)}, u32[]{:S(2)}) collective-permute-start(bf16[896,128]{1,0:T(8,128)(2,1)S(1)} %get-tuple-element.28), channel_id=1, source_target_pairs={{0,4},{1,13},{2,6},{3,15},{4,0},{5,9},{6,2},{7,11},{8,12},{9,5},{1... | collective-permute-start | bytes 688136 | tf_op jit(solution)/shard_map/ppermute | solution.py:440
  11.7 1.9 %collective-permute-start.3 = (bf16[1792,128]{1,0:T(8,128)(2,1)S(1)}, bf16[1792,128]{1,0:T(8,128)(2,1)S(1)}, u32[]{:S(2)}, u32[]{:S(2)}) collective-permute-start(bf16[1792,128]{1,0:T(8,128)(2,1)S(1)} %forward_next3.1), channel_id=1, source_target_pairs={{0,1},{1,0},{2,3},{3,2},{4,5},{5,4},{6,7},{7,6},{8,9},{9,8},{10,11... | collective-permute-start | bytes 1376264 | tf_op jit(solution)/shard_map/ppermute | solution.py:436
  13.7 8.4 %collective-permute-start.4 = (bf16[896,128]{1,0:T(8,128)(2,1)S(1)}, bf16[896,128]{1,0:T(8,128)(2,1)S(1)}, u32[]{:S(2)}, u32[]{:S(2)}) collective-permute-start(bf16[896,128]{1,0:T(8,128)(2,1)S(1)} %get-tuple-element.30), channel_id=1, source_target_pairs={{0,6},{1,11},{2,4},{3,9},{4,2},{5,15},{6,0},{7,13},{8,14},{9,3},{1... | collective-permute-start | bytes 688136 | tf_op jit(solution)/shard_map/ppermute | solution.py:440
  15.6 6.5 %collective-permute-start.5 = (bf16[896,128]{1,0:T(8,128)(2,1)S(1)}, bf16[896,128]{1,0:T(8,128)(2,1)S(1)}, u32[]{:S(2)}, u32[]{:S(2)}) collective-permute-start(bf16[896,128]{1,0:T(8,128)(2,1)S(1)} %get-tuple-element.31), channel_id=1, source_target_pairs={{0,0},{1,9},{2,2},{3,11},{4,4},{5,13},{6,6},{7,15},{8,8},{9,1},{10... | collective-permute-start | bytes 688136 | tf_op jit(solution)/shard_map/ppermute | solution.py:440
  22.2 1.6 %collective-permute-start.6 = (bf16[896,128]{1,0:T(8,128)(2,1)S(1)}, bf16[896,128]{1,0:T(8,128)(2,1)S(1)}, u32[]{:S(2)}, u32[]{:S(2)}) collective-permute-start(bf16[896,128]{1,0:T(8,128)(2,1)S(1)} %part_sum.1.refs_0_), channel_id=1, source_target_pairs={{0,1},{1,0},{2,3},{3,2},{4,5},{5,4},{6,7},{7,6},{8,9},{9,8},{10,11... | collective-permute-start | bytes 688136 | tf_op jit(solution)/shard_map/ppermute | solution.py:436
  23.9 6.1 %collective-permute-start.7 = (bf16[896,128]{1,0:T(8,128)(2,1)S(1)}, bf16[896,128]{1,0:T(8,128)(2,1)S(1)}, u32[]{:S(2)}, u32[]{:S(2)}) collective-permute-start(bf16[896,128]{1,0:T(8,128)(2,1)S(1)} %chunk_sum.1.chunk), channel_id=1, source_target_pairs={{0,2},{1,15},{2,0},{3,13},{4,6},{5,11},{6,4},{7,9},{8,10},{9,7},{1... | collective-permute-start | bytes 688136 | tf_op jit(solution)/shard_map/ppermute | solution.py:440
  25.5 13.5 %collective-permute-start.8 = (bf16[896,128]{1,0:T(8,128)(2,1)S(1)}, bf16[896,128]{1,0:T(8,128)(2,1)S(1)}, u32[]{:S(2)}, u32[]{:S(2)}) collective-permute-start(bf16[896,128]{1,0:T(8,128)(2,1)S(1)} %chunk_sum.1.chunk), channel_id=1, source_target_pairs={{0,4},{1,13},{2,6},{3,15},{4,0},{5,9},{6,2},{7,11},{8,12},{9,5},{1... | collective-permute-start | bytes 688136 | tf_op jit(solution)/shard_map/ppermute | solution.py:440
  27.6 11.4 %collective-permute-start.11 = (bf16[896,128]{1,0:T(8,128)(2,1)S(1)}, bf16[896,128]{1,0:T(8,128)(2,1)S(1)}, u32[]{:S(2)}, u32[]{:S(2)}) collective-permute-start(bf16[896,128]{1,0:T(8,128)(2,1)S(1)} %chunk_sum.1.chunk), channel_id=1, source_target_pairs={{0,6},{1,11},{2,4},{3,9},{4,2},{5,15},{6,0},{7,13},{8,14},{9,3},{1... | collective-permute-start | bytes 688136 | tf_op jit(solution)/shard_map/ppermute | solution.py:440
  28.6 10.9 %collective-permute-start.12 = (bf16[896,128]{1,0:T(8,128)(2,1)S(1)}, bf16[896,128]{1,0:T(8,128)(2,1)S(1)}, u32[]{:S(2)}, u32[]{:S(2)}) collective-permute-start(bf16[896,128]{1,0:T(8,128)(2,1)S(1)} %chunk_sum.1.chunk), channel_id=1, source_target_pairs={{0,0},{1,9},{2,2},{3,11},{4,4},{5,13},{6,6},{7,15},{8,8},{9,1},{10... | collective-permute-start | bytes 688136 | tf_op jit(solution)/shard_map/ppermute | solution.py:440
  30.0 9.7 %collective-permute-start.9 = (bf16[896,128]{1,0:T(8,128)(2,1)S(1)}, bf16[896,128]{1,0:T(8,128)(2,1)S(1)}, u32[]{:S(2)}, u32[]{:S(2)}) collective-permute-start(bf16[896,128]{1,0:T(8,128)(2,1)S(1)} %collective-permute-done.7.n0), channel_id=1, source_target_pairs={{0,1},{1,0},{2,3},{3,2},{4,5},{5,4},{6,7},{7,6},{8,9},{9,8},{10,11... | collective-permute-start | bytes 688136 | tf_op jit(solution)/shard_map/ppermute | solution.py:436
  39.0 1.5 %collective-permute-start.10 = (bf16[896,128]{1,0:T(8,128)(2,1)S(1)}, bf16[896,128]{1,0:T(8,128)(2,1)S(1)}, u32[]{:S(2)}, u32[]{:S(2)}) collective-permute-start(bf16[896,128]{1,0:T(8,128)(2,1)S(1)} %collective-permute-done.8.n1), channel_id=1, source_target_pairs={{0,1},{1,0},{2,3},{3,2},{4,5},{5,4},{6,7},{7,6},{8,9},{9,8},{10,11... | collective-permute-start | bytes 688136 | tf_op jit(solution)/shard_map/ppermute | solution.py:436
  39.0 2.7 %collective-permute-start.13 = (bf16[896,128]{1,0:T(8,128)(2,1)S(1)}, bf16[896,128]{1,0:T(8,128)(2,1)S(1)}, u32[]{:S(2)}, u32[]{:S(2)}) collective-permute-start(bf16[896,128]{1,0:T(8,128)(2,1)S(1)} %collective-permute-done.11.n2), channel_id=1, source_target_pairs={{0,1},{1,0},{2,3},{3,2},{4,5},{5,4},{6,7},{7,6},{8,9},{9,8},{10,11... | collective-permute-start | bytes 688136 | tf_op jit(solution)/shard_map/ppermute | solution.py:436
  39.5 2.2 %collective-permute-start.14 = (bf16[896,128]{1,0:T(8,128)(2,1)S(1)}, bf16[896,128]{1,0:T(8,128)(2,1)S(1)}, u32[]{:S(2)}, u32[]{:S(2)}) collective-permute-start(bf16[896,128]{1,0:T(8,128)(2,1)S(1)} %collective-permute-done.12.n3), channel_id=1, source_target_pairs={{0,1},{1,0},{2,3},{3,2},{4,5},{5,4},{6,7},{7,6},{8,9},{9,8},{10,11... | collective-permute-start | bytes 688136 | tf_op jit(solution)/shard_map/ppermute | solution.py:436
  43.1 6.3 %collective-permute-start.15 = (bf16[256,128]{1,0:T(8,128)(2,1)S(1)}, bf16[256,128]{1,0:T(8,128)(2,1)S(1)}, u32[]{:S(2)}, u32[]{:S(2)}) collective-permute-start(bf16[256,128]{1,0:T(8,128)(2,1)S(1)} %get-tuple-element.35), channel_id=1, source_target_pairs={{0,128},{1,129},{2,130},{3,131},{4,132},{5,133},{6,134},{7,135},{8... | collective-permute-start | bytes 196616 | tf_op jit(solution)/shard_map/ppermute | solution.py:465
  44.4 5.0 %collective-permute-start.16 = (bf16[256,128]{1,0:T(8,128)(2,1)S(1)}, bf16[256,128]{1,0:T(8,128)(2,1)S(1)}, u32[]{:S(2)}, u32[]{:S(2)}) collective-permute-start(bf16[256,128]{1,0:T(8,128)(2,1)S(1)} %get-tuple-element.36), channel_id=1, source_target_pairs={{0,64},{1,193},{2,66},{3,195},{4,68},{5,197},{6,70},{7,199},{8,72}... | collective-permute-start | bytes 196616 | tf_op jit(solution)/shard_map/ppermute | solution.py:465
  46.6 5.5 %collective-permute-start.17 = (bf16[256,128]{1,0:T(8,128)(2,1)S(1)}, bf16[256,128]{1,0:T(8,128)(2,1)S(1)}, u32[]{:S(2)}, u32[]{:S(2)}) collective-permute-start(bf16[256,128]{1,0:T(8,128)(2,1)S(1)} %get-tuple-element.37), channel_id=1, source_target_pairs={{0,192},{1,65},{2,194},{3,67},{4,196},{5,69},{6,198},{7,71},{8,200... | collective-permute-start | bytes 196616 | tf_op jit(solution)/shard_map/ppermute | solution.py:465
  52.1 5.5 %collective-permute-start.18 = (bf16[128,128]{1,0:T(8,128)(2,1)S(1)}, bf16[128,128]{1,0:T(8,128)(2,1)S(1)}, u32[]{:S(2)}, u32[]{:S(2)}) collective-permute-start(bf16[128,128]{1,0:T(8,128)(2,1)S(1)} %get-tuple-element.41), channel_id=1, source_target_pairs={{0,16},{16,0},{32,48},{48,32},{64,80},{80,64},{96,112},{112,96},{1... | collective-permute-start | bytes 98312 | tf_op jit(solution)/shard_map/ppermute | solution.py:467
  57.6 8.7 %collective-permute-start.19 = (bf16[64,128]{1,0:T(8,128)(2,1)S(1)}, bf16[64,128]{1,0:T(8,128)(2,1)S(1)}, u32[]{:S(2)}, u32[]{:S(2)}) collective-permute-start(bf16[64,128]{1,0:T(8,128)(2,1)S(1)} %get-tuple-element.43), channel_id=1, source_target_pairs={{0,48},{16,32},{32,16},{48,0},{64,112},{80,96},{96,80},{112,64},{1... | collective-permute-start | bytes 49160 | tf_op jit(solution)/shard_map/ppermute | solution.py:468

commit v10 on v9

--- a/solution.py
+++ b/solution.py
@@ -28,6 +28,7 @@
 )
 NEAR_EARLY, NEAR_LATE, FAR_EARLY, FAR_LATE = range(4)
 LINE = ((2, 2), (1, 3), (3, 1))
+HIGH = ((2, 2), (1, 3), (3, 1))
 
 
 def vm():
@@ -366,70 +367,58 @@
     )(lists, turned, first, *near, *far)
 
 
-def line_kernel(own, g0, g1, g2, keep, send, acc):
+def line_kernel(own, g0, g1, g2, keep, s0, s1, s2, acc):
     total = own[...]
     for got in (g0, g1, g2):
         total = total + got[...].astype(jnp.float32)
     acc[...] = total
     _, zh = kmer_place()
-    size = keep.shape[0] // 2
-    peer = zh + 1 - 2 * lax.rem(zh, 2)
-    for k, (mine, theirs) in enumerate(((zh, peer), (3 - zh, 3 - peer))):
-        keep[pl.ds(k * size, size), :] = acc[share_at(mine, size), :]
-        send[pl.ds(k * size, size), :] = acc[share_at(theirs, size), :].astype(jnp.bfloat16)
+    _, _, c = place()
+    size = keep.shape[0]
+    for moves, send in zip(HIGH, (s0, s1, s2)):
+        peer = jnp.bitwise_xor(zh, jnp.where(c == 0, moves[0], moves[1]))
+        send[...] = acc[share_at(peer, size), :].astype(jnp.bfloat16)
+    keep[...] = acc[share_at(zh, size), :]
 
 
 def line_sum(own, got):
-    half = own.shape[0] // 2
+    share = own.shape[0] // 4
+    send = jax.ShapeDtypeStruct((share, TILE), jnp.bfloat16)
     return pl.pallas_call(
         line_kernel,
-        out_shape=[
-            jax.ShapeDtypeStruct((half, TILE), jnp.float32),
-            jax.ShapeDtypeStruct((half, TILE), jnp.bfloat16),
-        ],
+        out_shape=[jax.ShapeDtypeStruct((share, TILE), jnp.float32), send, send, send],
         in_specs=[vm()] * 4,
-        out_specs=[vm()] * 2,
+        out_specs=[vm()] * 4,
         scratch_shapes=[pltpu.VMEM(own.shape, jnp.float32)],
         compiler_params=params(),
         name="line_sum",
     )(own, *got)
 
 
-def halve_kernel(own, got, keep, send):
-    size = keep.shape[0]
-    total = own[...] + got[...].astype(jnp.float32)
-    keep[...] = total[:size]
-    send[...] = total[size:].astype(jnp.bfloat16)
-
-
-def halve_sum(own, got):
-    half = own.shape[0] // 2
-    return pl.pallas_call(
-        halve_kernel,
-        out_shape=[
-            jax.ShapeDtypeStruct((half, TILE), jnp.float32),
-            jax.ShapeDtypeStruct((half, TILE), jnp.bfloat16),
-        ],
-        in_specs=[vm()] * 2,
-        out_specs=[vm()] * 2,
-        compiler_params=params(),
-        name="halve_sum",
-    )(own, got)
-
-
-def last_kernel(factor, own, got, out):
-    out[...] = (own[...] + got[...].astype(jnp.float32)) * factor
+def last_kernel(factor, own, g0, g1, g2, out):
+    total = own[...]
+    for got in (g0, g1, g2):
+        total = total + got[...].astype(jnp.float32)
+    out[...] = total * factor
 
 
 def last_sum(factor, own, got):
     return pl.pallas_call(
         functools.partial(last_kernel, factor),
         out_shape=jax.ShapeDtypeStruct(own.shape, jnp.float32),
-        in_specs=[vm()] * 2,
+        in_specs=[vm()] * 4,
         out_specs=vm(),
         compiler_params=params(),
         name="last_sum",
-    )(own, got)
+    )(own, *got)
+
+
+def high_pairs(moves):
+    return [
+        (i * 16 + j, (i // 4 * 4 + (i % 4 ^ moves[j % 2])) * 16 + j)
+        for i in range(16)
+        for j in range(16)
+    ]
 
 
 def swap(value):
@@ -463,9 +452,8 @@
     keep, *shares = backward_late(lists, turned, first, near[2:], far[2:])
     sketch = sketch_rows(after(chunk, *shares))
     got = [lax.ppermute(s, ("kmer", "samp"), y_pairs(r)) for r, s in enumerate(shares)]
-    keep, share = line_sum(keep, got)
-    keep, share = halve_sum(keep, lax.ppermute(share, "kmer", [(i, i ^ 1) for i in range(16)]))
-    got = lax.ppermute(share, "kmer", [(i, i // 4 * 4 + 3 - i % 4) for i in range(16)])
+    keep, *shares = line_sum(keep, got)
+    got = [lax.ppermute(s, ("kmer", "samp"), high_pairs(m)) for s, m in zip(shares, HIGH)]
     factor = 1.0 / (KB_DEV * TILE * kmers) ** 0.5
     return sketch, last_sum(factor, keep, got)
 

time: 66.3 us -> 67.5 us (1.018); the launches traced: 66.9 us -> 66.9 us
  waiting for transfers between devices: 25.4 us -> 28.1 us
  starting transfers between devices: 29.5 us -> 26.9 us
    ppermute x2 -> x3, starting transfers between devices: 10.6 us -> 8.33 us  [shards(): lax.ppermute(s, ('kmer', 'samp'), high_pairs(m))]
    ppermute x2 -> x3, waiting for transfers between devices: 2.96 us -> 5.19 us  [shards(): lax.ppermute(s, ('kmer', 'samp'), high_pairs(m))]
  transfers between devices with their start and end apart: 20 -> 21, of which waited for: 11 -> 11; matrix products, arithmetic and copies ran while one was open for 0% -> 0% of each run, Pallas kernels for 8% -> 8%
where the time goes in v10:
time: 67.5 us; the launch traced here: 66.9 us
  waiting for transfers between devices  28.1 us (42%)
  starting transfers between devices  26.9 us (40%)
  Pallas kernels  10.5 us (16%)
  between operations  1.42 us (2%)
    ppermute x8, waiting for transfers between devices, trade(): return lax.ppermute(value, 'samp', round_pairs(p))  13.6 us
    ppermute x8, starting transfers between devices, trade(): return lax.ppermute(value, 'samp', round_pairs(p))  12.6 us
    ppermute x3, starting transfers between devices, shards(): lax.ppermute(s, ('kmer', 'samp'), high_pairs(m))  8.33 us
    ppermute x3, waiting for transfers between devices, shards(): lax.ppermute(s, ('kmer', 'samp'), y_pairs(r))  5.47 us
    ppermute x3, waiting for transfers between devices, shards(): lax.ppermute(s, ('kmer', 'samp'), high_pairs(m))  5.19 us
    ppermute x7, waiting for transfers between devices, swap(): return lax.ppermute(value, 'samp', [(s, s ^ 1) for s in range(16)])  3.83 us
    ppermute x3, starting transfers between devices, shards(): lax.ppermute(s, ('kmer', 'samp'), y_pairs(r))  3.23 us
    pallas_call x1, Pallas kernels, forward_first(): pl.pallas_call(forward_first_kernel, out_shape=[jax.ShapeDtypeStruct((PAR...  3.08 us
  transfers between devices with their start and end apart: 21, of which 11 were waited for; matrix products, arithmetic and copies ran while one was open for 0% of the time, Pallas kernels for 8%

profile of v10, /device:TPU:24, one launch (start us, length us, event | category | flops | bytes accessed | tf_op | source)
XLA Modules:
  0.0 66.9 jit_solution(16196472595284486076)
XLA Ops:
  1.3 3.1 %forward_first.1 = (bf16[1792,128]{1,0:T(8,128)(2,1)S(1)}, bf16[88,128,128]{2,1,0:T(8,128)(2,1)S(1)}, bf16[1024,128]{1,0:T(8,128)(2,1)S(1)}, s32[512]{0:T(512)S(1)}) custom-call(s32[88]{0:T(128)} %rows.1, s32[88]{0:T(128)} %cols.1, s32[1]{0:T(128)S(6)} %copy.7.count, bf16[88,128,128]{2,1,0:T(8,128)(2,1)} %tiles.1, bf16[1024,128]{1,0:T(8,128)(2,1)} %omega.1), custom_call_target="tpu_custom_call" | custom-call | tf_op jit(solution)/shard_map/forward_first/pallas_call | solution.py:177
  4.5 1.0 %forward_next0.1.a = bf16[1792,128]{1,0:T(8,128)(2,1)S(1)} custom-call(s32[512]{0:T(512)S(1)} %get-tuple-element.23.lists, bf16[88,128,128]{2,1,0:T(8,128)(2,1)S(1)} %get-tuple-element.32.held.tiles, bf16[1024,128]{1,0:T(8,128)(2,1)S(1)} %get-tuple-element.25.table), custom_call_target="tpu_custom_call" | custom-call | flops 18454937600 | bytes 144179200 | tf_op jit(solution)/shard_map/forward_next0/pallas_call | solution.py:206
  5.4 0.8 %collective-permute-done.b = bf16[1792,128]{1,0:T(8,128)(2,1)S(1)} collective-permute-done((bf16[1792,128]{1,0:T(8,128)(2,1)S(1)}, bf16[1792,128]{1,0:T(8,128)(2,1)S(1)}, u32[]{:S(2)}, u32[]{:S(2)}) %collective-permute-start) | collective-permute-done | bytes 458784 | tf_op jit(solution)/shard_map/ppermute | solution.py:425
  6.4 1.6 %collective-permute-start.1 = (bf16[896,128]{1,0:T(8,128)(2,1)S(1)}, bf16[896,128]{1,0:T(8,128)(2,1)S(1)}, u32[]{:S(2)}, u32[]{:S(2)}) collective-permute-start(bf16[896,128]{1,0:T(8,128)(2,1)S(1)} %get-tuple-element.27), channel_id=1, source_target_pairs={{0,2},{1,15},{2,0},{3,13},{4,6},{5,11},{6,4},{7,9},{8,10},{9,7},{1... | collective-permute-start | bytes 688136 | tf_op jit(solution)/shard_map/ppermute | solution.py:429
  8.0 2.7 %collective-permute-start.2 = (bf16[896,128]{1,0:T(8,128)(2,1)S(1)}, bf16[896,128]{1,0:T(8,128)(2,1)S(1)}, u32[]{:S(2)}, u32[]{:S(2)}) collective-permute-start(bf16[896,128]{1,0:T(8,128)(2,1)S(1)} %get-tuple-element.28), channel_id=1, source_target_pairs={{0,4},{1,13},{2,6},{3,15},{4,0},{5,9},{6,2},{7,11},{8,12},{9,5},{1... | collective-permute-start | bytes 688136 | tf_op jit(solution)/shard_map/ppermute | solution.py:429
  10.7 1.0 %forward_next3.1 = bf16[1792,128]{1,0:T(8,128)(2,1)S(1)} custom-call(s32[512]{0:T(512)S(1)} %get-tuple-element.23.lists, bf16[88,128,128]{2,1,0:T(8,128)(2,1)S(1)} %get-tuple-element.32.held.tiles, bf16[1024,128]{1,0:T(8,128)(2,1)S(1)} %get-tuple-element.25.table), custom_call_target="tpu_custom_call" | custom-call | flops 18454937600 | bytes 144179200 | tf_op jit(solution)/shard_map/forward_next3/pallas_call | solution.py:206
  11.9 1.0 %forward_next1.1.a = bf16[1792,128]{1,0:T(8,128)(2,1)S(1)} custom-call(s32[512]{0:T(512)S(1)} %get-tuple-element.23.lists, bf16[88,128,128]{2,1,0:T(8,128)(2,1)S(1)} %get-tuple-element.32.held.tiles, bf16[1024,128]{1,0:T(8,128)(2,1)S(1)} %get-tuple-element.25.table), custom_call_target="tpu_custom_call" | custom-call | flops 18454937600 | bytes 144179200 | tf_op jit(solution)/shard_map/forward_next1/pallas_call | solution.py:206
  12.8 0.7 %collective-permute-done.3.b = bf16[1792,128]{1,0:T(8,128)(2,1)S(1)} collective-permute-done((bf16[1792,128]{1,0:T(8,128)(2,1)S(1)}, bf16[1792,128]{1,0:T(8,128)(2,1)S(1)}, u32[]{:S(2)}, u32[]{:S(2)}) %collective-permute-start.3) | collective-permute-done | bytes 458784 | tf_op jit(solution)/shard_map/ppermute | solution.py:425
  13.7 2.2 %collective-permute-start.4 = (bf16[896,128]{1,0:T(8,128)(2,1)S(1)}, bf16[896,128]{1,0:T(8,128)(2,1)S(1)}, u32[]{:S(2)}, u32[]{:S(2)}) collective-permute-start(bf16[896,128]{1,0:T(8,128)(2,1)S(1)} %get-tuple-element.30), channel_id=1, source_target_pairs={{0,6},{1,11},{2,4},{3,9},{4,2},{5,15},{6,0},{7,13},{8,14},{9,3},{1... | collective-permute-start | bytes 688136 | tf_op jit(solution)/shard_map/ppermute | solution.py:429
  15.8 0.7 collective-permute-start.5
  16.9 5.2 %collective-permute-done.2.refs_1_ = bf16[896,128]{1,0:T(8,128)(2,1)S(1)} collective-permute-done((bf16[896,128]{1,0:T(8,128)(2,1)S(1)}, bf16[896,128]{1,0:T(8,128)(2,1)S(1)}, u32[]{:S(2)}, u32[]{:S(2)}) %collective-permute-start.2) | collective-permute-done | bytes 229408 | tf_op jit(solution)/shard_map/ppermute | solution.py:429
  22.4 1.4 %collective-permute-done.6.refs_1_ = bf16[896,128]{1,0:T(8,128)(2,1)S(1)} collective-permute-done((bf16[896,128]{1,0:T(8,128)(2,1)S(1)}, bf16[896,128]{1,0:T(8,128)(2,1)S(1)}, u32[]{:S(2)}, u32[]{:S(2)}) %collective-permute-start.6) | collective-permute-done | bytes 229408 | tf_op jit(solution)/shard_map/ppermute | solution.py:425
  23.8 1.4 %collective-permute-start.7 = (bf16[896,128]{1,0:T(8,128)(2,1)S(1)}, bf16[896,128]{1,0:T(8,128)(2,1)S(1)}, u32[]{:S(2)}, u32[]{:S(2)}) collective-permute-start(bf16[896,128]{1,0:T(8,128)(2,1)S(1)} %chunk_sum.1.chunk), channel_id=1, source_target_pairs={{0,2},{1,15},{2,0},{3,13},{4,6},{5,11},{6,4},{7,9},{8,10},{9,7},{1... | collective-permute-start | bytes 688136 | tf_op jit(solution)/shard_map/ppermute | solution.py:429
  25.2 2.7 %collective-permute-start.8 = (bf16[896,128]{1,0:T(8,128)(2,1)S(1)}, bf16[896,128]{1,0:T(8,128)(2,1)S(1)}, u32[]{:S(2)}, u32[]{:S(2)}) collective-permute-start(bf16[896,128]{1,0:T(8,128)(2,1)S(1)} %chunk_sum.1.chunk), channel_id=1, source_target_pairs={{0,4},{1,13},{2,6},{3,15},{4,0},{5,9},{6,2},{7,11},{8,12},{9,5},{1... | collective-permute-start | bytes 688136 | tf_op jit(solution)/shard_map/ppermute | solution.py:429
  27.9 0.7 %collective-permute-start.11 = (bf16[896,128]{1,0:T(8,128)(2,1)S(1)}, bf16[896,128]{1,0:T(8,128)(2,1)S(1)}, u32[]{:S(2)}, u32[]{:S(2)}) collective-permute-start(bf16[896,128]{1,0:T(8,128)(2,1)S(1)} %chunk_sum.1.chunk), channel_id=1, source_target_pairs={{0,6},{1,11},{2,4},{3,9},{4,2},{5,15},{6,0},{7,13},{8,14},{9,3},{1... | collective-permute-start | bytes 688136 | tf_op jit(solution)/shard_map/ppermute | solution.py:429
  28.6 0.7 collective-permute-start.12
  29.3 0.7 collective-permute-done.7.n0
  29.9 1.6 %collective-permute-start.9 = (bf16[896,128]{1,0:T(8,128)(2,1)S(1)}, bf16[896,128]{1,0:T(8,128)(2,1)S(1)}, u32[]{:S(2)}, u32[]{:S(2)}) collective-permute-start(bf16[896,128]{1,0:T(8,128)(2,1)S(1)} %collective-permute-done.7.n0), channel_id=1, source_target_pairs={{0,1},{1,0},{2,3},{3,2},{4,5},{5,4},{6,7},{7,6},{8,9},{9,8},{10,11... | collective-permute-start | bytes 688136 | tf_op jit(solution)/shard_map/ppermute | solution.py:425
  31.6 7.7 %collective-permute-done.8.n1 = bf16[896,128]{1,0:T(8,128)(2,1)S(1)} collective-permute-done((bf16[896,128]{1,0:T(8,128)(2,1)S(1)}, bf16[896,128]{1,0:T(8,128)(2,1)S(1)}, u32[]{:S(2)}, u32[]{:S(2)}) %collective-permute-start.8) | collective-permute-done | bytes 229408 | tf_op jit(solution)/shard_map/ppermute | solution.py:429
  39.9 0.9 %collective-permute-done.10.f1 = bf16[896,128]{1,0:T(8,128)(2,1)S(1)} collective-permute-done((bf16[896,128]{1,0:T(8,128)(2,1)S(1)}, bf16[896,128]{1,0:T(8,128)(2,1)S(1)}, u32[]{:S(2)}, u32[]{:S(2)}) %collective-permute-start.10) | collective-permute-done | bytes 229408 | tf_op jit(solution)/shard_map/ppermute | solution.py:425
  40.8 1.2 %backward_early.1.first = f32[1152,128]{1,0:T(8,128)S(1)} custom-call(s32[512]{0:T(512)S(1)} %get-tuple-element.23.lists, bf16[88,128,128]{2,1,0:T(8,128)(2,1)S(1)} %turn_tiles.1.turned, bf16[896,128]{1,0:T(8,128)(2,1)S(1)} %collective-permute-done.7.n0, bf16[896,128]{1,0:T(8,128)(2,1)S(1)} %collective-permute-done.8.n1, ...), custom_call_target="tpu_custom_call" | custom-call | flops 18454937600 | bytes 144179200 | tf_op jit(solution)/shard_map/backward_early/pallas_call | solution.py:322
  42.1 1.3 %backward_late.1 = (f32[256,128]{1,0:T(8,128)S(1)}, bf16[256,128]{1,0:T(8,128)(2,1)S(1)}, bf16[256,128]{1,0:T(8,128)(2,1)S(1)}, bf16[256,128]{1,0:T(8,128)(2,1)S(1)}) custom-call(s32[512]{0:T(512)S(1)} %get-tuple-element.23.lists, bf16[88,128,128]{2,1,0:T(8,128)(2,1)S(1)} %turn_tiles.1.turned, f32[1152,128]{1,0:T(8,128)S(1)} %backward_early.1.first, ...), custom_call_target="tpu_custom_call" | custom-call | tf_op jit(solution)/shard_map/backward_late/pallas_call | solution.py:356
  43.3 1.1 %collective-permute-start.15 = (bf16[256,128]{1,0:T(8,128)(2,1)S(1)}, bf16[256,128]{1,0:T(8,128)(2,1)S(1)}, u32[]{:S(2)}, u32[]{:S(2)}) collective-permute-start(bf16[256,128]{1,0:T(8,128)(2,1)S(1)} %get-tuple-element.35), channel_id=1, source_target_pairs={{0,128},{1,129},{2,130},{3,131},{4,132},{5,133},{6,134},{7,135},{8... | collective-permute-start | bytes 196616 | tf_op jit(solution)/shard_map/ppermute | solution.py:454
  44.4 2.2 %collective-permute-start.16 = (bf16[256,128]{1,0:T(8,128)(2,1)S(1)}, bf16[256,128]{1,0:T(8,128)(2,1)S(1)}, u32[]{:S(2)}, u32[]{:S(2)}) collective-permute-start(bf16[256,128]{1,0:T(8,128)(2,1)S(1)} %get-tuple-element.36), channel_id=1, source_target_pairs={{0,64},{1,193},{2,66},{3,195},{4,68},{5,197},{6,70},{7,199},{8,72}... | collective-permute-start | bytes 196616 | tf_op jit(solution)/shard_map/ppermute | solution.py:454
  46.6 2.7 %collective-permute-done.15.g0 = bf16[256,128]{1,0:T(8,128)(2,1)S(1)} collective-permute-done((bf16[256,128]{1,0:T(8,128)(2,1)S(1)}, bf16[256,128]{1,0:T(8,128)(2,1)S(1)}, u32[]{:S(2)}, u32[]{:S(2)}) %collective-permute-start.15) | collective-permute-done | bytes 65568 | tf_op jit(solution)/shard_map/ppermute | solution.py:454
  49.3 2.8 %collective-permute-done.17.g2 = bf16[256,128]{1,0:T(8,128)(2,1)S(1)} collective-permute-done((bf16[256,128]{1,0:T(8,128)(2,1)S(1)}, bf16[256,128]{1,0:T(8,128)(2,1)S(1)}, u32[]{:S(2)}, u32[]{:S(2)}) %collective-permute-start.17) | collective-permute-done | bytes 65568 | tf_op jit(solution)/shard_map/ppermute | solution.py:454
  52.1 6.8 %collective-permute-start.18 = (bf16[64,128]{1,0:T(8,128)(2,1)S(1)}, bf16[64,128]{1,0:T(8,128)(2,1)S(1)}, u32[]{:S(2)}, u32[]{:S(2)}) collective-permute-start(bf16[64,128]{1,0:T(8,128)(2,1)S(1)} %get-tuple-element.41), channel_id=1, source_target_pairs={{0,32},{1,33},{2,34},{3,35},{4,36},{5,37},{6,38},{7,39},{8,40},{9,... | collective-permute-start | bytes 49160 | tf_op jit(solution)/shard_map/ppermute | solution.py:456
  58.9 1.5 %collective-permute-start.19 = (bf16[64,128]{1,0:T(8,128)(2,1)S(1)}, bf16[64,128]{1,0:T(8,128)(2,1)S(1)}, u32[]{:S(2)}, u32[]{:S(2)}) collective-permute-start(bf16[64,128]{1,0:T(8,128)(2,1)S(1)} %get-tuple-element.42), channel_id=1, source_target_pairs={{0,16},{1,49},{2,18},{3,51},{4,20},{5,53},{6,22},{7,55},{8,24},{9,... | collective-permute-start | bytes 49160 | tf_op jit(solution)/shard_map/ppermute | solution.py:456
  60.4 0.7 sketch_rows.1
  61.1 2.5 %collective-permute-done.19.g1 = bf16[64,128]{1,0:T(8,128)(2,1)S(1)} collective-permute-done((bf16[64,128]{1,0:T(8,128)(2,1)S(1)}, bf16[64,128]{1,0:T(8,128)(2,1)S(1)}, u32[]{:S(2)}, u32[]{:S(2)}) %collective-permute-start.19) | collective-permute-done | bytes 16416 | tf_op jit(solution)/shard_map/ppermute | solution.py:456
  63.6 2.7 %collective-permute-done.20.g2 = bf16[64,128]{1,0:T(8,128)(2,1)S(1)} collective-permute-done((bf16[64,128]{1,0:T(8,128)(2,1)S(1)}, bf16[64,128]{1,0:T(8,128)(2,1)S(1)}, u32[]{:S(2)}, u32[]{:S(2)}) %collective-permute-start.20) | collective-permute-done | bytes 16416 | tf_op jit(solution)/shard_map/ppermute | solution.py:456
  66.3 0.6 last_sum.1
  (24 shorter events, 2.0 us)
Async XLA Ops:
  4.4 1.9 %collective-permute-start = (bf16[1792,128]{1,0:T(8,128)(2,1)S(1)}, bf16[1792,128]{1,0:T(8,128)(2,1)S(1)}, u32[]{:S(2)}, u32[]{:S(2)}) collective-permute-start(bf16[1792,128]{1,0:T(8,128)(2,1)S(1)} %get-tuple-element.26), channel_id=1, source_target_pairs={{0,1},{1,0},{2,3},{3,2},{4,5},{5,4},{6,7},{7,6},{8,9},{9,8},{10,11... | collective-permute-start | bytes 1376264 | tf_op jit(solution)/shard_map/ppermute | solution.py:425
  6.4 10.5 %collective-permute-start.1 = (bf16[896,128]{1,0:T(8,128)(2,1)S(1)}, bf16[896,128]{1,0:T(8,128)(2,1)S(1)}, u32[]{:S(2)}, u32[]{:S(2)}) collective-permute-start(bf16[896,128]{1,0:T(8,128)(2,1)S(1)} %get-tuple-element.27), channel_id=1, source_target_pairs={{0,2},{1,15},{2,0},{3,13},{4,6},{5,11},{6,4},{7,9},{8,10},{9,7},{1... | collective-permute-start | bytes 688136 | tf_op jit(solution)/shard_map/ppermute | solution.py:429
  8.0 14.1 %collective-permute-start.2 = (bf16[896,128]{1,0:T(8,128)(2,1)S(1)}, bf16[896,128]{1,0:T(8,128)(2,1)S(1)}, u32[]{:S(2)}, u32[]{:S(2)}) collective-permute-start(bf16[896,128]{1,0:T(8,128)(2,1)S(1)} %get-tuple-element.28), channel_id=1, source_target_pairs={{0,4},{1,13},{2,6},{3,15},{4,0},{5,9},{6,2},{7,11},{8,12},{9,5},{1... | collective-permute-start | bytes 688136 | tf_op jit(solution)/shard_map/ppermute | solution.py:429
  11.6 1.9 %collective-permute-start.3 = (bf16[1792,128]{1,0:T(8,128)(2,1)S(1)}, bf16[1792,128]{1,0:T(8,128)(2,1)S(1)}, u32[]{:S(2)}, u32[]{:S(2)}) collective-permute-start(bf16[1792,128]{1,0:T(8,128)(2,1)S(1)} %forward_next3.1), channel_id=1, source_target_pairs={{0,1},{1,0},{2,3},{3,2},{4,5},{5,4},{6,7},{7,6},{8,9},{9,8},{10,11... | collective-permute-start | bytes 1376264 | tf_op jit(solution)/shard_map/ppermute | solution.py:425
  13.7 8.4 %collective-permute-start.4 = (bf16[896,128]{1,0:T(8,128)(2,1)S(1)}, bf16[896,128]{1,0:T(8,128)(2,1)S(1)}, u32[]{:S(2)}, u32[]{:S(2)}) collective-permute-start(bf16[896,128]{1,0:T(8,128)(2,1)S(1)} %get-tuple-element.30), channel_id=1, source_target_pairs={{0,6},{1,11},{2,4},{3,9},{4,2},{5,15},{6,0},{7,13},{8,14},{9,3},{1... | collective-permute-start | bytes 688136 | tf_op jit(solution)/shard_map/ppermute | solution.py:429
  15.8 6.2 %collective-permute-start.5 = (bf16[896,128]{1,0:T(8,128)(2,1)S(1)}, bf16[896,128]{1,0:T(8,128)(2,1)S(1)}, u32[]{:S(2)}, u32[]{:S(2)}) collective-permute-start(bf16[896,128]{1,0:T(8,128)(2,1)S(1)} %get-tuple-element.31), channel_id=1, source_target_pairs={{0,0},{1,9},{2,2},{3,11},{4,4},{5,13},{6,6},{7,15},{8,8},{9,1},{10... | collective-permute-start | bytes 688136 | tf_op jit(solution)/shard_map/ppermute | solution.py:429
  22.2 1.6 %collective-permute-start.6 = (bf16[896,128]{1,0:T(8,128)(2,1)S(1)}, bf16[896,128]{1,0:T(8,128)(2,1)S(1)}, u32[]{:S(2)}, u32[]{:S(2)}) collective-permute-start(bf16[896,128]{1,0:T(8,128)(2,1)S(1)} %part_sum.1.refs_0_), channel_id=1, source_target_pairs={{0,1},{1,0},{2,3},{3,2},{4,5},{5,4},{6,7},{7,6},{8,9},{9,8},{10,11... | collective-permute-start | bytes 688136 | tf_op jit(solution)/shard_map/ppermute | solution.py:425
  23.8 6.1 %collective-permute-start.7 = (bf16[896,128]{1,0:T(8,128)(2,1)S(1)}, bf16[896,128]{1,0:T(8,128)(2,1)S(1)}, u32[]{:S(2)}, u32[]{:S(2)}) collective-permute-start(bf16[896,128]{1,0:T(8,128)(2,1)S(1)} %chunk_sum.1.chunk), channel_id=1, source_target_pairs={{0,2},{1,15},{2,0},{3,13},{4,6},{5,11},{6,4},{7,9},{8,10},{9,7},{1... | collective-permute-start | bytes 688136 | tf_op jit(solution)/shard_map/ppermute | solution.py:429
  25.2 14.1 %collective-permute-start.8 = (bf16[896,128]{1,0:T(8,128)(2,1)S(1)}, bf16[896,128]{1,0:T(8,128)(2,1)S(1)}, u32[]{:S(2)}, u32[]{:S(2)}) collective-permute-start(bf16[896,128]{1,0:T(8,128)(2,1)S(1)} %chunk_sum.1.chunk), channel_id=1, source_target_pairs={{0,4},{1,13},{2,6},{3,15},{4,0},{5,9},{6,2},{7,11},{8,12},{9,5},{1... | collective-permute-start | bytes 688136 | tf_op jit(solution)/shard_map/ppermute | solution.py:429
  27.9 11.4 %collective-permute-start.11 = (bf16[896,128]{1,0:T(8,128)(2,1)S(1)}, bf16[896,128]{1,0:T(8,128)(2,1)S(1)}, u32[]{:S(2)}, u32[]{:S(2)}) collective-permute-start(bf16[896,128]{1,0:T(8,128)(2,1)S(1)} %chunk_sum.1.chunk), channel_id=1, source_target_pairs={{0,6},{1,11},{2,4},{3,9},{4,2},{5,15},{6,0},{7,13},{8,14},{9,3},{1... | collective-permute-start | bytes 688136 | tf_op jit(solution)/shard_map/ppermute | solution.py:429
  28.6 11.2 %collective-permute-start.12 = (bf16[896,128]{1,0:T(8,128)(2,1)S(1)}, bf16[896,128]{1,0:T(8,128)(2,1)S(1)}, u32[]{:S(2)}, u32[]{:S(2)}) collective-permute-start(bf16[896,128]{1,0:T(8,128)(2,1)S(1)} %chunk_sum.1.chunk), channel_id=1, source_target_pairs={{0,0},{1,9},{2,2},{3,11},{4,4},{5,13},{6,6},{7,15},{8,8},{9,1},{10... | collective-permute-start | bytes 688136 | tf_op jit(solution)/shard_map/ppermute | solution.py:429
  29.9 10.0 %collective-permute-start.9 = (bf16[896,128]{1,0:T(8,128)(2,1)S(1)}, bf16[896,128]{1,0:T(8,128)(2,1)S(1)}, u32[]{:S(2)}, u32[]{:S(2)}) collective-permute-start(bf16[896,128]{1,0:T(8,128)(2,1)S(1)} %collective-permute-done.7.n0), channel_id=1, source_target_pairs={{0,1},{1,0},{2,3},{3,2},{4,5},{5,4},{6,7},{7,6},{8,9},{9,8},{10,11... | collective-permute-start | bytes 688136 | tf_op jit(solution)/shard_map/ppermute | solution.py:425
  39.3 1.5 %collective-permute-start.10 = (bf16[896,128]{1,0:T(8,128)(2,1)S(1)}, bf16[896,128]{1,0:T(8,128)(2,1)S(1)}, u32[]{:S(2)}, u32[]{:S(2)}) collective-permute-start(bf16[896,128]{1,0:T(8,128)(2,1)S(1)} %collective-permute-done.8.n1), channel_id=1, source_target_pairs={{0,1},{1,0},{2,3},{3,2},{4,5},{5,4},{6,7},{7,6},{8,9},{9,8},{10,11... | collective-permute-start | bytes 688136 | tf_op jit(solution)/shard_map/ppermute | solution.py:425
  39.3 2.7 %collective-permute-start.13 = (bf16[896,128]{1,0:T(8,128)(2,1)S(1)}, bf16[896,128]{1,0:T(8,128)(2,1)S(1)}, u32[]{:S(2)}, u32[]{:S(2)}) collective-permute-start(bf16[896,128]{1,0:T(8,128)(2,1)S(1)} %collective-permute-done.11.n2), channel_id=1, source_target_pairs={{0,1},{1,0},{2,3},{3,2},{4,5},{5,4},{6,7},{7,6},{8,9},{9,8},{10,11... | collective-permute-start | bytes 688136 | tf_op jit(solution)/shard_map/ppermute | solution.py:425
  39.8 2.2 %collective-permute-start.14 = (bf16[896,128]{1,0:T(8,128)(2,1)S(1)}, bf16[896,128]{1,0:T(8,128)(2,1)S(1)}, u32[]{:S(2)}, u32[]{:S(2)}) collective-permute-start(bf16[896,128]{1,0:T(8,128)(2,1)S(1)} %collective-permute-done.12.n3), channel_id=1, source_target_pairs={{0,1},{1,0},{2,3},{3,2},{4,5},{5,4},{6,7},{7,6},{8,9},{9,8},{10,11... | collective-permute-start | bytes 688136 | tf_op jit(solution)/shard_map/ppermute | solution.py:425
  43.3 5.9 %collective-permute-start.15 = (bf16[256,128]{1,0:T(8,128)(2,1)S(1)}, bf16[256,128]{1,0:T(8,128)(2,1)S(1)}, u32[]{:S(2)}, u32[]{:S(2)}) collective-permute-start(bf16[256,128]{1,0:T(8,128)(2,1)S(1)} %get-tuple-element.35), channel_id=1, source_target_pairs={{0,128},{1,129},{2,130},{3,131},{4,132},{5,133},{6,134},{7,135},{8... | collective-permute-start | bytes 196616 | tf_op jit(solution)/shard_map/ppermute | solution.py:454
  44.4 4.9 %collective-permute-start.16 = (bf16[256,128]{1,0:T(8,128)(2,1)S(1)}, bf16[256,128]{1,0:T(8,128)(2,1)S(1)}, u32[]{:S(2)}, u32[]{:S(2)}) collective-permute-start(bf16[256,128]{1,0:T(8,128)(2,1)S(1)} %get-tuple-element.36), channel_id=1, source_target_pairs={{0,64},{1,193},{2,66},{3,195},{4,68},{5,197},{6,70},{7,199},{8,72}... | collective-permute-start | bytes 196616 | tf_op jit(solution)/shard_map/ppermute | solution.py:454
  46.6 5.5 %collective-permute-start.17 = (bf16[256,128]{1,0:T(8,128)(2,1)S(1)}, bf16[256,128]{1,0:T(8,128)(2,1)S(1)}, u32[]{:S(2)}, u32[]{:S(2)}) collective-permute-start(bf16[256,128]{1,0:T(8,128)(2,1)S(1)} %get-tuple-element.37), channel_id=1, source_target_pairs={{0,192},{1,65},{2,194},{3,67},{4,196},{5,69},{6,198},{7,71},{8,200... | collective-permute-start | bytes 196616 | tf_op jit(solution)/shard_map/ppermute | solution.py:454
  52.1 9.0 %collective-permute-start.18 = (bf16[64,128]{1,0:T(8,128)(2,1)S(1)}, bf16[64,128]{1,0:T(8,128)(2,1)S(1)}, u32[]{:S(2)}, u32[]{:S(2)}) collective-permute-start(bf16[64,128]{1,0:T(8,128)(2,1)S(1)} %get-tuple-element.41), channel_id=1, source_target_pairs={{0,32},{1,33},{2,34},{3,35},{4,36},{5,37},{6,38},{7,39},{8,40},{9,... | collective-permute-start | bytes 49160 | tf_op jit(solution)/shard_map/ppermute | solution.py:456
  58.9 4.6 %collective-permute-start.19 = (bf16[64,128]{1,0:T(8,128)(2,1)S(1)}, bf16[64,128]{1,0:T(8,128)(2,1)S(1)}, u32[]{:S(2)}, u32[]{:S(2)}) collective-permute-start(bf16[64,128]{1,0:T(8,128)(2,1)S(1)} %get-tuple-element.42), channel_id=1, source_target_pairs={{0,16},{1,49},{2,18},{3,51},{4,20},{5,53},{6,22},{7,55},{8,24},{9,... | collective-permute-start | bytes 49160 | tf_op jit(solution)/shard_map/ppermute | solution.py:456
  60.4 5.8 %collective-permute-start.20 = (bf16[64,128]{1,0:T(8,128)(2,1)S(1)}, bf16[64,128]{1,0:T(8,128)(2,1)S(1)}, u32[]{:S(2)}, u32[]{:S(2)}) collective-permute-start(bf16[64,128]{1,0:T(8,128)(2,1)S(1)} %get-tuple-element.43), channel_id=1, source_target_pairs={{0,48},{1,17},{2,50},{3,19},{4,52},{5,21},{6,54},{7,23},{8,56},{9,... | collective-permute-start | bytes 49160 | tf_op jit(solution)/shard_map/ppermute | solution.py:456
